TPU v7x, 32 devices: a whole 2x2x4 slice. The times are simulated.
32 devices in a mesh: atoms: 8 (over z, core), kvec: 4 (over y, x).
Axes of the slice: x: 2, y: 2, z: 4, core: 2. Of those that a mesh axis runs over, the one named last changes fastest.
Arguments:
- positions: float32 [3, 8192], P(None, ('atoms', 'kvec')), may hold values from 0 to 8
- features: bfloat16 [8192, 128], P(('atoms', 'kvec')), may hold values from -6 to 6
- atom_mask: int32 [8192], P(('atoms', 'kvec')), may hold values 0 or 1
- neighbours: int32 [64, 12], P(('atoms', 'kvec')), may hold values from 0 to 63, as said below
- lattice: int32 [3, 12288], P(None, 'kvec'), may hold values from -15 to 15, as said below
- pair_weight: bfloat16 [1024, 128], replicated, may hold values from -0.1875 to 0.1875
- kfilter: float32 [8, 128], replicated, may hold values from -4 to 4
- norm_gain: float32 [128], replicated, may hold values from 0.25 to 1.75
- w_in: bfloat16 [128, 512], replicated, may hold values from -0.5 to 0.5
- w_out: bfloat16 [512, 128], replicated, may hold values from -0.25 to 0.25
Outputs:
- updated: bfloat16 [8192, 128], P(('atoms', 'kvec'))
Inputs may be any that keep to these rules, and one draw needn't show every extreme that they name: `neighbours`: group of a block = its id // 8. The 12 ids of a block are different and each lies in the block's group, the group below or the group above it, cyclically over the 8 groups. `lattice`: the 12288 wavevectors are distinct, none is zero, and no two are negatives of each other.
All inputs are finite; a program needn't handle non-finite values. No bound on the sum of `atom_mask` on one device may be relied on, other than what follows from the above.
Results may differ from a plain program's by a relative error of at most 0.017.
Values may be sent and summed in bfloat16 or wider, within the bound.
No kernel may reach another device: no remote copies, remote signals or barrier semaphores. Data moves between devices by JAX's collectives and lax.ppermute only.
A program may use at most 64 MiB of HBM per device.

v0:
```python
import functools
import math

import jax
import jax.numpy as jnp
from jax import lax
from jax.experimental import pallas as pl
from jax.experimental.pallas import tpu as pltpu
from jax.sharding import PartitionSpec as P

KW = 12288
BLOCK_ATOMS = 128
F32 = jnp.float32
BF16 = jnp.bfloat16

SIN_COEF = (4.442879586561992, -7.307818050390618, 3.5977887417720016, -0.7912382192058507)
ROUND = 12582912.0
SLACK = 1e-5
TAIL = 16


def params(mib=16):
    return pltpu.CompilerParams(vmem_limit_bytes=mib << 20)


SMEM = pl.BlockSpec(memory_space=pltpu.SMEM)
VMEM = pl.BlockSpec(memory_space=pltpu.VMEM)
ANY = pl.BlockSpec(memory_space=pl.ANY)


def horner(u, coef):
    acc = coef[-1] * u + coef[-2]
    for c in reversed(coef[:-2]):
        acc = acc * u + c
    return acc


def pack_kernel(features_hbm, mask_hbm, pos_hbm, out_ref, features_ref, mask_ref, pos_ref, scr, sems):
    copies = [
        pltpu.make_async_copy(source, target, sems.at[i])
        for i, (source, target) in enumerate(
            ((features_hbm, features_ref), (mask_hbm, mask_ref), (pos_hbm, pos_ref))
        )
    ]
    for copy in copies:
        copy.start()
    for copy in copies:
        copy.wait()
    channels = features_ref.shape[1]
    mask = mask_ref[...].astype(F32)
    out_ref[0:channels, :] = (features_ref[...].astype(F32).T * mask).astype(BF16)
    value = pos_ref[...] * 0.125
    high = value.astype(BF16).astype(F32)
    rest = value - high
    mid = rest.astype(BF16).astype(F32)
    scr[...] = jnp.zeros_like(scr)
    scr[0:3, :] = high
    scr[3:6, :] = mid
    scr[6:9, :] = rest - mid
    out_ref[channels : channels + TAIL, :] = scr[...].astype(BF16)


def pack(features, mask, positions):
    shard, channels = features.shape
    anywhere = pl.BlockSpec(memory_space=pltpu.HBM)
    return pl.pallas_call(
        pack_kernel,
        in_specs=[anywhere] * 3,
        out_specs=VMEM,
        out_shape=jax.ShapeDtypeStruct((channels + TAIL, shard), BF16),
        scratch_shapes=[
            pltpu.VMEM((shard, channels), BF16),
            pltpu.VMEM((1, shard), jnp.int32),
            pltpu.VMEM((3, shard), F32),
            pltpu.VMEM((TAIL, shard), F32),
            pltpu.SemaphoreType.DMA((3,)),
        ],
        compiler_params=params(),
        name="pack",
    )(*(pltpu.with_memory_space_constraint(x, pltpu.HBM) for x in (features, mask[None, :], positions)))


def setup_kernel(far, nbasis, scale, lattice_ref, kfilter_ref, wave_ref, kfilt_ref, scr):
    blocks, width, _ = wave_ref.shape
    a_index = lax.axis_index("atoms")
    part = a_index % 2 + 2 * (a_index // 4)
    count = blocks * width
    for j in range(blocks):
        lattice = jnp.zeros((3, width), F32)
        for p in range(2 * far):
            at = p * count + j * width
            mine = (part == p).astype(F32)
            lattice += lattice_ref[:, at : at + width].astype(F32) * mine
        scr[...] = jnp.zeros_like(scr)
        for copy in range(3):
            scr[3 * copy : 3 * copy + 3, :] = lattice
        wave_ref[j] = scr[...].T.astype(BF16)
        wave = lattice * (2.0 * math.pi / 8.0)
        kmag = jnp.sqrt(
            wave[0:1] * wave[0:1] + wave[1:2] * wave[1:2] + wave[2:3] * wave[2:3]
        )
        total = jnp.zeros(kfilt_ref.shape[1:], F32)
        for p in range(nbasis):
            basis = jnp.exp(-0.5 * ((kmag - (p + 0.5) * (21.0 / nbasis)) / (21.0 / nbasis)) ** 2)
            total += kfilter_ref[:, p : p + 1] * basis
        kfilt_ref[j] = total * scale


def setup(lattice, kfilter, far, width, scale):
    nbasis, channels = kfilter.shape
    blocks = lattice.shape[1] // (2 * far * width)
    return pl.pallas_call(
        functools.partial(setup_kernel, far, nbasis, scale),
        in_specs=[VMEM] * 2,
        out_specs=[VMEM] * 2,
        out_shape=[
            jax.ShapeDtypeStruct((blocks, width, TAIL), BF16),
            jax.ShapeDtypeStruct((blocks, channels, width), F32),
        ],
        scratch_shapes=[pltpu.VMEM((TAIL, width), F32)],
        compiler_params=params(),
        name="setup",
    )(lattice, kfilter.T)


def wave_kernel(counts, start, waits, low, *refs):
    refs = list(refs)
    take = lambda n: [refs.pop(0) for _ in range(n)]
    (lattice_ref,) = take(1)
    messages = take(len(counts))
    before_ref = None if start else take(1)[0]
    take(waits)
    table_ref, total_ref = take(2)
    low_ref = take(1)[0] if low else None
    feat_scr, pos_scr = take(2)
    phases, buffers = take(2), take(2)
    blocks, width, _ = lattice_ref.shape
    pairs, channels, both = feat_scr.shape
    shard = both // 2
    place = 0
    for ref, count in zip(messages, counts):
        for p in range(count):
            lanes = slice(place % 2 * shard, (place % 2 + 1) * shard)
            feat_scr[place // 2, :, lanes] = ref[p, 0:channels, :]
            pos_scr[place // 2, :, lanes] = ref[p, channels:, :]
            place += 1
    if start:
        total_ref[...] = jnp.zeros_like(total_ref)
    else:
        total_ref[...] = before_ref[...]
    for buffer in buffers:
        buffer[...] = jnp.zeros_like(buffer)
    steps = pairs * blocks

    def phase(i, side):
        phases[side][...] = jnp.dot(
            lattice_ref[i % blocks],
            pos_scr[i // blocks, :, side * shard : (side + 1) * shard],
            preferred_element_type=F32,
        )

    def table(i, side):
        pair, block = i // blocks, i % blocks
        lanes = pl.ds(pl.multiple_of(pair * both + side * shard, shard), shard)
        rows = 16
        for at in range(0, width, rows):
            turns = phases[side][at : at + rows, :]
            r = turns - ((turns + ROUND) - ROUND)
            s = horner(r * r, SIN_COEF) * r
            square = s * s
            w = (2.0 + SLACK) - square
            cosine = (1.0 - square).astype(BF16)
            sine = (s * (w * lax.rsqrt(w))).astype(BF16)
            buffers[side][0, at : at + rows, :] = cosine
            buffers[side][1, at : at + rows, :] = sine
            table_ref[block, at : at + rows, lanes] = cosine
            table_ref[blocks + block, at : at + rows, lanes] = sine

    def product(i):
        pair, block = i // blocks, i % blocks
        for half in range(2):
            parts = [
                lax.dot_general(
                    feat_scr[pair, :, side * shard : (side + 1) * shard],
                    buffers[side][half],
                    (((1,), (1,)), ((), ())),
                    preferred_element_type=F32,
                )
                for side in range(2)
            ]
            total_ref[half * blocks + block] += parts[0] + parts[1]

    phase(0, 0)
    phase(0, 1)

    def body(i, carry):
        later = jnp.minimum(i + 1, steps - 1)
        product(jnp.maximum(i - 1, 0))
        table(i, 0)
        phase(later, 0)
        table(i, 1)
        phase(later, 1)
        return carry

    lax.fori_loop(0, steps, body, 0)
    product(steps - 1)
    if low:
        low_ref[...] = total_ref[...].astype(BF16)


def wave(lattice, messages, before, after=(), low=False):
    blocks, width, _ = lattice.shape
    counts = tuple(x.shape[0] for x in messages)
    pieces = sum(counts)
    rows, shard = messages[0].shape[1:]
    channels = rows - TAIL
    args = [lattice, *messages] + ([] if before is None else [before])
    factor = (2 * blocks, channels, width)
    shapes = [
        jax.ShapeDtypeStruct((2 * blocks, width, pieces * shard), BF16),
        jax.ShapeDtypeStruct(factor, F32),
    ]
    if low:
        shapes.append(jax.ShapeDtypeStruct(factor, BF16))
    pairs = blocks * width * pieces * shard
    return pl.pallas_call(
        functools.partial(wave_kernel, counts, before is None, len(after), low),
        in_specs=[VMEM] * len(args) + [ANY] * len(after),
        out_specs=[VMEM] * len(shapes),
        out_shape=shapes,
        scratch_shapes=[
            pltpu.VMEM((pieces // 2, channels, 2 * shard), BF16),
            pltpu.VMEM((pieces // 2, TAIL, 2 * shard), BF16),
            pltpu.VMEM((width, shard), F32),
            pltpu.VMEM((width, shard), F32),
            pltpu.VMEM((2, width, shard), BF16),
            pltpu.VMEM((2, width, shard), BF16),
        ],
        compiler_params=params(),
        cost_estimate=pl.CostEstimate(
            flops=4 * pairs * channels, bytes_accessed=4 * pairs, transcendentals=pairs
        ),
        name="wave",
    )(*args, *after)


def collect_kernel(picks, *refs):
    for p, (array, index) in enumerate(picks):
        ref = refs[array]
        refs[-1][p] = ref[...] if index is None else ref[index]


def collect(arrays, picks, after=()):
    return pl.pallas_call(
        functools.partial(collect_kernel, picks),
        in_specs=[VMEM] * len(arrays) + [ANY] * len(after),
        out_specs=VMEM,
        out_shape=jax.ShapeDtypeStruct((len(picks), *arrays[0].shape[-2:]), BF16),
        compiler_params=params(),
        name="collect",
    )(*arrays, *after)


def transform(filt_ref, parts, out_ref, shard):
    blocks = filt_ref.shape[0]
    at = 0
    for table_ref, first, pieces in parts:
        for p in range(first, first + pieces):
            acc = jnp.dot(
                filt_ref[0], table_ref[0, :, p * shard : (p + 1) * shard], preferred_element_type=F32
            )
            for j in range(1, blocks):
                acc += jnp.dot(
                    filt_ref[j],
                    table_ref[j, :, p * shard : (p + 1) * shard],
                    preferred_element_type=F32,
                )
            out_ref[:, at : at + shard] = acc.astype(out_ref.dtype)
            at += shard


def away_kernel(runs, shard, own_ref, other_ref, kfilt_ref, _, *refs):
    table_refs, (filt_ref, out_ref) = refs[:-2], refs[-2:]
    count = kfilt_ref.shape[0]
    for j in range(2 * count):
        total = own_ref[j] + other_ref[j].astype(F32)
        filt_ref[j] = (total * kfilt_ref[j % count]).astype(BF16)
    transform(filt_ref, [(t, *r) for t, r in zip(table_refs, runs)], out_ref, shard)


def here_kernel(runs, shard, filt_ref, *refs):
    transform(filt_ref, [(t, *r) for t, r in zip(refs[:-1], runs)], refs[-1], shard)


def inverse_cost(filt, atoms):
    return pl.CostEstimate(
        flops=2 * math.prod(filt.shape) * atoms,
        bytes_accessed=2 * math.prod(filt.shape[::2]) * atoms,
        transcendentals=0,
    )


def inverse_away(own, other, kfilt, after, tables, runs, shard):
    channels = own.shape[1]
    atoms = shard * sum(r[1] for r in runs)
    return pl.pallas_call(
        functools.partial(away_kernel, runs, shard),
        in_specs=[VMEM] * 3 + [ANY] + [VMEM] * len(tables),
        out_specs=[VMEM] * 2,
        out_shape=[
            jax.ShapeDtypeStruct(own.shape, BF16),
            jax.ShapeDtypeStruct((channels, atoms), BF16),
        ],
        compiler_params=params(),
        cost_estimate=inverse_cost(own, atoms),
        name="away",
    )(own, other, kfilt, after, *tables)


def inverse_here(filt, tables, runs, shard):
    channels = filt.shape[1]
    atoms = shard * sum(r[1] for r in runs)
    return pl.pallas_call(
        functools.partial(here_kernel, runs, shard),
        in_specs=[VMEM] * (1 + len(tables)),
        out_specs=VMEM,
        out_shape=jax.ShapeDtypeStruct((channels, atoms), F32),
        compiler_params=params(),
        cost_estimate=inverse_cost(filt, atoms),
        name="here",
    )(filt, *tables)


def join_kernel(here_ref, arrived_ref, own_ref, *send_refs):
    width = own_ref.shape[1]
    for p in range(len(send_refs) + 1):
        lanes = slice(p * width, (p + 1) * width)
        total = here_ref[:, lanes] + arrived_ref[:, lanes].astype(F32)
        if p:
            send_refs[p - 1][...] = total.astype(BF16)
        else:
            own_ref[...] = total


def join(here, arrived, pieces):
    channels, atoms = here.shape
    shape = (channels, atoms // pieces)
    return pl.pallas_call(
        join_kernel,
        in_specs=[VMEM] * 2,
        out_specs=[VMEM] * pieces,
        out_shape=[jax.ShapeDtypeStruct(shape, F32)]
        + [jax.ShapeDtypeStruct(shape, BF16)] * (pieces - 1),
        compiler_params=params(),
        name="join",
    )(here, arrived)


def pair_kernel(nbasis, pieces, output_scale, picks, arrays, neighbours_ref, own_pos_ref, *refs):
    message_refs, refs = refs[:arrays], refs[arrays:]
    weight_ref, out_ref, feat_scr, pos_scr, own_scr, basis_scr, acc_scr = refs
    block = BLOCK_ATOMS
    width = 12.0 / nbasis
    own_blocks, neighbours = neighbours_ref.shape
    shard = own_blocks * block
    channels = out_ref.shape[1]

    views = [message_refs[array].at[index] for array, index in picks]
    for place, ref in enumerate(views):
        lanes = slice(place * shard, (place + 1) * shard)
        feat_scr[:, lanes] = ref[0:channels, :]
        parts = ref[channels:, :].astype(F32)
        pos_scr[0:3, lanes] = (parts[0:3] + parts[3:6] + parts[6:9]) * 8.0

    a_index = lax.axis_index("atoms")
    k_index = lax.axis_index("kvec")
    n_atoms = lax.axis_size("atoms")
    group_blk = own_blocks * pieces
    first = (a_index * pieces + k_index) * own_blocks
    toward = jnp.where(a_index % 2 == 0, 1, n_atoms - 1)

    def place_of(ident):
        group, within = ident // group_blk, ident % group_blk
        ahead = (group - a_index + n_atoms) % n_atoms
        which = jnp.where(ahead == 0, 0, jnp.where(ahead == toward, 1, 2))
        piece = (within // own_blocks) ^ k_index
        return (which * pieces + piece) * own_blocks + within % own_blocks

    rows = 64
    diagonal = lax.broadcasted_iota(jnp.int32, (rows, block), 0) - lax.broadcasted_iota(
        jnp.int32, (rows, block), 1
    )
    for b in range(own_blocks):
        for d in range(3):
            row = own_pos_ref[d : d + 1, b * block : (b + 1) * block]
            own_scr[d] = jnp.broadcast_to(row, (block, block)).T
        acc_scr[...] = jnp.zeros_like(acc_scr)

        def pair(jp, carry):
            near_feat = []
            for h in range(2):
                ident = neighbours_ref[b, 2 * jp + h]
                lanes = pl.ds(pl.multiple_of(place_of(ident) * block, block), block)
                same = ident == first + b
                near_feat.append(feat_scr[:, lanes])
                near = [pos_scr[d : d + 1, lanes] for d in range(3)]
                for part in range(block // rows):
                    at = part * rows
                    dist2 = (own_scr[0, at : at + rows, :] - near[0]) ** 2
                    dist2 += (own_scr[1, at : at + rows, :] - near[1]) ** 2
                    dist2 += (own_scr[2, at : at + rows, :] - near[2]) ** 2
                    radius = dist2 * lax.rsqrt(jnp.maximum(dist2, 1e-30))
                    env = output_scale / (1.0 + dist2 * (1.0 / 16.0))
                    env = jnp.where((diagonal + at == 0) & same, 0.0, env)
                    v = radius * (1.0 / width) - 0.5
                    value = jnp.exp(-0.5 * v * v) * env
                    ratio = jnp.exp(v)
                    for k in range(nbasis):
                        if k:
                            value = value * ratio
                        basis_scr[
                            k * block + at : k * block + at + rows, h * block : (h + 1) * block
                        ] = value.astype(BF16)
            acc_scr[...] += lax.dot_general(
                basis_scr[...],
                jnp.concatenate(near_feat, axis=1),
                (((1,), (1,)), ((), ())),
                preferred_element_type=F32,
            )
            return carry

        lax.fori_loop(0, neighbours // 2, pair, 0)
        total = jnp.zeros((block, channels), F32)
        for k in range(nbasis):
            gathered = (acc_scr[k * block : (k + 1) * block, :] * math.exp(-0.5 * k * k)).astype(BF16)
            total += jnp.dot(
                gathered,
                weight_ref[k * channels : (k + 1) * channels, :],
                preferred_element_type=F32,
            )
        out_ref[b * block : (b + 1) * block, :] = total


def pair_message(neighbours, own_pos, arrays, picks, weight):
    channels = weight.shape[1]
    nbasis = weight.shape[0] // channels
    pieces = len(picks) // 3
    shard = own_pos.shape[1]
    count = neighbours.shape[1]
    scale = float(count * BLOCK_ATOMS) ** (-0.5)
    window = 3 * pieces * shard
    return pl.pallas_call(
        functools.partial(pair_kernel, nbasis, pieces, scale, picks, len(arrays)),
        in_specs=[SMEM] + [VMEM] * (2 + len(arrays)),
        out_specs=VMEM,
        out_shape=jax.ShapeDtypeStruct((shard, channels), F32),
        scratch_shapes=[
            pltpu.VMEM((channels, window), BF16),
            pltpu.VMEM((8, window), F32),
            pltpu.VMEM((3, BLOCK_ATOMS, BLOCK_ATOMS), F32),
            pltpu.VMEM((nbasis * BLOCK_ATOMS, 2 * BLOCK_ATOMS), BF16),
            pltpu.VMEM((nbasis * BLOCK_ATOMS, channels), F32),
        ],
        compiler_params=params(),
        cost_estimate=pl.CostEstimate(
            flops=2 * shard * count * BLOCK_ATOMS * (nbasis * channels + 40),
            bytes_accessed=2 * window * channels,
            transcendentals=3 * shard * count * BLOCK_ATOMS,
        ),
        name="pair",
    )(neighbours, own_pos, *arrays, weight)


def update_kernel(*refs):
    features_ref, pair_ref, gain_ref, w_in_ref, w_out_ref = refs[:5]
    parts, out_ref = refs[5:-1], refs[-1]
    long_t = parts[0][...].astype(F32)
    for part in parts[1:]:
        long_t = long_t + part[...].astype(F32)
    total = features_ref[...].astype(F32) + pair_ref[...] + long_t.T
    mean = jnp.mean(total * total, axis=-1, keepdims=True)
    normed = (total * lax.rsqrt(mean + 1e-06) * gain_ref[...]).astype(BF16)
    pre = jnp.dot(normed, w_in_ref[...], preferred_element_type=F32)
    hidden = (pre / (1.0 + jnp.exp(-pre))).astype(BF16)
    out_ref[...] = (
        total + jnp.dot(hidden, w_out_ref[...], preferred_element_type=F32)
    ).astype(BF16)


def update(features, pair_msg, gain, w_in, w_out, parts):
    return pl.pallas_call(
        update_kernel,
        in_specs=[VMEM] * (5 + len(parts)),
        out_specs=VMEM,
        out_shape=jax.ShapeDtypeStruct(features.shape, BF16),
        compiler_params=params(),
        name="update",
    )(features, pair_msg, gain[None, :], w_in, w_out, *parts)


def swap(value, axis, bits):
    return lax.ppermute(value, axis, [(i, i ^ bits) for i in range(lax.axis_size(axis))])


def per_device(
    positions,
    features,
    atom_mask,
    neighbours,
    lattice,
    pair_weight,
    kfilter,
    norm_gain,
    w_in,
    w_out,
):
    shard, _ = features.shape
    n_atoms = lax.axis_size("atoms")
    n_kvec = lax.axis_size("kvec")
    far = n_atoms // 4
    count = lattice.shape[1] // (2 * far)
    width = 256 if count % 256 == 0 else count

    message = pack(features, atom_mask, positions)
    scale = float(n_atoms * n_kvec * shard * KW) ** (-0.5)
    waves, kfilt = setup(lattice, kfilter, far, width, scale)
    distant = [swap(message, "atoms", 4 * z) for z in range(1, far)]
    bundle = collect([message, *distant], [(z, None) for z in range(far)], after=(waves,))
    bundle_x = swap(bundle, "atoms", 1)
    arrived = [None] * n_kvec
    for k in range(n_kvec - 1, 0, -1):
        arrived[k] = swap(bundle, "kvec", k)
    arrived = arrived[1:]

    table_0, total = wave(waves, [bundle, bundle_x], None)
    every = [(k, z) for k in range(n_kvec - 1) for z in range(far)]
    gathered = collect(arrived, every, after=(total,))
    gathered_x = swap(gathered, "atoms", 1)
    table_1, total = wave(waves, [gathered], total)
    halo_pairs = [(a, (a + 2) % n_atoms if a % 2 == 0 else (a - 2) % n_atoms) for a in range(n_atoms)]
    near = [(0, 0)] + [(1, k * far) for k in range(n_kvec - 1)]
    halo = lax.ppermute(collect([bundle_x, gathered_x], near), "atoms", halo_pairs)
    table_2, total, low = wave(waves, [gathered_x], total, low=True)
    other = swap(low, "atoms", 2)

    picks = near + [(2 + array, index) for array, index in near]
    picks += [(4, k) for k in range(n_kvec)]
    pair_msg = pair_message(
        neighbours,
        positions,
        [bundle, gathered, bundle_x, gathered_x, halo],
        picks,
        pair_weight,
    )

    rest = far * (n_kvec - 1)
    filt, away = inverse_away(
        total, other, kfilt, pair_msg, [table_0, table_2], [(far, far), (0, rest)], shard
    )
    crossed = swap(away, "atoms", 1)
    here = inverse_here(filt, [table_0, table_1], [(0, far), (0, rest)], shard)
    own, *sends = join(here, crossed, n_kvec)
    came = [swap(sends[k - 1], "kvec", k).astype(F32) for k in range(n_kvec - 1, 0, -1)]
    for item in came:
        own = own + item
    parts = [own[:, :shard]]
    for z in range(1, far):
        parts.append(swap(own[:, z * shard : (z + 1) * shard].astype(BF16), "atoms", 4 * z))
    return update(features, pair_msg, norm_gain, w_in, w_out, parts)


def solution(mesh):
    return jax.shard_map(
        per_device,
        mesh=mesh,
        in_specs=(
            P(None, ("atoms", "kvec")),
            P(("atoms", "kvec"), None),
            P(("atoms", "kvec")),
            P(("atoms", "kvec"), None),
            P(None, "kvec"),
            P(),
            P(),
            P(),
            P(),
            P(),
        ),
        out_specs=P(("atoms", "kvec"), None),
        check_vma=False,
    )
```

profile of v0, /device:TPU:0, one launch (start us, length us, event | category | flops | bytes accessed | tf_op | source)
XLA Modules:
  0.0 77.1 jit_solution(14277431041969449012)
XLA Ops:
  0.0 1.0 %pack.1.refs_0_ = bf16[144,256]{1,0:T(8,128)(2,1)S(1)} custom-call(bf16[256,128]{1,0:T(8,128)(2,1)} %refs_0_.1, s32[1,256]{1,0:T(1,128)} %bitcast.5, f32[3,256]{1,0:T(4,128)} %own_pos_ref.1), custom_call_target="tpu_custom_call" | custom-call | tf_op jit(solution)/shard_map/pack/pallas_call | solution.py:66
  1.0 4.1 %collective-permute-start = (bf16[144,256]{1,0:T(8,128)(2,1)S(1)}, bf16[144,256]{1,0:T(8,128)(2,1)S(1)}, u32[]{:S(2)}, u32[]{:S(2)}) collective-permute-start(bf16[144,256]{1,0:T(8,128)(2,1)S(1)} %pack.1.refs_0_), channel_id=1, source_target_pairs={{0,16},{4,20},{8,24},{12,28},{16,0},{20,4},{24,8},{28,12},{1,17},{... | collective-permute-start | bytes 221192 | tf_op jit(solution)/shard_map/ppermute | solution.py:502
  5.1 0.8 %copy.11 = f32[8,128]{0,1:T(8,128)S(1)} copy(f32[8,128]{1,0:T(8,128)} %param.16) | data formatting | bytes 8192 | tf_op args[6]
  5.9 0.8 %copy-done.3 = s32[3,3072]{1,0:T(4,128)S(1)} copy-done((s32[3,3072]{1,0:T(4,128)S(1)}, s32[3,3072]{1,0:T(4,128)}, u32[]{:S(2)}) %copy-start.3) | copy-done | bytes 36888
  6.7 0.6 setup.1
  7.4 1.7 %collective-permute-done.refs_1_ = bf16[144,256]{1,0:T(8,128)(2,1)S(1)} collective-permute-done((bf16[144,256]{1,0:T(8,128)(2,1)S(1)}, bf16[144,256]{1,0:T(8,128)(2,1)S(1)}, u32[]{:S(2)}, u32[]{:S(2)}) %collective-permute-start) | collective-permute-done | bytes 73760 | tf_op jit(solution)/shard_map/ppermute | solution.py:502
  9.2 2.7 %collective-permute-start.3 = (bf16[2,144,256]{2,1,0:T(8,128)(2,1)S(1)}, bf16[2,144,256]{2,1,0:T(8,128)(2,1)S(1)}, u32[]{:S(2)}, u32[]{:S(2)}) collective-permute-start(bf16[2,144,256]{2,1,0:T(8,128)(2,1)S(1)} %collect.3.refs_1_.refs_0_), channel_id=1, source_target_pairs={{0,3},{1,2},{2,1},{3,0},{4,7},{5,6},{6,5},{7,4},{8,11},{9,10},{10,... | collective-permute-start | bytes 442376 | tf_op jit(solution)/shard_map/ppermute | solution.py:502
  12.7 4.2 %wave.3 = (bf16[6,256,1024]{2,1,0:T(8,128)(2,1)S(1)}, f32[6,128,256]{2,1,0:T(8,128)S(1)}) custom-call(bf16[3,256,16]{2,1,0:T(8,128)(2,1)S(1)} %get-tuple-element.20.refs_2_.refs_0_, bf16[2,144,256]{2,1,0:T(8,128)(2,1)S(1)} %collect.3.refs_1_.refs_0_, bf16[2,144,256]{2,1,0:T(8,128)(2,1)S(1)} %collective-permute-done.4.refs_2_.refs_0_), custom_call_target="tpu_custom_call" | custom-call | flops 402653184 | bytes 3145728 | tf_op jit(solution)/shard_map/wave/pallas_call | solution.py:226
  17.0 2.5 %collective-permute-done.2.refs_1_ = bf16[2,144,256]{2,1,0:T(8,128)(2,1)S(1)} collective-permute-done((bf16[2,144,256]{2,1,0:T(8,128)(2,1)S(1)}, bf16[2,144,256]{2,1,0:T(8,128)(2,1)S(1)}, u32[]{:S(2)}, u32[]{:S(2)}) %collective-permute-start.2) | collective-permute-done | bytes 147488 | tf_op jit(solution)/shard_map/ppermute | solution.py:502
  19.9 5.9 %wave.4 = (bf16[6,256,1536]{2,1,0:T(8,128)(2,1)S(1)}, f32[6,128,256]{2,1,0:T(8,128)S(1)}) custom-call(bf16[3,256,16]{2,1,0:T(8,128)(2,1)S(1)} %get-tuple-element.20.refs_2_.refs_0_, bf16[6,144,256]{2,1,0:T(8,128)(2,1)S(1)} %collect.4.refs_1_, f32[6,128,256]{2,1,0:T(8,128)S(1)} %get-tuple-element.21.refs_3_.refs_2_), custom_call_target="tpu_custom_call" | custom-call | flops 603979776 | bytes 4718592 | tf_op jit(solution)/shard_map/wave/pallas_call | solution.py:226
  25.8 5.9 %wave.5 = (bf16[6,256,1536]{2,1,0:T(8,128)(2,1)S(1)}, f32[6,128,256]{2,1,0:T(8,128)S(1)}, bf16[6,128,256]{2,1,0:T(8,128)(2,1)S(1)}) custom-call(bf16[3,256,16]{2,1,0:T(8,128)(2,1)S(1)} %get-tuple-element.20.refs_2_.refs_0_, bf16[6,144,256]{2,1,0:T(8,128)(2,1)S(1)} %collective-permute-done.5.refs_1_.refs_3_, f32[6,128,256]{2,1,0:T(8,128)S(1)} %get-tuple-element.22.refs_2_), custom_call_target="tpu_custom_call" | custom-call | flops 603979776 | bytes 4718592 | tf_op jit(solution)/shard_map/wave/pallas_call | solution.py:226
  32.3 1.6 %collective-permute-start.6 = (bf16[4,144,256]{2,1,0:T(8,128)(2,1)S(1)}, bf16[4,144,256]{2,1,0:T(8,128)(2,1)S(1)}, u32[]{:S(2)}, u32[]{:S(2)}) collective-permute-start(bf16[4,144,256]{2,1,0:T(8,128)(2,1)S(1)} %collect.5), channel_id=1, source_target_pairs={{0,8},{4,28},{8,16},{12,4},{16,24},{20,12},{24,0},{28,20},{1,9},{5... | collective-permute-start | bytes 884744 | tf_op jit(solution)/shard_map/ppermute | solution.py:542
  33.9 17.3 %collective-permute-done.6.refs_4_ = bf16[4,144,256]{2,1,0:T(8,128)(2,1)S(1)} collective-permute-done((bf16[4,144,256]{2,1,0:T(8,128)(2,1)S(1)}, bf16[4,144,256]{2,1,0:T(8,128)(2,1)S(1)}, u32[]{:S(2)}, u32[]{:S(2)}) %collective-permute-start.6) | collective-permute-done | bytes 294944 | tf_op jit(solution)/shard_map/ppermute | solution.py:542
  51.2 6.6 %pair.1._.refs_1_ = f32[256,128]{1,0:T(8,128)S(1)} custom-call(s32[2,12]{1,0:T(2,128)S(1)} %copy-done.7, f32[3,256]{1,0:T(4,128)S(1)} %copy-done.4, bf16[2,144,256]{2,1,0:T(8,128)(2,1)S(1)} %collect.3.refs_1_.refs_0_, bf16[6,144,256]{2,1,0:T(8,128)(2,1)S(1)} %collect.4.refs_1_, bf16[2,144,256]{2,1,0:T(8,128)(2,1)S(1)} %collective-permute-done.4.refs_2_.refs_0_, ...), custom_call_target="tpu_custom_call" | custom-call | flops 836763648 | bytes 786432 | tf_op jit(solution)/shard_map/pair/pallas_call | solution.py:452
  57.8 1.0 %away.1 = (bf16[6,128,256]{2,1,0:T(8,128)(2,1)S(1)}, bf16[128,2048]{1,0:T(8,128)(2,1)S(1)}) custom-call(f32[6,128,256]{2,1,0:T(8,128)S(1)} %get-tuple-element.23.own_ref, bf16[6,128,256]{2,1,0:T(8,128)(2,1)S(1)} %collective-permute-done.7.other_ref, f32[3,128,256]{2,1,0:T(8,128)S(1)} %get-tuple-element.25.kfilt_ref, f32[256,128]{1,0:T(8,128)S(1)} %pair.1._.refs_1_, ...), custom_call_target="tpu_custom_call" | custom-call | flops 805306368 | bytes 6291456 | tf_op jit(solution)/shard_map/away/pallas_call | solution.py:306
  59.0 1.0 %here.1.here_ref = f32[128,2048]{1,0:T(8,128)S(1)} custom-call(bf16[6,128,256]{2,1,0:T(8,128)(2,1)S(1)} %get-tuple-element.28.filt_ref, bf16[6,256,1024]{2,1,0:T(8,128)(2,1)S(1)} %get-tuple-element.26.refs_0_, bf16[6,256,1536]{2,1,0:T(8,128)(2,1)S(1)} %get-tuple-element.29.refs_1_), custom_call_target="tpu_custom_call" | custom-call | flops 805306368 | bytes 6291456 | tf_op jit(solution)/shard_map/here/pallas_call | solution.py:323
  60.0 0.8 %collective-permute-done.8.arrived_ref = bf16[128,2048]{1,0:T(8,128)(2,1)S(1)} collective-permute-done((bf16[128,2048]{1,0:T(8,128)(2,1)S(1)}, bf16[128,2048]{1,0:T(8,128)(2,1)S(1)}, u32[]{:S(2)}, u32[]{:S(2)}) %collective-permute-start.8) | collective-permute-done | bytes 524320 | tf_op jit(solution)/shard_map/ppermute | solution.py:502
  61.0 1.7 %collective-permute-start.9 = (bf16[128,512]{1,0:T(8,128)(2,1)S(1)}, bf16[128,512]{1,0:T(8,128)(2,1)S(1)}, u32[]{:S(2)}, u32[]{:S(2)}) collective-permute-start(bf16[128,512]{1,0:T(8,128)(2,1)S(1)} %get-tuple-element.32), channel_id=1, source_target_pairs={{0,3},{1,2},{2,1},{3,0},{4,7},{5,6},{6,5},{7,4},{8,11},{9,10},{10,... | collective-permute-start | bytes 393224 | tf_op jit(solution)/shard_map/ppermute | solution.py:502
  62.7 1.3 %collective-permute-start.10 = (bf16[128,512]{1,0:T(8,128)(2,1)S(1)}, bf16[128,512]{1,0:T(8,128)(2,1)S(1)}, u32[]{:S(2)}, u32[]{:S(2)}) collective-permute-start(bf16[128,512]{1,0:T(8,128)(2,1)S(1)} %get-tuple-element.33), channel_id=1, source_target_pairs={{0,2},{1,3},{2,0},{3,1},{4,6},{5,7},{6,4},{7,5},{8,10},{9,11},{10,... | collective-permute-start | bytes 393224 | tf_op jit(solution)/shard_map/ppermute | solution.py:502
  64.0 0.5 collective-permute-start.11
  64.5 3.8 %collective-permute-done.9 = bf16[128,512]{1,0:T(8,128)(2,1)S(1)} collective-permute-done((bf16[128,512]{1,0:T(8,128)(2,1)S(1)}, bf16[128,512]{1,0:T(8,128)(2,1)S(1)}, u32[]{:S(2)}, u32[]{:S(2)}) %collective-permute-start.9) | collective-permute-done | bytes 131104 | tf_op jit(solution)/shard_map/ppermute | solution.py:502
  68.3 2.0 %collective-permute-done.10 = bf16[128,512]{1,0:T(8,128)(2,1)S(1)} collective-permute-done((bf16[128,512]{1,0:T(8,128)(2,1)S(1)}, bf16[128,512]{1,0:T(8,128)(2,1)S(1)}, u32[]{:S(2)}, u32[]{:S(2)}) %collective-permute-start.10) | collective-permute-done | bytes 131104 | tf_op jit(solution)/shard_map/ppermute | solution.py:502
  70.5 5.4 %collective-permute-done.12.refs_6_ = bf16[128,256]{1,0:T(8,128)(2,1)S(1)} collective-permute-done((bf16[128,256]{1,0:T(8,128)(2,1)S(1)}, bf16[128,256]{1,0:T(8,128)(2,1)S(1)}, u32[]{:S(2)}, u32[]{:S(2)}) %collective-permute-start.12) | collective-permute-done | bytes 65568 | tf_op jit(solution)/shard_map/ppermute | solution.py:502
  75.9 1.2 %update.1 = bf16[256,128]{1,0:T(8,128)(2,1)} custom-call(bf16[256,128]{1,0:T(8,128)(2,1)S(1)} %copy-done, f32[256,128]{1,0:T(8,128)S(1)} %pair.1._.refs_1_, f32[1,128]{1,0:T(1,128)S(1)} %bitcast.4, bf16[128,512]{1,0:T(8,128)(2,1)S(1)} %copy-done.1, bf16[512,128]{1,0:T(8,128)(2,1)S(1)} %copy-done.2, f32[128,256]{1,0:T(8,128)S(1)} %slice.9.refs_5_, ...), custom_call_target="tpu_custom_call" | custom-call | tf_op jit(solution)/shard_map/update/pallas_call | solution.py:491
  (35 shorter events, 2.3 us)
Async XLA Ops:
  0.0 51.2 %copy-start.4 = (f32[3,256]{1,0:T(4,128)S(1)}, f32[3,256]{1,0:T(4,128)}, u32[]{:S(2)}) copy-start(f32[3,256]{1,0:T(4,128)} %own_pos_ref.1) | copy-start | bytes 9220
  0.0 51.2 %copy-start.7 = (s32[2,12]{1,0:T(2,128)S(1)}, s32[2,12]{1,0:T(2,128)}, u32[]{:S(2)}) copy-start(s32[2,12]{1,0:T(2,128)} %neighbours_ref.1) | copy-start | bytes 292
  1.0 8.0 %collective-permute-start = (bf16[144,256]{1,0:T(8,128)(2,1)S(1)}, bf16[144,256]{1,0:T(8,128)(2,1)S(1)}, u32[]{:S(2)}, u32[]{:S(2)}) collective-permute-start(bf16[144,256]{1,0:T(8,128)(2,1)S(1)} %pack.1.refs_0_), channel_id=1, source_target_pairs={{0,16},{4,20},{8,24},{12,28},{16,0},{20,4},{24,8},{28,12},{1,17},{... | collective-permute-start | bytes 221192 | tf_op jit(solution)/shard_map/ppermute | solution.py:502
  5.9 0.8 %copy-start.3 = (s32[3,3072]{1,0:T(4,128)S(1)}, s32[3,3072]{1,0:T(4,128)}, u32[]{:S(2)}) copy-start(s32[3,3072]{1,0:T(4,128)} %lattice_ref.1) | copy-start | bytes 110596
  6.7 44.4 %copy-start.6 = (bf16[1024,128]{1,0:T(8,128)(2,1)S(1)}, bf16[1024,128]{1,0:T(8,128)(2,1)}, u32[]{:S(2)}) copy-start(bf16[1024,128]{1,0:T(8,128)(2,1)} %refs_5_.1) | copy-start | bytes 786436
  9.1 3.6 %collective-permute-start.4 = (bf16[2,144,256]{2,1,0:T(8,128)(2,1)S(1)}, bf16[2,144,256]{2,1,0:T(8,128)(2,1)S(1)}, u32[]{:S(2)}, u32[]{:S(2)}) collective-permute-start(bf16[2,144,256]{2,1,0:T(8,128)(2,1)S(1)} %collect.3.refs_1_.refs_0_), channel_id=1, source_target_pairs={{0,4},{4,0},{8,12},{12,8},{16,20},{20,16},{24,28},{28,24},{1,5},{5... | collective-permute-start | bytes 442376 | tf_op jit(solution)/shard_map/ppermute | solution.py:502
  9.2 7.8 %collective-permute-start.3 = (bf16[2,144,256]{2,1,0:T(8,128)(2,1)S(1)}, bf16[2,144,256]{2,1,0:T(8,128)(2,1)S(1)}, u32[]{:S(2)}, u32[]{:S(2)}) collective-permute-start(bf16[2,144,256]{2,1,0:T(8,128)(2,1)S(1)} %collect.3.refs_1_.refs_0_), channel_id=1, source_target_pairs={{0,3},{1,2},{2,1},{3,0},{4,7},{5,6},{6,5},{7,4},{8,11},{9,10},{10,... | collective-permute-start | bytes 442376 | tf_op jit(solution)/shard_map/ppermute | solution.py:502
  11.9 7.6 %collective-permute-start.2 = (bf16[2,144,256]{2,1,0:T(8,128)(2,1)S(1)}, bf16[2,144,256]{2,1,0:T(8,128)(2,1)S(1)}, u32[]{:S(2)}, u32[]{:S(2)}) collective-permute-start(bf16[2,144,256]{2,1,0:T(8,128)(2,1)S(1)} %collect.3.refs_1_.refs_0_), channel_id=1, source_target_pairs={{0,2},{1,3},{2,0},{3,1},{4,6},{5,7},{6,4},{7,5},{8,10},{9,11},{10,... | collective-permute-start | bytes 442376 | tf_op jit(solution)/shard_map/ppermute | solution.py:502
  12.4 7.4 %collective-permute-start.1 = (bf16[2,144,256]{2,1,0:T(8,128)(2,1)S(1)}, bf16[2,144,256]{2,1,0:T(8,128)(2,1)S(1)}, u32[]{:S(2)}, u32[]{:S(2)}) collective-permute-start(bf16[2,144,256]{2,1,0:T(8,128)(2,1)S(1)} %collect.3.refs_1_.refs_0_), channel_id=1, source_target_pairs={{0,1},{1,0},{2,3},{3,2},{4,5},{5,4},{6,7},{7,6},{8,9},{9,8},{10,11... | collective-permute-start | bytes 442376 | tf_op jit(solution)/shard_map/ppermute | solution.py:502
  19.8 6.0 %collective-permute-start.5 = (bf16[6,144,256]{2,1,0:T(8,128)(2,1)S(1)}, bf16[6,144,256]{2,1,0:T(8,128)(2,1)S(1)}, u32[]{:S(2)}, u32[]{:S(2)}) collective-permute-start(bf16[6,144,256]{2,1,0:T(8,128)(2,1)S(1)} %collect.4.refs_1_), channel_id=1, source_target_pairs={{0,4},{4,0},{8,12},{12,8},{16,20},{20,16},{24,28},{28,24},{1,5},{5... | collective-permute-start | bytes 1327112 | tf_op jit(solution)/shard_map/ppermute | solution.py:502
  31.7 26.1 %collective-permute-start.7 = (bf16[6,128,256]{2,1,0:T(8,128)(2,1)S(1)}, bf16[6,128,256]{2,1,0:T(8,128)(2,1)S(1)}, u32[]{:S(2)}, u32[]{:S(2)}) collective-permute-start(bf16[6,128,256]{2,1,0:T(8,128)(2,1)S(1)} %get-tuple-element.24), channel_id=1, source_target_pairs={{0,8},{4,12},{8,0},{12,4},{16,24},{20,28},{24,16},{28,20},{1,9},{5... | collective-permute-start | bytes 1179656 | tf_op jit(solution)/shard_map/ppermute | solution.py:502
  32.3 18.9 %collective-permute-start.6 = (bf16[4,144,256]{2,1,0:T(8,128)(2,1)S(1)}, bf16[4,144,256]{2,1,0:T(8,128)(2,1)S(1)}, u32[]{:S(2)}, u32[]{:S(2)}) collective-permute-start(bf16[4,144,256]{2,1,0:T(8,128)(2,1)S(1)} %collect.5), channel_id=1, source_target_pairs={{0,8},{4,28},{8,16},{12,4},{16,24},{20,12},{24,0},{28,20},{1,9},{5... | collective-permute-start | bytes 884744 | tf_op jit(solution)/shard_map/ppermute | solution.py:542
  58.9 2.0 %collective-permute-start.8 = (bf16[128,2048]{1,0:T(8,128)(2,1)S(1)}, bf16[128,2048]{1,0:T(8,128)(2,1)S(1)}, u32[]{:S(2)}, u32[]{:S(2)}) collective-permute-start(bf16[128,2048]{1,0:T(8,128)(2,1)S(1)} %get-tuple-element.30), channel_id=1, source_target_pairs={{0,4},{4,0},{8,12},{12,8},{16,20},{20,16},{24,28},{28,24},{1,5},{5... | collective-permute-start | bytes 1572872 | tf_op jit(solution)/shard_map/ppermute | solution.py:502
  59.0 16.9 %copy-start = (bf16[256,128]{1,0:T(8,128)(2,1)S(1)}, bf16[256,128]{1,0:T(8,128)(2,1)}, u32[]{:S(2)}) copy-start(bf16[256,128]{1,0:T(8,128)(2,1)} %refs_0_.1) | copy-start | bytes 196612
  59.0 16.9 %copy-start.1 = (bf16[128,512]{1,0:T(8,128)(2,1)S(1)}, bf16[128,512]{1,0:T(8,128)(2,1)}, u32[]{:S(2)}) copy-start(bf16[128,512]{1,0:T(8,128)(2,1)} %refs_3_.1) | copy-start | bytes 393220
  59.0 16.9 %copy-start.2 = (bf16[512,128]{1,0:T(8,128)(2,1)S(1)}, bf16[512,128]{1,0:T(8,128)(2,1)}, u32[]{:S(2)}) copy-start(bf16[512,128]{1,0:T(8,128)(2,1)} %refs_4_.1) | copy-start | bytes 393220
  59.0 16.9 %copy-start.5 = (f32[128]{0:T(128)S(1)}, f32[128]{0:T(128)}, u32[]{:S(2)}) copy-start(f32[128]{0:T(128)} %param.17) | copy-start | bytes 1540
  61.0 7.3 %collective-permute-start.9 = (bf16[128,512]{1,0:T(8,128)(2,1)S(1)}, bf16[128,512]{1,0:T(8,128)(2,1)S(1)}, u32[]{:S(2)}, u32[]{:S(2)}) collective-permute-start(bf16[128,512]{1,0:T(8,128)(2,1)S(1)} %get-tuple-element.32), channel_id=1, source_target_pairs={{0,3},{1,2},{2,1},{3,0},{4,7},{5,6},{6,5},{7,4},{8,11},{9,10},{10,... | collective-permute-start | bytes 393224 | tf_op jit(solution)/shard_map/ppermute | solution.py:502
  62.7 7.6 %collective-permute-start.10 = (bf16[128,512]{1,0:T(8,128)(2,1)S(1)}, bf16[128,512]{1,0:T(8,128)(2,1)S(1)}, u32[]{:S(2)}, u32[]{:S(2)}) collective-permute-start(bf16[128,512]{1,0:T(8,128)(2,1)S(1)} %get-tuple-element.33), channel_id=1, source_target_pairs={{0,2},{1,3},{2,0},{3,1},{4,6},{5,7},{6,4},{7,5},{8,10},{9,11},{10,... | collective-permute-start | bytes 393224 | tf_op jit(solution)/shard_map/ppermute | solution.py:502
  64.0 6.3 %collective-permute-start.11 = (bf16[128,512]{1,0:T(8,128)(2,1)S(1)}, bf16[128,512]{1,0:T(8,128)(2,1)S(1)}, u32[]{:S(2)}, u32[]{:S(2)}) collective-permute-start(bf16[128,512]{1,0:T(8,128)(2,1)S(1)} %get-tuple-element.34), channel_id=1, source_target_pairs={{0,1},{1,0},{2,3},{3,2},{4,5},{5,4},{6,7},{7,6},{8,9},{9,8},{10,11... | collective-permute-start | bytes 393224 | tf_op jit(solution)/shard_map/ppermute | solution.py:502
  70.3 5.5 %collective-permute-start.12 = (bf16[128,256]{1,0:T(8,128)(2,1)S(1)}, bf16[128,256]{1,0:T(8,128)(2,1)S(1)}, u32[]{:S(2)}, u32[]{:S(2)}) collective-permute-start(bf16[128,256]{1,0:T(8,128)(2,1)S(1)} %slice.12), channel_id=1, source_target_pairs={{0,16},{4,20},{8,24},{12,28},{16,0},{20,4},{24,8},{28,12},{1,17},{... | collective-permute-start | bytes 196616 | tf_op jit(solution)/shard_map/ppermute | solution.py:502
where the time goes:
time: 77.3 us; the launch traced here: 77.1 us
  waiting for transfers between devices  33.7 us (44%)
  Pallas kernels  27.8 us (36%)
  starting transfers between devices  13.7 us (18%)
  local copies, waits for them, and re-layouts  1.64 us (2%)
    ppermute x1, waiting for transfers between devices, per_device(): lax.ppermute(collect([bundle_x, gathered_x], near), 'atoms', halo_pairs)  17.3 us
    ppermute x12, waiting for transfers between devices, swap(): lax.ppermute(value, axis, [(i, i ^ bits) for i in range(lax.axis_size(axi...  16.5 us
    pallas_call x3, Pallas kernels, wave(): pl.pallas_call(functools.partial(wave_kernel, counts, before is None, len...  16.1 us
    ppermute x12, starting transfers between devices, swap(): lax.ppermute(value, axis, [(i, i ^ bits) for i in range(lax.axis_size(axi...  12.1 us
    pallas_call x1, Pallas kernels, pair_message(): pl.pallas_call(functools.partial(pair_kernel, nbasis, pieces, scale, pick...  6.64 us
    ppermute x1, starting transfers between devices, per_device(): lax.ppermute(collect([bundle_x, gathered_x], near), 'atoms', halo_pairs)  1.63 us
    unnamed x17, local copies, waits for them, and re-layouts  1.62 us
  transfers between devices with their start and end apart: 13, of which 8 were waited for; matrix products, arithmetic and copies ran while one was open for 1% of the time, Pallas kernels for 24%

commit v1 on v0

--- a/solution.py
+++ b/solution.py
@@ -35,11 +35,19 @@
     return acc
 
 
-def pack_kernel(features_hbm, mask_hbm, pos_hbm, out_ref, features_ref, mask_ref, pos_ref, scr, sems):
+def pack_kernel(*refs):
+    features_hbm, mask_hbm, pos_hbm, lattice_hbm, kfilter_hbm = refs[:5]
+    out_ref, lattice_ref, kfilter_ref, features_ref, mask_ref, pos_ref, scr, sems = refs[5:]
     copies = [
         pltpu.make_async_copy(source, target, sems.at[i])
         for i, (source, target) in enumerate(
-            ((features_hbm, features_ref), (mask_hbm, mask_ref), (pos_hbm, pos_ref))
+            (
+                (features_hbm, features_ref),
+                (mask_hbm, mask_ref),
+                (pos_hbm, pos_ref),
+                (lattice_hbm, lattice_ref),
+                (kfilter_hbm, kfilter_ref),
+            )
         )
     ]
     for copy in copies:
@@ -60,24 +68,28 @@
     out_ref[channels : channels + TAIL, :] = scr[...].astype(BF16)
 
 
-def pack(features, mask, positions):
+def pack(features, mask, positions, lattice, kfilter):
     shard, channels = features.shape
-    anywhere = pl.BlockSpec(memory_space=pltpu.HBM)
+    arrays = (features, mask[None, :], positions, lattice, kfilter)
     return pl.pallas_call(
         pack_kernel,
-        in_specs=[anywhere] * 3,
-        out_specs=VMEM,
-        out_shape=jax.ShapeDtypeStruct((channels + TAIL, shard), BF16),
+        in_specs=[pl.BlockSpec(memory_space=pltpu.HBM)] * 5,
+        out_specs=[VMEM] * 3,
+        out_shape=[
+            jax.ShapeDtypeStruct((channels + TAIL, shard), BF16),
+            jax.ShapeDtypeStruct(lattice.shape, lattice.dtype),
+            jax.ShapeDtypeStruct(kfilter.shape, kfilter.dtype),
+        ],
         scratch_shapes=[
             pltpu.VMEM((shard, channels), BF16),
             pltpu.VMEM((1, shard), jnp.int32),
             pltpu.VMEM((3, shard), F32),
             pltpu.VMEM((TAIL, shard), F32),
-            pltpu.SemaphoreType.DMA((3,)),
+            pltpu.SemaphoreType.DMA((5,)),
         ],
         compiler_params=params(),
         name="pack",
-    )(*(pltpu.with_memory_space_constraint(x, pltpu.HBM) for x in (features, mask[None, :], positions)))
+    )(*(pltpu.with_memory_space_constraint(x, pltpu.HBM) for x in arrays))
 
 
 def setup_kernel(far, nbasis, scale, lattice_ref, kfilter_ref, wave_ref, kfilt_ref, scr):
@@ -85,6 +97,7 @@
     a_index = lax.axis_index("atoms")
     part = a_index % 2 + 2 * (a_index // 4)
     count = blocks * width
+    kfilter = kfilter_ref[...].T
     for j in range(blocks):
         lattice = jnp.zeros((3, width), F32)
         for p in range(2 * far):
@@ -102,7 +115,7 @@
         total = jnp.zeros(kfilt_ref.shape[1:], F32)
         for p in range(nbasis):
             basis = jnp.exp(-0.5 * ((kmag - (p + 0.5) * (21.0 / nbasis)) / (21.0 / nbasis)) ** 2)
-            total += kfilter_ref[:, p : p + 1] * basis
+            total += kfilter[:, p : p + 1] * basis
         kfilt_ref[j] = total * scale
 
 
@@ -120,7 +133,7 @@
         scratch_shapes=[pltpu.VMEM((TAIL, width), F32)],
         compiler_params=params(),
         name="setup",
-    )(lattice, kfilter.T)
+    )(lattice, kfilter)
 
 
 def wave_kernel(counts, start, waits, low, *refs):
@@ -133,86 +146,83 @@
     table_ref, total_ref = take(2)
     low_ref = take(1)[0] if low else None
     feat_scr, pos_scr = take(2)
-    phases, buffers = take(2), take(2)
     blocks, width, _ = lattice_ref.shape
+    phases, buffers = take(blocks), take(blocks)
     pairs, channels, both = feat_scr.shape
     shard = both // 2
     place = 0
     for ref, count in zip(messages, counts):
         for p in range(count):
             lanes = slice(place % 2 * shard, (place % 2 + 1) * shard)
-            feat_scr[place // 2, :, lanes] = ref[p, 0:channels, :]
-            pos_scr[place // 2, :, lanes] = ref[p, channels:, :]
+            item = ref if len(ref.shape) == 2 else ref.at[p]
+            feat_scr[place // 2, :, lanes] = item[0:channels, :]
+            pos_scr[place // 2, :, lanes] = item[channels:, :]
             place += 1
     if start:
         total_ref[...] = jnp.zeros_like(total_ref)
     else:
         total_ref[...] = before_ref[...]
-    for buffer in buffers:
-        buffer[...] = jnp.zeros_like(buffer)
-    steps = pairs * blocks
-
-    def phase(i, side):
-        phases[side][...] = jnp.dot(
-            lattice_ref[i % blocks],
-            pos_scr[i // blocks, :, side * shard : (side + 1) * shard],
-            preferred_element_type=F32,
+    buffers[-1][...] = jnp.zeros_like(buffers[-1])
+
+    def phase(pair, block):
+        phases[block][...] = jnp.dot(
+            lattice_ref[block], pos_scr[pair], preferred_element_type=F32
         )
 
-    def table(i, side):
-        pair, block = i // blocks, i % blocks
-        lanes = pl.ds(pl.multiple_of(pair * both + side * shard, shard), shard)
+    def table(pair, block):
         rows = 16
-        for at in range(0, width, rows):
-            turns = phases[side][at : at + rows, :]
-            r = turns - ((turns + ROUND) - ROUND)
-            s = horner(r * r, SIN_COEF) * r
-            square = s * s
-            w = (2.0 + SLACK) - square
-            cosine = (1.0 - square).astype(BF16)
-            sine = (s * (w * lax.rsqrt(w))).astype(BF16)
-            buffers[side][0, at : at + rows, :] = cosine
-            buffers[side][1, at : at + rows, :] = sine
-            table_ref[block, at : at + rows, lanes] = cosine
-            table_ref[blocks + block, at : at + rows, lanes] = sine
-
-    def product(i):
-        pair, block = i // blocks, i % blocks
+        for side in range(2):
+            part = slice(side * shard, (side + 1) * shard)
+            lanes = pl.ds(pl.multiple_of(pair * both + side * shard, shard), shard)
+            for at in range(0, width, rows):
+                turns = phases[block][at : at + rows, part]
+                r = turns - ((turns + ROUND) - ROUND)
+                s = horner(r * r, SIN_COEF) * r
+                square = s * s
+                w = (2.0 + SLACK) - square
+                cosine = (1.0 - square).astype(BF16)
+                sine = (s * (w * lax.rsqrt(w))).astype(BF16)
+                buffers[block][0, at : at + rows, part] = cosine
+                buffers[block][1, at : at + rows, part] = sine
+                table_ref[block, at : at + rows, lanes] = cosine
+                table_ref[blocks + block, at : at + rows, lanes] = sine
+
+    def product(pair, block):
         for half in range(2):
-            parts = [
-                lax.dot_general(
-                    feat_scr[pair, :, side * shard : (side + 1) * shard],
-                    buffers[side][half],
-                    (((1,), (1,)), ((), ())),
-                    preferred_element_type=F32,
-                )
-                for side in range(2)
-            ]
-            total_ref[half * blocks + block] += parts[0] + parts[1]
+            total_ref[half * blocks + block] += lax.dot_general(
+                feat_scr[pair],
+                buffers[block][half],
+                (((1,), (1,)), ((), ())),
+                preferred_element_type=F32,
+            )
+
+    def body(pair, carry):
+        before = jnp.maximum(pair - 1, 0)
+        later = jnp.minimum(pair + 1, pairs - 1)
+        for block in range(blocks):
+            if block + 1 < blocks:
+                phase(pair, block + 1)
+            if blocks == 1:
+                product(before, 0)
+            table(pair, block)
+            if block == 0:
+                phase(later, 0)
+            if blocks > 1:
+                product(pair if block else before, (block - 1) % blocks)
+        return carry
 
     phase(0, 0)
-    phase(0, 1)
-
-    def body(i, carry):
-        later = jnp.minimum(i + 1, steps - 1)
-        product(jnp.maximum(i - 1, 0))
-        table(i, 0)
-        phase(later, 0)
-        table(i, 1)
-        phase(later, 1)
-        return carry
-
-    lax.fori_loop(0, steps, body, 0)
-    product(steps - 1)
+    lax.fori_loop(0, pairs, body, 0)
+    product(pairs - 1, blocks - 1)
     if low:
         low_ref[...] = total_ref[...].astype(BF16)
 
 
 def wave(lattice, messages, before, after=(), low=False):
     blocks, width, _ = lattice.shape
-    counts = tuple(x.shape[0] for x in messages)
+    counts = tuple(x.shape[0] if x.ndim == 3 else 1 for x in messages)
     pieces = sum(counts)
-    rows, shard = messages[0].shape[1:]
+    rows, shard = messages[0].shape[-2:]
     channels = rows - TAIL
     args = [lattice, *messages] + ([] if before is None else [before])
     factor = (2 * blocks, channels, width)
@@ -231,10 +241,8 @@
         scratch_shapes=[
             pltpu.VMEM((pieces // 2, channels, 2 * shard), BF16),
             pltpu.VMEM((pieces // 2, TAIL, 2 * shard), BF16),
-            pltpu.VMEM((width, shard), F32),
-            pltpu.VMEM((width, shard), F32),
-            pltpu.VMEM((2, width, shard), BF16),
-            pltpu.VMEM((2, width, shard), BF16),
+            *[pltpu.VMEM((width, 2 * shard), F32)] * blocks,
+            *[pltpu.VMEM((2, width, 2 * shard), BF16)] * blocks,
         ],
         compiler_params=params(),
         cost_estimate=pl.CostEstimate(
@@ -285,11 +293,11 @@
     for j in range(2 * count):
         total = own_ref[j] + other_ref[j].astype(F32)
         filt_ref[j] = (total * kfilt_ref[j % count]).astype(BF16)
-    transform(filt_ref, [(t, *r) for t, r in zip(table_refs, runs)], out_ref, shard)
+    transform(filt_ref, [(table_refs[t], p, 1) for t, p in runs], out_ref, shard)
 
 
 def here_kernel(runs, shard, filt_ref, *refs):
-    transform(filt_ref, [(t, *r) for t, r in zip(refs[:-1], runs)], refs[-1], shard)
+    transform(filt_ref, [(refs[t], p, 1) for t, p in runs], refs[-1], shard)
 
 
 def inverse_cost(filt, atoms):
@@ -300,9 +308,15 @@
     )
 
 
-def inverse_away(own, other, kfilt, after, tables, runs, shard):
+def used(tables, runs):
+    names = sorted({t for t, _ in runs})
+    return [tables[t] for t in names], tuple((names.index(t), p) for t, p in runs)
+
+
+def inverse_first(own, other, kfilt, after, tables, runs, shard):
     channels = own.shape[1]
-    atoms = shard * sum(r[1] for r in runs)
+    tables, runs = used(tables, runs)
+    atoms = shard * len(runs)
     return pl.pallas_call(
         functools.partial(away_kernel, runs, shard),
         in_specs=[VMEM] * 3 + [ANY] + [VMEM] * len(tables),
@@ -313,21 +327,22 @@
         ],
         compiler_params=params(),
         cost_estimate=inverse_cost(own, atoms),
-        name="away",
+        name="first",
     )(own, other, kfilt, after, *tables)
 
 
-def inverse_here(filt, tables, runs, shard):
+def inverse(filt, tables, runs, shard, dtype):
     channels = filt.shape[1]
-    atoms = shard * sum(r[1] for r in runs)
+    tables, runs = used(tables, runs)
+    atoms = shard * len(runs)
     return pl.pallas_call(
         functools.partial(here_kernel, runs, shard),
         in_specs=[VMEM] * (1 + len(tables)),
         out_specs=VMEM,
-        out_shape=jax.ShapeDtypeStruct((channels, atoms), F32),
+        out_shape=jax.ShapeDtypeStruct((channels, atoms), dtype),
         compiler_params=params(),
         cost_estimate=inverse_cost(filt, atoms),
-        name="here",
+        name="inverse",
     )(filt, *tables)
 
 
@@ -365,7 +380,10 @@
     shard = own_blocks * block
     channels = out_ref.shape[1]
 
-    views = [message_refs[array].at[index] for array, index in picks]
+    views = [
+        message_refs[array] if index is None else message_refs[array].at[index]
+        for array, index in picks
+    ]
     for place, ref in enumerate(views):
         lanes = slice(place * shard, (place + 1) * shard)
         feat_scr[:, lanes] = ref[0:channels, :]
@@ -521,51 +539,66 @@
     count = lattice.shape[1] // (2 * far)
     width = 256 if count % 256 == 0 else count
 
-    message = pack(features, atom_mask, positions)
+    message, lattice, kfilter = pack(features, atom_mask, positions, lattice, kfilter)
     scale = float(n_atoms * n_kvec * shard * KW) ** (-0.5)
     waves, kfilt = setup(lattice, kfilter, far, width, scale)
-    distant = [swap(message, "atoms", 4 * z) for z in range(1, far)]
-    bundle = collect([message, *distant], [(z, None) for z in range(far)], after=(waves,))
-    bundle_x = swap(bundle, "atoms", 1)
-    arrived = [None] * n_kvec
-    for k in range(n_kvec - 1, 0, -1):
-        arrived[k] = swap(bundle, "kvec", k)
-    arrived = arrived[1:]
-
-    table_0, total = wave(waves, [bundle, bundle_x], None)
-    every = [(k, z) for k in range(n_kvec - 1) for z in range(far)]
-    gathered = collect(arrived, every, after=(total,))
-    gathered_x = swap(gathered, "atoms", 1)
-    table_1, total = wave(waves, [gathered], total)
-    halo_pairs = [(a, (a + 2) % n_atoms if a % 2 == 0 else (a - 2) % n_atoms) for a in range(n_atoms)]
-    near = [(0, 0)] + [(1, k * far) for k in range(n_kvec - 1)]
-    halo = lax.ppermute(collect([bundle_x, gathered_x], near), "atoms", halo_pairs)
-    table_2, total, low = wave(waves, [gathered_x], total, low=True)
+    others = range(n_kvec - 1, 0, -1)
+    zs = range(1, far)
+    message_x = swap(message, "atoms", 1)
+    near = {k: swap(message, "kvec", k) for k in others}
+    distant = [swap(message, "atoms", 4 * z) for z in zs]
+    distant = collect(distant, [(z, None) for z in range(far - 1)])
+    distant_x = swap(distant, "atoms", 1)
+    relayed = {k: swap(distant, "kvec", k) for k in others}
+
+    where = {}
+    table_0, total = wave(waves, [message, message_x], None)
+    where[0, 0, 0], where[1, 0, 0] = (0, 0), (0, 1)
+    near_own = collect([near[k] for k in others], [(i, None) for i in range(n_kvec - 1)], after=(total,))
+    near_x = swap(near_own, "atoms", 1)
+    halo_pairs = [(a, (a + 1) % n_atoms if a % 2 else (a - 1) % n_atoms) for a in range(n_atoms)]
+    own_group = [message, near_own]
+    picks = [(0, None)] + [(1, n_kvec - 1 - k) for k in range(1, n_kvec)]
+    halo = lax.ppermute(collect(own_group, picks), "atoms", halo_pairs)
+    table_1, total = wave(waves, [near_own, near_x], total)
+    for i, k in enumerate(others):
+        where[0, 0, k], where[1, 0, k] = (1, i), (1, n_kvec - 1 + i)
+    every = [(i, z) for i in range(n_kvec - 1) for z in range(far - 1)]
+    far_own = collect([relayed[k] for k in others], every, after=(total,))
+    far_x = swap(far_own, "atoms", 1)
+    table_2, total = wave(waves, [distant, far_own], total)
+    table_3, total, low = wave(waves, [distant_x, far_x], total, low=True)
+    for core, table in ((0, 2), (1, 3)):
+        for z in zs:
+            where[core, z, 0] = (table, z - 1)
+            for i, k in enumerate(others):
+                where[core, z, k] = (table, (1 + i) * (far - 1) + z - 1)
+    tables = [table_0, table_1, table_2, table_3]
     other = swap(low, "atoms", 2)
 
-    picks = near + [(2 + array, index) for array, index in near]
+    arrays = [message, message_x, near_own, near_x, halo]
+    picks = [(0, None)] + [(2, n_kvec - 1 - k) for k in range(1, n_kvec)]
+    picks += [(1, None)] + [(3, n_kvec - 1 - k) for k in range(1, n_kvec)]
     picks += [(4, k) for k in range(n_kvec)]
-    pair_msg = pair_message(
-        neighbours,
-        positions,
-        [bundle, gathered, bundle_x, gathered_x, halo],
-        picks,
-        pair_weight,
-    )
-
-    rest = far * (n_kvec - 1)
-    filt, away = inverse_away(
-        total, other, kfilt, pair_msg, [table_0, table_2], [(far, far), (0, rest)], shard
-    )
-    crossed = swap(away, "atoms", 1)
-    here = inverse_here(filt, [table_0, table_1], [(0, far), (0, rest)], shard)
-    own, *sends = join(here, crossed, n_kvec)
-    came = [swap(sends[k - 1], "kvec", k).astype(F32) for k in range(n_kvec - 1, 0, -1)]
-    for item in came:
-        own = own + item
-    parts = [own[:, :shard]]
-    for z in range(1, far):
-        parts.append(swap(own[:, z * shard : (z + 1) * shard].astype(BF16), "atoms", 4 * z))
+    pair_msg = pair_message(neighbours, positions, arrays, tuple(picks), pair_weight)
+
+    def runs(core, distances):
+        return tuple(where[core, z, k] for k in range(n_kvec) for z in distances)
+
+    filt, away_far = inverse_first(total, other, kfilt, pair_msg, tables, runs(1, zs), shard)
+    crossed_far = swap(away_far, "atoms", 1)
+    away_near = inverse(filt, tables, runs(1, (0,)), shard, BF16)
+    crossed_near = swap(away_near, "atoms", 1)
+    here_far = inverse(filt, tables, runs(0, zs), shard, F32)
+    sum_far, *sends = join(here_far, crossed_far, n_kvec)
+    for k in others:
+        sum_far = sum_far + swap(sends[k - 1], "kvec", k).astype(F32)
+    sum_far = sum_far.astype(BF16)
+    here_near = inverse(filt, tables, runs(0, (0,)), shard, F32)
+    own_near, *sends = join(here_near, crossed_near, n_kvec)
+    parts = [own_near] + [swap(sends[k - 1], "kvec", k) for k in others]
+    for z in zs:
+        parts.append(swap(sum_far[:, (z - 1) * shard : z * shard], "atoms", 4 * z))
     return update(features, pair_msg, norm_gain, w_in, w_out, parts)
 
 

time: 77.3 us -> 77.7 us (level)
  starting transfers between devices: 13.7 us -> 23.2 us
  waiting for transfers between devices: 33.7 us -> 27.8 us
  local copies, waits for them, and re-layouts: 1.64 us -> 0.03 us
  Pallas kernels: 27.8 us -> 26.2 us
    ppermute x12 -> x21, starting transfers between devices: 12.1 us -> 20.6 us  [swap(): lax.ppermute(value, axis, [(i, i ^ bits) for i in range(lax.axis_size(axi...]
    ppermute x12 -> x21, waiting for transfers between devices: 16.5 us -> 12.5 us  [swap(): lax.ppermute(value, axis, [(i, i ^ bits) for i in range(lax.axis_size(axi...]
    ppermute x1, waiting for transfers between devices: 17.3 us -> 15.3 us  [per_device(): halo = lax.ppermute(collect(own_group, picks), 'atoms', halo_pairs)]
    pallas_call x3 -> x4, Pallas kernels: 16.1 us -> 14.3 us  [wave(): pl.pallas_call(functools.partial(wave_kernel, counts, before is None, len...]
    unnamed x17 -> x14, local copies, waits for them, and re-layouts: 1.62 us -> 0.03 us
    ppermute x1, starting transfers between devices: 1.63 us -> 2.58 us  [per_device(): halo = lax.ppermute(collect(own_group, picks), 'atoms', halo_pairs)]
    pallas_call x3 -> x5, Pallas kernels: 3.04 us -> 3.35 us  [the longest x3 1.73 us: inverse(): pl.pallas_call(functools.partial(here_kernel, runs, shard), in_specs=[VME...]
  transfers between devices with their start and end apart: 13 -> 22, of which waited for: 8 -> 8; matrix products, arithmetic and copies ran while one was open for 1% -> 0% of each run, Pallas kernels for 24% -> 25%
where the time goes in v1:
time: 77.7 us; the launch traced here: 77.5 us
  waiting for transfers between devices  27.8 us (36%)
  Pallas kernels  26.2 us (34%)
  starting transfers between devices  23.2 us (30%)
    ppermute x21, starting transfers between devices, swap(): lax.ppermute(value, axis, [(i, i ^ bits) for i in range(lax.axis_size(axi...  20.6 us
    ppermute x1, waiting for transfers between devices, per_device(): halo = lax.ppermute(collect(own_group, picks), 'atoms', halo_pairs)  15.3 us
    pallas_call x4, Pallas kernels, wave(): pl.pallas_call(functools.partial(wave_kernel, counts, before is None, len...  14.3 us
    ppermute x21, waiting for transfers between devices, swap(): lax.ppermute(value, axis, [(i, i ^ bits) for i in range(lax.axis_size(axi...  12.5 us
    pallas_call x1, Pallas kernels, pair_message(): pl.pallas_call(functools.partial(pair_kernel, nbasis, pieces, scale, pick...  6.66 us
    ppermute x1, starting transfers between devices, per_device(): halo = lax.ppermute(collect(own_group, picks), 'atoms', halo_pairs)  2.58 us
    pallas_call x3, Pallas kernels, inverse(): pl.pallas_call(functools.partial(here_kernel, runs, shard), in_specs=[VME...  1.73 us
  transfers between devices with their start and end apart: 22, of which 8 were waited for; matrix products, arithmetic and copies ran while one was open for 0% of the time, Pallas kernels for 25%

profile of v1, /device:TPU:0, one launch (start us, length us, event | category | flops | bytes accessed | tf_op | source)
XLA Modules:
  0.0 77.5 jit_solution(6876192005602907518)
XLA Ops:
  0.0 1.0 %pack.1 = (bf16[144,256]{1,0:T(8,128)(2,1)S(1)}, s32[3,3072]{1,0:T(4,128)S(1)}, f32[8,128]{1,0:T(8,128)S(1)}) custom-call(bf16[256,128]{1,0:T(8,128)(2,1)} %refs_0_.3, s32[1,256]{1,0:T(1,128)} %bitcast.3, f32[3,256]{1,0:T(4,128)} %own_pos_ref.1, s32[3,3072]{1,0:T(4,128)} %refs_3_.2, f32[8,128]{1,0:T(8,128)} %refs_4_.2), custom_call_target="tpu_custom_call" | custom-call | tf_op jit(solution)/shard_map/pack/pallas_call | solution.py:74
  1.6 2.6 %collective-permute-start.3 = (bf16[144,256]{1,0:T(8,128)(2,1)S(1)}, bf16[144,256]{1,0:T(8,128)(2,1)S(1)}, u32[]{:S(2)}, u32[]{:S(2)}) collective-permute-start(bf16[144,256]{1,0:T(8,128)(2,1)S(1)} %get-tuple-element.29.refs_1_.refs_0_), channel_id=1, source_target_pairs={{0,1},{1,0},{2,3},{3,2},{4,5},{5,4},{6,7},{7,6},{8,9},{9,8},{10,11... | collective-permute-start | bytes 221192 | tf_op jit(solution)/shard_map/ppermute | solution.py:520
  4.1 1.5 %collective-permute-start.2 = (bf16[144,256]{1,0:T(8,128)(2,1)S(1)}, bf16[144,256]{1,0:T(8,128)(2,1)S(1)}, u32[]{:S(2)}, u32[]{:S(2)}) collective-permute-start(bf16[144,256]{1,0:T(8,128)(2,1)S(1)} %get-tuple-element.29.refs_1_.refs_0_), channel_id=1, source_target_pairs={{0,2},{1,3},{2,0},{3,1},{4,6},{5,7},{6,4},{7,5},{8,10},{9,11},{10,... | collective-permute-start | bytes 221192 | tf_op jit(solution)/shard_map/ppermute | solution.py:520
  6.2 1.5 %wave.4 = (bf16[6,256,512]{2,1,0:T(8,128)(2,1)S(1)}, f32[6,128,256]{2,1,0:T(8,128)S(1)}) custom-call(bf16[3,256,16]{2,1,0:T(8,128)(2,1)S(1)} %get-tuple-element.32.refs_0_, bf16[144,256]{1,0:T(8,128)(2,1)S(1)} %get-tuple-element.29.refs_1_.refs_0_, bf16[144,256]{1,0:T(8,128)(2,1)S(1)} %collective-permute-done.refs_2_.refs_1_), custom_call_target="tpu_custom_call" | custom-call | flops 201326592 | bytes 1572864 | tf_op jit(solution)/shard_map/wave/pallas_call | solution.py:236
  7.7 0.8 collective-permute-done.2.refs_1_
  8.5 2.4 %collective-permute-done.1.refs_0_ = bf16[144,256]{1,0:T(8,128)(2,1)S(1)} collective-permute-done((bf16[144,256]{1,0:T(8,128)(2,1)S(1)}, bf16[144,256]{1,0:T(8,128)(2,1)S(1)}, u32[]{:S(2)}, u32[]{:S(2)}) %collective-permute-start.1) | collective-permute-done | bytes 73760 | tf_op jit(solution)/shard_map/ppermute | solution.py:520
  11.0 2.7 %collective-permute-start.6 = (bf16[144,256]{1,0:T(8,128)(2,1)S(1)}, bf16[144,256]{1,0:T(8,128)(2,1)S(1)}, u32[]{:S(2)}, u32[]{:S(2)}) collective-permute-start(bf16[144,256]{1,0:T(8,128)(2,1)S(1)} %get-tuple-element.29.refs_1_.refs_0_), channel_id=1, source_target_pairs={{0,16},{4,20},{8,24},{12,28},{16,0},{20,4},{24,8},{28,12},{1,17},{... | collective-permute-start | bytes 221192 | tf_op jit(solution)/shard_map/ppermute | solution.py:520
  13.7 4.5 %collective-permute-done.6.refs_0_ = bf16[144,256]{1,0:T(8,128)(2,1)S(1)} collective-permute-done((bf16[144,256]{1,0:T(8,128)(2,1)S(1)}, bf16[144,256]{1,0:T(8,128)(2,1)S(1)}, u32[]{:S(2)}, u32[]{:S(2)}) %collective-permute-start.6) | collective-permute-done | bytes 73760 | tf_op jit(solution)/shard_map/ppermute | solution.py:520
  19.5 2.3 %collective-permute-start.8 = (bf16[1,144,256]{2,1,0:T(8,128)(2,1)S(1)}, bf16[1,144,256]{2,1,0:T(8,128)(2,1)S(1)}, u32[]{:S(2)}, u32[]{:S(2)}) collective-permute-start(bf16[1,144,256]{2,1,0:T(8,128)(2,1)S(1)} %collect.6.refs_1_), channel_id=1, source_target_pairs={{0,3},{1,2},{2,1},{3,0},{4,7},{5,6},{6,5},{7,4},{8,11},{9,10},{10,... | collective-permute-start | bytes 221192 | tf_op jit(solution)/shard_map/ppermute | solution.py:520
  21.7 5.3 %wave.5 = (bf16[6,256,1536]{2,1,0:T(8,128)(2,1)S(1)}, f32[6,128,256]{2,1,0:T(8,128)S(1)}) custom-call(bf16[3,256,16]{2,1,0:T(8,128)(2,1)S(1)} %get-tuple-element.32.refs_0_, bf16[3,144,256]{2,1,0:T(8,128)(2,1)S(1)} %collect.4.refs_1_.refs_2_, bf16[3,144,256]{2,1,0:T(8,128)(2,1)S(1)} %collective-permute-done.4.refs_3_.refs_2_, ...), custom_call_target="tpu_custom_call" | custom-call | flops 603979776 | bytes 4718592 | tf_op jit(solution)/shard_map/wave/pallas_call | solution.py:236
  27.7 3.7 %wave.6 = (bf16[6,256,1024]{2,1,0:T(8,128)(2,1)S(1)}, f32[6,128,256]{2,1,0:T(8,128)S(1)}) custom-call(bf16[3,256,16]{2,1,0:T(8,128)(2,1)S(1)} %get-tuple-element.32.refs_0_, bf16[1,144,256]{2,1,0:T(8,128)(2,1)S(1)} %collect.6.refs_1_, bf16[3,144,256]{2,1,0:T(8,128)(2,1)S(1)} %collect.7.refs_2_, f32[6,128,256]{2,1,0:T(8,128)S(1)} %get-tuple-element.34.refs_3_), custom_call_target="tpu_custom_call" | custom-call | flops 402653184 | bytes 3145728 | tf_op jit(solution)/shard_map/wave/pallas_call | solution.py:236
  31.5 3.7 %wave.7 = (bf16[6,256,1024]{2,1,0:T(8,128)(2,1)S(1)}, f32[6,128,256]{2,1,0:T(8,128)S(1)}, bf16[6,128,256]{2,1,0:T(8,128)(2,1)S(1)}) custom-call(bf16[3,256,16]{2,1,0:T(8,128)(2,1)S(1)} %get-tuple-element.32.refs_0_, bf16[1,144,256]{2,1,0:T(8,128)(2,1)S(1)} %collective-permute-done.7.refs_1_, bf16[3,144,256]{2,1,0:T(8,128)(2,1)S(1)} %collective-permute-done.11.refs_2_, ...), custom_call_target="tpu_custom_call" | custom-call | flops 402653184 | bytes 3145728 | tf_op jit(solution)/shard_map/wave/pallas_call | solution.py:236
  35.2 0.7 collective-permute-start.12
  36.0 2.6 %collective-permute-start.5 = (bf16[4,144,256]{2,1,0:T(8,128)(2,1)S(1)}, bf16[4,144,256]{2,1,0:T(8,128)(2,1)S(1)}, u32[]{:S(2)}, u32[]{:S(2)}) collective-permute-start(bf16[4,144,256]{2,1,0:T(8,128)(2,1)S(1)} %collect.5), channel_id=1, source_target_pairs={{0,28},{4,8},{8,4},{12,16},{16,12},{20,24},{24,20},{28,0},{1,29},{... | collective-permute-start | bytes 884744 | tf_op jit(solution)/shard_map/ppermute | solution.py:562
  38.5 15.3 %collective-permute-done.5.refs_4_ = bf16[4,144,256]{2,1,0:T(8,128)(2,1)S(1)} collective-permute-done((bf16[4,144,256]{2,1,0:T(8,128)(2,1)S(1)}, bf16[4,144,256]{2,1,0:T(8,128)(2,1)S(1)}, u32[]{:S(2)}, u32[]{:S(2)}) %collective-permute-start.5) | collective-permute-done | bytes 294944 | tf_op jit(solution)/shard_map/ppermute | solution.py:562
  53.8 6.7 %pair.1._.refs_1_ = f32[256,128]{1,0:T(8,128)S(1)} custom-call(s32[2,12]{1,0:T(2,128)S(1)} %copy-done.6, f32[3,256]{1,0:T(4,128)S(1)} %copy-done.3, bf16[144,256]{1,0:T(8,128)(2,1)S(1)} %get-tuple-element.29.refs_1_.refs_0_, bf16[144,256]{1,0:T(8,128)(2,1)S(1)} %collective-permute-done.refs_2_.refs_1_, bf16[3,144,256]{2,1,0:T(8,128)(2,1)S(1)} %collect.4.refs_1_.refs_2_, ...), custom_call_target="tpu_custom_call" | custom-call | flops 836763648 | bytes 786432 | tf_op jit(solution)/shard_map/pair/pallas_call | solution.py:470
  63.0 0.7 collective-permute-start.18
  63.7 1.3 %collective-permute-start.19 = (bf16[128,256]{1,0:T(8,128)(2,1)S(1)}, bf16[128,256]{1,0:T(8,128)(2,1)S(1)}, u32[]{:S(2)}, u32[]{:S(2)}) collective-permute-start(bf16[128,256]{1,0:T(8,128)(2,1)S(1)} %get-tuple-element.51), channel_id=1, source_target_pairs={{0,2},{1,3},{2,0},{3,1},{4,6},{5,7},{6,4},{7,5},{8,10},{9,11},{10,... | collective-permute-start | bytes 196616 | tf_op jit(solution)/shard_map/ppermute | solution.py:520
  65.1 1.6 %collective-permute-start.20 = (bf16[128,256]{1,0:T(8,128)(2,1)S(1)}, bf16[128,256]{1,0:T(8,128)(2,1)S(1)}, u32[]{:S(2)}, u32[]{:S(2)}) collective-permute-start(bf16[128,256]{1,0:T(8,128)(2,1)S(1)} %get-tuple-element.52), channel_id=1, source_target_pairs={{0,1},{1,0},{2,3},{3,2},{4,5},{5,4},{6,7},{7,6},{8,9},{9,8},{10,11... | collective-permute-start | bytes 196616 | tf_op jit(solution)/shard_map/ppermute | solution.py:520
  68.0 1.3 %collective-permute-start.15 = (bf16[128,256]{1,0:T(8,128)(2,1)S(1)}, bf16[128,256]{1,0:T(8,128)(2,1)S(1)}, u32[]{:S(2)}, u32[]{:S(2)}) collective-permute-start(bf16[128,256]{1,0:T(8,128)(2,1)S(1)} %get-tuple-element.45), channel_id=1, source_target_pairs={{0,2},{1,3},{2,0},{3,1},{4,6},{5,7},{6,4},{7,5},{8,10},{9,11},{10,... | collective-permute-start | bytes 196616 | tf_op jit(solution)/shard_map/ppermute | solution.py:520
  69.3 1.5 %collective-permute-start.16 = (bf16[128,256]{1,0:T(8,128)(2,1)S(1)}, bf16[128,256]{1,0:T(8,128)(2,1)S(1)}, u32[]{:S(2)}, u32[]{:S(2)}) collective-permute-start(bf16[128,256]{1,0:T(8,128)(2,1)S(1)} %get-tuple-element.46), channel_id=1, source_target_pairs={{0,1},{1,0},{2,3},{3,2},{4,5},{5,4},{6,7},{7,6},{8,9},{9,8},{10,11... | collective-permute-start | bytes 196616 | tf_op jit(solution)/shard_map/ppermute | solution.py:520
  71.4 1.2 %collective-permute-done.14.refs_6_ = bf16[128,256]{1,0:T(8,128)(2,1)S(1)} collective-permute-done((bf16[128,256]{1,0:T(8,128)(2,1)S(1)}, bf16[128,256]{1,0:T(8,128)(2,1)S(1)}, u32[]{:S(2)}, u32[]{:S(2)}) %collective-permute-start.14) | collective-permute-done | bytes 65568 | tf_op jit(solution)/shard_map/ppermute | solution.py:520
  73.6 2.6 %collective-permute-done.21.refs_9_ = bf16[128,256]{1,0:T(8,128)(2,1)S(1)} collective-permute-done((bf16[128,256]{1,0:T(8,128)(2,1)S(1)}, bf16[128,256]{1,0:T(8,128)(2,1)S(1)}, u32[]{:S(2)}, u32[]{:S(2)}) %collective-permute-start.21) | collective-permute-done | bytes 65568 | tf_op jit(solution)/shard_map/ppermute | solution.py:520
  76.3 1.3 %update.1 = bf16[256,128]{1,0:T(8,128)(2,1)} custom-call(bf16[256,128]{1,0:T(8,128)(2,1)S(1)} %copy-done, f32[256,128]{1,0:T(8,128)S(1)} %pair.1._.refs_1_, f32[1,128]{1,0:T(1,128)S(1)} %bitcast.2, bf16[128,512]{1,0:T(8,128)(2,1)S(1)} %copy-done.1, bf16[512,128]{1,0:T(8,128)(2,1)S(1)} %copy-done.2, f32[128,256]{1,0:T(8,128)S(1)} %get-tuple-element.43.refs_5_, ...), custom_call_target="tpu_custom_call" | custom-call | tf_op jit(solution)/shard_map/update/pallas_call | solution.py:509
  (53 shorter events, 8.5 us)
Async XLA Ops:
  1.0 5.1 %collective-permute-start = (bf16[144,256]{1,0:T(8,128)(2,1)S(1)}, bf16[144,256]{1,0:T(8,128)(2,1)S(1)}, u32[]{:S(2)}, u32[]{:S(2)}) collective-permute-start(bf16[144,256]{1,0:T(8,128)(2,1)S(1)} %get-tuple-element.29.refs_1_.refs_0_), channel_id=1, source_target_pairs={{0,4},{4,0},{8,12},{12,8},{16,20},{20,16},{24,28},{28,24},{1,5},{5... | collective-permute-start | bytes 221192 | tf_op jit(solution)/shard_map/ppermute | solution.py:520
  1.6 6.1 %collective-permute-start.3 = (bf16[144,256]{1,0:T(8,128)(2,1)S(1)}, bf16[144,256]{1,0:T(8,128)(2,1)S(1)}, u32[]{:S(2)}, u32[]{:S(2)}) collective-permute-start(bf16[144,256]{1,0:T(8,128)(2,1)S(1)} %get-tuple-element.29.refs_1_.refs_0_), channel_id=1, source_target_pairs={{0,1},{1,0},{2,3},{3,2},{4,5},{5,4},{6,7},{7,6},{8,9},{9,8},{10,11... | collective-permute-start | bytes 221192 | tf_op jit(solution)/shard_map/ppermute | solution.py:520
  4.1 4.4 %collective-permute-start.2 = (bf16[144,256]{1,0:T(8,128)(2,1)S(1)}, bf16[144,256]{1,0:T(8,128)(2,1)S(1)}, u32[]{:S(2)}, u32[]{:S(2)}) collective-permute-start(bf16[144,256]{1,0:T(8,128)(2,1)S(1)} %get-tuple-element.29.refs_1_.refs_0_), channel_id=1, source_target_pairs={{0,2},{1,3},{2,0},{3,1},{4,6},{5,7},{6,4},{7,5},{8,10},{9,11},{10,... | collective-permute-start | bytes 221192 | tf_op jit(solution)/shard_map/ppermute | solution.py:520
  5.7 5.3 %collective-permute-start.1 = (bf16[144,256]{1,0:T(8,128)(2,1)S(1)}, bf16[144,256]{1,0:T(8,128)(2,1)S(1)}, u32[]{:S(2)}, u32[]{:S(2)}) collective-permute-start(bf16[144,256]{1,0:T(8,128)(2,1)S(1)} %get-tuple-element.29.refs_1_.refs_0_), channel_id=1, source_target_pairs={{0,3},{1,2},{2,1},{3,0},{4,7},{5,6},{6,5},{7,4},{8,11},{9,10},{10,... | collective-permute-start | bytes 221192 | tf_op jit(solution)/shard_map/ppermute | solution.py:520
  10.9 10.8 %collective-permute-start.4 = (bf16[3,144,256]{2,1,0:T(8,128)(2,1)S(1)}, bf16[3,144,256]{2,1,0:T(8,128)(2,1)S(1)}, u32[]{:S(2)}, u32[]{:S(2)}) collective-permute-start(bf16[3,144,256]{2,1,0:T(8,128)(2,1)S(1)} %collect.4.refs_1_.refs_2_), channel_id=1, source_target_pairs={{0,4},{4,0},{8,12},{12,8},{16,20},{20,16},{24,28},{28,24},{1,5},{5... | collective-permute-start | bytes 663560 | tf_op jit(solution)/shard_map/ppermute | solution.py:520
  11.0 7.1 %collective-permute-start.6 = (bf16[144,256]{1,0:T(8,128)(2,1)S(1)}, bf16[144,256]{1,0:T(8,128)(2,1)S(1)}, u32[]{:S(2)}, u32[]{:S(2)}) collective-permute-start(bf16[144,256]{1,0:T(8,128)(2,1)S(1)} %get-tuple-element.29.refs_1_.refs_0_), channel_id=1, source_target_pairs={{0,16},{4,20},{8,24},{12,28},{16,0},{20,4},{24,8},{28,12},{1,17},{... | collective-permute-start | bytes 221192 | tf_op jit(solution)/shard_map/ppermute | solution.py:520
  18.2 35.6 %copy-start.3 = (f32[3,256]{1,0:T(4,128)S(1)}, f32[3,256]{1,0:T(4,128)}, u32[]{:S(2)}) copy-start(f32[3,256]{1,0:T(4,128)} %own_pos_ref.1) | copy-start | bytes 9220
  18.2 35.6 %copy-start.5 = (bf16[1024,128]{1,0:T(8,128)(2,1)S(1)}, bf16[1024,128]{1,0:T(8,128)(2,1)}, u32[]{:S(2)}) copy-start(bf16[1024,128]{1,0:T(8,128)(2,1)} %refs_5_.1) | copy-start | bytes 786436
  18.2 8.9 %collective-permute-start.10 = (bf16[1,144,256]{2,1,0:T(8,128)(2,1)S(1)}, bf16[1,144,256]{2,1,0:T(8,128)(2,1)S(1)}, u32[]{:S(2)}, u32[]{:S(2)}) collective-permute-start(bf16[1,144,256]{2,1,0:T(8,128)(2,1)S(1)} %collect.6.refs_1_), channel_id=1, source_target_pairs={{0,1},{1,0},{2,3},{3,2},{4,5},{5,4},{6,7},{7,6},{8,9},{9,8},{10,11... | collective-permute-start | bytes 221192 | tf_op jit(solution)/shard_map/ppermute | solution.py:520
  18.8 8.3 %collective-permute-start.9 = (bf16[1,144,256]{2,1,0:T(8,128)(2,1)S(1)}, bf16[1,144,256]{2,1,0:T(8,128)(2,1)S(1)}, u32[]{:S(2)}, u32[]{:S(2)}) collective-permute-start(bf16[1,144,256]{2,1,0:T(8,128)(2,1)S(1)} %collect.6.refs_1_), channel_id=1, source_target_pairs={{0,2},{1,3},{2,0},{3,1},{4,6},{5,7},{6,4},{7,5},{8,10},{9,11},{10,... | collective-permute-start | bytes 221192 | tf_op jit(solution)/shard_map/ppermute | solution.py:520
  19.5 7.6 %collective-permute-start.8 = (bf16[1,144,256]{2,1,0:T(8,128)(2,1)S(1)}, bf16[1,144,256]{2,1,0:T(8,128)(2,1)S(1)}, u32[]{:S(2)}, u32[]{:S(2)}) collective-permute-start(bf16[1,144,256]{2,1,0:T(8,128)(2,1)S(1)} %collect.6.refs_1_), channel_id=1, source_target_pairs={{0,3},{1,2},{2,1},{3,0},{4,7},{5,6},{6,5},{7,4},{8,11},{9,10},{10,... | collective-permute-start | bytes 221192 | tf_op jit(solution)/shard_map/ppermute | solution.py:520
  27.2 4.3 %collective-permute-start.11 = (bf16[3,144,256]{2,1,0:T(8,128)(2,1)S(1)}, bf16[3,144,256]{2,1,0:T(8,128)(2,1)S(1)}, u32[]{:S(2)}, u32[]{:S(2)}) collective-permute-start(bf16[3,144,256]{2,1,0:T(8,128)(2,1)S(1)} %collect.7.refs_2_), channel_id=1, source_target_pairs={{0,4},{4,0},{8,12},{12,8},{16,20},{20,16},{24,28},{28,24},{1,5},{5... | collective-permute-start | bytes 663560 | tf_op jit(solution)/shard_map/ppermute | solution.py:520
  27.2 4.2 %collective-permute-start.7 = (bf16[1,144,256]{2,1,0:T(8,128)(2,1)S(1)}, bf16[1,144,256]{2,1,0:T(8,128)(2,1)S(1)}, u32[]{:S(2)}, u32[]{:S(2)}) collective-permute-start(bf16[1,144,256]{2,1,0:T(8,128)(2,1)S(1)} %collect.6.refs_1_), channel_id=1, source_target_pairs={{0,4},{4,0},{8,12},{12,8},{16,20},{20,16},{24,28},{28,24},{1,5},{5... | collective-permute-start | bytes 221192 | tf_op jit(solution)/shard_map/ppermute | solution.py:520
  35.2 25.3 %collective-permute-start.12 = (bf16[6,128,256]{2,1,0:T(8,128)(2,1)S(1)}, bf16[6,128,256]{2,1,0:T(8,128)(2,1)S(1)}, u32[]{:S(2)}, u32[]{:S(2)}) collective-permute-start(bf16[6,128,256]{2,1,0:T(8,128)(2,1)S(1)} %get-tuple-element.37), channel_id=1, source_target_pairs={{0,8},{4,12},{8,0},{12,4},{16,24},{20,28},{24,16},{28,20},{1,9},{5... | collective-permute-start | bytes 1179656 | tf_op jit(solution)/shard_map/ppermute | solution.py:520
  36.0 17.9 %collective-permute-start.5 = (bf16[4,144,256]{2,1,0:T(8,128)(2,1)S(1)}, bf16[4,144,256]{2,1,0:T(8,128)(2,1)S(1)}, u32[]{:S(2)}, u32[]{:S(2)}) collective-permute-start(bf16[4,144,256]{2,1,0:T(8,128)(2,1)S(1)} %collect.5), channel_id=1, source_target_pairs={{0,28},{4,8},{8,4},{12,16},{16,12},{20,24},{24,20},{28,0},{1,29},{... | collective-permute-start | bytes 884744 | tf_op jit(solution)/shard_map/ppermute | solution.py:562
  61.1 1.8 %collective-permute-start.17 = (bf16[128,1024]{1,0:T(8,128)(2,1)S(1)}, bf16[128,1024]{1,0:T(8,128)(2,1)S(1)}, u32[]{:S(2)}, u32[]{:S(2)}) collective-permute-start(bf16[128,1024]{1,0:T(8,128)(2,1)S(1)} %get-tuple-element.48), channel_id=1, source_target_pairs={{0,4},{4,0},{8,12},{12,8},{16,20},{20,16},{24,28},{28,24},{1,5},{5... | collective-permute-start | bytes 786440 | tf_op jit(solution)/shard_map/ppermute | solution.py:520
  61.8 5.4 %collective-permute-start.13 = (bf16[128,1024]{1,0:T(8,128)(2,1)S(1)}, bf16[128,1024]{1,0:T(8,128)(2,1)S(1)}, u32[]{:S(2)}, u32[]{:S(2)}) collective-permute-start(bf16[128,1024]{1,0:T(8,128)(2,1)S(1)} %inverse.4), channel_id=1, source_target_pairs={{0,4},{4,0},{8,12},{12,8},{16,20},{20,16},{24,28},{28,24},{1,5},{5... | collective-permute-start | bytes 786440 | tf_op jit(solution)/shard_map/ppermute | solution.py:520
  63.0 6.3 %collective-permute-start.18 = (bf16[128,256]{1,0:T(8,128)(2,1)S(1)}, bf16[128,256]{1,0:T(8,128)(2,1)S(1)}, u32[]{:S(2)}, u32[]{:S(2)}) collective-permute-start(bf16[128,256]{1,0:T(8,128)(2,1)S(1)} %get-tuple-element.50), channel_id=1, source_target_pairs={{0,3},{1,2},{2,1},{3,0},{4,7},{5,6},{6,5},{7,4},{8,11},{9,10},{10,... | collective-permute-start | bytes 196616 | tf_op jit(solution)/shard_map/ppermute | solution.py:520
  63.7 7.1 %collective-permute-start.19 = (bf16[128,256]{1,0:T(8,128)(2,1)S(1)}, bf16[128,256]{1,0:T(8,128)(2,1)S(1)}, u32[]{:S(2)}, u32[]{:S(2)}) collective-permute-start(bf16[128,256]{1,0:T(8,128)(2,1)S(1)} %get-tuple-element.51), channel_id=1, source_target_pairs={{0,2},{1,3},{2,0},{3,1},{4,6},{5,7},{6,4},{7,5},{8,10},{9,11},{10,... | collective-permute-start | bytes 196616 | tf_op jit(solution)/shard_map/ppermute | solution.py:520
  65.1 5.8 %collective-permute-start.20 = (bf16[128,256]{1,0:T(8,128)(2,1)S(1)}, bf16[128,256]{1,0:T(8,128)(2,1)S(1)}, u32[]{:S(2)}, u32[]{:S(2)}) collective-permute-start(bf16[128,256]{1,0:T(8,128)(2,1)S(1)} %get-tuple-element.52), channel_id=1, source_target_pairs={{0,1},{1,0},{2,3},{3,2},{4,5},{5,4},{6,7},{7,6},{8,9},{9,8},{10,11... | collective-permute-start | bytes 196616 | tf_op jit(solution)/shard_map/ppermute | solution.py:520
  67.3 5.3 %collective-permute-start.14 = (bf16[128,256]{1,0:T(8,128)(2,1)S(1)}, bf16[128,256]{1,0:T(8,128)(2,1)S(1)}, u32[]{:S(2)}, u32[]{:S(2)}) collective-permute-start(bf16[128,256]{1,0:T(8,128)(2,1)S(1)} %get-tuple-element.44), channel_id=1, source_target_pairs={{0,3},{1,2},{2,1},{3,0},{4,7},{5,6},{6,5},{7,4},{8,11},{9,10},{10,... | collective-permute-start | bytes 196616 | tf_op jit(solution)/shard_map/ppermute | solution.py:520
  68.0 5.0 %collective-permute-start.15 = (bf16[128,256]{1,0:T(8,128)(2,1)S(1)}, bf16[128,256]{1,0:T(8,128)(2,1)S(1)}, u32[]{:S(2)}, u32[]{:S(2)}) collective-permute-start(bf16[128,256]{1,0:T(8,128)(2,1)S(1)} %get-tuple-element.45), channel_id=1, source_target_pairs={{0,2},{1,3},{2,0},{3,1},{4,6},{5,7},{6,4},{7,5},{8,10},{9,11},{10,... | collective-permute-start | bytes 196616 | tf_op jit(solution)/shard_map/ppermute | solution.py:520
  69.3 4.3 %collective-permute-start.16 = (bf16[128,256]{1,0:T(8,128)(2,1)S(1)}, bf16[128,256]{1,0:T(8,128)(2,1)S(1)}, u32[]{:S(2)}, u32[]{:S(2)}) collective-permute-start(bf16[128,256]{1,0:T(8,128)(2,1)S(1)} %get-tuple-element.46), channel_id=1, source_target_pairs={{0,1},{1,0},{2,3},{3,2},{4,5},{5,4},{6,7},{7,6},{8,9},{9,8},{10,11... | collective-permute-start | bytes 196616 | tf_op jit(solution)/shard_map/ppermute | solution.py:520
  70.9 5.4 %collective-permute-start.21 = (bf16[128,256]{1,0:T(8,128)(2,1)S(1)}, bf16[128,256]{1,0:T(8,128)(2,1)S(1)}, u32[]{:S(2)}, u32[]{:S(2)}) collective-permute-start(bf16[128,256]{1,0:T(8,128)(2,1)S(1)} %add_convert_fusion), channel_id=1, source_target_pairs={{0,16},{4,20},{8,24},{12,28},{16,0},{20,4},{24,8},{28,12},{1,17},{... | collective-permute-start | bytes 196616 | tf_op jit(solution)/shard_map/ppermute | solution.py:520
  (5 other events, 80.4 us)

commit v2 on v1

v2 whole, which is shorter than its diff:
```python
import functools
import math

import jax
import jax.numpy as jnp
from jax import lax
from jax.experimental import pallas as pl
from jax.experimental.pallas import tpu as pltpu
from jax.sharding import PartitionSpec as P

KW = 12288
BLOCK_ATOMS = 128
F32 = jnp.float32
BF16 = jnp.bfloat16

SIN_COEF = (4.442879586561992, -7.307818050390618, 3.5977887417720016, -0.7912382192058507)
ROUND = 12582912.0
SLACK = 1e-5
TAIL = 16


def params(mib=16):
    return pltpu.CompilerParams(vmem_limit_bytes=mib << 20)


SMEM = pl.BlockSpec(memory_space=pltpu.SMEM)
VMEM = pl.BlockSpec(memory_space=pltpu.VMEM)
ANY = pl.BlockSpec(memory_space=pl.ANY)


def horner(u, coef):
    acc = coef[-1] * u + coef[-2]
    for c in reversed(coef[:-2]):
        acc = acc * u + c
    return acc


def pack_kernel(*refs):
    features_hbm, mask_hbm, pos_hbm, lattice_hbm, kfilter_hbm = refs[:5]
    out_ref, lattice_ref, kfilter_ref, features_ref, mask_ref, pos_ref, scr, sems = refs[5:]
    copies = [
        pltpu.make_async_copy(source, target, sems.at[i])
        for i, (source, target) in enumerate(
            (
                (features_hbm, features_ref),
                (mask_hbm, mask_ref),
                (pos_hbm, pos_ref),
                (lattice_hbm, lattice_ref),
                (kfilter_hbm, kfilter_ref),
            )
        )
    ]
    for copy in copies:
        copy.start()
    for copy in copies:
        copy.wait()
    channels = features_ref.shape[1]
    mask = mask_ref[...].astype(F32)
    out_ref[0:channels, :] = (features_ref[...].astype(F32).T * mask).astype(BF16)
    value = pos_ref[...] * 0.125
    high = value.astype(BF16).astype(F32)
    rest = value - high
    mid = rest.astype(BF16).astype(F32)
    scr[...] = jnp.zeros_like(scr)
    scr[0:3, :] = high
    scr[3:6, :] = mid
    scr[6:9, :] = rest - mid
    out_ref[channels : channels + TAIL, :] = scr[...].astype(BF16)


def pack(features, mask, positions, lattice, kfilter):
    shard, channels = features.shape
    arrays = (features, mask[None, :], positions, lattice, kfilter)
    return pl.pallas_call(
        pack_kernel,
        in_specs=[pl.BlockSpec(memory_space=pltpu.HBM)] * 5,
        out_specs=[VMEM] * 3,
        out_shape=[
            jax.ShapeDtypeStruct((channels + TAIL, shard), BF16),
            jax.ShapeDtypeStruct(lattice.shape, lattice.dtype),
            jax.ShapeDtypeStruct(kfilter.shape, kfilter.dtype),
        ],
        scratch_shapes=[
            pltpu.VMEM((shard, channels), BF16),
            pltpu.VMEM((1, shard), jnp.int32),
            pltpu.VMEM((3, shard), F32),
            pltpu.VMEM((TAIL, shard), F32),
            pltpu.SemaphoreType.DMA((5,)),
        ],
        compiler_params=params(),
        name="pack",
    )(*(pltpu.with_memory_space_constraint(x, pltpu.HBM) for x in arrays))


def setup_kernel(far, nbasis, scale, lattice_ref, kfilter_ref, wave_ref, kfilt_ref, scr):
    blocks, width, _ = wave_ref.shape
    a_index = lax.axis_index("atoms")
    part = a_index % 2 + 2 * (a_index // 4)
    count = blocks * width
    kfilter = kfilter_ref[...].T
    for j in range(blocks):
        lattice = jnp.zeros((3, width), F32)
        for p in range(2 * far):
            at = p * count + j * width
            mine = (part == p).astype(F32)
            lattice += lattice_ref[:, at : at + width].astype(F32) * mine
        scr[...] = jnp.zeros_like(scr)
        for copy in range(3):
            scr[3 * copy : 3 * copy + 3, :] = lattice
        wave_ref[j] = scr[...].T.astype(BF16)
        wave = lattice * (2.0 * math.pi / 8.0)
        kmag = jnp.sqrt(
            wave[0:1] * wave[0:1] + wave[1:2] * wave[1:2] + wave[2:3] * wave[2:3]
        )
        total = jnp.zeros(kfilt_ref.shape[1:], F32)
        for p in range(nbasis):
            basis = jnp.exp(-0.5 * ((kmag - (p + 0.5) * (21.0 / nbasis)) / (21.0 / nbasis)) ** 2)
            total += kfilter[:, p : p + 1] * basis
        kfilt_ref[j] = total * scale


def setup(lattice, kfilter, far, width, scale):
    nbasis, channels = kfilter.shape
    blocks = lattice.shape[1] // (2 * far * width)
    return pl.pallas_call(
        functools.partial(setup_kernel, far, nbasis, scale),
        in_specs=[VMEM] * 2,
        out_specs=[VMEM] * 2,
        out_shape=[
            jax.ShapeDtypeStruct((blocks, width, TAIL), BF16),
            jax.ShapeDtypeStruct((blocks, channels, width), F32),
        ],
        scratch_shapes=[pltpu.VMEM((TAIL, width), F32)],
        compiler_params=params(),
        name="setup",
    )(lattice, kfilter)


def wave_kernel(picks, arrays, first, start, waits, low, *refs):
    refs = list(refs)
    take = lambda n: [refs.pop(0) for _ in range(n)]
    (lattice_ref,) = take(1)
    messages = take(arrays)
    before_ref = None if start else take(1)[0]
    take(waits)
    table_ref, total_ref = take(2)
    low_ref = take(1)[0] if low else None
    feat_scr, pos_scr, phase_scr = refs
    blocks, width = table_ref.shape[0] // 2, table_ref.shape[1]
    every = lattice_ref.shape[0]
    pairs, _, both = pos_scr.shape
    channels = feat_scr.shape[0]
    shard = both // 2
    for place, (array, index) in enumerate(picks):
        item = messages[array] if index is None else messages[array].at[index]
        feat_scr[:, place * shard : (place + 1) * shard] = item[0:channels, :]
        lanes = slice(place % 2 * shard, (place % 2 + 1) * shard)
        pos_scr[place // 2, :, lanes] = item[channels:, :]
    steps = pairs * blocks

    def phase(i):
        phase_scr[...] = jnp.dot(
            lattice_ref[first + i % blocks], pos_scr[i // blocks], preferred_element_type=F32
        )

    def table(i):
        pair, block = i // blocks, i % blocks
        lanes = pl.ds(pl.multiple_of(pair * both, both), both)
        rows = 16
        for at in range(0, width, rows):
            turns = phase_scr[at : at + rows, :]
            r = turns - ((turns + ROUND) - ROUND)
            s = horner(r * r, SIN_COEF) * r
            square = s * s
            w = (2.0 + SLACK) - square
            table_ref[block, at : at + rows, lanes] = (1.0 - square).astype(BF16)
            table_ref[blocks + block, at : at + rows, lanes] = (s * (w * lax.rsqrt(w))).astype(BF16)

    def body(i, carry):
        table(i)
        phase(jnp.minimum(i + 1, steps - 1))
        return carry

    phase(0)
    lax.fori_loop(0, steps, body, 0)
    for j in range(2 * blocks):
        part = lax.dot_general(
            feat_scr[...], table_ref[j], (((1,), (1,)), ((), ())), preferred_element_type=F32
        )
        if not start:
            part += before_ref[j // blocks * every + first + j % blocks]
        total_ref[j] = part
        if low:
            low_ref[j] = part.astype(BF16)


def wave(lattice, arrays, picks, before, subset=None, after=(), low=False):
    every, width, _ = lattice.shape
    first, blocks = subset or (0, every)
    pieces = len(picks)
    rows, shard = arrays[0].shape[-2:]
    channels = rows - TAIL
    args = [lattice, *arrays] + ([] if before is None else [before])
    factor = (2 * blocks, channels, width)
    shapes = [
        jax.ShapeDtypeStruct((2 * blocks, width, pieces * shard), BF16),
        jax.ShapeDtypeStruct(factor, F32),
    ]
    if low:
        shapes.append(jax.ShapeDtypeStruct(factor, BF16))
    pairs = blocks * width * pieces * shard
    return pl.pallas_call(
        functools.partial(
            wave_kernel, tuple(picks), len(arrays), first, before is None, len(after), low
        ),
        in_specs=[VMEM] * len(args) + [ANY] * len(after),
        out_specs=[VMEM] * len(shapes),
        out_shape=shapes,
        scratch_shapes=[
            pltpu.VMEM((channels, pieces * shard), BF16),
            pltpu.VMEM((pieces // 2, TAIL, 2 * shard), BF16),
            pltpu.VMEM((width, 2 * shard), F32),
        ],
        compiler_params=params(),
        cost_estimate=pl.CostEstimate(
            flops=4 * pairs * channels, bytes_accessed=4 * pairs, transcendentals=pairs
        ),
        name="wave",
    )(*args, *after)


def collect_kernel(picks, *refs):
    for p, (array, index) in enumerate(picks):
        ref = refs[array]
        refs[-1][p] = ref[...] if index is None else ref[index]


def collect(arrays, picks, after=()):
    return pl.pallas_call(
        functools.partial(collect_kernel, picks),
        in_specs=[VMEM] * len(arrays) + [ANY] * len(after),
        out_specs=VMEM,
        out_shape=jax.ShapeDtypeStruct((len(picks), *arrays[0].shape[-2:]), BF16),
        compiler_params=params(),
        name="collect",
    )(*arrays, *after)


def transform(filt_ref, table_refs, pieces, out_ref, shard):
    for at, places in enumerate(pieces):
        acc = None
        for j, (table, index, place) in enumerate(places):
            part = jnp.dot(
                filt_ref[j],
                table_refs[table][index, :, place * shard : (place + 1) * shard],
                preferred_element_type=F32,
            )
            acc = part if acc is None else acc + part
        out_ref[:, at * shard : (at + 1) * shard] = acc.astype(out_ref.dtype)


def first_kernel(pieces, shard, parts, blocks, *refs):
    own_refs, other_refs, refs = refs[:parts], refs[parts : 2 * parts], refs[2 * parts :]
    kfilt_ref, table_refs, (filt_ref, out_ref) = refs[0], refs[2:-2], refs[-2:]
    count = kfilt_ref.shape[0]
    for half in range(2):
        for j in range(count):
            part, index = j // blocks, half * blocks + j % blocks
            total = own_refs[part][index] + other_refs[part][index].astype(F32)
            filt_ref[half * count + j] = (total * kfilt_ref[j]).astype(BF16)
    transform(filt_ref, table_refs, pieces, out_ref, shard)


def inverse_kernel(pieces, shard, filt_ref, *refs):
    transform(filt_ref, refs[:-1], pieces, refs[-1], shard)


def inverse_cost(count, channels, width, atoms):
    return pl.CostEstimate(
        flops=2 * count * channels * width * atoms,
        bytes_accessed=2 * count * width * atoms,
        transcendentals=0,
    )


def used(tables, pieces):
    names = sorted({place[0] for places in pieces for place in places})
    moved = tuple(tuple((names.index(t), i, p) for t, i, p in places) for places in pieces)
    return [tables[t] for t in names], moved


def inverse_first(own, other, kfilt, after, tables, pieces, shard):
    count, channels, width = kfilt.shape
    tables, pieces = used(tables, pieces)
    atoms = shard * len(pieces)
    blocks = count // len(own)
    return pl.pallas_call(
        functools.partial(first_kernel, pieces, shard, len(own), blocks),
        in_specs=[VMEM] * (2 * len(own) + 1) + [ANY] + [VMEM] * len(tables),
        out_specs=[VMEM] * 2,
        out_shape=[
            jax.ShapeDtypeStruct((2 * count, channels, width), BF16),
            jax.ShapeDtypeStruct((channels, atoms), BF16),
        ],
        compiler_params=params(),
        cost_estimate=inverse_cost(2 * count, channels, width, atoms),
        name="first",
    )(*own, *other, kfilt, after, *tables)


def inverse(filt, tables, pieces, shard, dtype):
    count, channels, width = filt.shape
    tables, pieces = used(tables, pieces)
    atoms = shard * len(pieces)
    return pl.pallas_call(
        functools.partial(inverse_kernel, pieces, shard),
        in_specs=[VMEM] * (1 + len(tables)),
        out_specs=VMEM,
        out_shape=jax.ShapeDtypeStruct((channels, atoms), dtype),
        compiler_params=params(),
        cost_estimate=inverse_cost(count, channels, width, atoms),
        name="inverse",
    )(filt, *tables)


def join_kernel(here_ref, arrived_ref, own_ref, *send_refs):
    width = own_ref.shape[1]
    for p in range(len(send_refs) + 1):
        lanes = slice(p * width, (p + 1) * width)
        total = here_ref[:, lanes] + arrived_ref[:, lanes].astype(F32)
        if p:
            send_refs[p - 1][...] = total.astype(BF16)
        else:
            own_ref[...] = total


def join(here, arrived, pieces):
    channels, atoms = here.shape
    shape = (channels, atoms // pieces)
    return pl.pallas_call(
        join_kernel,
        in_specs=[VMEM] * 2,
        out_specs=[VMEM] * pieces,
        out_shape=[jax.ShapeDtypeStruct(shape, F32)]
        + [jax.ShapeDtypeStruct(shape, BF16)] * (pieces - 1),
        compiler_params=params(),
        name="join",
    )(here, arrived)


def pair_kernel(nbasis, pieces, output_scale, picks, arrays, neighbours_ref, own_pos_ref, *refs):
    message_refs, refs = refs[:arrays], refs[arrays:]
    weight_ref, _, out_ref, feat_scr, pos_scr, own_scr, basis_scr, near_scr = refs
    block = BLOCK_ATOMS
    width = 12.0 / nbasis
    own_blocks, neighbours = neighbours_ref.shape
    shard = own_blocks * block
    channels = out_ref.shape[0]

    views = [
        message_refs[array] if index is None else message_refs[array].at[index]
        for array, index in picks
    ]
    for place, ref in enumerate(views):
        lanes = slice(place * shard, (place + 1) * shard)
        feat_scr[:, lanes] = ref[0:channels, :]
        parts = ref[channels:, :].astype(F32)
        pos_scr[0:3, lanes] = (parts[0:3] + parts[3:6] + parts[6:9]) * 8.0

    a_index = lax.axis_index("atoms")
    k_index = lax.axis_index("kvec")
    n_atoms = lax.axis_size("atoms")
    group_blk = own_blocks * pieces
    first = (a_index * pieces + k_index) * own_blocks
    toward = jnp.where(a_index % 2 == 0, 1, n_atoms - 1)

    def place_of(ident):
        group, within = ident // group_blk, ident % group_blk
        ahead = (group - a_index + n_atoms) % n_atoms
        which = jnp.where(ahead == 0, 0, jnp.where(ahead == toward, 1, 2))
        piece = (within // own_blocks) ^ k_index
        return (which * pieces + piece) * own_blocks + within % own_blocks

    rows = 32
    diagonal = lax.broadcasted_iota(jnp.int32, (rows, block), 0) - lax.broadcasted_iota(
        jnp.int32, (rows, block), 1
    )
    for b in range(own_blocks):
        for d in range(3):
            row = own_pos_ref[d : d + 1, b * block : (b + 1) * block]
            own_scr[d] = jnp.broadcast_to(row, (block, block)).T

        def pair(n, carry):
            ident = neighbours_ref[b, n]
            lanes = pl.ds(pl.multiple_of(place_of(ident) * block, block), block)
            here = pl.ds(pl.multiple_of(n * block, block), block)
            near_scr[:, here] = feat_scr[:, lanes]
            same = ident == first + b
            near = [pos_scr[d : d + 1, lanes] for d in range(3)]
            for at in range(0, block, rows):
                dist2 = (own_scr[0, at : at + rows, :] - near[0]) ** 2
                dist2 += (own_scr[1, at : at + rows, :] - near[1]) ** 2
                dist2 += (own_scr[2, at : at + rows, :] - near[2]) ** 2
                radius = dist2 * lax.rsqrt(jnp.maximum(dist2, 1e-30))
                env = output_scale / (1.0 + dist2 * (1.0 / 16.0))
                env = jnp.where((diagonal + at == 0) & same, 0.0, env)
                v = radius * (1.0 / width) - 0.5
                value = jnp.exp(-0.5 * v * v) * env
                ratio = jnp.exp(v)
                for k in range(nbasis):
                    if k:
                        value = value * ratio
                    basis_scr[k * block + at : k * block + at + rows, here] = value.astype(BF16)
            return carry

        lax.fori_loop(0, neighbours, pair, 0)
        total = jnp.zeros((channels, block), F32)
        for k in range(nbasis):
            gathered = lax.dot_general(
                near_scr[...],
                basis_scr[k * block : (k + 1) * block, :],
                (((1,), (1,)), ((), ())),
                preferred_element_type=F32,
            )
            total += lax.dot_general(
                weight_ref[k * channels : (k + 1) * channels, :],
                (gathered * math.exp(-0.5 * k * k)).astype(BF16),
                (((0,), (0,)), ((), ())),
                preferred_element_type=F32,
            )
        out_ref[:, b * block : (b + 1) * block] = total


def pair_message(neighbours, own_pos, arrays, picks, weight, after):
    channels = weight.shape[1]
    nbasis = weight.shape[0] // channels
    pieces = len(picks) // 3
    shard = own_pos.shape[1]
    count = neighbours.shape[1]
    scale = float(count * BLOCK_ATOMS) ** (-0.5)
    window = 3 * pieces * shard
    return pl.pallas_call(
        functools.partial(pair_kernel, nbasis, pieces, scale, picks, len(arrays)),
        in_specs=[SMEM] + [VMEM] * (2 + len(arrays)) + [ANY],
        out_specs=VMEM,
        out_shape=jax.ShapeDtypeStruct((channels, shard), F32),
        scratch_shapes=[
            pltpu.VMEM((channels, window), BF16),
            pltpu.VMEM((8, window), F32),
            pltpu.VMEM((3, BLOCK_ATOMS, BLOCK_ATOMS), F32),
            pltpu.VMEM((nbasis * BLOCK_ATOMS, count * BLOCK_ATOMS), BF16),
            pltpu.VMEM((channels, count * BLOCK_ATOMS), BF16),
        ],
        compiler_params=params(),
        cost_estimate=pl.CostEstimate(
            flops=2 * shard * count * BLOCK_ATOMS * (nbasis * channels + 40),
            bytes_accessed=2 * window * channels,
            transcendentals=3 * shard * count * BLOCK_ATOMS,
        ),
        name="pair",
    )(neighbours, own_pos, *arrays, weight, after)


def update_kernel(*refs):
    features_ref, pair_ref, gain_ref, w_in_ref, w_out_ref = refs[:5]
    parts, out_ref = refs[5:-1], refs[-1]
    long_t = parts[0][...].astype(F32)
    for part in parts[1:]:
        long_t = long_t + part[...].astype(F32)
    total = features_ref[...].astype(F32) + (pair_ref[...] + long_t).T
    mean = jnp.mean(total * total, axis=-1, keepdims=True)
    normed = (total * lax.rsqrt(mean + 1e-06) * gain_ref[...]).astype(BF16)
    pre = jnp.dot(normed, w_in_ref[...], preferred_element_type=F32)
    hidden = (pre / (1.0 + jnp.exp(-pre))).astype(BF16)
    out_ref[...] = (
        total + jnp.dot(hidden, w_out_ref[...], preferred_element_type=F32)
    ).astype(BF16)


def update(features, pair_msg, gain, w_in, w_out, parts):
    return pl.pallas_call(
        update_kernel,
        in_specs=[VMEM] * (5 + len(parts)),
        out_specs=VMEM,
        out_shape=jax.ShapeDtypeStruct(features.shape, BF16),
        compiler_params=params(),
        name="update",
    )(features, pair_msg, gain[None, :], w_in, w_out, *parts)


def swap(value, axis, bits):
    return lax.ppermute(value, axis, [(i, i ^ bits) for i in range(lax.axis_size(axis))])


def per_device(
    positions,
    features,
    atom_mask,
    neighbours,
    lattice,
    pair_weight,
    kfilter,
    norm_gain,
    w_in,
    w_out,
):
    shard, _ = features.shape
    n_atoms = lax.axis_size("atoms")
    n_kvec = lax.axis_size("kvec")
    far = n_atoms // 4
    count = lattice.shape[1] // (2 * far)
    width = 256 if count % 256 == 0 else count

    message, lattice, kfilter = pack(features, atom_mask, positions, lattice, kfilter)
    scale = float(n_atoms * n_kvec * shard * KW) ** (-0.5)
    waves, kfilt = setup(lattice, kfilter, far, width, scale)
    others = range(n_kvec - 1, 0, -1)
    zs = range(1, far)
    message_x = swap(message, "atoms", 1)
    near = {k: swap(message, "kvec", k) for k in others}
    distant = [swap(message, "atoms", 4 * z) for z in zs]
    blocks = waves.shape[0]
    tables, where = [], {}

    def keep(table, names):
        tables.append(table)
        for place, name in enumerate(names):
            where[name] = tuple((len(tables) - 1, j, place) for j in range(2 * blocks))

    table, total = wave(waves, [message, message_x], [(0, None), (1, None)], None)
    keep(table, [(0, 0, 0), (1, 0, 0)])
    near_own = collect([near[k] for k in others], [(i, None) for i in range(n_kvec - 1)], after=(total,))
    near_x = swap(near_own, "atoms", 1)
    names = [(0, 0, k) for k in others] + [(1, 0, k) for k in others]
    picks = [(core, i) for core in range(2) for i in range(n_kvec - 1)]
    table, total = wave(waves, [near_own], picks[:2], total)
    keep(table, names[:2])
    distant = collect(distant, [(z, None) for z in range(far - 1)], after=(total,))
    distant_x = swap(distant, "atoms", 1)
    relayed = {k: swap(distant, "kvec", k) for k in others}
    halo_pairs = [(a, (a + 1) % n_atoms if a % 2 else (a - 1) % n_atoms) for a in range(n_atoms)]
    group = [(0, None)] + [(1, n_kvec - 1 - k) for k in range(1, n_kvec)]
    halo = lax.ppermute(collect([message, near_own], group), "atoms", halo_pairs)
    table, total = wave(waves, [near_own, near_x], picks[2:], total)
    keep(table, names[2:])
    every = [(i, z) for i in range(n_kvec - 1) for z in range(far - 1)]
    far_own = collect([relayed[k] for k in others], every, after=(total,))
    far_x = swap(far_own, "atoms", 1)
    picks = [(0, z) for z in range(far - 1)] + [(1, i) for i in range(len(every))]
    spots = [(z, k) for k in (0, *others) for z in zs]
    table, total = wave(waves, [distant, far_own], picks, total)
    keep(table, [(0, *spot) for spot in spots])
    own_factors, other_factors, low = [], [], None
    for j in range(blocks):
        after = () if low is None else (low,)
        table, part, low = wave(
            waves, [distant_x, far_x], picks, total, subset=(j, 1), after=after, low=True
        )
        tables.append(table)
        own_factors.append(part)
        other_factors.append(swap(low, "atoms", 2))
    for place, spot in enumerate(spots):
        first = len(tables) - blocks
        where[1, *spot] = tuple((first + j, half, place) for half in range(2) for j in range(blocks))

    arrays = [message, message_x, near_own, near_x, halo]
    picks = [(0, None)] + [(2, n_kvec - 1 - k) for k in range(1, n_kvec)]
    picks += [(1, None)] + [(3, n_kvec - 1 - k) for k in range(1, n_kvec)]
    picks += [(4, k) for k in range(n_kvec)]
    pair_msg = pair_message(neighbours, positions, arrays, tuple(picks), pair_weight, low)

    def runs(core, distances):
        return tuple(where[core, z, k] for k in range(n_kvec) for z in distances)

    filt, away_far = inverse_first(
        own_factors, other_factors, kfilt, pair_msg, tables, runs(1, zs), shard
    )
    crossed_far = swap(away_far, "atoms", 1)
    away_near = inverse(filt, tables, runs(1, (0,)), shard, BF16)
    crossed_near = swap(away_near, "atoms", 1)
    here_far = inverse(filt, tables, runs(0, zs), shard, F32)
    sum_far, *sends = join(here_far, crossed_far, n_kvec)
    for k in others:
        sum_far = sum_far + swap(sends[k - 1], "kvec", k).astype(F32)
    sum_far = sum_far.astype(BF16)
    here_near = inverse(filt, tables, runs(0, (0,)), shard, F32)
    own_near, *sends = join(here_near, crossed_near, n_kvec)
    parts = [own_near] + [swap(sends[k - 1], "kvec", k) for k in others]
    for z in zs:
        parts.append(swap(sum_far[:, (z - 1) * shard : z * shard], "atoms", 4 * z))
    return update(features, pair_msg, norm_gain, w_in, w_out, parts)


def solution(mesh):
    return jax.shard_map(
        per_device,
        mesh=mesh,
        in_specs=(
            P(None, ("atoms", "kvec")),
            P(("atoms", "kvec"), None),
            P(("atoms", "kvec")),
            P(("atoms", "kvec"), None),
            P(None, "kvec"),
            P(),
            P(),
            P(),
            P(),
            P(),
        ),
        out_specs=P(("atoms", "kvec"), None),
        check_vma=False,
    )
```

time: 77.7 us -> 66 us (0.85)
  waiting for transfers between devices: 27.8 us -> 12.4 us
  starting transfers between devices: 23.2 us -> 25.3 us
  Pallas kernels: 26.2 us -> 27.8 us
    ppermute x1, waiting for transfers between devices: 15.3 us -> 0.01 us  [per_device(): lax.ppermute(collect([message, near_own], group), 'atoms', halo_pairs)]
    ppermute x1, starting transfers between devices: 2.58 us -> 4.26 us  [per_device(): lax.ppermute(collect([message, near_own], group), 'atoms', halo_pairs)]
    pallas_call x8 -> x11, Pallas kernels: 16.6 us -> 17.5 us  [the longest x7 15.2 us: wave(): pl.pallas_call(functools.partial(wave_kernel, tuple(picks), len(arrays),...]
    ppermute x21 -> x23, starting transfers between devices: 20.6 us -> 21 us  [swap(): lax.ppermute(value, axis, [(i, i ^ bits) for i in range(lax.axis_size(axi...]
    ppermute x21 -> x23, waiting for transfers between devices: 12.5 us -> 12.4 us  [swap(): lax.ppermute(value, axis, [(i, i ^ bits) for i in range(lax.axis_size(axi...]
  transfers between devices with their start and end apart: 22 -> 24, of which waited for: 8 -> 9; matrix products, arithmetic and copies ran while one was open for 0% -> 0% of each run, Pallas kernels for 25% -> 38%
where the time goes in v2:
time: 66 us; the launch traced here: 65.9 us
  Pallas kernels  27.8 us (42%)
  starting transfers between devices  25.3 us (38%)
  waiting for transfers between devices  12.4 us (19%)
    ppermute x23, starting transfers between devices, swap(): lax.ppermute(value, axis, [(i, i ^ bits) for i in range(lax.axis_size(axi...  21 us
    pallas_call x7, Pallas kernels, wave(): pl.pallas_call(functools.partial(wave_kernel, tuple(picks), len(arrays),...  15.2 us
    ppermute x23, waiting for transfers between devices, swap(): lax.ppermute(value, axis, [(i, i ^ bits) for i in range(lax.axis_size(axi...  12.4 us
    pallas_call x1, Pallas kernels, pair_message(): pl.pallas_call(functools.partial(pair_kernel, nbasis, pieces, scale, pick...  7.4 us
    ppermute x1, starting transfers between devices, per_device(): lax.ppermute(collect([message, near_own], group), 'atoms', halo_pairs)  4.26 us
    pallas_call x3, Pallas kernels, inverse(): pl.pallas_call(functools.partial(inverse_kernel, pieces, shard), in_specs...  1.77 us
  transfers between devices with their start and end apart: 24, of which 9 were waited for; matrix products, arithmetic and copies ran while one was open for 0% of the time, Pallas kernels for 38%

profile of v2, /device:TPU:0, one launch (start us, length us, event | category | flops | bytes accessed | tf_op | source)
XLA Modules:
  0.0 65.9 jit_solution(4011552675509594095)
XLA Ops:
  1.6 3.5 %collective-permute-start.1 = (bf16[144,256]{1,0:T(8,128)(2,1)S(1)}, bf16[144,256]{1,0:T(8,128)(2,1)S(1)}, u32[]{:S(2)}, u32[]{:S(2)}) collective-permute-start(bf16[144,256]{1,0:T(8,128)(2,1)S(1)} %get-tuple-element.37.refs_1_.refs_0_), channel_id=1, source_target_pairs={{0,3},{1,2},{2,1},{3,0},{4,7},{5,6},{6,5},{7,4},{8,11},{9,10},{10,... | collective-permute-start | bytes 221192 | tf_op jit(solution)/shard_map/ppermute | solution.py:492
  6.2 1.9 %wave.7 = (bf16[6,256,512]{2,1,0:T(8,128)(2,1)S(1)}, f32[6,128,256]{2,1,0:T(8,128)S(1)}) custom-call(bf16[3,256,16]{2,1,0:T(8,128)(2,1)S(1)} %get-tuple-element.40.refs_0_, bf16[144,256]{1,0:T(8,128)(2,1)S(1)} %get-tuple-element.37.refs_1_.refs_0_, bf16[144,256]{1,0:T(8,128)(2,1)S(1)} %collective-permute-done.refs_2_.refs_1_), custom_call_target="tpu_custom_call" | custom-call | flops 201326592 | bytes 1572864 | tf_op jit(solution)/shard_map/wave/pallas_call | solution.py:212
  8.1 1.4 %collective-permute-done.2.refs_1_ = bf16[144,256]{1,0:T(8,128)(2,1)S(1)} collective-permute-done((bf16[144,256]{1,0:T(8,128)(2,1)S(1)}, bf16[144,256]{1,0:T(8,128)(2,1)S(1)}, u32[]{:S(2)}, u32[]{:S(2)}) %collective-permute-start.2) | collective-permute-done | bytes 73760 | tf_op jit(solution)/shard_map/ppermute | solution.py:492
  10.0 2.7 %collective-permute-start.6 = (bf16[144,256]{1,0:T(8,128)(2,1)S(1)}, bf16[144,256]{1,0:T(8,128)(2,1)S(1)}, u32[]{:S(2)}, u32[]{:S(2)}) collective-permute-start(bf16[144,256]{1,0:T(8,128)(2,1)S(1)} %get-tuple-element.37.refs_1_.refs_0_), channel_id=1, source_target_pairs={{0,16},{4,20},{8,24},{12,28},{16,0},{20,4},{24,8},{28,12},{1,17},{... | collective-permute-start | bytes 221192 | tf_op jit(solution)/shard_map/ppermute | solution.py:492
  12.7 1.9 %wave.8 = (bf16[6,256,512]{2,1,0:T(8,128)(2,1)S(1)}, f32[6,128,256]{2,1,0:T(8,128)S(1)}) custom-call(bf16[3,256,16]{2,1,0:T(8,128)(2,1)S(1)} %get-tuple-element.40.refs_0_, bf16[3,144,256]{2,1,0:T(8,128)(2,1)S(1)} %collect.4.refs_1_.refs_2_, f32[6,128,256]{2,1,0:T(8,128)S(1)} %get-tuple-element.41.refs_3_.refs_2_), custom_call_target="tpu_custom_call" | custom-call | flops 201326592 | bytes 1572864 | tf_op jit(solution)/shard_map/wave/pallas_call | solution.py:212
  14.6 2.6 %collective-permute-done.6.refs_0_ = bf16[144,256]{1,0:T(8,128)(2,1)S(1)} collective-permute-done((bf16[144,256]{1,0:T(8,128)(2,1)S(1)}, bf16[144,256]{1,0:T(8,128)(2,1)S(1)}, u32[]{:S(2)}, u32[]{:S(2)}) %collective-permute-start.6) | collective-permute-done | bytes 73760 | tf_op jit(solution)/shard_map/ppermute | solution.py:492
  17.2 1.4 %collective-permute-start.10 = (bf16[1,144,256]{2,1,0:T(8,128)(2,1)S(1)}, bf16[1,144,256]{2,1,0:T(8,128)(2,1)S(1)}, u32[]{:S(2)}, u32[]{:S(2)}) collective-permute-start(bf16[1,144,256]{2,1,0:T(8,128)(2,1)S(1)} %collect.6.refs_1_), channel_id=1, source_target_pairs={{0,1},{1,0},{2,3},{3,2},{4,5},{5,4},{6,7},{7,6},{8,9},{9,8},{10,11... | collective-permute-start | bytes 221192 | tf_op jit(solution)/shard_map/ppermute | solution.py:492
  18.6 1.6 %collective-permute-start.8 = (bf16[1,144,256]{2,1,0:T(8,128)(2,1)S(1)}, bf16[1,144,256]{2,1,0:T(8,128)(2,1)S(1)}, u32[]{:S(2)}, u32[]{:S(2)}) collective-permute-start(bf16[1,144,256]{2,1,0:T(8,128)(2,1)S(1)} %collect.6.refs_1_), channel_id=1, source_target_pairs={{0,3},{1,2},{2,1},{3,0},{4,7},{5,6},{6,5},{7,4},{8,11},{9,10},{10,... | collective-permute-start | bytes 221192 | tf_op jit(solution)/shard_map/ppermute | solution.py:492
  20.7 3.5 %wave.9 = (bf16[6,256,1024]{2,1,0:T(8,128)(2,1)S(1)}, f32[6,128,256]{2,1,0:T(8,128)S(1)}) custom-call(bf16[3,256,16]{2,1,0:T(8,128)(2,1)S(1)} %get-tuple-element.40.refs_0_, bf16[3,144,256]{2,1,0:T(8,128)(2,1)S(1)} %collect.4.refs_1_.refs_2_, bf16[3,144,256]{2,1,0:T(8,128)(2,1)S(1)} %collective-permute-done.4.refs_2_.refs_3_, ...), custom_call_target="tpu_custom_call" | custom-call | flops 402653184 | bytes 3145728 | tf_op jit(solution)/shard_map/wave/pallas_call | solution.py:212
  24.8 4.3 %collective-permute-start.5 = (bf16[4,144,256]{2,1,0:T(8,128)(2,1)S(1)}, bf16[4,144,256]{2,1,0:T(8,128)(2,1)S(1)}, u32[]{:S(2)}, u32[]{:S(2)}) collective-permute-start(bf16[4,144,256]{2,1,0:T(8,128)(2,1)S(1)} %collect.5), channel_id=1, source_target_pairs={{0,28},{4,8},{8,4},{12,16},{16,12},{20,24},{24,20},{28,0},{1,29},{... | collective-permute-start | bytes 884744 | tf_op jit(solution)/shard_map/ppermute | solution.py:543
  29.0 3.4 %wave.10 = (bf16[6,256,1024]{2,1,0:T(8,128)(2,1)S(1)}, f32[6,128,256]{2,1,0:T(8,128)S(1)}) custom-call(bf16[3,256,16]{2,1,0:T(8,128)(2,1)S(1)} %get-tuple-element.40.refs_0_, bf16[1,144,256]{2,1,0:T(8,128)(2,1)S(1)} %collect.6.refs_1_, bf16[3,144,256]{2,1,0:T(8,128)(2,1)S(1)} %collect.7.refs_2_, f32[6,128,256]{2,1,0:T(8,128)S(1)} %get-tuple-element.43.refs_3_), custom_call_target="tpu_custom_call" | custom-call | flops 402653184 | bytes 3145728 | tf_op jit(solution)/shard_map/wave/pallas_call | solution.py:212
  32.5 1.5 %wave.11 = (bf16[2,256,1024]{2,1,0:T(8,128)(2,1)S(1)}, f32[2,128,256]{2,1,0:T(8,128)S(1)}, bf16[2,128,256]{2,1,0:T(8,128)(2,1)S(1)}) custom-call(bf16[3,256,16]{2,1,0:T(8,128)(2,1)S(1)} %get-tuple-element.40.refs_0_, bf16[1,144,256]{2,1,0:T(8,128)(2,1)S(1)} %collective-permute-done.7.refs_1_, bf16[3,144,256]{2,1,0:T(8,128)(2,1)S(1)} %collective-permute-done.11.refs_2_, ...), custom_call_target="tpu_custom_call" | custom-call | flops 134217728 | bytes 1048576 | tf_op jit(solution)/shard_map/wave/pallas_call | solution.py:212
  34.0 1.5 %wave.12 = (bf16[2,256,1024]{2,1,0:T(8,128)(2,1)S(1)}, f32[2,128,256]{2,1,0:T(8,128)S(1)}, bf16[2,128,256]{2,1,0:T(8,128)(2,1)S(1)}) custom-call(bf16[3,256,16]{2,1,0:T(8,128)(2,1)S(1)} %get-tuple-element.40.refs_0_, bf16[1,144,256]{2,1,0:T(8,128)(2,1)S(1)} %collective-permute-done.7.refs_1_, bf16[3,144,256]{2,1,0:T(8,128)(2,1)S(1)} %collective-permute-done.11.refs_2_, ...), custom_call_target="tpu_custom_call" | custom-call | flops 134217728 | bytes 1048576 | tf_op jit(solution)/shard_map/wave/pallas_call | solution.py:212
  35.5 1.5 %wave.13 = (bf16[2,256,1024]{2,1,0:T(8,128)(2,1)S(1)}, f32[2,128,256]{2,1,0:T(8,128)S(1)}, bf16[2,128,256]{2,1,0:T(8,128)(2,1)S(1)}) custom-call(bf16[3,256,16]{2,1,0:T(8,128)(2,1)S(1)} %get-tuple-element.40.refs_0_, bf16[1,144,256]{2,1,0:T(8,128)(2,1)S(1)} %collective-permute-done.7.refs_1_, bf16[3,144,256]{2,1,0:T(8,128)(2,1)S(1)} %collective-permute-done.11.refs_2_, ...), custom_call_target="tpu_custom_call" | custom-call | flops 134217728 | bytes 1048576 | tf_op jit(solution)/shard_map/wave/pallas_call | solution.py:212
  37.1 2.0 %collective-permute-start.13 = (bf16[2,128,256]{2,1,0:T(8,128)(2,1)S(1)}, bf16[2,128,256]{2,1,0:T(8,128)(2,1)S(1)}, u32[]{:S(2)}, u32[]{:S(2)}) collective-permute-start(bf16[2,128,256]{2,1,0:T(8,128)(2,1)S(1)} %get-tuple-element.46.refs_4_), channel_id=1, source_target_pairs={{0,8},{4,12},{8,0},{12,4},{16,24},{20,28},{24,16},{28,20},{1,9},{5... | collective-permute-start | bytes 393224 | tf_op jit(solution)/shard_map/ppermute | solution.py:492
  39.2 7.4 %pair.1.refs_7_.refs_1_ = f32[128,256]{1,0:T(8,128)S(1)} custom-call(s32[2,12]{1,0:T(2,128)S(1)} %copy-done.6, f32[3,256]{1,0:T(4,128)S(1)} %copy-done.3, bf16[144,256]{1,0:T(8,128)(2,1)S(1)} %get-tuple-element.37.refs_1_.refs_0_, bf16[144,256]{1,0:T(8,128)(2,1)S(1)} %collective-permute-done.refs_2_.refs_1_, ...), custom_call_target="tpu_custom_call" | custom-call | flops 836763648 | bytes 786432 | tf_op jit(solution)/shard_map/pair/pallas_call | solution.py:442
  46.6 2.0 %collective-permute-done.12.refs_3_ = bf16[2,128,256]{2,1,0:T(8,128)(2,1)S(1)} collective-permute-done((bf16[2,128,256]{2,1,0:T(8,128)(2,1)S(1)}, bf16[2,128,256]{2,1,0:T(8,128)(2,1)S(1)}, u32[]{:S(2)}, u32[]{:S(2)}) %collective-permute-start.12) | collective-permute-done | bytes 131104 | tf_op jit(solution)/shard_map/ppermute | solution.py:492
  51.1 1.5 %collective-permute-start.20 = (bf16[128,256]{1,0:T(8,128)(2,1)S(1)}, bf16[128,256]{1,0:T(8,128)(2,1)S(1)}, u32[]{:S(2)}, u32[]{:S(2)}) collective-permute-start(bf16[128,256]{1,0:T(8,128)(2,1)S(1)} %get-tuple-element.66), channel_id=1, source_target_pairs={{0,3},{1,2},{2,1},{3,0},{4,7},{5,6},{6,5},{7,4},{8,11},{9,10},{10,... | collective-permute-start | bytes 196616 | tf_op jit(solution)/shard_map/ppermute | solution.py:492
  53.3 1.4 %collective-permute-start.22 = (bf16[128,256]{1,0:T(8,128)(2,1)S(1)}, bf16[128,256]{1,0:T(8,128)(2,1)S(1)}, u32[]{:S(2)}, u32[]{:S(2)}) collective-permute-start(bf16[128,256]{1,0:T(8,128)(2,1)S(1)} %get-tuple-element.68), channel_id=1, source_target_pairs={{0,1},{1,0},{2,3},{3,2},{4,5},{5,4},{6,7},{7,6},{8,9},{9,8},{10,11... | collective-permute-start | bytes 196616 | tf_op jit(solution)/shard_map/ppermute | solution.py:492
  55.4 1.5 %collective-permute-start.16 = (bf16[128,256]{1,0:T(8,128)(2,1)S(1)}, bf16[128,256]{1,0:T(8,128)(2,1)S(1)}, u32[]{:S(2)}, u32[]{:S(2)}) collective-permute-start(bf16[128,256]{1,0:T(8,128)(2,1)S(1)} %get-tuple-element.60), channel_id=1, source_target_pairs={{0,3},{1,2},{2,1},{3,0},{4,7},{5,6},{6,5},{7,4},{8,11},{9,10},{10,... | collective-permute-start | bytes 196616 | tf_op jit(solution)/shard_map/ppermute | solution.py:492
  57.5 1.4 %collective-permute-start.18 = (bf16[128,256]{1,0:T(8,128)(2,1)S(1)}, bf16[128,256]{1,0:T(8,128)(2,1)S(1)}, u32[]{:S(2)}, u32[]{:S(2)}) collective-permute-start(bf16[128,256]{1,0:T(8,128)(2,1)S(1)} %get-tuple-element.62), channel_id=1, source_target_pairs={{0,1},{1,0},{2,3},{3,2},{4,5},{5,4},{6,7},{7,6},{8,9},{9,8},{10,11... | collective-permute-start | bytes 196616 | tf_op jit(solution)/shard_map/ppermute | solution.py:492
  59.1 2.0 %collective-permute-done.16.refs_6_ = bf16[128,256]{1,0:T(8,128)(2,1)S(1)} collective-permute-done((bf16[128,256]{1,0:T(8,128)(2,1)S(1)}, bf16[128,256]{1,0:T(8,128)(2,1)S(1)}, u32[]{:S(2)}, u32[]{:S(2)}) %collective-permute-start.16) | collective-permute-done | bytes 65568 | tf_op jit(solution)/shard_map/ppermute | solution.py:492
  61.8 2.8 %collective-permute-done.23.refs_9_ = bf16[128,256]{1,0:T(8,128)(2,1)S(1)} collective-permute-done((bf16[128,256]{1,0:T(8,128)(2,1)S(1)}, bf16[128,256]{1,0:T(8,128)(2,1)S(1)}, u32[]{:S(2)}, u32[]{:S(2)}) %collective-permute-start.23) | collective-permute-done | bytes 65568 | tf_op jit(solution)/shard_map/ppermute | solution.py:492
  64.6 1.3 %update.1 = bf16[256,128]{1,0:T(8,128)(2,1)} custom-call(bf16[256,128]{1,0:T(8,128)(2,1)S(1)} %copy-done, f32[128,256]{1,0:T(8,128)S(1)} %pair.1.refs_7_.refs_1_, f32[1,128]{1,0:T(1,128)S(1)} %bitcast.2, bf16[128,512]{1,0:T(8,128)(2,1)S(1)} %copy-done.1, bf16[512,128]{1,0:T(8,128)(2,1)S(1)} %copy-done.2, f32[128,256]{1,0:T(8,128)S(1)} %get-tuple-element.59.refs_5_, ...), custom_call_target="tpu_custom_call" | custom-call | tf_op jit(solution)/shard_map/update/pallas_call | solution.py:481
  (60 shorter events, 9.7 us)
Async XLA Ops:
  1.0 5.2 %collective-permute-start = (bf16[144,256]{1,0:T(8,128)(2,1)S(1)}, bf16[144,256]{1,0:T(8,128)(2,1)S(1)}, u32[]{:S(2)}, u32[]{:S(2)}) collective-permute-start(bf16[144,256]{1,0:T(8,128)(2,1)S(1)} %get-tuple-element.37.refs_1_.refs_0_), channel_id=1, source_target_pairs={{0,4},{4,0},{8,12},{12,8},{16,20},{20,16},{24,28},{28,24},{1,5},{5... | collective-permute-start | bytes 221192 | tf_op jit(solution)/shard_map/ppermute | solution.py:492
  1.6 6.5 %collective-permute-start.1 = (bf16[144,256]{1,0:T(8,128)(2,1)S(1)}, bf16[144,256]{1,0:T(8,128)(2,1)S(1)}, u32[]{:S(2)}, u32[]{:S(2)}) collective-permute-start(bf16[144,256]{1,0:T(8,128)(2,1)S(1)} %get-tuple-element.37.refs_1_.refs_0_), channel_id=1, source_target_pairs={{0,3},{1,2},{2,1},{3,0},{4,7},{5,6},{6,5},{7,4},{8,11},{9,10},{10,... | collective-permute-start | bytes 221192 | tf_op jit(solution)/shard_map/ppermute | solution.py:492
  5.1 4.4 %collective-permute-start.2 = (bf16[144,256]{1,0:T(8,128)(2,1)S(1)}, bf16[144,256]{1,0:T(8,128)(2,1)S(1)}, u32[]{:S(2)}, u32[]{:S(2)}) collective-permute-start(bf16[144,256]{1,0:T(8,128)(2,1)S(1)} %get-tuple-element.37.refs_1_.refs_0_), channel_id=1, source_target_pairs={{0,2},{1,3},{2,0},{3,1},{4,6},{5,7},{6,4},{7,5},{8,10},{9,11},{10,... | collective-permute-start | bytes 221192 | tf_op jit(solution)/shard_map/ppermute | solution.py:492
  5.6 4.4 %collective-permute-start.3 = (bf16[144,256]{1,0:T(8,128)(2,1)S(1)}, bf16[144,256]{1,0:T(8,128)(2,1)S(1)}, u32[]{:S(2)}, u32[]{:S(2)}) collective-permute-start(bf16[144,256]{1,0:T(8,128)(2,1)S(1)} %get-tuple-element.37.refs_1_.refs_0_), channel_id=1, source_target_pairs={{0,1},{1,0},{2,3},{3,2},{4,5},{5,4},{6,7},{7,6},{8,9},{9,8},{10,11... | collective-permute-start | bytes 221192 | tf_op jit(solution)/shard_map/ppermute | solution.py:492
  10.0 10.7 %collective-permute-start.4 = (bf16[3,144,256]{2,1,0:T(8,128)(2,1)S(1)}, bf16[3,144,256]{2,1,0:T(8,128)(2,1)S(1)}, u32[]{:S(2)}, u32[]{:S(2)}) collective-permute-start(bf16[3,144,256]{2,1,0:T(8,128)(2,1)S(1)} %collect.4.refs_1_.refs_2_), channel_id=1, source_target_pairs={{0,4},{4,0},{8,12},{12,8},{16,20},{20,16},{24,28},{28,24},{1,5},{5... | collective-permute-start | bytes 663560 | tf_op jit(solution)/shard_map/ppermute | solution.py:492
  10.0 7.1 %collective-permute-start.6 = (bf16[144,256]{1,0:T(8,128)(2,1)S(1)}, bf16[144,256]{1,0:T(8,128)(2,1)S(1)}, u32[]{:S(2)}, u32[]{:S(2)}) collective-permute-start(bf16[144,256]{1,0:T(8,128)(2,1)S(1)} %get-tuple-element.37.refs_1_.refs_0_), channel_id=1, source_target_pairs={{0,16},{4,20},{8,24},{12,28},{16,0},{20,4},{24,8},{28,12},{1,17},{... | collective-permute-start | bytes 221192 | tf_op jit(solution)/shard_map/ppermute | solution.py:492
  17.2 7.0 %collective-permute-start.10 = (bf16[1,144,256]{2,1,0:T(8,128)(2,1)S(1)}, bf16[1,144,256]{2,1,0:T(8,128)(2,1)S(1)}, u32[]{:S(2)}, u32[]{:S(2)}) collective-permute-start(bf16[1,144,256]{2,1,0:T(8,128)(2,1)S(1)} %collect.6.refs_1_), channel_id=1, source_target_pairs={{0,1},{1,0},{2,3},{3,2},{4,5},{5,4},{6,7},{7,6},{8,9},{9,8},{10,11... | collective-permute-start | bytes 221192 | tf_op jit(solution)/shard_map/ppermute | solution.py:492
  18.6 5.6 %collective-permute-start.8 = (bf16[1,144,256]{2,1,0:T(8,128)(2,1)S(1)}, bf16[1,144,256]{2,1,0:T(8,128)(2,1)S(1)}, u32[]{:S(2)}, u32[]{:S(2)}) collective-permute-start(bf16[1,144,256]{2,1,0:T(8,128)(2,1)S(1)} %collect.6.refs_1_), channel_id=1, source_target_pairs={{0,3},{1,2},{2,1},{3,0},{4,7},{5,6},{6,5},{7,4},{8,11},{9,10},{10,... | collective-permute-start | bytes 221192 | tf_op jit(solution)/shard_map/ppermute | solution.py:492
  20.2 4.4 %collective-permute-start.9 = (bf16[1,144,256]{2,1,0:T(8,128)(2,1)S(1)}, bf16[1,144,256]{2,1,0:T(8,128)(2,1)S(1)}, u32[]{:S(2)}, u32[]{:S(2)}) collective-permute-start(bf16[1,144,256]{2,1,0:T(8,128)(2,1)S(1)} %collect.6.refs_1_), channel_id=1, source_target_pairs={{0,2},{1,3},{2,0},{3,1},{4,6},{5,7},{6,4},{7,5},{8,10},{9,11},{10,... | collective-permute-start | bytes 221192 | tf_op jit(solution)/shard_map/ppermute | solution.py:492
  24.7 7.8 %collective-permute-start.11 = (bf16[3,144,256]{2,1,0:T(8,128)(2,1)S(1)}, bf16[3,144,256]{2,1,0:T(8,128)(2,1)S(1)}, u32[]{:S(2)}, u32[]{:S(2)}) collective-permute-start(bf16[3,144,256]{2,1,0:T(8,128)(2,1)S(1)} %collect.7.refs_2_), channel_id=1, source_target_pairs={{0,4},{4,0},{8,12},{12,8},{16,20},{20,16},{24,28},{28,24},{1,5},{5... | collective-permute-start | bytes 663560 | tf_op jit(solution)/shard_map/ppermute | solution.py:492
  24.8 14.4 %collective-permute-start.5 = (bf16[4,144,256]{2,1,0:T(8,128)(2,1)S(1)}, bf16[4,144,256]{2,1,0:T(8,128)(2,1)S(1)}, u32[]{:S(2)}, u32[]{:S(2)}) collective-permute-start(bf16[4,144,256]{2,1,0:T(8,128)(2,1)S(1)} %collect.5), channel_id=1, source_target_pairs={{0,28},{4,8},{8,4},{12,16},{16,12},{20,24},{24,20},{28,0},{1,29},{... | collective-permute-start | bytes 884744 | tf_op jit(solution)/shard_map/ppermute | solution.py:543
  29.0 3.5 %collective-permute-start.7 = (bf16[1,144,256]{2,1,0:T(8,128)(2,1)S(1)}, bf16[1,144,256]{2,1,0:T(8,128)(2,1)S(1)}, u32[]{:S(2)}, u32[]{:S(2)}) collective-permute-start(bf16[1,144,256]{2,1,0:T(8,128)(2,1)S(1)} %collect.6.refs_1_), channel_id=1, source_target_pairs={{0,4},{4,0},{8,12},{12,8},{16,20},{20,16},{24,28},{28,24},{1,5},{5... | collective-permute-start | bytes 221192 | tf_op jit(solution)/shard_map/ppermute | solution.py:492
  37.0 9.6 %collective-permute-start.14 = (bf16[2,128,256]{2,1,0:T(8,128)(2,1)S(1)}, bf16[2,128,256]{2,1,0:T(8,128)(2,1)S(1)}, u32[]{:S(2)}, u32[]{:S(2)}) collective-permute-start(bf16[2,128,256]{2,1,0:T(8,128)(2,1)S(1)} %get-tuple-element.47.refs_6_), channel_id=1, source_target_pairs={{0,8},{4,12},{8,0},{12,4},{16,24},{20,28},{24,16},{28,20},{1,9},{5... | collective-permute-start | bytes 393224 | tf_op jit(solution)/shard_map/ppermute | solution.py:492
  37.1 9.5 %collective-permute-start.13 = (bf16[2,128,256]{2,1,0:T(8,128)(2,1)S(1)}, bf16[2,128,256]{2,1,0:T(8,128)(2,1)S(1)}, u32[]{:S(2)}, u32[]{:S(2)}) collective-permute-start(bf16[2,128,256]{2,1,0:T(8,128)(2,1)S(1)} %get-tuple-element.46.refs_4_), channel_id=1, source_target_pairs={{0,8},{4,12},{8,0},{12,4},{16,24},{20,28},{24,16},{28,20},{1,9},{5... | collective-permute-start | bytes 393224 | tf_op jit(solution)/shard_map/ppermute | solution.py:492
  39.1 9.5 %collective-permute-start.12 = (bf16[2,128,256]{2,1,0:T(8,128)(2,1)S(1)}, bf16[2,128,256]{2,1,0:T(8,128)(2,1)S(1)}, u32[]{:S(2)}, u32[]{:S(2)}) collective-permute-start(bf16[2,128,256]{2,1,0:T(8,128)(2,1)S(1)} %get-tuple-element.45.refs_4_), channel_id=1, source_target_pairs={{0,8},{4,12},{8,0},{12,4},{16,24},{20,28},{24,16},{28,20},{1,9},{5... | collective-permute-start | bytes 393224 | tf_op jit(solution)/shard_map/ppermute | solution.py:492
  49.2 1.8 %collective-permute-start.19 = (bf16[128,1024]{1,0:T(8,128)(2,1)S(1)}, bf16[128,1024]{1,0:T(8,128)(2,1)S(1)}, u32[]{:S(2)}, u32[]{:S(2)}) collective-permute-start(bf16[128,1024]{1,0:T(8,128)(2,1)S(1)} %get-tuple-element.64), channel_id=1, source_target_pairs={{0,4},{4,0},{8,12},{12,8},{16,20},{20,16},{24,28},{28,24},{1,5},{5... | collective-permute-start | bytes 786440 | tf_op jit(solution)/shard_map/ppermute | solution.py:492
  49.9 5.4 %collective-permute-start.15 = (bf16[128,1024]{1,0:T(8,128)(2,1)S(1)}, bf16[128,1024]{1,0:T(8,128)(2,1)S(1)}, u32[]{:S(2)}, u32[]{:S(2)}) collective-permute-start(bf16[128,1024]{1,0:T(8,128)(2,1)S(1)} %inverse.4), channel_id=1, source_target_pairs={{0,4},{4,0},{8,12},{12,8},{16,20},{20,16},{24,28},{28,24},{1,5},{5... | collective-permute-start | bytes 786440 | tf_op jit(solution)/shard_map/ppermute | solution.py:492
  51.1 6.4 %collective-permute-start.20 = (bf16[128,256]{1,0:T(8,128)(2,1)S(1)}, bf16[128,256]{1,0:T(8,128)(2,1)S(1)}, u32[]{:S(2)}, u32[]{:S(2)}) collective-permute-start(bf16[128,256]{1,0:T(8,128)(2,1)S(1)} %get-tuple-element.66), channel_id=1, source_target_pairs={{0,3},{1,2},{2,1},{3,0},{4,7},{5,6},{6,5},{7,4},{8,11},{9,10},{10,... | collective-permute-start | bytes 196616 | tf_op jit(solution)/shard_map/ppermute | solution.py:492
  52.6 6.3 %collective-permute-start.21 = (bf16[128,256]{1,0:T(8,128)(2,1)S(1)}, bf16[128,256]{1,0:T(8,128)(2,1)S(1)}, u32[]{:S(2)}, u32[]{:S(2)}) collective-permute-start(bf16[128,256]{1,0:T(8,128)(2,1)S(1)} %get-tuple-element.67), channel_id=1, source_target_pairs={{0,2},{1,3},{2,0},{3,1},{4,6},{5,7},{6,4},{7,5},{8,10},{9,11},{10,... | collective-permute-start | bytes 196616 | tf_op jit(solution)/shard_map/ppermute | solution.py:492
  53.3 5.7 %collective-permute-start.22 = (bf16[128,256]{1,0:T(8,128)(2,1)S(1)}, bf16[128,256]{1,0:T(8,128)(2,1)S(1)}, u32[]{:S(2)}, u32[]{:S(2)}) collective-permute-start(bf16[128,256]{1,0:T(8,128)(2,1)S(1)} %get-tuple-element.68), channel_id=1, source_target_pairs={{0,1},{1,0},{2,3},{3,2},{4,5},{5,4},{6,7},{7,6},{8,9},{9,8},{10,11... | collective-permute-start | bytes 196616 | tf_op jit(solution)/shard_map/ppermute | solution.py:492
  55.4 5.7 %collective-permute-start.16 = (bf16[128,256]{1,0:T(8,128)(2,1)S(1)}, bf16[128,256]{1,0:T(8,128)(2,1)S(1)}, u32[]{:S(2)}, u32[]{:S(2)}) collective-permute-start(bf16[128,256]{1,0:T(8,128)(2,1)S(1)} %get-tuple-element.60), channel_id=1, source_target_pairs={{0,3},{1,2},{2,1},{3,0},{4,7},{5,6},{6,5},{7,4},{8,11},{9,10},{10,... | collective-permute-start | bytes 196616 | tf_op jit(solution)/shard_map/ppermute | solution.py:492
  56.9 4.7 %collective-permute-start.17 = (bf16[128,256]{1,0:T(8,128)(2,1)S(1)}, bf16[128,256]{1,0:T(8,128)(2,1)S(1)}, u32[]{:S(2)}, u32[]{:S(2)}) collective-permute-start(bf16[128,256]{1,0:T(8,128)(2,1)S(1)} %get-tuple-element.61), channel_id=1, source_target_pairs={{0,2},{1,3},{2,0},{3,1},{4,6},{5,7},{6,4},{7,5},{8,10},{9,11},{10,... | collective-permute-start | bytes 196616 | tf_op jit(solution)/shard_map/ppermute | solution.py:492
  57.5 4.3 %collective-permute-start.18 = (bf16[128,256]{1,0:T(8,128)(2,1)S(1)}, bf16[128,256]{1,0:T(8,128)(2,1)S(1)}, u32[]{:S(2)}, u32[]{:S(2)}) collective-permute-start(bf16[128,256]{1,0:T(8,128)(2,1)S(1)} %get-tuple-element.62), channel_id=1, source_target_pairs={{0,1},{1,0},{2,3},{3,2},{4,5},{5,4},{6,7},{7,6},{8,9},{9,8},{10,11... | collective-permute-start | bytes 196616 | tf_op jit(solution)/shard_map/ppermute | solution.py:492
  59.0 5.6 %collective-permute-start.23 = (bf16[128,256]{1,0:T(8,128)(2,1)S(1)}, bf16[128,256]{1,0:T(8,128)(2,1)S(1)}, u32[]{:S(2)}, u32[]{:S(2)}) collective-permute-start(bf16[128,256]{1,0:T(8,128)(2,1)S(1)} %add_convert_fusion), channel_id=1, source_target_pairs={{0,16},{4,20},{8,24},{12,28},{16,0},{20,4},{24,8},{28,12},{1,17},{... | collective-permute-start | bytes 196616 | tf_op jit(solution)/shard_map/ppermute | solution.py:492
  (7 other events, 83.3 us)

commit v3 on v2

--- a/solution.py
+++ b/solution.py
@@ -14,7 +14,6 @@
 BF16 = jnp.bfloat16
 
 SIN_COEF = (4.442879586561992, -7.307818050390618, 3.5977887417720016, -0.7912382192058507)
-ROUND = 12582912.0
 SLACK = 1e-5
 TAIL = 16
 
@@ -145,53 +144,75 @@
     take(waits)
     table_ref, total_ref = take(2)
     low_ref = take(1)[0] if low else None
-    feat_scr, pos_scr, phase_scr = refs
+    feat_scr, pos_scr = take(2)
+    phases, buffers = take(2), take(2)
     blocks, width = table_ref.shape[0] // 2, table_ref.shape[1]
     every = lattice_ref.shape[0]
-    pairs, _, both = pos_scr.shape
-    channels = feat_scr.shape[0]
+    pairs, channels, both = feat_scr.shape
     shard = both // 2
     for place, (array, index) in enumerate(picks):
         item = messages[array] if index is None else messages[array].at[index]
-        feat_scr[:, place * shard : (place + 1) * shard] = item[0:channels, :]
         lanes = slice(place % 2 * shard, (place % 2 + 1) * shard)
+        feat_scr[place // 2, :, lanes] = item[0:channels, :]
         pos_scr[place // 2, :, lanes] = item[channels:, :]
+    for j in range(2 * blocks):
+        if start:
+            total_ref[j] = jnp.zeros_like(total_ref[j])
+        else:
+            total_ref[j] = before_ref[j // blocks * every + first + j % blocks]
+    buffers[1][...] = jnp.zeros_like(buffers[1])
     steps = pairs * blocks
 
-    def phase(i):
-        phase_scr[...] = jnp.dot(
+    def phase(i, slot):
+        i = jnp.minimum(i, steps - 1)
+        phases[slot][...] = jnp.dot(
             lattice_ref[first + i % blocks], pos_scr[i // blocks], preferred_element_type=F32
         )
 
-    def table(i):
+    def product(i, slot, half):
         pair, block = i // blocks, i % blocks
+        total_ref[half * blocks + block] += lax.dot_general(
+            feat_scr[pair], buffers[slot][half], (((1,), (1,)), ((), ())), preferred_element_type=F32
+        )
+
+    def unit(i, slot):
+        pair, block = i // blocks, i % blocks
+        before = jnp.maximum(i - 1, 0)
         lanes = pl.ds(pl.multiple_of(pair * both, both), both)
         rows = 16
-        for at in range(0, width, rows):
-            turns = phase_scr[at : at + rows, :]
-            r = turns - ((turns + ROUND) - ROUND)
+        for n, at in enumerate(range(0, width, rows)):
+            if n == 4:
+                product(before, 1 - slot, 0)
+            if n == 10:
+                product(before, 1 - slot, 1)
+            turns = phases[slot][at : at + rows, :]
+            r = turns - jnp.round(turns)
             s = horner(r * r, SIN_COEF) * r
             square = s * s
             w = (2.0 + SLACK) - square
-            table_ref[block, at : at + rows, lanes] = (1.0 - square).astype(BF16)
-            table_ref[blocks + block, at : at + rows, lanes] = (s * (w * lax.rsqrt(w))).astype(BF16)
-
-    def body(i, carry):
-        table(i)
-        phase(jnp.minimum(i + 1, steps - 1))
+            cosine = (1.0 - square).astype(BF16)
+            sine = (s * (w * lax.rsqrt(w))).astype(BF16)
+            buffers[slot][0, at : at + rows, :] = cosine
+            buffers[slot][1, at : at + rows, :] = sine
+            table_ref[block, at : at + rows, lanes] = cosine
+            table_ref[blocks + block, at : at + rows, lanes] = sine
+        phase(i + 2, slot)
+
+    phase(0, 0)
+    phase(1, 1)
+
+    def body(n, carry):
+        unit(2 * n, 0)
+        unit(2 * n + 1, 1)
         return carry
 
-    phase(0)
-    lax.fori_loop(0, steps, body, 0)
-    for j in range(2 * blocks):
-        part = lax.dot_general(
-            feat_scr[...], table_ref[j], (((1,), (1,)), ((), ())), preferred_element_type=F32
-        )
-        if not start:
-            part += before_ref[j // blocks * every + first + j % blocks]
-        total_ref[j] = part
-        if low:
-            low_ref[j] = part.astype(BF16)
+    lax.fori_loop(0, steps // 2, body, 0)
+    if steps % 2:
+        unit(steps - 1, 0)
+    for half in range(2):
+        product(steps - 1, (steps - 1) % 2, half)
+    if low:
+        low_ref[...] = total_ref[...].astype(BF16)
 
 
 def wave(lattice, arrays, picks, before, subset=None, after=(), low=False):
@@ -217,9 +238,12 @@
         out_specs=[VMEM] * len(shapes),
         out_shape=shapes,
         scratch_shapes=[
-            pltpu.VMEM((channels, pieces * shard), BF16),
+            pltpu.VMEM((pieces // 2, channels, 2 * shard), BF16),
             pltpu.VMEM((pieces // 2, TAIL, 2 * shard), BF16),
             pltpu.VMEM((width, 2 * shard), F32),
+            pltpu.VMEM((width, 2 * shard), F32),
+            pltpu.VMEM((2, width, 2 * shard), BF16),
+            pltpu.VMEM((2, width, 2 * shard), BF16),
         ],
         compiler_params=params(),
         cost_estimate=pl.CostEstimate(
@@ -350,12 +374,13 @@
 
 def pair_kernel(nbasis, pieces, output_scale, picks, arrays, neighbours_ref, own_pos_ref, *refs):
     message_refs, refs = refs[:arrays], refs[arrays:]
-    weight_ref, _, out_ref, feat_scr, pos_scr, own_scr, basis_scr, near_scr = refs
+    weight_ref, _, out_ref, feat_scr, pos_scr, own_scr, basis_scr, near_scr, spot_scr = refs
     block = BLOCK_ATOMS
+    both = 2 * block
     width = 12.0 / nbasis
     own_blocks, neighbours = neighbours_ref.shape
     shard = own_blocks * block
-    channels = out_ref.shape[0]
+    channels = out_ref.shape[1]
 
     views = [
         message_refs[array] if index is None else message_refs[array].at[index]
@@ -366,6 +391,10 @@
         feat_scr[:, lanes] = ref[0:channels, :]
         parts = ref[channels:, :].astype(F32)
         pos_scr[0:3, lanes] = (parts[0:3] + parts[3:6] + parts[6:9]) * 8.0
+    for b in range(own_blocks):
+        for d in range(3):
+            row = own_pos_ref[d : d + 1, b * block : (b + 1) * block]
+            own_scr[b, d] = jnp.broadcast_to(row, (both, block)).T
 
     a_index = lax.axis_index("atoms")
     k_index = lax.axis_index("kvec")
@@ -374,61 +403,72 @@
     first = (a_index * pieces + k_index) * own_blocks
     toward = jnp.where(a_index % 2 == 0, 1, n_atoms - 1)
 
+    def divide(value, by):
+        if by & (by - 1):
+            return value // by, value % by
+        return lax.shift_right_logical(value, by.bit_length() - 1), value & (by - 1)
+
     def place_of(ident):
-        group, within = ident // group_blk, ident % group_blk
-        ahead = (group - a_index + n_atoms) % n_atoms
+        group, within = divide(ident, group_blk)
+        ahead = divide(group - a_index + n_atoms, n_atoms)[1]
         which = jnp.where(ahead == 0, 0, jnp.where(ahead == toward, 1, 2))
-        piece = (within // own_blocks) ^ k_index
-        return (which * pieces + piece) * own_blocks + within % own_blocks
-
-    rows = 32
-    diagonal = lax.broadcasted_iota(jnp.int32, (rows, block), 0) - lax.broadcasted_iota(
-        jnp.int32, (rows, block), 1
-    )
+        piece, rest = divide(within, own_blocks)
+        return (which * pieces + (piece ^ k_index)) * own_blocks + rest
+
+    rows = 16
+    row_index = lax.broadcasted_iota(jnp.int32, (rows, both), 0)
+    lane = lax.broadcasted_iota(jnp.int32, (1, both), 1)
+    per_block = neighbours // 2
+    log2e = math.log2(math.e)
+
+    def unit(b, pair, carry):
+        own_place = jnp.full((1, both), -1, jnp.int32)
+        for h in range(2):
+            ident = neighbours_ref[b, 2 * pair + h]
+            lanes = pl.ds(pl.multiple_of(place_of(ident) * block, block), block)
+            here = pl.ds(pl.multiple_of(pair * both + h * block, block), block)
+            near_scr[b, :, here] = feat_scr[:, lanes]
+            spot_scr[0:3, h * block : (h + 1) * block] = pos_scr[0:3, lanes]
+            inside = (lane >= h * block) & (lane < (h + 1) * block) & (ident == first + b)
+            own_place = jnp.where(inside, lane - h * block, own_place)
+        lanes = pl.ds(pl.multiple_of(pair * both, both), both)
+        for at in range(0, block, rows):
+            dist2 = (own_scr[b, 0, at : at + rows, :] - spot_scr[0:1, :]) ** 2
+            dist2 += (own_scr[b, 1, at : at + rows, :] - spot_scr[1:2, :]) ** 2
+            dist2 += (own_scr[b, 2, at : at + rows, :] - spot_scr[2:3, :]) ** 2
+            radius = dist2 * lax.rsqrt(jnp.maximum(dist2, 1e-30))
+            env = (16.0 * output_scale) / (16.0 + dist2)
+            env = jnp.where(row_index + at == own_place, 0.0, env)
+            v = radius * (log2e / width) - 0.5 * log2e
+            value = jnp.exp2(v * v * (-0.5 / log2e)) * env
+            ratio = jnp.exp2(v)
+            for k in range(nbasis):
+                if k:
+                    value = value * ratio
+                basis_scr[b, k * block + at : k * block + at + rows, lanes] = value.astype(BF16)
+        return carry
+
     for b in range(own_blocks):
-        for d in range(3):
-            row = own_pos_ref[d : d + 1, b * block : (b + 1) * block]
-            own_scr[d] = jnp.broadcast_to(row, (block, block)).T
-
-        def pair(n, carry):
-            ident = neighbours_ref[b, n]
-            lanes = pl.ds(pl.multiple_of(place_of(ident) * block, block), block)
-            here = pl.ds(pl.multiple_of(n * block, block), block)
-            near_scr[:, here] = feat_scr[:, lanes]
-            same = ident == first + b
-            near = [pos_scr[d : d + 1, lanes] for d in range(3)]
-            for at in range(0, block, rows):
-                dist2 = (own_scr[0, at : at + rows, :] - near[0]) ** 2
-                dist2 += (own_scr[1, at : at + rows, :] - near[1]) ** 2
-                dist2 += (own_scr[2, at : at + rows, :] - near[2]) ** 2
-                radius = dist2 * lax.rsqrt(jnp.maximum(dist2, 1e-30))
-                env = output_scale / (1.0 + dist2 * (1.0 / 16.0))
-                env = jnp.where((diagonal + at == 0) & same, 0.0, env)
-                v = radius * (1.0 / width) - 0.5
-                value = jnp.exp(-0.5 * v * v) * env
-                ratio = jnp.exp(v)
-                for k in range(nbasis):
-                    if k:
-                        value = value * ratio
-                    basis_scr[k * block + at : k * block + at + rows, here] = value.astype(BF16)
-            return carry
-
-        lax.fori_loop(0, neighbours, pair, 0)
-        total = jnp.zeros((channels, block), F32)
-        for k in range(nbasis):
+        lax.fori_loop(0, per_block, functools.partial(unit, b), 0)
+    for b in range(own_blocks):
+        total = jnp.zeros((block, channels), F32)
+        for k in range(0, nbasis, 2):
             gathered = lax.dot_general(
-                near_scr[...],
-                basis_scr[k * block : (k + 1) * block, :],
+                basis_scr[b, k * block : (k + 2) * block, :],
+                near_scr[b],
                 (((1,), (1,)), ((), ())),
                 preferred_element_type=F32,
             )
-            total += lax.dot_general(
-                weight_ref[k * channels : (k + 1) * channels, :],
-                (gathered * math.exp(-0.5 * k * k)).astype(BF16),
-                (((0,), (0,)), ((), ())),
+            parts = [
+                gathered[h * block : (h + 1) * block] * math.exp(-0.5 * (k + h) * (k + h))
+                for h in range(2)
+            ]
+            total += jnp.dot(
+                jnp.concatenate(parts, axis=1).astype(BF16),
+                weight_ref[k * channels : (k + 2) * channels, :],
                 preferred_element_type=F32,
             )
-        out_ref[:, b * block : (b + 1) * block] = total
+        out_ref[b * block : (b + 1) * block, :] = total
 
 
 def pair_message(neighbours, own_pos, arrays, picks, weight, after):
@@ -439,17 +479,19 @@
     count = neighbours.shape[1]
     scale = float(count * BLOCK_ATOMS) ** (-0.5)
     window = 3 * pieces * shard
+    blocks = shard // BLOCK_ATOMS
     return pl.pallas_call(
         functools.partial(pair_kernel, nbasis, pieces, scale, picks, len(arrays)),
         in_specs=[SMEM] + [VMEM] * (2 + len(arrays)) + [ANY],
         out_specs=VMEM,
-        out_shape=jax.ShapeDtypeStruct((channels, shard), F32),
+        out_shape=jax.ShapeDtypeStruct((shard, channels), F32),
         scratch_shapes=[
             pltpu.VMEM((channels, window), BF16),
             pltpu.VMEM((8, window), F32),
-            pltpu.VMEM((3, BLOCK_ATOMS, BLOCK_ATOMS), F32),
-            pltpu.VMEM((nbasis * BLOCK_ATOMS, count * BLOCK_ATOMS), BF16),
-            pltpu.VMEM((channels, count * BLOCK_ATOMS), BF16),
+            pltpu.VMEM((blocks, 3, BLOCK_ATOMS, 2 * BLOCK_ATOMS), F32),
+            pltpu.VMEM((blocks, nbasis * BLOCK_ATOMS, count * BLOCK_ATOMS), BF16),
+            pltpu.VMEM((blocks, channels, count * BLOCK_ATOMS), BF16),
+            pltpu.VMEM((8, 2 * BLOCK_ATOMS), F32),
         ],
         compiler_params=params(),
         cost_estimate=pl.CostEstimate(
@@ -467,7 +509,7 @@
     long_t = parts[0][...].astype(F32)
     for part in parts[1:]:
         long_t = long_t + part[...].astype(F32)
-    total = features_ref[...].astype(F32) + (pair_ref[...] + long_t).T
+    total = features_ref[...].astype(F32) + pair_ref[...] + long_t.T
     mean = jnp.mean(total * total, axis=-1, keepdims=True)
     normed = (total * lax.rsqrt(mean + 1e-06) * gain_ref[...]).astype(BF16)
     pre = jnp.dot(normed, w_in_ref[...], preferred_element_type=F32)

time: 66 us -> 64.7 us (0.980)
  Pallas kernels: 27.8 us -> 24.3 us
  waiting for transfers between devices: 12.4 us -> 14.6 us
    pallas_call x7, Pallas kernels: 15.2 us -> 12.8 us  [wave(): pl.pallas_call(functools.partial(wave_kernel, tuple(picks), len(arrays),...]
    ppermute x23, waiting for transfers between devices: 12.4 us -> 14.6 us  [swap(): lax.ppermute(value, axis, [(i, i ^ bits) for i in range(lax.axis_size(axi...]
    pallas_call x1, Pallas kernels: 7.4 us -> 6.25 us  [pair_message(): pl.pallas_call(functools.partial(pair_kernel, nbasis, pieces, scale, pick...]
  transfers between devices with their start and end apart: 24 -> 24, of which waited for: 9 -> 11; matrix products, arithmetic and copies ran while one was open for 0% -> 0% of each run, Pallas kernels for 38% -> 33%
where the time goes in v3:
time: 64.7 us; the launch traced here: 64.6 us
  starting transfers between devices  25.3 us (39%)
  Pallas kernels  24.3 us (38%)
  waiting for transfers between devices  14.6 us (23%)
    ppermute x23, starting transfers between devices, swap(): lax.ppermute(value, axis, [(i, i ^ bits) for i in range(lax.axis_size(axi...  21 us
    ppermute x23, waiting for transfers between devices, swap(): lax.ppermute(value, axis, [(i, i ^ bits) for i in range(lax.axis_size(axi...  14.6 us
    pallas_call x7, Pallas kernels, wave(): pl.pallas_call(functools.partial(wave_kernel, tuple(picks), len(arrays),...  12.8 us
    pallas_call x1, Pallas kernels, pair_message(): pl.pallas_call(functools.partial(pair_kernel, nbasis, pieces, scale, pick...  6.25 us
    ppermute x1, starting transfers between devices, per_device(): lax.ppermute(collect([message, near_own], group), 'atoms', halo_pairs)  4.26 us
    pallas_call x3, Pallas kernels, inverse(): pl.pallas_call(functools.partial(inverse_kernel, pieces, shard), in_specs...  1.74 us
  transfers between devices with their start and end apart: 24, of which 11 were waited for; matrix products, arithmetic and copies ran while one was open for 0% of the time, Pallas kernels for 33%

profile of v3, /device:TPU:0, one launch (start us, length us, event | category | flops | bytes accessed | tf_op | source)
XLA Modules:
  0.0 64.6 jit_solution(1757468791007718595)
XLA Ops:
  1.6 3.5 %collective-permute-start.1 = (bf16[144,256]{1,0:T(8,128)(2,1)S(1)}, bf16[144,256]{1,0:T(8,128)(2,1)S(1)}, u32[]{:S(2)}, u32[]{:S(2)}) collective-permute-start(bf16[144,256]{1,0:T(8,128)(2,1)S(1)} %get-tuple-element.37.refs_1_.refs_0_), channel_id=1, source_target_pairs={{0,3},{1,2},{2,1},{3,0},{4,7},{5,6},{6,5},{7,4},{8,11},{9,10},{10,... | collective-permute-start | bytes 221192 | tf_op jit(solution)/shard_map/ppermute | solution.py:534
  6.2 1.5 %wave.7 = (bf16[6,256,512]{2,1,0:T(8,128)(2,1)S(1)}, f32[6,128,256]{2,1,0:T(8,128)S(1)}) custom-call(bf16[3,256,16]{2,1,0:T(8,128)(2,1)S(1)} %get-tuple-element.40.refs_0_, bf16[144,256]{1,0:T(8,128)(2,1)S(1)} %get-tuple-element.37.refs_1_.refs_0_, bf16[144,256]{1,0:T(8,128)(2,1)S(1)} %collective-permute-done.refs_2_.refs_1_), custom_call_target="tpu_custom_call" | custom-call | flops 201326592 | bytes 1572864 | tf_op jit(solution)/shard_map/wave/pallas_call | solution.py:233
  8.0 1.6 %collective-permute-done.2.refs_1_ = bf16[144,256]{1,0:T(8,128)(2,1)S(1)} collective-permute-done((bf16[144,256]{1,0:T(8,128)(2,1)S(1)}, bf16[144,256]{1,0:T(8,128)(2,1)S(1)}, u32[]{:S(2)}, u32[]{:S(2)}) %collective-permute-start.2) | collective-permute-done | bytes 73760 | tf_op jit(solution)/shard_map/ppermute | solution.py:534
  10.0 2.7 %collective-permute-start.6 = (bf16[144,256]{1,0:T(8,128)(2,1)S(1)}, bf16[144,256]{1,0:T(8,128)(2,1)S(1)}, u32[]{:S(2)}, u32[]{:S(2)}) collective-permute-start(bf16[144,256]{1,0:T(8,128)(2,1)S(1)} %get-tuple-element.37.refs_1_.refs_0_), channel_id=1, source_target_pairs={{0,16},{4,20},{8,24},{12,28},{16,0},{20,4},{24,8},{28,12},{1,17},{... | collective-permute-start | bytes 221192 | tf_op jit(solution)/shard_map/ppermute | solution.py:534
  12.7 1.5 %wave.8 = (bf16[6,256,512]{2,1,0:T(8,128)(2,1)S(1)}, f32[6,128,256]{2,1,0:T(8,128)S(1)}) custom-call(bf16[3,256,16]{2,1,0:T(8,128)(2,1)S(1)} %get-tuple-element.40.refs_0_, bf16[3,144,256]{2,1,0:T(8,128)(2,1)S(1)} %collect.4.refs_1_.refs_2_, f32[6,128,256]{2,1,0:T(8,128)S(1)} %get-tuple-element.41.refs_3_.refs_2_), custom_call_target="tpu_custom_call" | custom-call | flops 201326592 | bytes 1572864 | tf_op jit(solution)/shard_map/wave/pallas_call | solution.py:233
  14.2 3.0 %collective-permute-done.6.refs_0_ = bf16[144,256]{1,0:T(8,128)(2,1)S(1)} collective-permute-done((bf16[144,256]{1,0:T(8,128)(2,1)S(1)}, bf16[144,256]{1,0:T(8,128)(2,1)S(1)}, u32[]{:S(2)}, u32[]{:S(2)}) %collective-permute-start.6) | collective-permute-done | bytes 73760 | tf_op jit(solution)/shard_map/ppermute | solution.py:534
  17.2 1.4 %collective-permute-start.10 = (bf16[1,144,256]{2,1,0:T(8,128)(2,1)S(1)}, bf16[1,144,256]{2,1,0:T(8,128)(2,1)S(1)}, u32[]{:S(2)}, u32[]{:S(2)}) collective-permute-start(bf16[1,144,256]{2,1,0:T(8,128)(2,1)S(1)} %collect.6.refs_1_), channel_id=1, source_target_pairs={{0,1},{1,0},{2,3},{3,2},{4,5},{5,4},{6,7},{7,6},{8,9},{9,8},{10,11... | collective-permute-start | bytes 221192 | tf_op jit(solution)/shard_map/ppermute | solution.py:534
  18.6 1.6 %collective-permute-start.8 = (bf16[1,144,256]{2,1,0:T(8,128)(2,1)S(1)}, bf16[1,144,256]{2,1,0:T(8,128)(2,1)S(1)}, u32[]{:S(2)}, u32[]{:S(2)}) collective-permute-start(bf16[1,144,256]{2,1,0:T(8,128)(2,1)S(1)} %collect.6.refs_1_), channel_id=1, source_target_pairs={{0,3},{1,2},{2,1},{3,0},{4,7},{5,6},{6,5},{7,4},{8,11},{9,10},{10,... | collective-permute-start | bytes 221192 | tf_op jit(solution)/shard_map/ppermute | solution.py:534
  20.7 3.2 %wave.9 = (bf16[6,256,1024]{2,1,0:T(8,128)(2,1)S(1)}, f32[6,128,256]{2,1,0:T(8,128)S(1)}) custom-call(bf16[3,256,16]{2,1,0:T(8,128)(2,1)S(1)} %get-tuple-element.40.refs_0_, bf16[3,144,256]{2,1,0:T(8,128)(2,1)S(1)} %collect.4.refs_1_.refs_2_, bf16[3,144,256]{2,1,0:T(8,128)(2,1)S(1)} %collective-permute-done.4.refs_2_.refs_3_, ...), custom_call_target="tpu_custom_call" | custom-call | flops 402653184 | bytes 3145728 | tf_op jit(solution)/shard_map/wave/pallas_call | solution.py:233
  24.8 4.3 %collective-permute-start.5 = (bf16[4,144,256]{2,1,0:T(8,128)(2,1)S(1)}, bf16[4,144,256]{2,1,0:T(8,128)(2,1)S(1)}, u32[]{:S(2)}, u32[]{:S(2)}) collective-permute-start(bf16[4,144,256]{2,1,0:T(8,128)(2,1)S(1)} %collect.5), channel_id=1, source_target_pairs={{0,28},{4,8},{8,4},{12,16},{16,12},{20,24},{24,20},{28,0},{1,29},{... | collective-permute-start | bytes 884744 | tf_op jit(solution)/shard_map/ppermute | solution.py:585
  29.0 3.0 %wave.10 = (bf16[6,256,1024]{2,1,0:T(8,128)(2,1)S(1)}, f32[6,128,256]{2,1,0:T(8,128)S(1)}) custom-call(bf16[3,256,16]{2,1,0:T(8,128)(2,1)S(1)} %get-tuple-element.40.refs_0_, bf16[1,144,256]{2,1,0:T(8,128)(2,1)S(1)} %collect.6.refs_1_, bf16[3,144,256]{2,1,0:T(8,128)(2,1)S(1)} %collect.7.refs_2_, f32[6,128,256]{2,1,0:T(8,128)S(1)} %get-tuple-element.43.refs_3_), custom_call_target="tpu_custom_call" | custom-call | flops 402653184 | bytes 3145728 | tf_op jit(solution)/shard_map/wave/pallas_call | solution.py:233
  32.1 1.2 %wave.11 = (bf16[2,256,1024]{2,1,0:T(8,128)(2,1)S(1)}, f32[2,128,256]{2,1,0:T(8,128)S(1)}, bf16[2,128,256]{2,1,0:T(8,128)(2,1)S(1)}) custom-call(bf16[3,256,16]{2,1,0:T(8,128)(2,1)S(1)} %get-tuple-element.40.refs_0_, bf16[1,144,256]{2,1,0:T(8,128)(2,1)S(1)} %collective-permute-done.7.refs_1_, bf16[3,144,256]{2,1,0:T(8,128)(2,1)S(1)} %collective-permute-done.11.refs_2_, ...), custom_call_target="tpu_custom_call" | custom-call | flops 134217728 | bytes 1048576 | tf_op jit(solution)/shard_map/wave/pallas_call | solution.py:233
  33.3 1.2 %wave.12 = (bf16[2,256,1024]{2,1,0:T(8,128)(2,1)S(1)}, f32[2,128,256]{2,1,0:T(8,128)S(1)}, bf16[2,128,256]{2,1,0:T(8,128)(2,1)S(1)}) custom-call(bf16[3,256,16]{2,1,0:T(8,128)(2,1)S(1)} %get-tuple-element.40.refs_0_, bf16[1,144,256]{2,1,0:T(8,128)(2,1)S(1)} %collective-permute-done.7.refs_1_, bf16[3,144,256]{2,1,0:T(8,128)(2,1)S(1)} %collective-permute-done.11.refs_2_, ...), custom_call_target="tpu_custom_call" | custom-call | flops 134217728 | bytes 1048576 | tf_op jit(solution)/shard_map/wave/pallas_call | solution.py:233
  34.5 1.2 %wave.13 = (bf16[2,256,1024]{2,1,0:T(8,128)(2,1)S(1)}, f32[2,128,256]{2,1,0:T(8,128)S(1)}, bf16[2,128,256]{2,1,0:T(8,128)(2,1)S(1)}) custom-call(bf16[3,256,16]{2,1,0:T(8,128)(2,1)S(1)} %get-tuple-element.40.refs_0_, bf16[1,144,256]{2,1,0:T(8,128)(2,1)S(1)} %collective-permute-done.7.refs_1_, bf16[3,144,256]{2,1,0:T(8,128)(2,1)S(1)} %collective-permute-done.11.refs_2_, ...), custom_call_target="tpu_custom_call" | custom-call | flops 134217728 | bytes 1048576 | tf_op jit(solution)/shard_map/wave/pallas_call | solution.py:233
  35.8 2.0 %collective-permute-start.13 = (bf16[2,128,256]{2,1,0:T(8,128)(2,1)S(1)}, bf16[2,128,256]{2,1,0:T(8,128)(2,1)S(1)}, u32[]{:S(2)}, u32[]{:S(2)}) collective-permute-start(bf16[2,128,256]{2,1,0:T(8,128)(2,1)S(1)} %get-tuple-element.46.refs_4_), channel_id=1, source_target_pairs={{0,8},{4,12},{8,0},{12,4},{16,24},{20,28},{24,16},{28,20},{1,9},{5... | collective-permute-start | bytes 393224 | tf_op jit(solution)/shard_map/ppermute | solution.py:534
  37.9 6.3 %pair.1.refs_7_.refs_1_ = f32[256,128]{1,0:T(8,128)S(1)} custom-call(s32[2,12]{1,0:T(2,128)S(1)} %copy-done.6, f32[3,256]{1,0:T(4,128)S(1)} %copy-done.3, bf16[144,256]{1,0:T(8,128)(2,1)S(1)} %get-tuple-element.37.refs_1_.refs_0_, bf16[144,256]{1,0:T(8,128)(2,1)S(1)} %collective-permute-done.refs_2_.refs_1_, ...), custom_call_target="tpu_custom_call" | custom-call | flops 836763648 | bytes 786432 | tf_op jit(solution)/shard_map/pair/pallas_call | solution.py:483
  45.0 2.3 %collective-permute-done.12.refs_3_ = bf16[2,128,256]{2,1,0:T(8,128)(2,1)S(1)} collective-permute-done((bf16[2,128,256]{2,1,0:T(8,128)(2,1)S(1)}, bf16[2,128,256]{2,1,0:T(8,128)(2,1)S(1)}, u32[]{:S(2)}, u32[]{:S(2)}) %collective-permute-start.12) | collective-permute-done | bytes 131104 | tf_op jit(solution)/shard_map/ppermute | solution.py:534
  49.8 1.5 %collective-permute-start.20 = (bf16[128,256]{1,0:T(8,128)(2,1)S(1)}, bf16[128,256]{1,0:T(8,128)(2,1)S(1)}, u32[]{:S(2)}, u32[]{:S(2)}) collective-permute-start(bf16[128,256]{1,0:T(8,128)(2,1)S(1)} %get-tuple-element.66), channel_id=1, source_target_pairs={{0,3},{1,2},{2,1},{3,0},{4,7},{5,6},{6,5},{7,4},{8,11},{9,10},{10,... | collective-permute-start | bytes 196616 | tf_op jit(solution)/shard_map/ppermute | solution.py:534
  51.9 1.4 %collective-permute-start.22 = (bf16[128,256]{1,0:T(8,128)(2,1)S(1)}, bf16[128,256]{1,0:T(8,128)(2,1)S(1)}, u32[]{:S(2)}, u32[]{:S(2)}) collective-permute-start(bf16[128,256]{1,0:T(8,128)(2,1)S(1)} %get-tuple-element.68), channel_id=1, source_target_pairs={{0,1},{1,0},{2,3},{3,2},{4,5},{5,4},{6,7},{7,6},{8,9},{9,8},{10,11... | collective-permute-start | bytes 196616 | tf_op jit(solution)/shard_map/ppermute | solution.py:534
  54.0 1.5 %collective-permute-start.16 = (bf16[128,256]{1,0:T(8,128)(2,1)S(1)}, bf16[128,256]{1,0:T(8,128)(2,1)S(1)}, u32[]{:S(2)}, u32[]{:S(2)}) collective-permute-start(bf16[128,256]{1,0:T(8,128)(2,1)S(1)} %get-tuple-element.60), channel_id=1, source_target_pairs={{0,3},{1,2},{2,1},{3,0},{4,7},{5,6},{6,5},{7,4},{8,11},{9,10},{10,... | collective-permute-start | bytes 196616 | tf_op jit(solution)/shard_map/ppermute | solution.py:534
  56.2 1.4 %collective-permute-start.18 = (bf16[128,256]{1,0:T(8,128)(2,1)S(1)}, bf16[128,256]{1,0:T(8,128)(2,1)S(1)}, u32[]{:S(2)}, u32[]{:S(2)}) collective-permute-start(bf16[128,256]{1,0:T(8,128)(2,1)S(1)} %get-tuple-element.62), channel_id=1, source_target_pairs={{0,1},{1,0},{2,3},{3,2},{4,5},{5,4},{6,7},{7,6},{8,9},{9,8},{10,11... | collective-permute-start | bytes 196616 | tf_op jit(solution)/shard_map/ppermute | solution.py:534
  57.8 2.0 %collective-permute-done.16.refs_6_ = bf16[128,256]{1,0:T(8,128)(2,1)S(1)} collective-permute-done((bf16[128,256]{1,0:T(8,128)(2,1)S(1)}, bf16[128,256]{1,0:T(8,128)(2,1)S(1)}, u32[]{:S(2)}, u32[]{:S(2)}) %collective-permute-start.16) | collective-permute-done | bytes 65568 | tf_op jit(solution)/shard_map/ppermute | solution.py:534
  60.4 2.8 %collective-permute-done.23.refs_9_ = bf16[128,256]{1,0:T(8,128)(2,1)S(1)} collective-permute-done((bf16[128,256]{1,0:T(8,128)(2,1)S(1)}, bf16[128,256]{1,0:T(8,128)(2,1)S(1)}, u32[]{:S(2)}, u32[]{:S(2)}) %collective-permute-start.23) | collective-permute-done | bytes 65568 | tf_op jit(solution)/shard_map/ppermute | solution.py:534
  63.3 1.3 %update.1 = bf16[256,128]{1,0:T(8,128)(2,1)} custom-call(bf16[256,128]{1,0:T(8,128)(2,1)S(1)} %copy-done, f32[256,128]{1,0:T(8,128)S(1)} %pair.1.refs_7_.refs_1_, f32[1,128]{1,0:T(1,128)S(1)} %bitcast.2, bf16[128,512]{1,0:T(8,128)(2,1)S(1)} %copy-done.1, bf16[512,128]{1,0:T(8,128)(2,1)S(1)} %copy-done.2, f32[128,256]{1,0:T(8,128)S(1)} %get-tuple-element.59.refs_5_, ...), custom_call_target="tpu_custom_call" | custom-call | tf_op jit(solution)/shard_map/update/pallas_call | solution.py:523
  (60 shorter events, 10.9 us)
Async XLA Ops:
  1.0 5.2 %collective-permute-start = (bf16[144,256]{1,0:T(8,128)(2,1)S(1)}, bf16[144,256]{1,0:T(8,128)(2,1)S(1)}, u32[]{:S(2)}, u32[]{:S(2)}) collective-permute-start(bf16[144,256]{1,0:T(8,128)(2,1)S(1)} %get-tuple-element.37.refs_1_.refs_0_), channel_id=1, source_target_pairs={{0,4},{4,0},{8,12},{12,8},{16,20},{20,16},{24,28},{28,24},{1,5},{5... | collective-permute-start | bytes 221192 | tf_op jit(solution)/shard_map/ppermute | solution.py:534
  1.6 6.4 %collective-permute-start.1 = (bf16[144,256]{1,0:T(8,128)(2,1)S(1)}, bf16[144,256]{1,0:T(8,128)(2,1)S(1)}, u32[]{:S(2)}, u32[]{:S(2)}) collective-permute-start(bf16[144,256]{1,0:T(8,128)(2,1)S(1)} %get-tuple-element.37.refs_1_.refs_0_), channel_id=1, source_target_pairs={{0,3},{1,2},{2,1},{3,0},{4,7},{5,6},{6,5},{7,4},{8,11},{9,10},{10,... | collective-permute-start | bytes 221192 | tf_op jit(solution)/shard_map/ppermute | solution.py:534
  5.1 4.4 %collective-permute-start.2 = (bf16[144,256]{1,0:T(8,128)(2,1)S(1)}, bf16[144,256]{1,0:T(8,128)(2,1)S(1)}, u32[]{:S(2)}, u32[]{:S(2)}) collective-permute-start(bf16[144,256]{1,0:T(8,128)(2,1)S(1)} %get-tuple-element.37.refs_1_.refs_0_), channel_id=1, source_target_pairs={{0,2},{1,3},{2,0},{3,1},{4,6},{5,7},{6,4},{7,5},{8,10},{9,11},{10,... | collective-permute-start | bytes 221192 | tf_op jit(solution)/shard_map/ppermute | solution.py:534
  5.6 4.4 %collective-permute-start.3 = (bf16[144,256]{1,0:T(8,128)(2,1)S(1)}, bf16[144,256]{1,0:T(8,128)(2,1)S(1)}, u32[]{:S(2)}, u32[]{:S(2)}) collective-permute-start(bf16[144,256]{1,0:T(8,128)(2,1)S(1)} %get-tuple-element.37.refs_1_.refs_0_), channel_id=1, source_target_pairs={{0,1},{1,0},{2,3},{3,2},{4,5},{5,4},{6,7},{7,6},{8,9},{9,8},{10,11... | collective-permute-start | bytes 221192 | tf_op jit(solution)/shard_map/ppermute | solution.py:534
  10.0 10.7 %collective-permute-start.4 = (bf16[3,144,256]{2,1,0:T(8,128)(2,1)S(1)}, bf16[3,144,256]{2,1,0:T(8,128)(2,1)S(1)}, u32[]{:S(2)}, u32[]{:S(2)}) collective-permute-start(bf16[3,144,256]{2,1,0:T(8,128)(2,1)S(1)} %collect.4.refs_1_.refs_2_), channel_id=1, source_target_pairs={{0,4},{4,0},{8,12},{12,8},{16,20},{20,16},{24,28},{28,24},{1,5},{5... | collective-permute-start | bytes 663560 | tf_op jit(solution)/shard_map/ppermute | solution.py:534
  10.0 7.1 %collective-permute-start.6 = (bf16[144,256]{1,0:T(8,128)(2,1)S(1)}, bf16[144,256]{1,0:T(8,128)(2,1)S(1)}, u32[]{:S(2)}, u32[]{:S(2)}) collective-permute-start(bf16[144,256]{1,0:T(8,128)(2,1)S(1)} %get-tuple-element.37.refs_1_.refs_0_), channel_id=1, source_target_pairs={{0,16},{4,20},{8,24},{12,28},{16,0},{20,4},{24,8},{28,12},{1,17},{... | collective-permute-start | bytes 221192 | tf_op jit(solution)/shard_map/ppermute | solution.py:534
  17.2 6.7 %collective-permute-start.10 = (bf16[1,144,256]{2,1,0:T(8,128)(2,1)S(1)}, bf16[1,144,256]{2,1,0:T(8,128)(2,1)S(1)}, u32[]{:S(2)}, u32[]{:S(2)}) collective-permute-start(bf16[1,144,256]{2,1,0:T(8,128)(2,1)S(1)} %collect.6.refs_1_), channel_id=1, source_target_pairs={{0,1},{1,0},{2,3},{3,2},{4,5},{5,4},{6,7},{7,6},{8,9},{9,8},{10,11... | collective-permute-start | bytes 221192 | tf_op jit(solution)/shard_map/ppermute | solution.py:534
  18.6 5.3 %collective-permute-start.8 = (bf16[1,144,256]{2,1,0:T(8,128)(2,1)S(1)}, bf16[1,144,256]{2,1,0:T(8,128)(2,1)S(1)}, u32[]{:S(2)}, u32[]{:S(2)}) collective-permute-start(bf16[1,144,256]{2,1,0:T(8,128)(2,1)S(1)} %collect.6.refs_1_), channel_id=1, source_target_pairs={{0,3},{1,2},{2,1},{3,0},{4,7},{5,6},{6,5},{7,4},{8,11},{9,10},{10,... | collective-permute-start | bytes 221192 | tf_op jit(solution)/shard_map/ppermute | solution.py:534
  20.2 4.4 %collective-permute-start.9 = (bf16[1,144,256]{2,1,0:T(8,128)(2,1)S(1)}, bf16[1,144,256]{2,1,0:T(8,128)(2,1)S(1)}, u32[]{:S(2)}, u32[]{:S(2)}) collective-permute-start(bf16[1,144,256]{2,1,0:T(8,128)(2,1)S(1)} %collect.6.refs_1_), channel_id=1, source_target_pairs={{0,2},{1,3},{2,0},{3,1},{4,6},{5,7},{6,4},{7,5},{8,10},{9,11},{10,... | collective-permute-start | bytes 221192 | tf_op jit(solution)/shard_map/ppermute | solution.py:534
  24.7 7.4 %collective-permute-start.11 = (bf16[3,144,256]{2,1,0:T(8,128)(2,1)S(1)}, bf16[3,144,256]{2,1,0:T(8,128)(2,1)S(1)}, u32[]{:S(2)}, u32[]{:S(2)}) collective-permute-start(bf16[3,144,256]{2,1,0:T(8,128)(2,1)S(1)} %collect.7.refs_2_), channel_id=1, source_target_pairs={{0,4},{4,0},{8,12},{12,8},{16,20},{20,16},{24,28},{28,24},{1,5},{5... | collective-permute-start | bytes 663560 | tf_op jit(solution)/shard_map/ppermute | solution.py:534
  24.8 13.1 %collective-permute-start.5 = (bf16[4,144,256]{2,1,0:T(8,128)(2,1)S(1)}, bf16[4,144,256]{2,1,0:T(8,128)(2,1)S(1)}, u32[]{:S(2)}, u32[]{:S(2)}) collective-permute-start(bf16[4,144,256]{2,1,0:T(8,128)(2,1)S(1)} %collect.5), channel_id=1, source_target_pairs={{0,28},{4,8},{8,4},{12,16},{16,12},{20,24},{24,20},{28,0},{1,29},{... | collective-permute-start | bytes 884744 | tf_op jit(solution)/shard_map/ppermute | solution.py:585
  29.0 3.0 %collective-permute-start.7 = (bf16[1,144,256]{2,1,0:T(8,128)(2,1)S(1)}, bf16[1,144,256]{2,1,0:T(8,128)(2,1)S(1)}, u32[]{:S(2)}, u32[]{:S(2)}) collective-permute-start(bf16[1,144,256]{2,1,0:T(8,128)(2,1)S(1)} %collect.6.refs_1_), channel_id=1, source_target_pairs={{0,4},{4,0},{8,12},{12,8},{16,20},{20,16},{24,28},{28,24},{1,5},{5... | collective-permute-start | bytes 221192 | tf_op jit(solution)/shard_map/ppermute | solution.py:534
  35.7 8.5 %collective-permute-start.14 = (bf16[2,128,256]{2,1,0:T(8,128)(2,1)S(1)}, bf16[2,128,256]{2,1,0:T(8,128)(2,1)S(1)}, u32[]{:S(2)}, u32[]{:S(2)}) collective-permute-start(bf16[2,128,256]{2,1,0:T(8,128)(2,1)S(1)} %get-tuple-element.47.refs_6_), channel_id=1, source_target_pairs={{0,8},{4,12},{8,0},{12,4},{16,24},{20,28},{24,16},{28,20},{1,9},{5... | collective-permute-start | bytes 393224 | tf_op jit(solution)/shard_map/ppermute | solution.py:534
  35.8 9.2 %collective-permute-start.13 = (bf16[2,128,256]{2,1,0:T(8,128)(2,1)S(1)}, bf16[2,128,256]{2,1,0:T(8,128)(2,1)S(1)}, u32[]{:S(2)}, u32[]{:S(2)}) collective-permute-start(bf16[2,128,256]{2,1,0:T(8,128)(2,1)S(1)} %get-tuple-element.46.refs_4_), channel_id=1, source_target_pairs={{0,8},{4,12},{8,0},{12,4},{16,24},{20,28},{24,16},{28,20},{1,9},{5... | collective-permute-start | bytes 393224 | tf_op jit(solution)/shard_map/ppermute | solution.py:534
  37.8 9.5 %collective-permute-start.12 = (bf16[2,128,256]{2,1,0:T(8,128)(2,1)S(1)}, bf16[2,128,256]{2,1,0:T(8,128)(2,1)S(1)}, u32[]{:S(2)}, u32[]{:S(2)}) collective-permute-start(bf16[2,128,256]{2,1,0:T(8,128)(2,1)S(1)} %get-tuple-element.45.refs_4_), channel_id=1, source_target_pairs={{0,8},{4,12},{8,0},{12,4},{16,24},{20,28},{24,16},{28,20},{1,9},{5... | collective-permute-start | bytes 393224 | tf_op jit(solution)/shard_map/ppermute | solution.py:534
  47.9 1.8 %collective-permute-start.19 = (bf16[128,1024]{1,0:T(8,128)(2,1)S(1)}, bf16[128,1024]{1,0:T(8,128)(2,1)S(1)}, u32[]{:S(2)}, u32[]{:S(2)}) collective-permute-start(bf16[128,1024]{1,0:T(8,128)(2,1)S(1)} %get-tuple-element.64), channel_id=1, source_target_pairs={{0,4},{4,0},{8,12},{12,8},{16,20},{20,16},{24,28},{28,24},{1,5},{5... | collective-permute-start | bytes 786440 | tf_op jit(solution)/shard_map/ppermute | solution.py:534
  48.6 5.4 %collective-permute-start.15 = (bf16[128,1024]{1,0:T(8,128)(2,1)S(1)}, bf16[128,1024]{1,0:T(8,128)(2,1)S(1)}, u32[]{:S(2)}, u32[]{:S(2)}) collective-permute-start(bf16[128,1024]{1,0:T(8,128)(2,1)S(1)} %inverse.4), channel_id=1, source_target_pairs={{0,4},{4,0},{8,12},{12,8},{16,20},{20,16},{24,28},{28,24},{1,5},{5... | collective-permute-start | bytes 786440 | tf_op jit(solution)/shard_map/ppermute | solution.py:534
  49.8 6.4 %collective-permute-start.20 = (bf16[128,256]{1,0:T(8,128)(2,1)S(1)}, bf16[128,256]{1,0:T(8,128)(2,1)S(1)}, u32[]{:S(2)}, u32[]{:S(2)}) collective-permute-start(bf16[128,256]{1,0:T(8,128)(2,1)S(1)} %get-tuple-element.66), channel_id=1, source_target_pairs={{0,3},{1,2},{2,1},{3,0},{4,7},{5,6},{6,5},{7,4},{8,11},{9,10},{10,... | collective-permute-start | bytes 196616 | tf_op jit(solution)/shard_map/ppermute | solution.py:534
  51.3 6.3 %collective-permute-start.21 = (bf16[128,256]{1,0:T(8,128)(2,1)S(1)}, bf16[128,256]{1,0:T(8,128)(2,1)S(1)}, u32[]{:S(2)}, u32[]{:S(2)}) collective-permute-start(bf16[128,256]{1,0:T(8,128)(2,1)S(1)} %get-tuple-element.67), channel_id=1, source_target_pairs={{0,2},{1,3},{2,0},{3,1},{4,6},{5,7},{6,4},{7,5},{8,10},{9,11},{10,... | collective-permute-start | bytes 196616 | tf_op jit(solution)/shard_map/ppermute | solution.py:534
  51.9 5.6 %collective-permute-start.22 = (bf16[128,256]{1,0:T(8,128)(2,1)S(1)}, bf16[128,256]{1,0:T(8,128)(2,1)S(1)}, u32[]{:S(2)}, u32[]{:S(2)}) collective-permute-start(bf16[128,256]{1,0:T(8,128)(2,1)S(1)} %get-tuple-element.68), channel_id=1, source_target_pairs={{0,1},{1,0},{2,3},{3,2},{4,5},{5,4},{6,7},{7,6},{8,9},{9,8},{10,11... | collective-permute-start | bytes 196616 | tf_op jit(solution)/shard_map/ppermute | solution.py:534
  54.0 5.7 %collective-permute-start.16 = (bf16[128,256]{1,0:T(8,128)(2,1)S(1)}, bf16[128,256]{1,0:T(8,128)(2,1)S(1)}, u32[]{:S(2)}, u32[]{:S(2)}) collective-permute-start(bf16[128,256]{1,0:T(8,128)(2,1)S(1)} %get-tuple-element.60), channel_id=1, source_target_pairs={{0,3},{1,2},{2,1},{3,0},{4,7},{5,6},{6,5},{7,4},{8,11},{9,10},{10,... | collective-permute-start | bytes 196616 | tf_op jit(solution)/shard_map/ppermute | solution.py:534
  55.5 4.7 %collective-permute-start.17 = (bf16[128,256]{1,0:T(8,128)(2,1)S(1)}, bf16[128,256]{1,0:T(8,128)(2,1)S(1)}, u32[]{:S(2)}, u32[]{:S(2)}) collective-permute-start(bf16[128,256]{1,0:T(8,128)(2,1)S(1)} %get-tuple-element.61), channel_id=1, source_target_pairs={{0,2},{1,3},{2,0},{3,1},{4,6},{5,7},{6,4},{7,5},{8,10},{9,11},{10,... | collective-permute-start | bytes 196616 | tf_op jit(solution)/shard_map/ppermute | solution.py:534
  56.2 4.3 %collective-permute-start.18 = (bf16[128,256]{1,0:T(8,128)(2,1)S(1)}, bf16[128,256]{1,0:T(8,128)(2,1)S(1)}, u32[]{:S(2)}, u32[]{:S(2)}) collective-permute-start(bf16[128,256]{1,0:T(8,128)(2,1)S(1)} %get-tuple-element.62), channel_id=1, source_target_pairs={{0,1},{1,0},{2,3},{3,2},{4,5},{5,4},{6,7},{7,6},{8,9},{9,8},{10,11... | collective-permute-start | bytes 196616 | tf_op jit(solution)/shard_map/ppermute | solution.py:534
  57.6 5.7 %collective-permute-start.23 = (bf16[128,256]{1,0:T(8,128)(2,1)S(1)}, bf16[128,256]{1,0:T(8,128)(2,1)S(1)}, u32[]{:S(2)}, u32[]{:S(2)}) collective-permute-start(bf16[128,256]{1,0:T(8,128)(2,1)S(1)} %add_convert_fusion), channel_id=1, source_target_pairs={{0,16},{4,20},{8,24},{12,28},{16,0},{20,4},{24,8},{28,12},{1,17},{... | collective-permute-start | bytes 196616 | tf_op jit(solution)/shard_map/ppermute | solution.py:534
  (7 other events, 79.5 us)

commit v4 on v3

--- a/solution.py
+++ b/solution.py
@@ -372,15 +372,15 @@
     )(here, arrived)
 
 
-def pair_kernel(nbasis, pieces, output_scale, picks, arrays, neighbours_ref, own_pos_ref, *refs):
+def pair_kernel(nbasis, pieces, output_scale, picks, arrays, own, neighbours_ref, own_pos_ref, *refs):
     message_refs, refs = refs[:arrays], refs[arrays:]
-    weight_ref, _, out_ref, feat_scr, pos_scr, own_scr, basis_scr, near_scr, spot_scr = refs
+    weight_ref, _, out_ref, feat_scr, pos_scr, own_scr, basis_scr, near_scr, spot_scr, acc_scr = refs
     block = BLOCK_ATOMS
     both = 2 * block
     width = 12.0 / nbasis
     own_blocks, neighbours = neighbours_ref.shape
     shard = own_blocks * block
-    channels = out_ref.shape[1]
+    channels = out_ref.shape[0]
 
     views = [
         message_refs[array] if index is None else message_refs[array].at[index]
@@ -391,10 +391,9 @@
         feat_scr[:, lanes] = ref[0:channels, :]
         parts = ref[channels:, :].astype(F32)
         pos_scr[0:3, lanes] = (parts[0:3] + parts[3:6] + parts[6:9]) * 8.0
-    for b in range(own_blocks):
-        for d in range(3):
-            row = own_pos_ref[d : d + 1, b * block : (b + 1) * block]
-            own_scr[b, d] = jnp.broadcast_to(row, (both, block)).T
+    for d in range(3):
+        row = own_pos_ref[d : d + 1, own * block : (own + 1) * block]
+        own_scr[d] = jnp.broadcast_to(row, (both, block)).T
 
     a_index = lax.axis_index("atoms")
     k_index = lax.axis_index("kvec")
@@ -421,21 +420,21 @@
     per_block = neighbours // 2
     log2e = math.log2(math.e)
 
-    def unit(b, pair, carry):
+    def unit(pair, carry):
         own_place = jnp.full((1, both), -1, jnp.int32)
         for h in range(2):
-            ident = neighbours_ref[b, 2 * pair + h]
+            ident = neighbours_ref[own, 2 * pair + h]
             lanes = pl.ds(pl.multiple_of(place_of(ident) * block, block), block)
             here = pl.ds(pl.multiple_of(pair * both + h * block, block), block)
-            near_scr[b, :, here] = feat_scr[:, lanes]
+            near_scr[:, here] = feat_scr[:, lanes]
             spot_scr[0:3, h * block : (h + 1) * block] = pos_scr[0:3, lanes]
-            inside = (lane >= h * block) & (lane < (h + 1) * block) & (ident == first + b)
+            inside = (lane >= h * block) & (lane < (h + 1) * block) & (ident == first + own)
             own_place = jnp.where(inside, lane - h * block, own_place)
         lanes = pl.ds(pl.multiple_of(pair * both, both), both)
         for at in range(0, block, rows):
-            dist2 = (own_scr[b, 0, at : at + rows, :] - spot_scr[0:1, :]) ** 2
-            dist2 += (own_scr[b, 1, at : at + rows, :] - spot_scr[1:2, :]) ** 2
-            dist2 += (own_scr[b, 2, at : at + rows, :] - spot_scr[2:3, :]) ** 2
+            dist2 = (own_scr[0, at : at + rows, :] - spot_scr[0:1, :]) ** 2
+            dist2 += (own_scr[1, at : at + rows, :] - spot_scr[1:2, :]) ** 2
+            dist2 += (own_scr[2, at : at + rows, :] - spot_scr[2:3, :]) ** 2
             radius = dist2 * lax.rsqrt(jnp.maximum(dist2, 1e-30))
             env = (16.0 * output_scale) / (16.0 + dist2)
             env = jnp.where(row_index + at == own_place, 0.0, env)
@@ -445,33 +444,26 @@
             for k in range(nbasis):
                 if k:
                     value = value * ratio
-                basis_scr[b, k * block + at : k * block + at + rows, lanes] = value.astype(BF16)
+                basis_scr[k * block + at : k * block + at + rows, lanes] = value.astype(BF16)
         return carry
 
-    for b in range(own_blocks):
-        lax.fori_loop(0, per_block, functools.partial(unit, b), 0)
-    for b in range(own_blocks):
-        total = jnp.zeros((block, channels), F32)
-        for k in range(0, nbasis, 2):
-            gathered = lax.dot_general(
-                basis_scr[b, k * block : (k + 2) * block, :],
-                near_scr[b],
-                (((1,), (1,)), ((), ())),
-                preferred_element_type=F32,
-            )
-            parts = [
-                gathered[h * block : (h + 1) * block] * math.exp(-0.5 * (k + h) * (k + h))
-                for h in range(2)
-            ]
-            total += jnp.dot(
-                jnp.concatenate(parts, axis=1).astype(BF16),
-                weight_ref[k * channels : (k + 2) * channels, :],
-                preferred_element_type=F32,
-            )
-        out_ref[b * block : (b + 1) * block, :] = total
-
-
-def pair_message(neighbours, own_pos, arrays, picks, weight, after):
+    lax.fori_loop(0, per_block, unit, 0)
+    acc_scr[...] = lax.dot_general(
+        near_scr[...], basis_scr[...], (((1,), (1,)), ((), ())), preferred_element_type=F32
+    )
+    total = jnp.zeros((channels, block), F32)
+    for n in range(nbasis):
+        part = acc_scr[:, n * block : (n + 1) * block] * math.exp(-0.5 * n * n)
+        total += lax.dot_general(
+            weight_ref[n * channels : (n + 1) * channels, :],
+            part.astype(BF16),
+            (((0,), (0,)), ((), ())),
+            preferred_element_type=F32,
+        )
+    out_ref[...] = total
+
+
+def pair_message(own, neighbours, own_pos, arrays, picks, weight, after):
     channels = weight.shape[1]
     nbasis = weight.shape[0] // channels
     pieces = len(picks) // 3
@@ -479,37 +471,38 @@
     count = neighbours.shape[1]
     scale = float(count * BLOCK_ATOMS) ** (-0.5)
     window = 3 * pieces * shard
-    blocks = shard // BLOCK_ATOMS
-    return pl.pallas_call(
-        functools.partial(pair_kernel, nbasis, pieces, scale, picks, len(arrays)),
+    return pl.pallas_call(
+        functools.partial(pair_kernel, nbasis, pieces, scale, picks, len(arrays), own),
         in_specs=[SMEM] + [VMEM] * (2 + len(arrays)) + [ANY],
         out_specs=VMEM,
-        out_shape=jax.ShapeDtypeStruct((shard, channels), F32),
+        out_shape=jax.ShapeDtypeStruct((channels, BLOCK_ATOMS), F32),
         scratch_shapes=[
             pltpu.VMEM((channels, window), BF16),
             pltpu.VMEM((8, window), F32),
-            pltpu.VMEM((blocks, 3, BLOCK_ATOMS, 2 * BLOCK_ATOMS), F32),
-            pltpu.VMEM((blocks, nbasis * BLOCK_ATOMS, count * BLOCK_ATOMS), BF16),
-            pltpu.VMEM((blocks, channels, count * BLOCK_ATOMS), BF16),
+            pltpu.VMEM((3, BLOCK_ATOMS, 2 * BLOCK_ATOMS), F32),
+            pltpu.VMEM((nbasis * BLOCK_ATOMS, count * BLOCK_ATOMS), BF16),
+            pltpu.VMEM((channels, count * BLOCK_ATOMS), BF16),
             pltpu.VMEM((8, 2 * BLOCK_ATOMS), F32),
+            pltpu.VMEM((channels, nbasis * BLOCK_ATOMS), F32),
         ],
         compiler_params=params(),
         cost_estimate=pl.CostEstimate(
-            flops=2 * shard * count * BLOCK_ATOMS * (nbasis * channels + 40),
+            flops=2 * BLOCK_ATOMS * count * BLOCK_ATOMS * (nbasis * channels + 40),
             bytes_accessed=2 * window * channels,
-            transcendentals=3 * shard * count * BLOCK_ATOMS,
+            transcendentals=3 * BLOCK_ATOMS * count * BLOCK_ATOMS,
         ),
         name="pair",
     )(neighbours, own_pos, *arrays, weight, after)
 
 
-def update_kernel(*refs):
-    features_ref, pair_ref, gain_ref, w_in_ref, w_out_ref = refs[:5]
-    parts, out_ref = refs[5:-1], refs[-1]
+def update_kernel(pairs, *refs):
+    features_ref, gain_ref, w_in_ref, w_out_ref = refs[:4]
+    pair_refs, parts, out_ref = refs[4 : 4 + pairs], refs[4 + pairs : -1], refs[-1]
     long_t = parts[0][...].astype(F32)
     for part in parts[1:]:
         long_t = long_t + part[...].astype(F32)
-    total = features_ref[...].astype(F32) + pair_ref[...] + long_t.T
+    pair_t = jnp.concatenate([ref[...] for ref in pair_refs], axis=1)
+    total = features_ref[...].astype(F32) + (pair_t + long_t).T
     mean = jnp.mean(total * total, axis=-1, keepdims=True)
     normed = (total * lax.rsqrt(mean + 1e-06) * gain_ref[...]).astype(BF16)
     pre = jnp.dot(normed, w_in_ref[...], preferred_element_type=F32)
@@ -519,15 +512,15 @@
     ).astype(BF16)
 
 
-def update(features, pair_msg, gain, w_in, w_out, parts):
-    return pl.pallas_call(
-        update_kernel,
-        in_specs=[VMEM] * (5 + len(parts)),
+def update(features, pairs, gain, w_in, w_out, parts):
+    return pl.pallas_call(
+        functools.partial(update_kernel, len(pairs)),
+        in_specs=[VMEM] * (4 + len(pairs) + len(parts)),
         out_specs=VMEM,
         out_shape=jax.ShapeDtypeStruct(features.shape, BF16),
         compiler_params=params(),
         name="update",
-    )(features, pair_msg, gain[None, :], w_in, w_out, *parts)
+    )(features, gain[None, :], w_in, w_out, *pairs, *parts)
 
 
 def swap(value, axis, bits):
@@ -609,13 +602,15 @@
     picks = [(0, None)] + [(2, n_kvec - 1 - k) for k in range(1, n_kvec)]
     picks += [(1, None)] + [(3, n_kvec - 1 - k) for k in range(1, n_kvec)]
     picks += [(4, k) for k in range(n_kvec)]
-    pair_msg = pair_message(neighbours, positions, arrays, tuple(picks), pair_weight, low)
+    pairs = []
+    for b in range(neighbours.shape[0]):
+        pairs.append(pair_message(b, neighbours, positions, arrays, tuple(picks), pair_weight, low))
 
     def runs(core, distances):
         return tuple(where[core, z, k] for k in range(n_kvec) for z in distances)
 
     filt, away_far = inverse_first(
-        own_factors, other_factors, kfilt, pair_msg, tables, runs(1, zs), shard
+        own_factors, other_factors, kfilt, pairs[0], tables, runs(1, zs), shard
     )
     crossed_far = swap(away_far, "atoms", 1)
     away_near = inverse(filt, tables, runs(1, (0,)), shard, BF16)
@@ -627,10 +622,12 @@
     sum_far = sum_far.astype(BF16)
     here_near = inverse(filt, tables, runs(0, (0,)), shard, F32)
     own_near, *sends = join(here_near, crossed_near, n_kvec)
-    parts = [own_near] + [swap(sends[k - 1], "kvec", k) for k in others]
+    parts = [own_near]
+    for k in others:
+        parts.append(swap(sends[k - 1], "kvec", k))
     for z in zs:
         parts.append(swap(sum_far[:, (z - 1) * shard : z * shard], "atoms", 4 * z))
-    return update(features, pair_msg, norm_gain, w_in, w_out, parts)
+    return update(features, pairs, norm_gain, w_in, w_out, parts)
 
 
 def solution(mesh):

time: 64.7 us -> 64.7 us (level)
    pallas_call x1 -> x2, Pallas kernels: 6.25 us -> 6.36 us  [pair_message(): pl.pallas_call(functools.partial(pair_kernel, nbasis, pieces, scale, pick...]
  transfers between devices with their start and end apart: 24 -> 24, of which waited for: 11 -> 9; matrix products, arithmetic and copies ran while one was open for 0% -> 0% of each run, Pallas kernels for 33% -> 33%
where the time goes in v4:
time: 64.7 us; the launch traced here: 64.6 us
  starting transfers between devices  25.3 us (39%)
  Pallas kernels  24.4 us (38%)
  waiting for transfers between devices  14.5 us (22%)
    ppermute x23, starting transfers between devices, swap(): lax.ppermute(value, axis, [(i, i ^ bits) for i in range(lax.axis_size(axi...  21 us
    ppermute x23, waiting for transfers between devices, swap(): lax.ppermute(value, axis, [(i, i ^ bits) for i in range(lax.axis_size(axi...  14.5 us
    pallas_call x7, Pallas kernels, wave(): pl.pallas_call(functools.partial(wave_kernel, tuple(picks), len(arrays),...  12.8 us
    pallas_call x2, Pallas kernels, pair_message(): pl.pallas_call(functools.partial(pair_kernel, nbasis, pieces, scale, pick...  6.36 us
    ppermute x1, starting transfers between devices, per_device(): lax.ppermute(collect([message, near_own], group), 'atoms', halo_pairs)  4.26 us
    pallas_call x3, Pallas kernels, inverse(): pl.pallas_call(functools.partial(inverse_kernel, pieces, shard), in_specs...  1.75 us
  transfers between devices with their start and end apart: 24, of which 9 were waited for; matrix products, arithmetic and copies ran while one was open for 0% of the time, Pallas kernels for 33%

profile of v4, /device:TPU:0, one launch (start us, length us, event | category | flops | bytes accessed | tf_op | source)
XLA Modules:
  0.0 64.6 jit_solution(12833316107186180867)
XLA Ops:
  1.6 3.5 %collective-permute-start.1 = (bf16[144,256]{1,0:T(8,128)(2,1)S(1)}, bf16[144,256]{1,0:T(8,128)(2,1)S(1)}, u32[]{:S(2)}, u32[]{:S(2)}) collective-permute-start(bf16[144,256]{1,0:T(8,128)(2,1)S(1)} %get-tuple-element.37.refs_1_.refs_0_), channel_id=1, source_target_pairs={{0,3},{1,2},{2,1},{3,0},{4,7},{5,6},{6,5},{7,4},{8,11},{9,10},{10,... | collective-permute-start | bytes 221192 | tf_op jit(solution)/shard_map/ppermute | solution.py:527
  6.2 1.5 %wave.7 = (bf16[6,256,512]{2,1,0:T(8,128)(2,1)S(1)}, f32[6,128,256]{2,1,0:T(8,128)S(1)}) custom-call(bf16[3,256,16]{2,1,0:T(8,128)(2,1)S(1)} %get-tuple-element.40.refs_0_, bf16[144,256]{1,0:T(8,128)(2,1)S(1)} %get-tuple-element.37.refs_1_.refs_0_, bf16[144,256]{1,0:T(8,128)(2,1)S(1)} %collective-permute-done.refs_2_.refs_1_), custom_call_target="tpu_custom_call" | custom-call | flops 201326592 | bytes 1572864 | tf_op jit(solution)/shard_map/wave/pallas_call | solution.py:233
  8.0 1.6 %collective-permute-done.2.refs_1_ = bf16[144,256]{1,0:T(8,128)(2,1)S(1)} collective-permute-done((bf16[144,256]{1,0:T(8,128)(2,1)S(1)}, bf16[144,256]{1,0:T(8,128)(2,1)S(1)}, u32[]{:S(2)}, u32[]{:S(2)}) %collective-permute-start.2) | collective-permute-done | bytes 73760 | tf_op jit(solution)/shard_map/ppermute | solution.py:527
  10.0 2.7 %collective-permute-start.6 = (bf16[144,256]{1,0:T(8,128)(2,1)S(1)}, bf16[144,256]{1,0:T(8,128)(2,1)S(1)}, u32[]{:S(2)}, u32[]{:S(2)}) collective-permute-start(bf16[144,256]{1,0:T(8,128)(2,1)S(1)} %get-tuple-element.37.refs_1_.refs_0_), channel_id=1, source_target_pairs={{0,16},{4,20},{8,24},{12,28},{16,0},{20,4},{24,8},{28,12},{1,17},{... | collective-permute-start | bytes 221192 | tf_op jit(solution)/shard_map/ppermute | solution.py:527
  12.7 1.5 %wave.8 = (bf16[6,256,512]{2,1,0:T(8,128)(2,1)S(1)}, f32[6,128,256]{2,1,0:T(8,128)S(1)}) custom-call(bf16[3,256,16]{2,1,0:T(8,128)(2,1)S(1)} %get-tuple-element.40.refs_0_, bf16[3,144,256]{2,1,0:T(8,128)(2,1)S(1)} %collect.4.refs_1_.refs_2_, f32[6,128,256]{2,1,0:T(8,128)S(1)} %get-tuple-element.41.refs_3_.refs_2_), custom_call_target="tpu_custom_call" | custom-call | flops 201326592 | bytes 1572864 | tf_op jit(solution)/shard_map/wave/pallas_call | solution.py:233
  14.2 3.0 %collective-permute-done.6.refs_0_ = bf16[144,256]{1,0:T(8,128)(2,1)S(1)} collective-permute-done((bf16[144,256]{1,0:T(8,128)(2,1)S(1)}, bf16[144,256]{1,0:T(8,128)(2,1)S(1)}, u32[]{:S(2)}, u32[]{:S(2)}) %collective-permute-start.6) | collective-permute-done | bytes 73760 | tf_op jit(solution)/shard_map/ppermute | solution.py:527
  17.2 1.4 %collective-permute-start.10 = (bf16[1,144,256]{2,1,0:T(8,128)(2,1)S(1)}, bf16[1,144,256]{2,1,0:T(8,128)(2,1)S(1)}, u32[]{:S(2)}, u32[]{:S(2)}) collective-permute-start(bf16[1,144,256]{2,1,0:T(8,128)(2,1)S(1)} %collect.6.refs_1_), channel_id=1, source_target_pairs={{0,1},{1,0},{2,3},{3,2},{4,5},{5,4},{6,7},{7,6},{8,9},{9,8},{10,11... | collective-permute-start | bytes 221192 | tf_op jit(solution)/shard_map/ppermute | solution.py:527
  18.6 1.6 %collective-permute-start.8 = (bf16[1,144,256]{2,1,0:T(8,128)(2,1)S(1)}, bf16[1,144,256]{2,1,0:T(8,128)(2,1)S(1)}, u32[]{:S(2)}, u32[]{:S(2)}) collective-permute-start(bf16[1,144,256]{2,1,0:T(8,128)(2,1)S(1)} %collect.6.refs_1_), channel_id=1, source_target_pairs={{0,3},{1,2},{2,1},{3,0},{4,7},{5,6},{6,5},{7,4},{8,11},{9,10},{10,... | collective-permute-start | bytes 221192 | tf_op jit(solution)/shard_map/ppermute | solution.py:527
  20.7 3.2 %wave.9 = (bf16[6,256,1024]{2,1,0:T(8,128)(2,1)S(1)}, f32[6,128,256]{2,1,0:T(8,128)S(1)}) custom-call(bf16[3,256,16]{2,1,0:T(8,128)(2,1)S(1)} %get-tuple-element.40.refs_0_, bf16[3,144,256]{2,1,0:T(8,128)(2,1)S(1)} %collect.4.refs_1_.refs_2_, bf16[3,144,256]{2,1,0:T(8,128)(2,1)S(1)} %collective-permute-done.4.refs_2_.refs_3_, ...), custom_call_target="tpu_custom_call" | custom-call | flops 402653184 | bytes 3145728 | tf_op jit(solution)/shard_map/wave/pallas_call | solution.py:233
  24.8 4.3 %collective-permute-start.5 = (bf16[4,144,256]{2,1,0:T(8,128)(2,1)S(1)}, bf16[4,144,256]{2,1,0:T(8,128)(2,1)S(1)}, u32[]{:S(2)}, u32[]{:S(2)}) collective-permute-start(bf16[4,144,256]{2,1,0:T(8,128)(2,1)S(1)} %collect.5), channel_id=1, source_target_pairs={{0,28},{4,8},{8,4},{12,16},{16,12},{20,24},{24,20},{28,0},{1,29},{... | collective-permute-start | bytes 884744 | tf_op jit(solution)/shard_map/ppermute | solution.py:578
  29.0 3.0 %wave.10 = (bf16[6,256,1024]{2,1,0:T(8,128)(2,1)S(1)}, f32[6,128,256]{2,1,0:T(8,128)S(1)}) custom-call(bf16[3,256,16]{2,1,0:T(8,128)(2,1)S(1)} %get-tuple-element.40.refs_0_, bf16[1,144,256]{2,1,0:T(8,128)(2,1)S(1)} %collect.6.refs_1_, bf16[3,144,256]{2,1,0:T(8,128)(2,1)S(1)} %collect.7.refs_2_, f32[6,128,256]{2,1,0:T(8,128)S(1)} %get-tuple-element.43.refs_3_), custom_call_target="tpu_custom_call" | custom-call | flops 402653184 | bytes 3145728 | tf_op jit(solution)/shard_map/wave/pallas_call | solution.py:233
  32.1 1.2 %wave.11 = (bf16[2,256,1024]{2,1,0:T(8,128)(2,1)S(1)}, f32[2,128,256]{2,1,0:T(8,128)S(1)}, bf16[2,128,256]{2,1,0:T(8,128)(2,1)S(1)}) custom-call(bf16[3,256,16]{2,1,0:T(8,128)(2,1)S(1)} %get-tuple-element.40.refs_0_, bf16[1,144,256]{2,1,0:T(8,128)(2,1)S(1)} %collective-permute-done.7.refs_1_, bf16[3,144,256]{2,1,0:T(8,128)(2,1)S(1)} %collective-permute-done.11.refs_2_, ...), custom_call_target="tpu_custom_call" | custom-call | flops 134217728 | bytes 1048576 | tf_op jit(solution)/shard_map/wave/pallas_call | solution.py:233
  34.5 1.2 %wave.13 = (bf16[2,256,1024]{2,1,0:T(8,128)(2,1)S(1)}, f32[2,128,256]{2,1,0:T(8,128)S(1)}, bf16[2,128,256]{2,1,0:T(8,128)(2,1)S(1)}) custom-call(bf16[3,256,16]{2,1,0:T(8,128)(2,1)S(1)} %get-tuple-element.40.refs_0_, bf16[1,144,256]{2,1,0:T(8,128)(2,1)S(1)} %collective-permute-done.7.refs_1_, bf16[3,144,256]{2,1,0:T(8,128)(2,1)S(1)} %collective-permute-done.11.refs_2_, ...), custom_call_target="tpu_custom_call" | custom-call | flops 134217728 | bytes 1048576 | tf_op jit(solution)/shard_map/wave/pallas_call | solution.py:233
  35.8 2.0 %collective-permute-start.13 = (bf16[2,128,256]{2,1,0:T(8,128)(2,1)S(1)}, bf16[2,128,256]{2,1,0:T(8,128)(2,1)S(1)}, u32[]{:S(2)}, u32[]{:S(2)}) collective-permute-start(bf16[2,128,256]{2,1,0:T(8,128)(2,1)S(1)} %get-tuple-element.46.refs_4_), channel_id=1, source_target_pairs={{0,8},{4,12},{8,0},{12,4},{16,24},{20,28},{24,16},{28,20},{1,9},{5... | collective-permute-start | bytes 393224 | tf_op jit(solution)/shard_map/ppermute | solution.py:527
  37.9 3.2 %pair.2.refs_7_.refs_4_ = f32[128,128]{1,0:T(8,128)S(1)} custom-call(s32[2,12]{1,0:T(2,128)S(1)} %copy-done.6, f32[3,256]{1,0:T(4,128)S(1)} %copy-done.3, bf16[144,256]{1,0:T(8,128)(2,1)S(1)} %get-tuple-element.37.refs_1_.refs_0_, bf16[144,256]{1,0:T(8,128)(2,1)S(1)} %collective-permute-done.refs_2_.refs_1_, ...), custom_call_target="tpu_custom_call" | custom-call | flops 418381824 | bytes 786432 | tf_op jit(solution)/shard_map/pair/pallas_call | solution.py:474
  42.1 2.8 %collective-permute-done.13.refs_4_ = bf16[2,128,256]{2,1,0:T(8,128)(2,1)S(1)} collective-permute-done((bf16[2,128,256]{2,1,0:T(8,128)(2,1)S(1)}, bf16[2,128,256]{2,1,0:T(8,128)(2,1)S(1)}, u32[]{:S(2)}, u32[]{:S(2)}) %collective-permute-start.13) | collective-permute-done | bytes 131104 | tf_op jit(solution)/shard_map/ppermute | solution.py:527
  45.0 2.3 %collective-permute-done.12.refs_3_ = bf16[2,128,256]{2,1,0:T(8,128)(2,1)S(1)} collective-permute-done((bf16[2,128,256]{2,1,0:T(8,128)(2,1)S(1)}, bf16[2,128,256]{2,1,0:T(8,128)(2,1)S(1)}, u32[]{:S(2)}, u32[]{:S(2)}) %collective-permute-start.12) | collective-permute-done | bytes 131104 | tf_op jit(solution)/shard_map/ppermute | solution.py:527
  49.8 1.5 %collective-permute-start.20 = (bf16[128,256]{1,0:T(8,128)(2,1)S(1)}, bf16[128,256]{1,0:T(8,128)(2,1)S(1)}, u32[]{:S(2)}, u32[]{:S(2)}) collective-permute-start(bf16[128,256]{1,0:T(8,128)(2,1)S(1)} %get-tuple-element.66), channel_id=1, source_target_pairs={{0,3},{1,2},{2,1},{3,0},{4,7},{5,6},{6,5},{7,4},{8,11},{9,10},{10,... | collective-permute-start | bytes 196616 | tf_op jit(solution)/shard_map/ppermute | solution.py:527
  52.0 1.4 %collective-permute-start.22 = (bf16[128,256]{1,0:T(8,128)(2,1)S(1)}, bf16[128,256]{1,0:T(8,128)(2,1)S(1)}, u32[]{:S(2)}, u32[]{:S(2)}) collective-permute-start(bf16[128,256]{1,0:T(8,128)(2,1)S(1)} %get-tuple-element.68), channel_id=1, source_target_pairs={{0,1},{1,0},{2,3},{3,2},{4,5},{5,4},{6,7},{7,6},{8,9},{9,8},{10,11... | collective-permute-start | bytes 196616 | tf_op jit(solution)/shard_map/ppermute | solution.py:527
  54.0 1.5 %collective-permute-start.16 = (bf16[128,256]{1,0:T(8,128)(2,1)S(1)}, bf16[128,256]{1,0:T(8,128)(2,1)S(1)}, u32[]{:S(2)}, u32[]{:S(2)}) collective-permute-start(bf16[128,256]{1,0:T(8,128)(2,1)S(1)} %get-tuple-element.60), channel_id=1, source_target_pairs={{0,3},{1,2},{2,1},{3,0},{4,7},{5,6},{6,5},{7,4},{8,11},{9,10},{10,... | collective-permute-start | bytes 196616 | tf_op jit(solution)/shard_map/ppermute | solution.py:527
  56.2 1.4 %collective-permute-start.18 = (bf16[128,256]{1,0:T(8,128)(2,1)S(1)}, bf16[128,256]{1,0:T(8,128)(2,1)S(1)}, u32[]{:S(2)}, u32[]{:S(2)}) collective-permute-start(bf16[128,256]{1,0:T(8,128)(2,1)S(1)} %get-tuple-element.62), channel_id=1, source_target_pairs={{0,1},{1,0},{2,3},{3,2},{4,5},{5,4},{6,7},{7,6},{8,9},{9,8},{10,11... | collective-permute-start | bytes 196616 | tf_op jit(solution)/shard_map/ppermute | solution.py:527
  57.8 3.2 %pair.3.refs_5_ = f32[128,128]{1,0:T(8,128)S(1)} custom-call(s32[2,12]{1,0:T(2,128)S(1)} %copy-done.6, f32[3,256]{1,0:T(4,128)S(1)} %copy-done.3, bf16[144,256]{1,0:T(8,128)(2,1)S(1)} %get-tuple-element.37.refs_1_.refs_0_, bf16[144,256]{1,0:T(8,128)(2,1)S(1)} %collective-permute-done.refs_2_.refs_1_, bf16[3,144,256]{2,1,0:T(8,128)(2,1)S(1)} %collect.4.refs_1_.refs_2_, ...), custom_call_target="tpu_custom_call" | custom-call | flops 418381824 | bytes 786432 | tf_op jit(solution)/shard_map/pair/pallas_call | solution.py:474
  61.0 2.3 %collective-permute-done.23.refs_10_ = bf16[128,256]{1,0:T(8,128)(2,1)S(1)} collective-permute-done((bf16[128,256]{1,0:T(8,128)(2,1)S(1)}, bf16[128,256]{1,0:T(8,128)(2,1)S(1)}, u32[]{:S(2)}, u32[]{:S(2)}) %collective-permute-start.23) | collective-permute-done | bytes 65568 | tf_op jit(solution)/shard_map/ppermute | solution.py:527
  63.3 1.3 %update.1 = bf16[256,128]{1,0:T(8,128)(2,1)} custom-call(bf16[256,128]{1,0:T(8,128)(2,1)S(1)} %copy-done, f32[1,128]{1,0:T(1,128)S(1)} %bitcast.2, bf16[128,512]{1,0:T(8,128)(2,1)S(1)} %copy-done.1, bf16[512,128]{1,0:T(8,128)(2,1)S(1)} %copy-done.2, f32[128,128]{1,0:T(8,128)S(1)} %pair.2.refs_7_.refs_4_, f32[128,128]{1,0:T(8,128)S(1)} %pair.3.refs_5_, ...), custom_call_target="tpu_custom_call" | custom-call | tf_op jit(solution)/shard_map/update/pallas_call | solution.py:516
  (61 shorter events, 11.8 us)
Async XLA Ops:
  1.0 5.2 %collective-permute-start = (bf16[144,256]{1,0:T(8,128)(2,1)S(1)}, bf16[144,256]{1,0:T(8,128)(2,1)S(1)}, u32[]{:S(2)}, u32[]{:S(2)}) collective-permute-start(bf16[144,256]{1,0:T(8,128)(2,1)S(1)} %get-tuple-element.37.refs_1_.refs_0_), channel_id=1, source_target_pairs={{0,4},{4,0},{8,12},{12,8},{16,20},{20,16},{24,28},{28,24},{1,5},{5... | collective-permute-start | bytes 221192 | tf_op jit(solution)/shard_map/ppermute | solution.py:527
  1.6 6.4 %collective-permute-start.1 = (bf16[144,256]{1,0:T(8,128)(2,1)S(1)}, bf16[144,256]{1,0:T(8,128)(2,1)S(1)}, u32[]{:S(2)}, u32[]{:S(2)}) collective-permute-start(bf16[144,256]{1,0:T(8,128)(2,1)S(1)} %get-tuple-element.37.refs_1_.refs_0_), channel_id=1, source_target_pairs={{0,3},{1,2},{2,1},{3,0},{4,7},{5,6},{6,5},{7,4},{8,11},{9,10},{10,... | collective-permute-start | bytes 221192 | tf_op jit(solution)/shard_map/ppermute | solution.py:527
  5.1 4.4 %collective-permute-start.2 = (bf16[144,256]{1,0:T(8,128)(2,1)S(1)}, bf16[144,256]{1,0:T(8,128)(2,1)S(1)}, u32[]{:S(2)}, u32[]{:S(2)}) collective-permute-start(bf16[144,256]{1,0:T(8,128)(2,1)S(1)} %get-tuple-element.37.refs_1_.refs_0_), channel_id=1, source_target_pairs={{0,2},{1,3},{2,0},{3,1},{4,6},{5,7},{6,4},{7,5},{8,10},{9,11},{10,... | collective-permute-start | bytes 221192 | tf_op jit(solution)/shard_map/ppermute | solution.py:527
  5.6 4.4 %collective-permute-start.3 = (bf16[144,256]{1,0:T(8,128)(2,1)S(1)}, bf16[144,256]{1,0:T(8,128)(2,1)S(1)}, u32[]{:S(2)}, u32[]{:S(2)}) collective-permute-start(bf16[144,256]{1,0:T(8,128)(2,1)S(1)} %get-tuple-element.37.refs_1_.refs_0_), channel_id=1, source_target_pairs={{0,1},{1,0},{2,3},{3,2},{4,5},{5,4},{6,7},{7,6},{8,9},{9,8},{10,11... | collective-permute-start | bytes 221192 | tf_op jit(solution)/shard_map/ppermute | solution.py:527
  10.0 10.7 %collective-permute-start.4 = (bf16[3,144,256]{2,1,0:T(8,128)(2,1)S(1)}, bf16[3,144,256]{2,1,0:T(8,128)(2,1)S(1)}, u32[]{:S(2)}, u32[]{:S(2)}) collective-permute-start(bf16[3,144,256]{2,1,0:T(8,128)(2,1)S(1)} %collect.4.refs_1_.refs_2_), channel_id=1, source_target_pairs={{0,4},{4,0},{8,12},{12,8},{16,20},{20,16},{24,28},{28,24},{1,5},{5... | collective-permute-start | bytes 663560 | tf_op jit(solution)/shard_map/ppermute | solution.py:527
  10.0 7.1 %collective-permute-start.6 = (bf16[144,256]{1,0:T(8,128)(2,1)S(1)}, bf16[144,256]{1,0:T(8,128)(2,1)S(1)}, u32[]{:S(2)}, u32[]{:S(2)}) collective-permute-start(bf16[144,256]{1,0:T(8,128)(2,1)S(1)} %get-tuple-element.37.refs_1_.refs_0_), channel_id=1, source_target_pairs={{0,16},{4,20},{8,24},{12,28},{16,0},{20,4},{24,8},{28,12},{1,17},{... | collective-permute-start | bytes 221192 | tf_op jit(solution)/shard_map/ppermute | solution.py:527
  17.2 6.7 %collective-permute-start.10 = (bf16[1,144,256]{2,1,0:T(8,128)(2,1)S(1)}, bf16[1,144,256]{2,1,0:T(8,128)(2,1)S(1)}, u32[]{:S(2)}, u32[]{:S(2)}) collective-permute-start(bf16[1,144,256]{2,1,0:T(8,128)(2,1)S(1)} %collect.6.refs_1_), channel_id=1, source_target_pairs={{0,1},{1,0},{2,3},{3,2},{4,5},{5,4},{6,7},{7,6},{8,9},{9,8},{10,11... | collective-permute-start | bytes 221192 | tf_op jit(solution)/shard_map/ppermute | solution.py:527
  18.6 5.3 %collective-permute-start.8 = (bf16[1,144,256]{2,1,0:T(8,128)(2,1)S(1)}, bf16[1,144,256]{2,1,0:T(8,128)(2,1)S(1)}, u32[]{:S(2)}, u32[]{:S(2)}) collective-permute-start(bf16[1,144,256]{2,1,0:T(8,128)(2,1)S(1)} %collect.6.refs_1_), channel_id=1, source_target_pairs={{0,3},{1,2},{2,1},{3,0},{4,7},{5,6},{6,5},{7,4},{8,11},{9,10},{10,... | collective-permute-start | bytes 221192 | tf_op jit(solution)/shard_map/ppermute | solution.py:527
  20.2 4.4 %collective-permute-start.9 = (bf16[1,144,256]{2,1,0:T(8,128)(2,1)S(1)}, bf16[1,144,256]{2,1,0:T(8,128)(2,1)S(1)}, u32[]{:S(2)}, u32[]{:S(2)}) collective-permute-start(bf16[1,144,256]{2,1,0:T(8,128)(2,1)S(1)} %collect.6.refs_1_), channel_id=1, source_target_pairs={{0,2},{1,3},{2,0},{3,1},{4,6},{5,7},{6,4},{7,5},{8,10},{9,11},{10,... | collective-permute-start | bytes 221192 | tf_op jit(solution)/shard_map/ppermute | solution.py:527
  24.7 7.4 %collective-permute-start.11 = (bf16[3,144,256]{2,1,0:T(8,128)(2,1)S(1)}, bf16[3,144,256]{2,1,0:T(8,128)(2,1)S(1)}, u32[]{:S(2)}, u32[]{:S(2)}) collective-permute-start(bf16[3,144,256]{2,1,0:T(8,128)(2,1)S(1)} %collect.7.refs_2_), channel_id=1, source_target_pairs={{0,4},{4,0},{8,12},{12,8},{16,20},{20,16},{24,28},{28,24},{1,5},{5... | collective-permute-start | bytes 663560 | tf_op jit(solution)/shard_map/ppermute | solution.py:527
  24.8 13.1 %collective-permute-start.5 = (bf16[4,144,256]{2,1,0:T(8,128)(2,1)S(1)}, bf16[4,144,256]{2,1,0:T(8,128)(2,1)S(1)}, u32[]{:S(2)}, u32[]{:S(2)}) collective-permute-start(bf16[4,144,256]{2,1,0:T(8,128)(2,1)S(1)} %collect.5), channel_id=1, source_target_pairs={{0,28},{4,8},{8,4},{12,16},{16,12},{20,24},{24,20},{28,0},{1,29},{... | collective-permute-start | bytes 884744 | tf_op jit(solution)/shard_map/ppermute | solution.py:578
  29.0 3.0 %collective-permute-start.7 = (bf16[1,144,256]{2,1,0:T(8,128)(2,1)S(1)}, bf16[1,144,256]{2,1,0:T(8,128)(2,1)S(1)}, u32[]{:S(2)}, u32[]{:S(2)}) collective-permute-start(bf16[1,144,256]{2,1,0:T(8,128)(2,1)S(1)} %collect.6.refs_1_), channel_id=1, source_target_pairs={{0,4},{4,0},{8,12},{12,8},{16,20},{20,16},{24,28},{28,24},{1,5},{5... | collective-permute-start | bytes 221192 | tf_op jit(solution)/shard_map/ppermute | solution.py:527
  35.7 6.4 %collective-permute-start.14 = (bf16[2,128,256]{2,1,0:T(8,128)(2,1)S(1)}, bf16[2,128,256]{2,1,0:T(8,128)(2,1)S(1)}, u32[]{:S(2)}, u32[]{:S(2)}) collective-permute-start(bf16[2,128,256]{2,1,0:T(8,128)(2,1)S(1)} %get-tuple-element.47.refs_6_), channel_id=1, source_target_pairs={{0,8},{4,12},{8,0},{12,4},{16,24},{20,28},{24,16},{28,20},{1,9},{5... | collective-permute-start | bytes 393224 | tf_op jit(solution)/shard_map/ppermute | solution.py:527
  35.8 9.2 %collective-permute-start.13 = (bf16[2,128,256]{2,1,0:T(8,128)(2,1)S(1)}, bf16[2,128,256]{2,1,0:T(8,128)(2,1)S(1)}, u32[]{:S(2)}, u32[]{:S(2)}) collective-permute-start(bf16[2,128,256]{2,1,0:T(8,128)(2,1)S(1)} %get-tuple-element.46.refs_4_), channel_id=1, source_target_pairs={{0,8},{4,12},{8,0},{12,4},{16,24},{20,28},{24,16},{28,20},{1,9},{5... | collective-permute-start | bytes 393224 | tf_op jit(solution)/shard_map/ppermute | solution.py:527
  37.8 9.5 %collective-permute-start.12 = (bf16[2,128,256]{2,1,0:T(8,128)(2,1)S(1)}, bf16[2,128,256]{2,1,0:T(8,128)(2,1)S(1)}, u32[]{:S(2)}, u32[]{:S(2)}) collective-permute-start(bf16[2,128,256]{2,1,0:T(8,128)(2,1)S(1)} %get-tuple-element.45.refs_4_), channel_id=1, source_target_pairs={{0,8},{4,12},{8,0},{12,4},{16,24},{20,28},{24,16},{28,20},{1,9},{5... | collective-permute-start | bytes 393224 | tf_op jit(solution)/shard_map/ppermute | solution.py:527
  47.9 1.8 %collective-permute-start.19 = (bf16[128,1024]{1,0:T(8,128)(2,1)S(1)}, bf16[128,1024]{1,0:T(8,128)(2,1)S(1)}, u32[]{:S(2)}, u32[]{:S(2)}) collective-permute-start(bf16[128,1024]{1,0:T(8,128)(2,1)S(1)} %get-tuple-element.64), channel_id=1, source_target_pairs={{0,4},{4,0},{8,12},{12,8},{16,20},{20,16},{24,28},{28,24},{1,5},{5... | collective-permute-start | bytes 786440 | tf_op jit(solution)/shard_map/ppermute | solution.py:527
  48.6 5.4 %collective-permute-start.15 = (bf16[128,1024]{1,0:T(8,128)(2,1)S(1)}, bf16[128,1024]{1,0:T(8,128)(2,1)S(1)}, u32[]{:S(2)}, u32[]{:S(2)}) collective-permute-start(bf16[128,1024]{1,0:T(8,128)(2,1)S(1)} %inverse.4), channel_id=1, source_target_pairs={{0,4},{4,0},{8,12},{12,8},{16,20},{20,16},{24,28},{28,24},{1,5},{5... | collective-permute-start | bytes 786440 | tf_op jit(solution)/shard_map/ppermute | solution.py:527
  49.8 6.4 %collective-permute-start.20 = (bf16[128,256]{1,0:T(8,128)(2,1)S(1)}, bf16[128,256]{1,0:T(8,128)(2,1)S(1)}, u32[]{:S(2)}, u32[]{:S(2)}) collective-permute-start(bf16[128,256]{1,0:T(8,128)(2,1)S(1)} %get-tuple-element.66), channel_id=1, source_target_pairs={{0,3},{1,2},{2,1},{3,0},{4,7},{5,6},{6,5},{7,4},{8,11},{9,10},{10,... | collective-permute-start | bytes 196616 | tf_op jit(solution)/shard_map/ppermute | solution.py:527
  51.3 6.3 %collective-permute-start.21 = (bf16[128,256]{1,0:T(8,128)(2,1)S(1)}, bf16[128,256]{1,0:T(8,128)(2,1)S(1)}, u32[]{:S(2)}, u32[]{:S(2)}) collective-permute-start(bf16[128,256]{1,0:T(8,128)(2,1)S(1)} %get-tuple-element.67), channel_id=1, source_target_pairs={{0,2},{1,3},{2,0},{3,1},{4,6},{5,7},{6,4},{7,5},{8,10},{9,11},{10,... | collective-permute-start | bytes 196616 | tf_op jit(solution)/shard_map/ppermute | solution.py:527
  52.0 5.6 %collective-permute-start.22 = (bf16[128,256]{1,0:T(8,128)(2,1)S(1)}, bf16[128,256]{1,0:T(8,128)(2,1)S(1)}, u32[]{:S(2)}, u32[]{:S(2)}) collective-permute-start(bf16[128,256]{1,0:T(8,128)(2,1)S(1)} %get-tuple-element.68), channel_id=1, source_target_pairs={{0,1},{1,0},{2,3},{3,2},{4,5},{5,4},{6,7},{7,6},{8,9},{9,8},{10,11... | collective-permute-start | bytes 196616 | tf_op jit(solution)/shard_map/ppermute | solution.py:527
  54.0 6.9 %collective-permute-start.16 = (bf16[128,256]{1,0:T(8,128)(2,1)S(1)}, bf16[128,256]{1,0:T(8,128)(2,1)S(1)}, u32[]{:S(2)}, u32[]{:S(2)}) collective-permute-start(bf16[128,256]{1,0:T(8,128)(2,1)S(1)} %get-tuple-element.60), channel_id=1, source_target_pairs={{0,3},{1,2},{2,1},{3,0},{4,7},{5,6},{6,5},{7,4},{8,11},{9,10},{10,... | collective-permute-start | bytes 196616 | tf_op jit(solution)/shard_map/ppermute | solution.py:527
  55.6 5.4 %collective-permute-start.17 = (bf16[128,256]{1,0:T(8,128)(2,1)S(1)}, bf16[128,256]{1,0:T(8,128)(2,1)S(1)}, u32[]{:S(2)}, u32[]{:S(2)}) collective-permute-start(bf16[128,256]{1,0:T(8,128)(2,1)S(1)} %get-tuple-element.61), channel_id=1, source_target_pairs={{0,2},{1,3},{2,0},{3,1},{4,6},{5,7},{6,4},{7,5},{8,10},{9,11},{10,... | collective-permute-start | bytes 196616 | tf_op jit(solution)/shard_map/ppermute | solution.py:527
  56.2 4.8 %collective-permute-start.18 = (bf16[128,256]{1,0:T(8,128)(2,1)S(1)}, bf16[128,256]{1,0:T(8,128)(2,1)S(1)}, u32[]{:S(2)}, u32[]{:S(2)}) collective-permute-start(bf16[128,256]{1,0:T(8,128)(2,1)S(1)} %get-tuple-element.62), channel_id=1, source_target_pairs={{0,1},{1,0},{2,3},{3,2},{4,5},{5,4},{6,7},{7,6},{8,9},{9,8},{10,11... | collective-permute-start | bytes 196616 | tf_op jit(solution)/shard_map/ppermute | solution.py:527
  57.6 5.7 %collective-permute-start.23 = (bf16[128,256]{1,0:T(8,128)(2,1)S(1)}, bf16[128,256]{1,0:T(8,128)(2,1)S(1)}, u32[]{:S(2)}, u32[]{:S(2)}) collective-permute-start(bf16[128,256]{1,0:T(8,128)(2,1)S(1)} %add_convert_fusion), channel_id=1, source_target_pairs={{0,16},{4,20},{8,24},{12,28},{16,0},{20,4},{24,8},{28,12},{1,17},{... | collective-permute-start | bytes 196616 | tf_op jit(solution)/shard_map/ppermute | solution.py:527
  (7 other events, 79.6 us)

commit v5 on v4

--- a/solution.py
+++ b/solution.py
@@ -576,27 +576,30 @@
     halo_pairs = [(a, (a + 1) % n_atoms if a % 2 else (a - 1) % n_atoms) for a in range(n_atoms)]
     group = [(0, None)] + [(1, n_kvec - 1 - k) for k in range(1, n_kvec)]
     halo = lax.ppermute(collect([message, near_own], group), "atoms", halo_pairs)
-    table, total = wave(waves, [near_own, near_x], picks[2:], total)
-    keep(table, names[2:])
+    middle = 2 + (len(picks) - 2) // 4 * 2
+    table, total = wave(waves, [near_own, near_x], picks[2:middle], total)
+    keep(table, names[2:middle])
     every = [(i, z) for i in range(n_kvec - 1) for z in range(far - 1)]
     far_own = collect([relayed[k] for k in others], every, after=(total,))
     far_x = swap(far_own, "atoms", 1)
-    picks = [(0, z) for z in range(far - 1)] + [(1, i) for i in range(len(every))]
-    spots = [(z, k) for k in (0, *others) for z in zs]
-    table, total = wave(waves, [distant, far_own], picks, total)
-    keep(table, [(0, *spot) for spot in spots])
+    table, total = wave(waves, [near_own, near_x], picks[middle:], total, after=(far_own,))
+    keep(table, names[middle:])
+    arrays = [distant, far_own, distant_x, far_x]
+    picks = []
+    for core in range(2):
+        picks += [(2 * core, z) for z in range(far - 1)]
+        picks += [(2 * core + 1, i) for i in range(len(every))]
+    spots = [(core, z, k) for core in range(2) for k in (0, *others) for z in zs]
     own_factors, other_factors, low = [], [], None
     for j in range(blocks):
         after = () if low is None else (low,)
-        table, part, low = wave(
-            waves, [distant_x, far_x], picks, total, subset=(j, 1), after=after, low=True
-        )
+        table, part, low = wave(waves, arrays, picks, total, subset=(j, 1), after=after, low=True)
         tables.append(table)
         own_factors.append(part)
         other_factors.append(swap(low, "atoms", 2))
     for place, spot in enumerate(spots):
         first = len(tables) - blocks
-        where[1, *spot] = tuple((first + j, half, place) for half in range(2) for j in range(blocks))
+        where[spot] = tuple((first + j, half, place) for half in range(2) for j in range(blocks))
 
     arrays = [message, message_x, near_own, near_x, halo]
     picks = [(0, None)] + [(2, n_kvec - 1 - k) for k in range(1, n_kvec)]

time: 64.7 us -> 66.1 us (1.022)
  waiting for transfers between devices: 14.5 us -> 15.9 us
    ppermute x23, waiting for transfers between devices: 14.5 us -> 15.9 us  [swap(): lax.ppermute(value, axis, [(i, i ^ bits) for i in range(lax.axis_size(axi...]
  transfers between devices with their start and end apart: 24 -> 24, of which waited for: 9 -> 11; matrix products, arithmetic and copies ran while one was open for 0% -> 0% of each run, Pallas kernels for 33% -> 33%
where the time goes in v5:
time: 66.1 us; the launch traced here: 65.9 us
  Pallas kernels  24.9 us (38%)
  starting transfers between devices  24.7 us (37%)
  waiting for transfers between devices  15.9 us (24%)
    ppermute x23, starting transfers between devices, swap(): lax.ppermute(value, axis, [(i, i ^ bits) for i in range(lax.axis_size(axi...  21.1 us
    ppermute x23, waiting for transfers between devices, swap(): lax.ppermute(value, axis, [(i, i ^ bits) for i in range(lax.axis_size(axi...  15.9 us
    pallas_call x7, Pallas kernels, wave(): pl.pallas_call(functools.partial(wave_kernel, tuple(picks), len(arrays),...  13.3 us
    pallas_call x2, Pallas kernels, pair_message(): pl.pallas_call(functools.partial(pair_kernel, nbasis, pieces, scale, pick...  6.35 us
    ppermute x1, starting transfers between devices, per_device(): lax.ppermute(collect([message, near_own], group), 'atoms', halo_pairs)  3.64 us
    pallas_call x3, Pallas kernels, inverse(): pl.pallas_call(functools.partial(inverse_kernel, pieces, shard), in_specs...  1.73 us
  transfers between devices with their start and end apart: 24, of which 11 were waited for; matrix products, arithmetic and copies ran while one was open for 0% of the time, Pallas kernels for 33%

profile of v5, /device:TPU:0, one launch (start us, length us, event | category | flops | bytes accessed | tf_op | source)
XLA Modules:
  0.0 65.9 jit_solution(4265370076362732996)
XLA Ops:
  1.6 3.5 %collective-permute-start.1 = (bf16[144,256]{1,0:T(8,128)(2,1)S(1)}, bf16[144,256]{1,0:T(8,128)(2,1)S(1)}, u32[]{:S(2)}, u32[]{:S(2)}) collective-permute-start(bf16[144,256]{1,0:T(8,128)(2,1)S(1)} %get-tuple-element.37.refs_1_.refs_0_), channel_id=1, source_target_pairs={{0,3},{1,2},{2,1},{3,0},{4,7},{5,6},{6,5},{7,4},{8,11},{9,10},{10,... | collective-permute-start | bytes 221192 | tf_op jit(solution)/shard_map/ppermute | solution.py:527
  6.2 1.5 %wave.7 = (bf16[6,256,512]{2,1,0:T(8,128)(2,1)S(1)}, f32[6,128,256]{2,1,0:T(8,128)S(1)}) custom-call(bf16[3,256,16]{2,1,0:T(8,128)(2,1)S(1)} %get-tuple-element.40.refs_0_, bf16[144,256]{1,0:T(8,128)(2,1)S(1)} %get-tuple-element.37.refs_1_.refs_0_, bf16[144,256]{1,0:T(8,128)(2,1)S(1)} %collective-permute-done.refs_2_.refs_1_), custom_call_target="tpu_custom_call" | custom-call | flops 201326592 | bytes 1572864 | tf_op jit(solution)/shard_map/wave/pallas_call | solution.py:233
  8.0 1.6 %collective-permute-done.2.refs_1_ = bf16[144,256]{1,0:T(8,128)(2,1)S(1)} collective-permute-done((bf16[144,256]{1,0:T(8,128)(2,1)S(1)}, bf16[144,256]{1,0:T(8,128)(2,1)S(1)}, u32[]{:S(2)}, u32[]{:S(2)}) %collective-permute-start.2) | collective-permute-done | bytes 73760 | tf_op jit(solution)/shard_map/ppermute | solution.py:527
  10.0 2.7 %collective-permute-start.6 = (bf16[144,256]{1,0:T(8,128)(2,1)S(1)}, bf16[144,256]{1,0:T(8,128)(2,1)S(1)}, u32[]{:S(2)}, u32[]{:S(2)}) collective-permute-start(bf16[144,256]{1,0:T(8,128)(2,1)S(1)} %get-tuple-element.37.refs_1_.refs_0_), channel_id=1, source_target_pairs={{0,16},{4,20},{8,24},{12,28},{16,0},{20,4},{24,8},{28,12},{1,17},{... | collective-permute-start | bytes 221192 | tf_op jit(solution)/shard_map/ppermute | solution.py:527
  12.7 1.5 %wave.8 = (bf16[6,256,512]{2,1,0:T(8,128)(2,1)S(1)}, f32[6,128,256]{2,1,0:T(8,128)S(1)}) custom-call(bf16[3,256,16]{2,1,0:T(8,128)(2,1)S(1)} %get-tuple-element.40.refs_0_, bf16[3,144,256]{2,1,0:T(8,128)(2,1)S(1)} %collect.4.refs_1_.refs_2_, f32[6,128,256]{2,1,0:T(8,128)S(1)} %get-tuple-element.41.refs_3_.refs_2_), custom_call_target="tpu_custom_call" | custom-call | flops 201326592 | bytes 1572864 | tf_op jit(solution)/shard_map/wave/pallas_call | solution.py:233
  14.2 3.0 %collective-permute-done.6.refs_0_ = bf16[144,256]{1,0:T(8,128)(2,1)S(1)} collective-permute-done((bf16[144,256]{1,0:T(8,128)(2,1)S(1)}, bf16[144,256]{1,0:T(8,128)(2,1)S(1)}, u32[]{:S(2)}, u32[]{:S(2)}) %collective-permute-start.6) | collective-permute-done | bytes 73760 | tf_op jit(solution)/shard_map/ppermute | solution.py:527
  17.2 1.5 %collective-permute-start.7 = (bf16[1,144,256]{2,1,0:T(8,128)(2,1)S(1)}, bf16[1,144,256]{2,1,0:T(8,128)(2,1)S(1)}, u32[]{:S(2)}, u32[]{:S(2)}) collective-permute-start(bf16[1,144,256]{2,1,0:T(8,128)(2,1)S(1)} %collect.6.refs_1_), channel_id=1, source_target_pairs={{0,3},{1,2},{2,1},{3,0},{4,7},{5,6},{6,5},{7,4},{8,11},{9,10},{10,... | collective-permute-start | bytes 221192 | tf_op jit(solution)/shard_map/ppermute | solution.py:527
  18.7 1.3 %collective-permute-start.8 = (bf16[1,144,256]{2,1,0:T(8,128)(2,1)S(1)}, bf16[1,144,256]{2,1,0:T(8,128)(2,1)S(1)}, u32[]{:S(2)}, u32[]{:S(2)}) collective-permute-start(bf16[1,144,256]{2,1,0:T(8,128)(2,1)S(1)} %collect.6.refs_1_), channel_id=1, source_target_pairs={{0,2},{1,3},{2,0},{3,1},{4,6},{5,7},{6,4},{7,5},{8,10},{9,11},{10,... | collective-permute-start | bytes 221192 | tf_op jit(solution)/shard_map/ppermute | solution.py:527
  20.7 1.5 %wave.9 = (bf16[6,256,512]{2,1,0:T(8,128)(2,1)S(1)}, f32[6,128,256]{2,1,0:T(8,128)S(1)}) custom-call(bf16[3,256,16]{2,1,0:T(8,128)(2,1)S(1)} %get-tuple-element.40.refs_0_, bf16[3,144,256]{2,1,0:T(8,128)(2,1)S(1)} %collect.4.refs_1_.refs_2_, bf16[3,144,256]{2,1,0:T(8,128)(2,1)S(1)} %collective-permute-done.4.refs_2_.refs_3_, ...), custom_call_target="tpu_custom_call" | custom-call | flops 201326592 | bytes 1572864 | tf_op jit(solution)/shard_map/wave/pallas_call | solution.py:233
  23.2 1.1 %collective-permute-done.9.refs_2_ = bf16[1,144,256]{2,1,0:T(8,128)(2,1)S(1)} collective-permute-done((bf16[1,144,256]{2,1,0:T(8,128)(2,1)S(1)}, bf16[1,144,256]{2,1,0:T(8,128)(2,1)S(1)}, u32[]{:S(2)}, u32[]{:S(2)}) %collective-permute-start.9) | collective-permute-done | bytes 73760 | tf_op jit(solution)/shard_map/ppermute | solution.py:527
  24.5 3.6 %collective-permute-start.5 = (bf16[4,144,256]{2,1,0:T(8,128)(2,1)S(1)}, bf16[4,144,256]{2,1,0:T(8,128)(2,1)S(1)}, u32[]{:S(2)}, u32[]{:S(2)}) collective-permute-start(bf16[4,144,256]{2,1,0:T(8,128)(2,1)S(1)} %collect.5), channel_id=1, source_target_pairs={{0,28},{4,8},{8,4},{12,16},{16,12},{20,24},{24,20},{28,0},{1,29},{... | collective-permute-start | bytes 884744 | tf_op jit(solution)/shard_map/ppermute | solution.py:578
  28.2 1.5 %wave.10 = (bf16[6,256,512]{2,1,0:T(8,128)(2,1)S(1)}, f32[6,128,256]{2,1,0:T(8,128)S(1)}) custom-call(bf16[3,256,16]{2,1,0:T(8,128)(2,1)S(1)} %get-tuple-element.40.refs_0_, bf16[3,144,256]{2,1,0:T(8,128)(2,1)S(1)} %collect.4.refs_1_.refs_2_, bf16[3,144,256]{2,1,0:T(8,128)(2,1)S(1)} %collective-permute-done.4.refs_2_.refs_3_, ...), custom_call_target="tpu_custom_call" | custom-call | flops 201326592 | bytes 1572864 | tf_op jit(solution)/shard_map/wave/pallas_call | solution.py:233
  29.7 2.5 %wave.11 = (bf16[2,256,2048]{2,1,0:T(8,128)(2,1)S(1)}, f32[2,128,256]{2,1,0:T(8,128)S(1)}, bf16[2,128,256]{2,1,0:T(8,128)(2,1)S(1)}) custom-call(bf16[3,256,16]{2,1,0:T(8,128)(2,1)S(1)} %get-tuple-element.40.refs_0_, bf16[1,144,256]{2,1,0:T(8,128)(2,1)S(1)} %collect.6.refs_1_, bf16[3,144,256]{2,1,0:T(8,128)(2,1)S(1)} %collect.7.refs_4_.refs_2_, ...), custom_call_target="tpu_custom_call" | custom-call | flops 268435456 | bytes 2097152 | tf_op jit(solution)/shard_map/wave/pallas_call | solution.py:233
  32.3 2.4 %wave.12 = (bf16[2,256,2048]{2,1,0:T(8,128)(2,1)S(1)}, f32[2,128,256]{2,1,0:T(8,128)S(1)}, bf16[2,128,256]{2,1,0:T(8,128)(2,1)S(1)}) custom-call(bf16[3,256,16]{2,1,0:T(8,128)(2,1)S(1)} %get-tuple-element.40.refs_0_, bf16[1,144,256]{2,1,0:T(8,128)(2,1)S(1)} %collect.6.refs_1_, bf16[3,144,256]{2,1,0:T(8,128)(2,1)S(1)} %collect.7.refs_4_.refs_2_, ...), custom_call_target="tpu_custom_call" | custom-call | flops 268435456 | bytes 2097152 | tf_op jit(solution)/shard_map/wave/pallas_call | solution.py:233
  34.6 2.4 %wave.13 = (bf16[2,256,2048]{2,1,0:T(8,128)(2,1)S(1)}, f32[2,128,256]{2,1,0:T(8,128)S(1)}, bf16[2,128,256]{2,1,0:T(8,128)(2,1)S(1)}) custom-call(bf16[3,256,16]{2,1,0:T(8,128)(2,1)S(1)} %get-tuple-element.40.refs_0_, bf16[1,144,256]{2,1,0:T(8,128)(2,1)S(1)} %collect.6.refs_1_, bf16[3,144,256]{2,1,0:T(8,128)(2,1)S(1)} %collect.7.refs_4_.refs_2_, ...), custom_call_target="tpu_custom_call" | custom-call | flops 268435456 | bytes 2097152 | tf_op jit(solution)/shard_map/wave/pallas_call | solution.py:233
  37.1 2.0 %collective-permute-start.13 = (bf16[2,128,256]{2,1,0:T(8,128)(2,1)S(1)}, bf16[2,128,256]{2,1,0:T(8,128)(2,1)S(1)}, u32[]{:S(2)}, u32[]{:S(2)}) collective-permute-start(bf16[2,128,256]{2,1,0:T(8,128)(2,1)S(1)} %get-tuple-element.46.refs_6_), channel_id=1, source_target_pairs={{0,8},{4,12},{8,0},{12,4},{16,24},{20,28},{24,16},{28,20},{1,9},{5... | collective-permute-start | bytes 393224 | tf_op jit(solution)/shard_map/ppermute | solution.py:527
  39.2 3.2 %pair.2.refs_7_.refs_4_ = f32[128,128]{1,0:T(8,128)S(1)} custom-call(s32[2,12]{1,0:T(2,128)S(1)} %copy-done.6, f32[3,256]{1,0:T(4,128)S(1)} %copy-done.3, bf16[144,256]{1,0:T(8,128)(2,1)S(1)} %get-tuple-element.37.refs_1_.refs_0_, bf16[144,256]{1,0:T(8,128)(2,1)S(1)} %collective-permute-done.refs_2_.refs_1_, ...), custom_call_target="tpu_custom_call" | custom-call | flops 418381824 | bytes 786432 | tf_op jit(solution)/shard_map/pair/pallas_call | solution.py:474
  43.4 2.8 %collective-permute-done.13.refs_4_ = bf16[2,128,256]{2,1,0:T(8,128)(2,1)S(1)} collective-permute-done((bf16[2,128,256]{2,1,0:T(8,128)(2,1)S(1)}, bf16[2,128,256]{2,1,0:T(8,128)(2,1)S(1)}, u32[]{:S(2)}, u32[]{:S(2)}) %collective-permute-start.13) | collective-permute-done | bytes 131104 | tf_op jit(solution)/shard_map/ppermute | solution.py:527
  46.2 2.3 %collective-permute-done.12.refs_3_ = bf16[2,128,256]{2,1,0:T(8,128)(2,1)S(1)} collective-permute-done((bf16[2,128,256]{2,1,0:T(8,128)(2,1)S(1)}, bf16[2,128,256]{2,1,0:T(8,128)(2,1)S(1)}, u32[]{:S(2)}, u32[]{:S(2)}) %collective-permute-start.12) | collective-permute-done | bytes 131104 | tf_op jit(solution)/shard_map/ppermute | solution.py:527
  51.1 1.7 %collective-permute-start.20 = (bf16[128,256]{1,0:T(8,128)(2,1)S(1)}, bf16[128,256]{1,0:T(8,128)(2,1)S(1)}, u32[]{:S(2)}, u32[]{:S(2)}) collective-permute-start(bf16[128,256]{1,0:T(8,128)(2,1)S(1)} %get-tuple-element.66), channel_id=1, source_target_pairs={{0,3},{1,2},{2,1},{3,0},{4,7},{5,6},{6,5},{7,4},{8,11},{9,10},{10,... | collective-permute-start | bytes 196616 | tf_op jit(solution)/shard_map/ppermute | solution.py:527
  55.4 1.7 %collective-permute-start.16 = (bf16[128,256]{1,0:T(8,128)(2,1)S(1)}, bf16[128,256]{1,0:T(8,128)(2,1)S(1)}, u32[]{:S(2)}, u32[]{:S(2)}) collective-permute-start(bf16[128,256]{1,0:T(8,128)(2,1)S(1)} %get-tuple-element.61), channel_id=1, source_target_pairs={{0,3},{1,2},{2,1},{3,0},{4,7},{5,6},{6,5},{7,4},{8,11},{9,10},{10,... | collective-permute-start | bytes 196616 | tf_op jit(solution)/shard_map/ppermute | solution.py:527
  59.1 3.2 %pair.3.refs_5_ = f32[128,128]{1,0:T(8,128)S(1)} custom-call(s32[2,12]{1,0:T(2,128)S(1)} %copy-done.6, f32[3,256]{1,0:T(4,128)S(1)} %copy-done.3, bf16[144,256]{1,0:T(8,128)(2,1)S(1)} %get-tuple-element.37.refs_1_.refs_0_, bf16[144,256]{1,0:T(8,128)(2,1)S(1)} %collective-permute-done.refs_2_.refs_1_, bf16[3,144,256]{2,1,0:T(8,128)(2,1)S(1)} %collect.4.refs_1_.refs_2_, ...), custom_call_target="tpu_custom_call" | custom-call | flops 418381824 | bytes 786432 | tf_op jit(solution)/shard_map/pair/pallas_call | solution.py:474
  62.3 2.3 %collective-permute-done.23.refs_10_ = bf16[128,256]{1,0:T(8,128)(2,1)S(1)} collective-permute-done((bf16[128,256]{1,0:T(8,128)(2,1)S(1)}, bf16[128,256]{1,0:T(8,128)(2,1)S(1)}, u32[]{:S(2)}, u32[]{:S(2)}) %collective-permute-start.23) | collective-permute-done | bytes 65568 | tf_op jit(solution)/shard_map/ppermute | solution.py:527
  64.6 1.3 %update.1 = bf16[256,128]{1,0:T(8,128)(2,1)} custom-call(bf16[256,128]{1,0:T(8,128)(2,1)S(1)} %copy-done, f32[1,128]{1,0:T(1,128)S(1)} %bitcast.2, bf16[128,512]{1,0:T(8,128)(2,1)S(1)} %copy-done.1, bf16[512,128]{1,0:T(8,128)(2,1)S(1)} %copy-done.2, f32[128,128]{1,0:T(8,128)S(1)} %pair.2.refs_7_.refs_4_, f32[128,128]{1,0:T(8,128)S(1)} %pair.3.refs_5_, ...), custom_call_target="tpu_custom_call" | custom-call | tf_op jit(solution)/shard_map/update/pallas_call | solution.py:516
  (61 shorter events, 13.6 us)
Async XLA Ops:
  1.0 5.2 %collective-permute-start = (bf16[144,256]{1,0:T(8,128)(2,1)S(1)}, bf16[144,256]{1,0:T(8,128)(2,1)S(1)}, u32[]{:S(2)}, u32[]{:S(2)}) collective-permute-start(bf16[144,256]{1,0:T(8,128)(2,1)S(1)} %get-tuple-element.37.refs_1_.refs_0_), channel_id=1, source_target_pairs={{0,4},{4,0},{8,12},{12,8},{16,20},{20,16},{24,28},{28,24},{1,5},{5... | collective-permute-start | bytes 221192 | tf_op jit(solution)/shard_map/ppermute | solution.py:527
  1.6 6.4 %collective-permute-start.1 = (bf16[144,256]{1,0:T(8,128)(2,1)S(1)}, bf16[144,256]{1,0:T(8,128)(2,1)S(1)}, u32[]{:S(2)}, u32[]{:S(2)}) collective-permute-start(bf16[144,256]{1,0:T(8,128)(2,1)S(1)} %get-tuple-element.37.refs_1_.refs_0_), channel_id=1, source_target_pairs={{0,3},{1,2},{2,1},{3,0},{4,7},{5,6},{6,5},{7,4},{8,11},{9,10},{10,... | collective-permute-start | bytes 221192 | tf_op jit(solution)/shard_map/ppermute | solution.py:527
  5.1 4.4 %collective-permute-start.2 = (bf16[144,256]{1,0:T(8,128)(2,1)S(1)}, bf16[144,256]{1,0:T(8,128)(2,1)S(1)}, u32[]{:S(2)}, u32[]{:S(2)}) collective-permute-start(bf16[144,256]{1,0:T(8,128)(2,1)S(1)} %get-tuple-element.37.refs_1_.refs_0_), channel_id=1, source_target_pairs={{0,2},{1,3},{2,0},{3,1},{4,6},{5,7},{6,4},{7,5},{8,10},{9,11},{10,... | collective-permute-start | bytes 221192 | tf_op jit(solution)/shard_map/ppermute | solution.py:527
  5.6 4.4 %collective-permute-start.3 = (bf16[144,256]{1,0:T(8,128)(2,1)S(1)}, bf16[144,256]{1,0:T(8,128)(2,1)S(1)}, u32[]{:S(2)}, u32[]{:S(2)}) collective-permute-start(bf16[144,256]{1,0:T(8,128)(2,1)S(1)} %get-tuple-element.37.refs_1_.refs_0_), channel_id=1, source_target_pairs={{0,1},{1,0},{2,3},{3,2},{4,5},{5,4},{6,7},{7,6},{8,9},{9,8},{10,11... | collective-permute-start | bytes 221192 | tf_op jit(solution)/shard_map/ppermute | solution.py:527
  10.0 10.7 %collective-permute-start.4 = (bf16[3,144,256]{2,1,0:T(8,128)(2,1)S(1)}, bf16[3,144,256]{2,1,0:T(8,128)(2,1)S(1)}, u32[]{:S(2)}, u32[]{:S(2)}) collective-permute-start(bf16[3,144,256]{2,1,0:T(8,128)(2,1)S(1)} %collect.4.refs_1_.refs_2_), channel_id=1, source_target_pairs={{0,4},{4,0},{8,12},{12,8},{16,20},{20,16},{24,28},{28,24},{1,5},{5... | collective-permute-start | bytes 663560 | tf_op jit(solution)/shard_map/ppermute | solution.py:527
  10.0 7.1 %collective-permute-start.6 = (bf16[144,256]{1,0:T(8,128)(2,1)S(1)}, bf16[144,256]{1,0:T(8,128)(2,1)S(1)}, u32[]{:S(2)}, u32[]{:S(2)}) collective-permute-start(bf16[144,256]{1,0:T(8,128)(2,1)S(1)} %get-tuple-element.37.refs_1_.refs_0_), channel_id=1, source_target_pairs={{0,16},{4,20},{8,24},{12,28},{16,0},{20,4},{24,8},{28,12},{1,17},{... | collective-permute-start | bytes 221192 | tf_op jit(solution)/shard_map/ppermute | solution.py:527
  17.2 5.3 %collective-permute-start.7 = (bf16[1,144,256]{2,1,0:T(8,128)(2,1)S(1)}, bf16[1,144,256]{2,1,0:T(8,128)(2,1)S(1)}, u32[]{:S(2)}, u32[]{:S(2)}) collective-permute-start(bf16[1,144,256]{2,1,0:T(8,128)(2,1)S(1)} %collect.6.refs_1_), channel_id=1, source_target_pairs={{0,3},{1,2},{2,1},{3,0},{4,7},{5,6},{6,5},{7,4},{8,11},{9,10},{10,... | collective-permute-start | bytes 221192 | tf_op jit(solution)/shard_map/ppermute | solution.py:527
  18.7 4.6 %collective-permute-start.8 = (bf16[1,144,256]{2,1,0:T(8,128)(2,1)S(1)}, bf16[1,144,256]{2,1,0:T(8,128)(2,1)S(1)}, u32[]{:S(2)}, u32[]{:S(2)}) collective-permute-start(bf16[1,144,256]{2,1,0:T(8,128)(2,1)S(1)} %collect.6.refs_1_), channel_id=1, source_target_pairs={{0,2},{1,3},{2,0},{3,1},{4,6},{5,7},{6,4},{7,5},{8,10},{9,11},{10,... | collective-permute-start | bytes 221192 | tf_op jit(solution)/shard_map/ppermute | solution.py:527
  20.0 4.4 %collective-permute-start.9 = (bf16[1,144,256]{2,1,0:T(8,128)(2,1)S(1)}, bf16[1,144,256]{2,1,0:T(8,128)(2,1)S(1)}, u32[]{:S(2)}, u32[]{:S(2)}) collective-permute-start(bf16[1,144,256]{2,1,0:T(8,128)(2,1)S(1)} %collect.6.refs_1_), channel_id=1, source_target_pairs={{0,1},{1,0},{2,3},{3,2},{4,5},{5,4},{6,7},{7,6},{8,9},{9,8},{10,11... | collective-permute-start | bytes 221192 | tf_op jit(solution)/shard_map/ppermute | solution.py:527
  24.4 5.3 %collective-permute-start.11 = (bf16[3,144,256]{2,1,0:T(8,128)(2,1)S(1)}, bf16[3,144,256]{2,1,0:T(8,128)(2,1)S(1)}, u32[]{:S(2)}, u32[]{:S(2)}) collective-permute-start(bf16[3,144,256]{2,1,0:T(8,128)(2,1)S(1)} %collect.7.refs_4_.refs_2_), channel_id=1, source_target_pairs={{0,4},{4,0},{8,12},{12,8},{16,20},{20,16},{24,28},{28,24},{1,5},{5... | collective-permute-start | bytes 663560 | tf_op jit(solution)/shard_map/ppermute | solution.py:527
  24.5 14.7 %collective-permute-start.5 = (bf16[4,144,256]{2,1,0:T(8,128)(2,1)S(1)}, bf16[4,144,256]{2,1,0:T(8,128)(2,1)S(1)}, u32[]{:S(2)}, u32[]{:S(2)}) collective-permute-start(bf16[4,144,256]{2,1,0:T(8,128)(2,1)S(1)} %collect.5), channel_id=1, source_target_pairs={{0,28},{4,8},{8,4},{12,16},{16,12},{20,24},{24,20},{28,0},{1,29},{... | collective-permute-start | bytes 884744 | tf_op jit(solution)/shard_map/ppermute | solution.py:578
  28.2 1.5 %collective-permute-start.10 = (bf16[1,144,256]{2,1,0:T(8,128)(2,1)S(1)}, bf16[1,144,256]{2,1,0:T(8,128)(2,1)S(1)}, u32[]{:S(2)}, u32[]{:S(2)}) collective-permute-start(bf16[1,144,256]{2,1,0:T(8,128)(2,1)S(1)} %collect.6.refs_1_), channel_id=1, source_target_pairs={{0,4},{4,0},{8,12},{12,8},{16,20},{20,16},{24,28},{28,24},{1,5},{5... | collective-permute-start | bytes 221192 | tf_op jit(solution)/shard_map/ppermute | solution.py:527
  37.0 6.4 %collective-permute-start.14 = (bf16[2,128,256]{2,1,0:T(8,128)(2,1)S(1)}, bf16[2,128,256]{2,1,0:T(8,128)(2,1)S(1)}, u32[]{:S(2)}, u32[]{:S(2)}) collective-permute-start(bf16[2,128,256]{2,1,0:T(8,128)(2,1)S(1)} %get-tuple-element.47.refs_6_), channel_id=1, source_target_pairs={{0,8},{4,12},{8,0},{12,4},{16,24},{20,28},{24,16},{28,20},{1,9},{5... | collective-permute-start | bytes 393224 | tf_op jit(solution)/shard_map/ppermute | solution.py:527
  37.1 9.2 %collective-permute-start.13 = (bf16[2,128,256]{2,1,0:T(8,128)(2,1)S(1)}, bf16[2,128,256]{2,1,0:T(8,128)(2,1)S(1)}, u32[]{:S(2)}, u32[]{:S(2)}) collective-permute-start(bf16[2,128,256]{2,1,0:T(8,128)(2,1)S(1)} %get-tuple-element.46.refs_6_), channel_id=1, source_target_pairs={{0,8},{4,12},{8,0},{12,4},{16,24},{20,28},{24,16},{28,20},{1,9},{5... | collective-permute-start | bytes 393224 | tf_op jit(solution)/shard_map/ppermute | solution.py:527
  39.1 9.5 %collective-permute-start.12 = (bf16[2,128,256]{2,1,0:T(8,128)(2,1)S(1)}, bf16[2,128,256]{2,1,0:T(8,128)(2,1)S(1)}, u32[]{:S(2)}, u32[]{:S(2)}) collective-permute-start(bf16[2,128,256]{2,1,0:T(8,128)(2,1)S(1)} %get-tuple-element.45.refs_6_), channel_id=1, source_target_pairs={{0,8},{4,12},{8,0},{12,4},{16,24},{20,28},{24,16},{28,20},{1,9},{5... | collective-permute-start | bytes 393224 | tf_op jit(solution)/shard_map/ppermute | solution.py:527
  49.2 1.8 %collective-permute-start.19 = (bf16[128,1024]{1,0:T(8,128)(2,1)S(1)}, bf16[128,1024]{1,0:T(8,128)(2,1)S(1)}, u32[]{:S(2)}, u32[]{:S(2)}) collective-permute-start(bf16[128,1024]{1,0:T(8,128)(2,1)S(1)} %get-tuple-element.64), channel_id=1, source_target_pairs={{0,4},{4,0},{8,12},{12,8},{16,20},{20,16},{24,28},{28,24},{1,5},{5... | collective-permute-start | bytes 786440 | tf_op jit(solution)/shard_map/ppermute | solution.py:527
  49.9 5.4 %collective-permute-start.15 = (bf16[128,1024]{1,0:T(8,128)(2,1)S(1)}, bf16[128,1024]{1,0:T(8,128)(2,1)S(1)}, u32[]{:S(2)}, u32[]{:S(2)}) collective-permute-start(bf16[128,1024]{1,0:T(8,128)(2,1)S(1)} %inverse.4), channel_id=1, source_target_pairs={{0,4},{4,0},{8,12},{12,8},{16,20},{20,16},{24,28},{28,24},{1,5},{5... | collective-permute-start | bytes 786440 | tf_op jit(solution)/shard_map/ppermute | solution.py:527
  51.1 6.7 %collective-permute-start.20 = (bf16[128,256]{1,0:T(8,128)(2,1)S(1)}, bf16[128,256]{1,0:T(8,128)(2,1)S(1)}, u32[]{:S(2)}, u32[]{:S(2)}) collective-permute-start(bf16[128,256]{1,0:T(8,128)(2,1)S(1)} %get-tuple-element.66), channel_id=1, source_target_pairs={{0,3},{1,2},{2,1},{3,0},{4,7},{5,6},{6,5},{7,4},{8,11},{9,10},{10,... | collective-permute-start | bytes 196616 | tf_op jit(solution)/shard_map/ppermute | solution.py:527
  52.8 6.1 %collective-permute-start.21 = (bf16[128,256]{1,0:T(8,128)(2,1)S(1)}, bf16[128,256]{1,0:T(8,128)(2,1)S(1)}, u32[]{:S(2)}, u32[]{:S(2)}) collective-permute-start(bf16[128,256]{1,0:T(8,128)(2,1)S(1)} %get-tuple-element.67), channel_id=1, source_target_pairs={{0,2},{1,3},{2,0},{3,1},{4,6},{5,7},{6,4},{7,5},{8,10},{9,11},{10,... | collective-permute-start | bytes 196616 | tf_op jit(solution)/shard_map/ppermute | solution.py:527
  53.6 5.4 %collective-permute-start.22 = (bf16[128,256]{1,0:T(8,128)(2,1)S(1)}, bf16[128,256]{1,0:T(8,128)(2,1)S(1)}, u32[]{:S(2)}, u32[]{:S(2)}) collective-permute-start(bf16[128,256]{1,0:T(8,128)(2,1)S(1)} %get-tuple-element.68), channel_id=1, source_target_pairs={{0,1},{1,0},{2,3},{3,2},{4,5},{5,4},{6,7},{7,6},{8,9},{9,8},{10,11... | collective-permute-start | bytes 196616 | tf_op jit(solution)/shard_map/ppermute | solution.py:527
  55.4 6.9 %collective-permute-start.16 = (bf16[128,256]{1,0:T(8,128)(2,1)S(1)}, bf16[128,256]{1,0:T(8,128)(2,1)S(1)}, u32[]{:S(2)}, u32[]{:S(2)}) collective-permute-start(bf16[128,256]{1,0:T(8,128)(2,1)S(1)} %get-tuple-element.61), channel_id=1, source_target_pairs={{0,3},{1,2},{2,1},{3,0},{4,7},{5,6},{6,5},{7,4},{8,11},{9,10},{10,... | collective-permute-start | bytes 196616 | tf_op jit(solution)/shard_map/ppermute | solution.py:527
  57.1 5.3 %collective-permute-start.17 = (bf16[128,256]{1,0:T(8,128)(2,1)S(1)}, bf16[128,256]{1,0:T(8,128)(2,1)S(1)}, u32[]{:S(2)}, u32[]{:S(2)}) collective-permute-start(bf16[128,256]{1,0:T(8,128)(2,1)S(1)} %get-tuple-element.62), channel_id=1, source_target_pairs={{0,2},{1,3},{2,0},{3,1},{4,6},{5,7},{6,4},{7,5},{8,10},{9,11},{10,... | collective-permute-start | bytes 196616 | tf_op jit(solution)/shard_map/ppermute | solution.py:527
  57.8 4.5 %collective-permute-start.18 = (bf16[128,256]{1,0:T(8,128)(2,1)S(1)}, bf16[128,256]{1,0:T(8,128)(2,1)S(1)}, u32[]{:S(2)}, u32[]{:S(2)}) collective-permute-start(bf16[128,256]{1,0:T(8,128)(2,1)S(1)} %get-tuple-element.63), channel_id=1, source_target_pairs={{0,1},{1,0},{2,3},{3,2},{4,5},{5,4},{6,7},{7,6},{8,9},{9,8},{10,11... | collective-permute-start | bytes 196616 | tf_op jit(solution)/shard_map/ppermute | solution.py:527
  59.0 5.6 %collective-permute-start.23 = (bf16[128,256]{1,0:T(8,128)(2,1)S(1)}, bf16[128,256]{1,0:T(8,128)(2,1)S(1)}, u32[]{:S(2)}, u32[]{:S(2)}) collective-permute-start(bf16[128,256]{1,0:T(8,128)(2,1)S(1)} %add_convert_fusion), channel_id=1, source_target_pairs={{0,16},{4,20},{8,24},{12,28},{16,0},{20,4},{24,8},{28,12},{1,17},{... | collective-permute-start | bytes 196616 | tf_op jit(solution)/shard_map/ppermute | solution.py:527
  (7 other events, 58.2 us)

commit v6 on v5

--- a/solution.py
+++ b/solution.py
@@ -562,16 +562,16 @@
         for place, name in enumerate(names):
             where[name] = tuple((len(tables) - 1, j, place) for j in range(2 * blocks))
 
-    table, total = wave(waves, [message, message_x], [(0, None), (1, None)], None)
-    keep(table, [(0, 0, 0), (1, 0, 0)])
-    near_own = collect([near[k] for k in others], [(i, None) for i in range(n_kvec - 1)], after=(total,))
+    near_own = collect(
+        [near[k] for k in others], [(i, None) for i in range(n_kvec - 1)], after=(waves,)
+    )
     near_x = swap(near_own, "atoms", 1)
     names = [(0, 0, k) for k in others] + [(1, 0, k) for k in others]
     picks = [(core, i) for core in range(2) for i in range(n_kvec - 1)]
-    table, total = wave(waves, [near_own], picks[:2], total)
-    keep(table, names[:2])
+    start = [(0, None), (1, None)] + [(2, index) for _, index in picks[:2]]
+    table, total = wave(waves, [message, message_x, near_own], start, None)
+    keep(table, [(0, 0, 0), (1, 0, 0)] + names[:2])
     distant = collect(distant, [(z, None) for z in range(far - 1)], after=(total,))
-    distant_x = swap(distant, "atoms", 1)
     relayed = {k: swap(distant, "kvec", k) for k in others}
     halo_pairs = [(a, (a + 1) % n_atoms if a % 2 else (a - 1) % n_atoms) for a in range(n_atoms)]
     group = [(0, None)] + [(1, n_kvec - 1 - k) for k in range(1, n_kvec)]
@@ -579,16 +579,13 @@
     middle = 2 + (len(picks) - 2) // 4 * 2
     table, total = wave(waves, [near_own, near_x], picks[2:middle], total)
     keep(table, names[2:middle])
-    every = [(i, z) for i in range(n_kvec - 1) for z in range(far - 1)]
-    far_own = collect([relayed[k] for k in others], every, after=(total,))
+    every = [(i, z) for i in range(n_kvec) for z in range(far - 1)]
+    far_own = collect([distant, *[relayed[k] for k in others]], every, after=(total,))
     far_x = swap(far_own, "atoms", 1)
     table, total = wave(waves, [near_own, near_x], picks[middle:], total, after=(far_own,))
     keep(table, names[middle:])
-    arrays = [distant, far_own, distant_x, far_x]
-    picks = []
-    for core in range(2):
-        picks += [(2 * core, z) for z in range(far - 1)]
-        picks += [(2 * core + 1, i) for i in range(len(every))]
+    arrays = [far_own, far_x]
+    picks = [(core, i) for core in range(2) for i in range(len(every))]
     spots = [(core, z, k) for core in range(2) for k in (0, *others) for z in zs]
     own_factors, other_factors, low = [], [], None
     for j in range(blocks):

time: 66.1 us -> 62.4 us (0.944)
  waiting for transfers between devices: 15.9 us -> 10.4 us
  starting transfers between devices: 24.7 us -> 26.8 us
    ppermute x23 -> x22, waiting for transfers between devices: 15.9 us -> 10.4 us  [swap(): lax.ppermute(value, axis, [(i, i ^ bits) for i in range(lax.axis_size(axi...]
    ppermute x23 -> x22, starting transfers between devices: 21.1 us -> 23 us  [swap(): lax.ppermute(value, axis, [(i, i ^ bits) for i in range(lax.axis_size(axi...]
    pallas_call x7 -> x6, Pallas kernels: 13.3 us -> 13.1 us  [wave(): pl.pallas_call(functools.partial(wave_kernel, tuple(picks), len(arrays),...]
  transfers between devices with their start and end apart: 24 -> 23, of which waited for: 11 -> 11; matrix products, arithmetic and copies ran while one was open for 0% -> 0% of each run, Pallas kernels for 33% -> 35%
where the time goes in v6:
time: 62.4 us; the launch traced here: 62.3 us
  starting transfers between devices  26.8 us (43%)
  Pallas kernels  24.7 us (40%)
  waiting for transfers between devices  10.4 us (17%)
    ppermute x22, starting transfers between devices, swap(): lax.ppermute(value, axis, [(i, i ^ bits) for i in range(lax.axis_size(axi...  23 us
    pallas_call x6, Pallas kernels, wave(): pl.pallas_call(functools.partial(wave_kernel, tuple(picks), len(arrays),...  13.1 us
    ppermute x22, waiting for transfers between devices, swap(): lax.ppermute(value, axis, [(i, i ^ bits) for i in range(lax.axis_size(axi...  10.4 us
    pallas_call x2, Pallas kernels, pair_message(): pl.pallas_call(functools.partial(pair_kernel, nbasis, pieces, scale, pick...  6.36 us
    ppermute x1, starting transfers between devices, per_device(): lax.ppermute(collect([message, near_own], group), 'atoms', halo_pairs)  3.72 us
    pallas_call x3, Pallas kernels, inverse(): pl.pallas_call(functools.partial(inverse_kernel, pieces, shard), in_specs...  1.74 us
    pallas_call x1, Pallas kernels, update(): pl.pallas_call(functools.partial(update_kernel, len(pairs)), in_specs=[VM...  1.26 us
  transfers between devices with their start and end apart: 23, of which 11 were waited for; matrix products, arithmetic and copies ran while one was open for 0% of the time, Pallas kernels for 35%

profile of v6, /device:TPU:0, one launch (start us, length us, event | category | flops | bytes accessed | tf_op | source)
XLA Modules:
  0.0 62.3 jit_solution(17298314756407266511)
XLA Ops:
  0.0 1.0 %pack.1 = (bf16[144,256]{1,0:T(8,128)(2,1)S(1)}, s32[3,3072]{1,0:T(4,128)S(1)}, f32[8,128]{1,0:T(8,128)S(1)}) custom-call(bf16[256,128]{1,0:T(8,128)(2,1)} %refs_0_.3, s32[1,256]{1,0:T(1,128)} %bitcast.3, f32[3,256]{1,0:T(4,128)} %own_pos_ref.3, s32[3,3072]{1,0:T(4,128)} %refs_3_.2, f32[8,128]{1,0:T(8,128)} %refs_4_.1), custom_call_target="tpu_custom_call" | custom-call | tf_op jit(solution)/shard_map/pack/pallas_call | solution.py:73
  1.0 4.0 %collective-permute-start.1 = (bf16[144,256]{1,0:T(8,128)(2,1)S(1)}, bf16[144,256]{1,0:T(8,128)(2,1)S(1)}, u32[]{:S(2)}, u32[]{:S(2)}) collective-permute-start(bf16[144,256]{1,0:T(8,128)(2,1)S(1)} %get-tuple-element.35.refs_0_.refs_1_), channel_id=1, source_target_pairs={{0,3},{1,2},{2,1},{3,0},{4,7},{5,6},{6,5},{7,4},{8,11},{9,10},{10,... | collective-permute-start | bytes 221192 | tf_op jit(solution)/shard_map/ppermute | solution.py:527
  6.1 1.2 %collective-permute-done.1.refs_0_ = bf16[144,256]{1,0:T(8,128)(2,1)S(1)} collective-permute-done((bf16[144,256]{1,0:T(8,128)(2,1)S(1)}, bf16[144,256]{1,0:T(8,128)(2,1)S(1)}, u32[]{:S(2)}, u32[]{:S(2)}) %collective-permute-start.1) | collective-permute-done | bytes 73760 | tf_op jit(solution)/shard_map/ppermute | solution.py:527
  7.4 2.0 %collective-permute-done.2.refs_1_ = bf16[144,256]{1,0:T(8,128)(2,1)S(1)} collective-permute-done((bf16[144,256]{1,0:T(8,128)(2,1)S(1)}, bf16[144,256]{1,0:T(8,128)(2,1)S(1)}, u32[]{:S(2)}, u32[]{:S(2)}) %collective-permute-start.2) | collective-permute-done | bytes 73760 | tf_op jit(solution)/shard_map/ppermute | solution.py:527
  10.5 2.6 %collective-permute-start.6 = (bf16[144,256]{1,0:T(8,128)(2,1)S(1)}, bf16[144,256]{1,0:T(8,128)(2,1)S(1)}, u32[]{:S(2)}, u32[]{:S(2)}) collective-permute-start(bf16[144,256]{1,0:T(8,128)(2,1)S(1)} %get-tuple-element.35.refs_0_.refs_1_), channel_id=1, source_target_pairs={{0,16},{4,20},{8,24},{12,28},{16,0},{20,4},{24,8},{28,12},{1,17},{... | collective-permute-start | bytes 221192 | tf_op jit(solution)/shard_map/ppermute | solution.py:527
  13.1 3.0 %wave.6 = (bf16[6,256,1024]{2,1,0:T(8,128)(2,1)S(1)}, f32[6,128,256]{2,1,0:T(8,128)S(1)}) custom-call(bf16[3,256,16]{2,1,0:T(8,128)(2,1)S(1)} %get-tuple-element.38.refs_3_.refs_0_, bf16[144,256]{1,0:T(8,128)(2,1)S(1)} %get-tuple-element.35.refs_0_.refs_1_, bf16[144,256]{1,0:T(8,128)(2,1)S(1)} %collective-permute-done.refs_2_.refs_1_, ...), custom_call_target="tpu_custom_call" | custom-call | flops 402653184 | bytes 3145728 | tf_op jit(solution)/shard_map/wave/pallas_call | solution.py:233
  16.1 1.2 %collective-permute-done.6.refs_0_ = bf16[144,256]{1,0:T(8,128)(2,1)S(1)} collective-permute-done((bf16[144,256]{1,0:T(8,128)(2,1)S(1)}, bf16[144,256]{1,0:T(8,128)(2,1)S(1)}, u32[]{:S(2)}, u32[]{:S(2)}) %collective-permute-start.6) | collective-permute-done | bytes 73760 | tf_op jit(solution)/shard_map/ppermute | solution.py:527
  17.3 1.5 %collective-permute-start.7 = (bf16[1,144,256]{2,1,0:T(8,128)(2,1)S(1)}, bf16[1,144,256]{2,1,0:T(8,128)(2,1)S(1)}, u32[]{:S(2)}, u32[]{:S(2)}) collective-permute-start(bf16[1,144,256]{2,1,0:T(8,128)(2,1)S(1)} %collect.6.refs_0_), channel_id=1, source_target_pairs={{0,3},{1,2},{2,1},{3,0},{4,7},{5,6},{6,5},{7,4},{8,11},{9,10},{10,... | collective-permute-start | bytes 221192 | tf_op jit(solution)/shard_map/ppermute | solution.py:527
  19.5 1.3 %collective-permute-start.9 = (bf16[1,144,256]{2,1,0:T(8,128)(2,1)S(1)}, bf16[1,144,256]{2,1,0:T(8,128)(2,1)S(1)}, u32[]{:S(2)}, u32[]{:S(2)}) collective-permute-start(bf16[1,144,256]{2,1,0:T(8,128)(2,1)S(1)} %collect.6.refs_0_), channel_id=1, source_target_pairs={{0,1},{1,0},{2,3},{3,2},{4,5},{5,4},{6,7},{7,6},{8,9},{9,8},{10,11... | collective-permute-start | bytes 221192 | tf_op jit(solution)/shard_map/ppermute | solution.py:527
  20.8 1.5 %wave.7 = (bf16[6,256,512]{2,1,0:T(8,128)(2,1)S(1)}, f32[6,128,256]{2,1,0:T(8,128)S(1)}) custom-call(bf16[3,256,16]{2,1,0:T(8,128)(2,1)S(1)} %get-tuple-element.38.refs_3_.refs_0_, bf16[3,144,256]{2,1,0:T(8,128)(2,1)S(1)} %collect.4.refs_1_.refs_3_.refs_2_, bf16[3,144,256]{2,1,0:T(8,128)(2,1)S(1)} %collective-permute-done.4.refs_2_.refs_3_, ...), custom_call_target="tpu_custom_call" | custom-call | flops 201326592 | bytes 1572864 | tf_op jit(solution)/shard_map/wave/pallas_call | solution.py:233
  24.0 3.7 %collective-permute-start.5 = (bf16[4,144,256]{2,1,0:T(8,128)(2,1)S(1)}, bf16[4,144,256]{2,1,0:T(8,128)(2,1)S(1)}, u32[]{:S(2)}, u32[]{:S(2)}) collective-permute-start(bf16[4,144,256]{2,1,0:T(8,128)(2,1)S(1)} %collect.5), channel_id=1, source_target_pairs={{0,28},{4,8},{8,4},{12,16},{16,12},{20,24},{24,20},{28,0},{1,29},{... | collective-permute-start | bytes 884744 | tf_op jit(solution)/shard_map/ppermute | solution.py:578
  27.7 1.5 %wave.8 = (bf16[6,256,512]{2,1,0:T(8,128)(2,1)S(1)}, f32[6,128,256]{2,1,0:T(8,128)S(1)}) custom-call(bf16[3,256,16]{2,1,0:T(8,128)(2,1)S(1)} %get-tuple-element.38.refs_3_.refs_0_, bf16[3,144,256]{2,1,0:T(8,128)(2,1)S(1)} %collect.4.refs_1_.refs_3_.refs_2_, bf16[3,144,256]{2,1,0:T(8,128)(2,1)S(1)} %collective-permute-done.4.refs_2_.refs_3_, ...), custom_call_target="tpu_custom_call" | custom-call | flops 201326592 | bytes 1572864 | tf_op jit(solution)/shard_map/wave/pallas_call | solution.py:233
  29.2 2.4 %wave.9 = (bf16[2,256,2048]{2,1,0:T(8,128)(2,1)S(1)}, f32[2,128,256]{2,1,0:T(8,128)S(1)}, bf16[2,128,256]{2,1,0:T(8,128)(2,1)S(1)}) custom-call(bf16[3,256,16]{2,1,0:T(8,128)(2,1)S(1)} %get-tuple-element.38.refs_3_.refs_0_, bf16[4,144,256]{2,1,0:T(8,128)(2,1)S(1)} %collect.7.refs_4_.refs_1_, bf16[4,144,256]{2,1,0:T(8,128)(2,1)S(1)} %collective-permute-done.10.refs_2_, ...), custom_call_target="tpu_custom_call" | custom-call | flops 268435456 | bytes 2097152 | tf_op jit(solution)/shard_map/wave/pallas_call | solution.py:233
  31.6 2.4 %wave.10 = (bf16[2,256,2048]{2,1,0:T(8,128)(2,1)S(1)}, f32[2,128,256]{2,1,0:T(8,128)S(1)}, bf16[2,128,256]{2,1,0:T(8,128)(2,1)S(1)}) custom-call(bf16[3,256,16]{2,1,0:T(8,128)(2,1)S(1)} %get-tuple-element.38.refs_3_.refs_0_, bf16[4,144,256]{2,1,0:T(8,128)(2,1)S(1)} %collect.7.refs_4_.refs_1_, bf16[4,144,256]{2,1,0:T(8,128)(2,1)S(1)} %collective-permute-done.10.refs_2_, ...), custom_call_target="tpu_custom_call" | custom-call | flops 268435456 | bytes 2097152 | tf_op jit(solution)/shard_map/wave/pallas_call | solution.py:233
  34.0 2.4 %wave.11 = (bf16[2,256,2048]{2,1,0:T(8,128)(2,1)S(1)}, f32[2,128,256]{2,1,0:T(8,128)S(1)}, bf16[2,128,256]{2,1,0:T(8,128)(2,1)S(1)}) custom-call(bf16[3,256,16]{2,1,0:T(8,128)(2,1)S(1)} %get-tuple-element.38.refs_3_.refs_0_, bf16[4,144,256]{2,1,0:T(8,128)(2,1)S(1)} %collect.7.refs_4_.refs_1_, bf16[4,144,256]{2,1,0:T(8,128)(2,1)S(1)} %collective-permute-done.10.refs_2_, ...), custom_call_target="tpu_custom_call" | custom-call | flops 268435456 | bytes 2097152 | tf_op jit(solution)/shard_map/wave/pallas_call | solution.py:233
  36.4 2.0 %collective-permute-start.12 = (bf16[2,128,256]{2,1,0:T(8,128)(2,1)S(1)}, bf16[2,128,256]{2,1,0:T(8,128)(2,1)S(1)}, u32[]{:S(2)}, u32[]{:S(2)}) collective-permute-start(bf16[2,128,256]{2,1,0:T(8,128)(2,1)S(1)} %get-tuple-element.43.refs_4_), channel_id=1, source_target_pairs={{0,8},{4,12},{8,0},{12,4},{16,24},{20,28},{24,16},{28,20},{1,9},{5... | collective-permute-start | bytes 393224 | tf_op jit(solution)/shard_map/ppermute | solution.py:527
  38.5 3.2 %pair.2.refs_7_.refs_4_ = f32[128,128]{1,0:T(8,128)S(1)} custom-call(s32[2,12]{1,0:T(2,128)S(1)} %copy-done.6, f32[3,256]{1,0:T(4,128)S(1)} %copy-done.3, bf16[144,256]{1,0:T(8,128)(2,1)S(1)} %get-tuple-element.35.refs_0_.refs_1_, bf16[144,256]{1,0:T(8,128)(2,1)S(1)} %collective-permute-done.refs_2_.refs_1_, ...), custom_call_target="tpu_custom_call" | custom-call | flops 418381824 | bytes 786432 | tf_op jit(solution)/shard_map/pair/pallas_call | solution.py:474
  41.8 1.4 %collective-permute-done.12.refs_4_ = bf16[2,128,256]{2,1,0:T(8,128)(2,1)S(1)} collective-permute-done((bf16[2,128,256]{2,1,0:T(8,128)(2,1)S(1)}, bf16[2,128,256]{2,1,0:T(8,128)(2,1)S(1)}, u32[]{:S(2)}, u32[]{:S(2)}) %collective-permute-start.12) | collective-permute-done | bytes 131104 | tf_op jit(solution)/shard_map/ppermute | solution.py:527
  43.2 1.4 %collective-permute-done.11.refs_3_ = bf16[2,128,256]{2,1,0:T(8,128)(2,1)S(1)} collective-permute-done((bf16[2,128,256]{2,1,0:T(8,128)(2,1)S(1)}, bf16[2,128,256]{2,1,0:T(8,128)(2,1)S(1)}, u32[]{:S(2)}, u32[]{:S(2)}) %collective-permute-start.11) | collective-permute-done | bytes 131104 | tf_op jit(solution)/shard_map/ppermute | solution.py:527
  47.2 2.2 %collective-permute-start.19 = (bf16[128,256]{1,0:T(8,128)(2,1)S(1)}, bf16[128,256]{1,0:T(8,128)(2,1)S(1)}, u32[]{:S(2)}, u32[]{:S(2)}) collective-permute-start(bf16[128,256]{1,0:T(8,128)(2,1)S(1)} %get-tuple-element.62), channel_id=1, source_target_pairs={{0,3},{1,2},{2,1},{3,0},{4,7},{5,6},{6,5},{7,4},{8,11},{9,10},{10,... | collective-permute-start | bytes 196616 | tf_op jit(solution)/shard_map/ppermute | solution.py:527
  51.4 2.2 %collective-permute-start.15 = (bf16[128,256]{1,0:T(8,128)(2,1)S(1)}, bf16[128,256]{1,0:T(8,128)(2,1)S(1)}, u32[]{:S(2)}, u32[]{:S(2)}) collective-permute-start(bf16[128,256]{1,0:T(8,128)(2,1)S(1)} %get-tuple-element.57), channel_id=1, source_target_pairs={{0,3},{1,2},{2,1},{3,0},{4,7},{5,6},{6,5},{7,4},{8,11},{9,10},{10,... | collective-permute-start | bytes 196616 | tf_op jit(solution)/shard_map/ppermute | solution.py:527
  55.1 1.8 %collective-permute-start.22 = (bf16[128,256]{1,0:T(8,128)(2,1)S(1)}, bf16[128,256]{1,0:T(8,128)(2,1)S(1)}, u32[]{:S(2)}, u32[]{:S(2)}) collective-permute-start(bf16[128,256]{1,0:T(8,128)(2,1)S(1)} %add_convert_fusion), channel_id=1, source_target_pairs={{0,16},{4,20},{8,24},{12,28},{16,0},{20,4},{24,8},{28,12},{1,17},{... | collective-permute-start | bytes 196616 | tf_op jit(solution)/shard_map/ppermute | solution.py:527
  56.8 3.2 %pair.3.refs_5_ = f32[128,128]{1,0:T(8,128)S(1)} custom-call(s32[2,12]{1,0:T(2,128)S(1)} %copy-done.6, f32[3,256]{1,0:T(4,128)S(1)} %copy-done.3, bf16[144,256]{1,0:T(8,128)(2,1)S(1)} %get-tuple-element.35.refs_0_.refs_1_, bf16[144,256]{1,0:T(8,128)(2,1)S(1)} %collective-permute-done.refs_2_.refs_1_, ...), custom_call_target="tpu_custom_call" | custom-call | flops 418381824 | bytes 786432 | tf_op jit(solution)/shard_map/pair/pallas_call | solution.py:474
  61.0 1.3 %update.1 = bf16[256,128]{1,0:T(8,128)(2,1)} custom-call(bf16[256,128]{1,0:T(8,128)(2,1)S(1)} %copy-done, f32[1,128]{1,0:T(1,128)S(1)} %bitcast.2, bf16[128,512]{1,0:T(8,128)(2,1)S(1)} %copy-done.1, bf16[512,128]{1,0:T(8,128)(2,1)S(1)} %copy-done.2, f32[128,128]{1,0:T(8,128)S(1)} %pair.2.refs_7_.refs_4_, f32[128,128]{1,0:T(8,128)S(1)} %pair.3.refs_5_, ...), custom_call_target="tpu_custom_call" | custom-call | tf_op jit(solution)/shard_map/update/pallas_call | solution.py:516
  (58 shorter events, 11.8 us)
Async XLA Ops:
  1.0 6.3 %collective-permute-start.1 = (bf16[144,256]{1,0:T(8,128)(2,1)S(1)}, bf16[144,256]{1,0:T(8,128)(2,1)S(1)}, u32[]{:S(2)}, u32[]{:S(2)}) collective-permute-start(bf16[144,256]{1,0:T(8,128)(2,1)S(1)} %get-tuple-element.35.refs_0_.refs_1_), channel_id=1, source_target_pairs={{0,3},{1,2},{2,1},{3,0},{4,7},{5,6},{6,5},{7,4},{8,11},{9,10},{10,... | collective-permute-start | bytes 221192 | tf_op jit(solution)/shard_map/ppermute | solution.py:527
  5.0 4.4 %collective-permute-start.2 = (bf16[144,256]{1,0:T(8,128)(2,1)S(1)}, bf16[144,256]{1,0:T(8,128)(2,1)S(1)}, u32[]{:S(2)}, u32[]{:S(2)}) collective-permute-start(bf16[144,256]{1,0:T(8,128)(2,1)S(1)} %get-tuple-element.35.refs_0_.refs_1_), channel_id=1, source_target_pairs={{0,2},{1,3},{2,0},{3,1},{4,6},{5,7},{6,4},{7,5},{8,10},{9,11},{10,... | collective-permute-start | bytes 221192 | tf_op jit(solution)/shard_map/ppermute | solution.py:527
  5.5 4.4 %collective-permute-start.3 = (bf16[144,256]{1,0:T(8,128)(2,1)S(1)}, bf16[144,256]{1,0:T(8,128)(2,1)S(1)}, u32[]{:S(2)}, u32[]{:S(2)}) collective-permute-start(bf16[144,256]{1,0:T(8,128)(2,1)S(1)} %get-tuple-element.35.refs_0_.refs_1_), channel_id=1, source_target_pairs={{0,1},{1,0},{2,3},{3,2},{4,5},{5,4},{6,7},{7,6},{8,9},{9,8},{10,11... | collective-permute-start | bytes 221192 | tf_op jit(solution)/shard_map/ppermute | solution.py:527
  9.9 10.9 %collective-permute-start.4 = (bf16[3,144,256]{2,1,0:T(8,128)(2,1)S(1)}, bf16[3,144,256]{2,1,0:T(8,128)(2,1)S(1)}, u32[]{:S(2)}, u32[]{:S(2)}) collective-permute-start(bf16[3,144,256]{2,1,0:T(8,128)(2,1)S(1)} %collect.4.refs_1_.refs_3_.refs_2_), channel_id=1, source_target_pairs={{0,4},{4,0},{8,12},{12,8},{16,20},{20,16},{24,28},{28,24},{1,5},{5... | collective-permute-start | bytes 663560 | tf_op jit(solution)/shard_map/ppermute | solution.py:527
  10.0 3.1 %collective-permute-start = (bf16[144,256]{1,0:T(8,128)(2,1)S(1)}, bf16[144,256]{1,0:T(8,128)(2,1)S(1)}, u32[]{:S(2)}, u32[]{:S(2)}) collective-permute-start(bf16[144,256]{1,0:T(8,128)(2,1)S(1)} %get-tuple-element.35.refs_0_.refs_1_), channel_id=1, source_target_pairs={{0,4},{4,0},{8,12},{12,8},{16,20},{20,16},{24,28},{28,24},{1,5},{5... | collective-permute-start | bytes 221192 | tf_op jit(solution)/shard_map/ppermute | solution.py:527
  10.5 6.8 %collective-permute-start.6 = (bf16[144,256]{1,0:T(8,128)(2,1)S(1)}, bf16[144,256]{1,0:T(8,128)(2,1)S(1)}, u32[]{:S(2)}, u32[]{:S(2)}) collective-permute-start(bf16[144,256]{1,0:T(8,128)(2,1)S(1)} %get-tuple-element.35.refs_0_.refs_1_), channel_id=1, source_target_pairs={{0,16},{4,20},{8,24},{12,28},{16,0},{20,4},{24,8},{28,12},{1,17},{... | collective-permute-start | bytes 221192 | tf_op jit(solution)/shard_map/ppermute | solution.py:527
  17.3 5.3 %collective-permute-start.7 = (bf16[1,144,256]{2,1,0:T(8,128)(2,1)S(1)}, bf16[1,144,256]{2,1,0:T(8,128)(2,1)S(1)}, u32[]{:S(2)}, u32[]{:S(2)}) collective-permute-start(bf16[1,144,256]{2,1,0:T(8,128)(2,1)S(1)} %collect.6.refs_0_), channel_id=1, source_target_pairs={{0,3},{1,2},{2,1},{3,0},{4,7},{5,6},{6,5},{7,4},{8,11},{9,10},{10,... | collective-permute-start | bytes 221192 | tf_op jit(solution)/shard_map/ppermute | solution.py:527
  18.8 4.6 %collective-permute-start.8 = (bf16[1,144,256]{2,1,0:T(8,128)(2,1)S(1)}, bf16[1,144,256]{2,1,0:T(8,128)(2,1)S(1)}, u32[]{:S(2)}, u32[]{:S(2)}) collective-permute-start(bf16[1,144,256]{2,1,0:T(8,128)(2,1)S(1)} %collect.6.refs_0_), channel_id=1, source_target_pairs={{0,2},{1,3},{2,0},{3,1},{4,6},{5,7},{6,4},{7,5},{8,10},{9,11},{10,... | collective-permute-start | bytes 221192 | tf_op jit(solution)/shard_map/ppermute | solution.py:527
  19.5 4.4 %collective-permute-start.9 = (bf16[1,144,256]{2,1,0:T(8,128)(2,1)S(1)}, bf16[1,144,256]{2,1,0:T(8,128)(2,1)S(1)}, u32[]{:S(2)}, u32[]{:S(2)}) collective-permute-start(bf16[1,144,256]{2,1,0:T(8,128)(2,1)S(1)} %collect.6.refs_0_), channel_id=1, source_target_pairs={{0,1},{1,0},{2,3},{3,2},{4,5},{5,4},{6,7},{7,6},{8,9},{9,8},{10,11... | collective-permute-start | bytes 221192 | tf_op jit(solution)/shard_map/ppermute | solution.py:527
  23.9 5.3 %collective-permute-start.10 = (bf16[4,144,256]{2,1,0:T(8,128)(2,1)S(1)}, bf16[4,144,256]{2,1,0:T(8,128)(2,1)S(1)}, u32[]{:S(2)}, u32[]{:S(2)}) collective-permute-start(bf16[4,144,256]{2,1,0:T(8,128)(2,1)S(1)} %collect.7.refs_4_.refs_1_), channel_id=1, source_target_pairs={{0,4},{4,0},{8,12},{12,8},{16,20},{20,16},{24,28},{28,24},{1,5},{5... | collective-permute-start | bytes 884744 | tf_op jit(solution)/shard_map/ppermute | solution.py:527
  24.0 14.5 %collective-permute-start.5 = (bf16[4,144,256]{2,1,0:T(8,128)(2,1)S(1)}, bf16[4,144,256]{2,1,0:T(8,128)(2,1)S(1)}, u32[]{:S(2)}, u32[]{:S(2)}) collective-permute-start(bf16[4,144,256]{2,1,0:T(8,128)(2,1)S(1)} %collect.5), channel_id=1, source_target_pairs={{0,28},{4,8},{8,4},{12,16},{16,12},{20,24},{24,20},{28,0},{1,29},{... | collective-permute-start | bytes 884744 | tf_op jit(solution)/shard_map/ppermute | solution.py:578
  36.3 5.5 %collective-permute-start.13 = (bf16[2,128,256]{2,1,0:T(8,128)(2,1)S(1)}, bf16[2,128,256]{2,1,0:T(8,128)(2,1)S(1)}, u32[]{:S(2)}, u32[]{:S(2)}) collective-permute-start(bf16[2,128,256]{2,1,0:T(8,128)(2,1)S(1)} %get-tuple-element.44.refs_6_), channel_id=1, source_target_pairs={{0,8},{4,12},{8,0},{12,4},{16,24},{20,28},{24,16},{28,20},{1,9},{5... | collective-permute-start | bytes 393224 | tf_op jit(solution)/shard_map/ppermute | solution.py:527
  36.4 6.8 %collective-permute-start.12 = (bf16[2,128,256]{2,1,0:T(8,128)(2,1)S(1)}, bf16[2,128,256]{2,1,0:T(8,128)(2,1)S(1)}, u32[]{:S(2)}, u32[]{:S(2)}) collective-permute-start(bf16[2,128,256]{2,1,0:T(8,128)(2,1)S(1)} %get-tuple-element.43.refs_4_), channel_id=1, source_target_pairs={{0,8},{4,12},{8,0},{12,4},{16,24},{20,28},{24,16},{28,20},{1,9},{5... | collective-permute-start | bytes 393224 | tf_op jit(solution)/shard_map/ppermute | solution.py:527
  38.4 6.2 %collective-permute-start.11 = (bf16[2,128,256]{2,1,0:T(8,128)(2,1)S(1)}, bf16[2,128,256]{2,1,0:T(8,128)(2,1)S(1)}, u32[]{:S(2)}, u32[]{:S(2)}) collective-permute-start(bf16[2,128,256]{2,1,0:T(8,128)(2,1)S(1)} %get-tuple-element.42.refs_4_), channel_id=1, source_target_pairs={{0,8},{4,12},{8,0},{12,4},{16,24},{20,28},{24,16},{28,20},{1,9},{5... | collective-permute-start | bytes 393224 | tf_op jit(solution)/shard_map/ppermute | solution.py:527
  45.3 1.8 %collective-permute-start.18 = (bf16[128,1024]{1,0:T(8,128)(2,1)S(1)}, bf16[128,1024]{1,0:T(8,128)(2,1)S(1)}, u32[]{:S(2)}, u32[]{:S(2)}) collective-permute-start(bf16[128,1024]{1,0:T(8,128)(2,1)S(1)} %get-tuple-element.60), channel_id=1, source_target_pairs={{0,4},{4,0},{8,12},{12,8},{16,20},{20,16},{24,28},{28,24},{1,5},{5... | collective-permute-start | bytes 786440 | tf_op jit(solution)/shard_map/ppermute | solution.py:527
  46.0 5.4 %collective-permute-start.14 = (bf16[128,1024]{1,0:T(8,128)(2,1)S(1)}, bf16[128,1024]{1,0:T(8,128)(2,1)S(1)}, u32[]{:S(2)}, u32[]{:S(2)}) collective-permute-start(bf16[128,1024]{1,0:T(8,128)(2,1)S(1)} %inverse.4), channel_id=1, source_target_pairs={{0,4},{4,0},{8,12},{12,8},{16,20},{20,16},{24,28},{28,24},{1,5},{5... | collective-permute-start | bytes 786440 | tf_op jit(solution)/shard_map/ppermute | solution.py:527
  47.2 6.9 %collective-permute-start.19 = (bf16[128,256]{1,0:T(8,128)(2,1)S(1)}, bf16[128,256]{1,0:T(8,128)(2,1)S(1)}, u32[]{:S(2)}, u32[]{:S(2)}) collective-permute-start(bf16[128,256]{1,0:T(8,128)(2,1)S(1)} %get-tuple-element.62), channel_id=1, source_target_pairs={{0,3},{1,2},{2,1},{3,0},{4,7},{5,6},{6,5},{7,4},{8,11},{9,10},{10,... | collective-permute-start | bytes 196616 | tf_op jit(solution)/shard_map/ppermute | solution.py:527
  49.4 5.7 %collective-permute-start.20 = (bf16[128,256]{1,0:T(8,128)(2,1)S(1)}, bf16[128,256]{1,0:T(8,128)(2,1)S(1)}, u32[]{:S(2)}, u32[]{:S(2)}) collective-permute-start(bf16[128,256]{1,0:T(8,128)(2,1)S(1)} %get-tuple-element.63), channel_id=1, source_target_pairs={{0,2},{1,3},{2,0},{3,1},{4,6},{5,7},{6,4},{7,5},{8,10},{9,11},{10,... | collective-permute-start | bytes 196616 | tf_op jit(solution)/shard_map/ppermute | solution.py:527
  49.9 5.2 %collective-permute-start.21 = (bf16[128,256]{1,0:T(8,128)(2,1)S(1)}, bf16[128,256]{1,0:T(8,128)(2,1)S(1)}, u32[]{:S(2)}, u32[]{:S(2)}) collective-permute-start(bf16[128,256]{1,0:T(8,128)(2,1)S(1)} %get-tuple-element.64), channel_id=1, source_target_pairs={{0,1},{1,0},{2,3},{3,2},{4,5},{5,4},{6,7},{7,6},{8,9},{9,8},{10,11... | collective-permute-start | bytes 196616 | tf_op jit(solution)/shard_map/ppermute | solution.py:527
  51.3 9.7 %copy-start = (bf16[256,128]{1,0:T(8,128)(2,1)S(1)}, bf16[256,128]{1,0:T(8,128)(2,1)}, u32[]{:S(2)}) copy-start(bf16[256,128]{1,0:T(8,128)(2,1)} %refs_0_.3) | copy-start | bytes 196612
  51.4 8.6 %collective-permute-start.15 = (bf16[128,256]{1,0:T(8,128)(2,1)S(1)}, bf16[128,256]{1,0:T(8,128)(2,1)S(1)}, u32[]{:S(2)}, u32[]{:S(2)}) collective-permute-start(bf16[128,256]{1,0:T(8,128)(2,1)S(1)} %get-tuple-element.57), channel_id=1, source_target_pairs={{0,3},{1,2},{2,1},{3,0},{4,7},{5,6},{6,5},{7,4},{8,11},{9,10},{10,... | collective-permute-start | bytes 196616 | tf_op jit(solution)/shard_map/ppermute | solution.py:527
  53.6 6.4 %collective-permute-start.16 = (bf16[128,256]{1,0:T(8,128)(2,1)S(1)}, bf16[128,256]{1,0:T(8,128)(2,1)S(1)}, u32[]{:S(2)}, u32[]{:S(2)}) collective-permute-start(bf16[128,256]{1,0:T(8,128)(2,1)S(1)} %get-tuple-element.58), channel_id=1, source_target_pairs={{0,2},{1,3},{2,0},{3,1},{4,6},{5,7},{6,4},{7,5},{8,10},{9,11},{10,... | collective-permute-start | bytes 196616 | tf_op jit(solution)/shard_map/ppermute | solution.py:527
  54.1 5.9 %collective-permute-start.17 = (bf16[128,256]{1,0:T(8,128)(2,1)S(1)}, bf16[128,256]{1,0:T(8,128)(2,1)S(1)}, u32[]{:S(2)}, u32[]{:S(2)}) collective-permute-start(bf16[128,256]{1,0:T(8,128)(2,1)S(1)} %get-tuple-element.59), channel_id=1, source_target_pairs={{0,1},{1,0},{2,3},{3,2},{4,5},{5,4},{6,7},{7,6},{8,9},{9,8},{10,11... | collective-permute-start | bytes 196616 | tf_op jit(solution)/shard_map/ppermute | solution.py:527
  55.1 5.9 %collective-permute-start.22 = (bf16[128,256]{1,0:T(8,128)(2,1)S(1)}, bf16[128,256]{1,0:T(8,128)(2,1)S(1)}, u32[]{:S(2)}, u32[]{:S(2)}) collective-permute-start(bf16[128,256]{1,0:T(8,128)(2,1)S(1)} %add_convert_fusion), channel_id=1, source_target_pairs={{0,16},{4,20},{8,24},{12,28},{16,0},{20,4},{24,8},{28,12},{1,17},{... | collective-permute-start | bytes 196616 | tf_op jit(solution)/shard_map/ppermute | solution.py:527
  (6 other events, 49.7 us)

commit v7 on v6

--- a/solution.py
+++ b/solution.py
@@ -562,15 +562,14 @@
         for place, name in enumerate(names):
             where[name] = tuple((len(tables) - 1, j, place) for j in range(2 * blocks))
 
-    near_own = collect(
-        [near[k] for k in others], [(i, None) for i in range(n_kvec - 1)], after=(waves,)
-    )
+    table, total = wave(waves, [message, message_x], [(0, None), (1, None)], None)
+    keep(table, [(0, 0, 0), (1, 0, 0)])
+    near_own = collect([near[k] for k in others], [(i, None) for i in range(n_kvec - 1)], after=(total,))
     near_x = swap(near_own, "atoms", 1)
     names = [(0, 0, k) for k in others] + [(1, 0, k) for k in others]
     picks = [(core, i) for core in range(2) for i in range(n_kvec - 1)]
-    start = [(0, None), (1, None)] + [(2, index) for _, index in picks[:2]]
-    table, total = wave(waves, [message, message_x, near_own], start, None)
-    keep(table, [(0, 0, 0), (1, 0, 0)] + names[:2])
+    table, total = wave(waves, [near_own], picks[:2], total)
+    keep(table, names[:2])
     distant = collect(distant, [(z, None) for z in range(far - 1)], after=(total,))
     relayed = {k: swap(distant, "kvec", k) for k in others}
     halo_pairs = [(a, (a + 1) % n_atoms if a % 2 else (a - 1) % n_atoms) for a in range(n_atoms)]

time: 62.4 us -> 63 us (level)
  waiting for transfers between devices: 10.4 us -> 11.3 us
    ppermute x22, waiting for transfers between devices: 10.4 us -> 11.3 us  [swap(): lax.ppermute(value, axis, [(i, i ^ bits) for i in range(lax.axis_size(axi...]
    pallas_call x6 -> x7, Pallas kernels: 13.1 us -> 13.3 us  [wave(): pl.pallas_call(functools.partial(wave_kernel, tuple(picks), len(arrays),...]
where the time goes in v7:
time: 63 us; the launch traced here: 62.9 us
  starting transfers between devices  26.3 us (42%)
  Pallas kernels  24.8 us (39%)
  waiting for transfers between devices  11.3 us (18%)
    ppermute x22, starting transfers between devices, swap(): lax.ppermute(value, axis, [(i, i ^ bits) for i in range(lax.axis_size(axi...  22.7 us
    pallas_call x7, Pallas kernels, wave(): pl.pallas_call(functools.partial(wave_kernel, tuple(picks), len(arrays),...  13.3 us
    ppermute x22, waiting for transfers between devices, swap(): lax.ppermute(value, axis, [(i, i ^ bits) for i in range(lax.axis_size(axi...  11.3 us
    pallas_call x2, Pallas kernels, pair_message(): pl.pallas_call(functools.partial(pair_kernel, nbasis, pieces, scale, pick...  6.36 us
    ppermute x1, starting transfers between devices, per_device(): lax.ppermute(collect([message, near_own], group), 'atoms', halo_pairs)  3.64 us
    pallas_call x3, Pallas kernels, inverse(): pl.pallas_call(functools.partial(inverse_kernel, pieces, shard), in_specs...  1.73 us
  transfers between devices with their start and end apart: 23, of which 11 were waited for; matrix products, arithmetic and copies ran while one was open for 0% of the time, Pallas kernels for 35%

profile of v7, /device:TPU:0, one launch (start us, length us, event | category | flops | bytes accessed | tf_op | source)
XLA Modules:
  0.0 62.9 jit_solution(15304071110757099109)
XLA Ops:
  1.6 3.5 %collective-permute-start.1 = (bf16[144,256]{1,0:T(8,128)(2,1)S(1)}, bf16[144,256]{1,0:T(8,128)(2,1)S(1)}, u32[]{:S(2)}, u32[]{:S(2)}) collective-permute-start(bf16[144,256]{1,0:T(8,128)(2,1)S(1)} %get-tuple-element.37.refs_1_.refs_0_), channel_id=1, source_target_pairs={{0,3},{1,2},{2,1},{3,0},{4,7},{5,6},{6,5},{7,4},{8,11},{9,10},{10,... | collective-permute-start | bytes 221192 | tf_op jit(solution)/shard_map/ppermute | solution.py:527
  6.2 1.5 %wave.7 = (bf16[6,256,512]{2,1,0:T(8,128)(2,1)S(1)}, f32[6,128,256]{2,1,0:T(8,128)S(1)}) custom-call(bf16[3,256,16]{2,1,0:T(8,128)(2,1)S(1)} %get-tuple-element.40.refs_0_, bf16[144,256]{1,0:T(8,128)(2,1)S(1)} %get-tuple-element.37.refs_1_.refs_0_, bf16[144,256]{1,0:T(8,128)(2,1)S(1)} %collective-permute-done.refs_2_.refs_1_), custom_call_target="tpu_custom_call" | custom-call | flops 201326592 | bytes 1572864 | tf_op jit(solution)/shard_map/wave/pallas_call | solution.py:233
  8.0 1.6 %collective-permute-done.2.refs_1_ = bf16[144,256]{1,0:T(8,128)(2,1)S(1)} collective-permute-done((bf16[144,256]{1,0:T(8,128)(2,1)S(1)}, bf16[144,256]{1,0:T(8,128)(2,1)S(1)}, u32[]{:S(2)}, u32[]{:S(2)}) %collective-permute-start.2) | collective-permute-done | bytes 73760 | tf_op jit(solution)/shard_map/ppermute | solution.py:527
  10.0 2.7 %collective-permute-start.6 = (bf16[144,256]{1,0:T(8,128)(2,1)S(1)}, bf16[144,256]{1,0:T(8,128)(2,1)S(1)}, u32[]{:S(2)}, u32[]{:S(2)}) collective-permute-start(bf16[144,256]{1,0:T(8,128)(2,1)S(1)} %get-tuple-element.37.refs_1_.refs_0_), channel_id=1, source_target_pairs={{0,16},{4,20},{8,24},{12,28},{16,0},{20,4},{24,8},{28,12},{1,17},{... | collective-permute-start | bytes 221192 | tf_op jit(solution)/shard_map/ppermute | solution.py:527
  12.7 1.5 %wave.8 = (bf16[6,256,512]{2,1,0:T(8,128)(2,1)S(1)}, f32[6,128,256]{2,1,0:T(8,128)S(1)}) custom-call(bf16[3,256,16]{2,1,0:T(8,128)(2,1)S(1)} %get-tuple-element.40.refs_0_, bf16[3,144,256]{2,1,0:T(8,128)(2,1)S(1)} %collect.4.refs_1_.refs_2_, f32[6,128,256]{2,1,0:T(8,128)S(1)} %get-tuple-element.41.refs_3_.refs_2_), custom_call_target="tpu_custom_call" | custom-call | flops 201326592 | bytes 1572864 | tf_op jit(solution)/shard_map/wave/pallas_call | solution.py:233
  14.2 3.0 %collective-permute-done.6.refs_0_ = bf16[144,256]{1,0:T(8,128)(2,1)S(1)} collective-permute-done((bf16[144,256]{1,0:T(8,128)(2,1)S(1)}, bf16[144,256]{1,0:T(8,128)(2,1)S(1)}, u32[]{:S(2)}, u32[]{:S(2)}) %collective-permute-start.6) | collective-permute-done | bytes 73760 | tf_op jit(solution)/shard_map/ppermute | solution.py:527
  17.2 1.5 %collective-permute-start.7 = (bf16[1,144,256]{2,1,0:T(8,128)(2,1)S(1)}, bf16[1,144,256]{2,1,0:T(8,128)(2,1)S(1)}, u32[]{:S(2)}, u32[]{:S(2)}) collective-permute-start(bf16[1,144,256]{2,1,0:T(8,128)(2,1)S(1)} %collect.6.refs_0_), channel_id=1, source_target_pairs={{0,3},{1,2},{2,1},{3,0},{4,7},{5,6},{6,5},{7,4},{8,11},{9,10},{10,... | collective-permute-start | bytes 221192 | tf_op jit(solution)/shard_map/ppermute | solution.py:527
  18.7 1.3 %collective-permute-start.8 = (bf16[1,144,256]{2,1,0:T(8,128)(2,1)S(1)}, bf16[1,144,256]{2,1,0:T(8,128)(2,1)S(1)}, u32[]{:S(2)}, u32[]{:S(2)}) collective-permute-start(bf16[1,144,256]{2,1,0:T(8,128)(2,1)S(1)} %collect.6.refs_0_), channel_id=1, source_target_pairs={{0,2},{1,3},{2,0},{3,1},{4,6},{5,7},{6,4},{7,5},{8,10},{9,11},{10,... | collective-permute-start | bytes 221192 | tf_op jit(solution)/shard_map/ppermute | solution.py:527
  20.7 1.5 %wave.9 = (bf16[6,256,512]{2,1,0:T(8,128)(2,1)S(1)}, f32[6,128,256]{2,1,0:T(8,128)S(1)}) custom-call(bf16[3,256,16]{2,1,0:T(8,128)(2,1)S(1)} %get-tuple-element.40.refs_0_, bf16[3,144,256]{2,1,0:T(8,128)(2,1)S(1)} %collect.4.refs_1_.refs_2_, bf16[3,144,256]{2,1,0:T(8,128)(2,1)S(1)} %collective-permute-done.4.refs_2_.refs_3_, ...), custom_call_target="tpu_custom_call" | custom-call | flops 201326592 | bytes 1572864 | tf_op jit(solution)/shard_map/wave/pallas_call | solution.py:233
  23.2 1.1 %collective-permute-done.9.refs_3_ = bf16[1,144,256]{2,1,0:T(8,128)(2,1)S(1)} collective-permute-done((bf16[1,144,256]{2,1,0:T(8,128)(2,1)S(1)}, bf16[1,144,256]{2,1,0:T(8,128)(2,1)S(1)}, u32[]{:S(2)}, u32[]{:S(2)}) %collective-permute-start.9) | collective-permute-done | bytes 73760 | tf_op jit(solution)/shard_map/ppermute | solution.py:527
  24.5 3.6 %collective-permute-start.5 = (bf16[4,144,256]{2,1,0:T(8,128)(2,1)S(1)}, bf16[4,144,256]{2,1,0:T(8,128)(2,1)S(1)}, u32[]{:S(2)}, u32[]{:S(2)}) collective-permute-start(bf16[4,144,256]{2,1,0:T(8,128)(2,1)S(1)} %collect.5), channel_id=1, source_target_pairs={{0,28},{4,8},{8,4},{12,16},{16,12},{20,24},{24,20},{28,0},{1,29},{... | collective-permute-start | bytes 884744 | tf_op jit(solution)/shard_map/ppermute | solution.py:577
  28.2 1.5 %wave.10 = (bf16[6,256,512]{2,1,0:T(8,128)(2,1)S(1)}, f32[6,128,256]{2,1,0:T(8,128)S(1)}) custom-call(bf16[3,256,16]{2,1,0:T(8,128)(2,1)S(1)} %get-tuple-element.40.refs_0_, bf16[3,144,256]{2,1,0:T(8,128)(2,1)S(1)} %collect.4.refs_1_.refs_2_, bf16[3,144,256]{2,1,0:T(8,128)(2,1)S(1)} %collective-permute-done.4.refs_2_.refs_3_, ...), custom_call_target="tpu_custom_call" | custom-call | flops 201326592 | bytes 1572864 | tf_op jit(solution)/shard_map/wave/pallas_call | solution.py:233
  29.7 2.5 %wave.11 = (bf16[2,256,2048]{2,1,0:T(8,128)(2,1)S(1)}, f32[2,128,256]{2,1,0:T(8,128)S(1)}, bf16[2,128,256]{2,1,0:T(8,128)(2,1)S(1)}) custom-call(bf16[3,256,16]{2,1,0:T(8,128)(2,1)S(1)} %get-tuple-element.40.refs_0_, bf16[4,144,256]{2,1,0:T(8,128)(2,1)S(1)} %collect.7.refs_4_.refs_1_, bf16[4,144,256]{2,1,0:T(8,128)(2,1)S(1)} %collective-permute-done.10.refs_2_, ...), custom_call_target="tpu_custom_call" | custom-call | flops 268435456 | bytes 2097152 | tf_op jit(solution)/shard_map/wave/pallas_call | solution.py:233
  32.3 2.4 %wave.12 = (bf16[2,256,2048]{2,1,0:T(8,128)(2,1)S(1)}, f32[2,128,256]{2,1,0:T(8,128)S(1)}, bf16[2,128,256]{2,1,0:T(8,128)(2,1)S(1)}) custom-call(bf16[3,256,16]{2,1,0:T(8,128)(2,1)S(1)} %get-tuple-element.40.refs_0_, bf16[4,144,256]{2,1,0:T(8,128)(2,1)S(1)} %collect.7.refs_4_.refs_1_, bf16[4,144,256]{2,1,0:T(8,128)(2,1)S(1)} %collective-permute-done.10.refs_2_, ...), custom_call_target="tpu_custom_call" | custom-call | flops 268435456 | bytes 2097152 | tf_op jit(solution)/shard_map/wave/pallas_call | solution.py:233
  34.6 2.4 %wave.13 = (bf16[2,256,2048]{2,1,0:T(8,128)(2,1)S(1)}, f32[2,128,256]{2,1,0:T(8,128)S(1)}, bf16[2,128,256]{2,1,0:T(8,128)(2,1)S(1)}) custom-call(bf16[3,256,16]{2,1,0:T(8,128)(2,1)S(1)} %get-tuple-element.40.refs_0_, bf16[4,144,256]{2,1,0:T(8,128)(2,1)S(1)} %collect.7.refs_4_.refs_1_, bf16[4,144,256]{2,1,0:T(8,128)(2,1)S(1)} %collective-permute-done.10.refs_2_, ...), custom_call_target="tpu_custom_call" | custom-call | flops 268435456 | bytes 2097152 | tf_op jit(solution)/shard_map/wave/pallas_call | solution.py:233
  37.1 2.0 %collective-permute-start.12 = (bf16[2,128,256]{2,1,0:T(8,128)(2,1)S(1)}, bf16[2,128,256]{2,1,0:T(8,128)(2,1)S(1)}, u32[]{:S(2)}, u32[]{:S(2)}) collective-permute-start(bf16[2,128,256]{2,1,0:T(8,128)(2,1)S(1)} %get-tuple-element.46.refs_4_), channel_id=1, source_target_pairs={{0,8},{4,12},{8,0},{12,4},{16,24},{20,28},{24,16},{28,20},{1,9},{5... | collective-permute-start | bytes 393224 | tf_op jit(solution)/shard_map/ppermute | solution.py:527
  39.2 3.2 %pair.2.refs_7_.refs_4_ = f32[128,128]{1,0:T(8,128)S(1)} custom-call(s32[2,12]{1,0:T(2,128)S(1)} %copy-done.6, f32[3,256]{1,0:T(4,128)S(1)} %copy-done.3, bf16[144,256]{1,0:T(8,128)(2,1)S(1)} %get-tuple-element.37.refs_1_.refs_0_, bf16[144,256]{1,0:T(8,128)(2,1)S(1)} %collective-permute-done.refs_2_.refs_1_, ...), custom_call_target="tpu_custom_call" | custom-call | flops 418381824 | bytes 786432 | tf_op jit(solution)/shard_map/pair/pallas_call | solution.py:474
  42.5 1.4 %collective-permute-done.12.refs_4_ = bf16[2,128,256]{2,1,0:T(8,128)(2,1)S(1)} collective-permute-done((bf16[2,128,256]{2,1,0:T(8,128)(2,1)S(1)}, bf16[2,128,256]{2,1,0:T(8,128)(2,1)S(1)}, u32[]{:S(2)}, u32[]{:S(2)}) %collective-permute-start.12) | collective-permute-done | bytes 131104 | tf_op jit(solution)/shard_map/ppermute | solution.py:527
  43.9 1.4 %collective-permute-done.11.refs_3_ = bf16[2,128,256]{2,1,0:T(8,128)(2,1)S(1)} collective-permute-done((bf16[2,128,256]{2,1,0:T(8,128)(2,1)S(1)}, bf16[2,128,256]{2,1,0:T(8,128)(2,1)S(1)}, u32[]{:S(2)}, u32[]{:S(2)}) %collective-permute-start.11) | collective-permute-done | bytes 131104 | tf_op jit(solution)/shard_map/ppermute | solution.py:527
  47.8 1.7 %collective-permute-start.19 = (bf16[128,256]{1,0:T(8,128)(2,1)S(1)}, bf16[128,256]{1,0:T(8,128)(2,1)S(1)}, u32[]{:S(2)}, u32[]{:S(2)}) collective-permute-start(bf16[128,256]{1,0:T(8,128)(2,1)S(1)} %get-tuple-element.66), channel_id=1, source_target_pairs={{0,3},{1,2},{2,1},{3,0},{4,7},{5,6},{6,5},{7,4},{8,11},{9,10},{10,... | collective-permute-start | bytes 196616 | tf_op jit(solution)/shard_map/ppermute | solution.py:527
  52.0 1.7 %collective-permute-start.15 = (bf16[128,256]{1,0:T(8,128)(2,1)S(1)}, bf16[128,256]{1,0:T(8,128)(2,1)S(1)}, u32[]{:S(2)}, u32[]{:S(2)}) collective-permute-start(bf16[128,256]{1,0:T(8,128)(2,1)S(1)} %get-tuple-element.61), channel_id=1, source_target_pairs={{0,3},{1,2},{2,1},{3,0},{4,7},{5,6},{6,5},{7,4},{8,11},{9,10},{10,... | collective-permute-start | bytes 196616 | tf_op jit(solution)/shard_map/ppermute | solution.py:527
  55.6 1.8 %collective-permute-start.22 = (bf16[128,256]{1,0:T(8,128)(2,1)S(1)}, bf16[128,256]{1,0:T(8,128)(2,1)S(1)}, u32[]{:S(2)}, u32[]{:S(2)}) collective-permute-start(bf16[128,256]{1,0:T(8,128)(2,1)S(1)} %add_convert_fusion), channel_id=1, source_target_pairs={{0,16},{4,20},{8,24},{12,28},{16,0},{20,4},{24,8},{28,12},{1,17},{... | collective-permute-start | bytes 196616 | tf_op jit(solution)/shard_map/ppermute | solution.py:527
  57.4 3.2 %pair.3.refs_5_ = f32[128,128]{1,0:T(8,128)S(1)} custom-call(s32[2,12]{1,0:T(2,128)S(1)} %copy-done.6, f32[3,256]{1,0:T(4,128)S(1)} %copy-done.3, bf16[144,256]{1,0:T(8,128)(2,1)S(1)} %get-tuple-element.37.refs_1_.refs_0_, bf16[144,256]{1,0:T(8,128)(2,1)S(1)} %collective-permute-done.refs_2_.refs_1_, bf16[3,144,256]{2,1,0:T(8,128)(2,1)S(1)} %collect.4.refs_1_.refs_2_, ...), custom_call_target="tpu_custom_call" | custom-call | flops 418381824 | bytes 786432 | tf_op jit(solution)/shard_map/pair/pallas_call | solution.py:474
  61.6 1.3 %update.1 = bf16[256,128]{1,0:T(8,128)(2,1)} custom-call(bf16[256,128]{1,0:T(8,128)(2,1)S(1)} %copy-done, f32[1,128]{1,0:T(1,128)S(1)} %bitcast.2, bf16[128,512]{1,0:T(8,128)(2,1)S(1)} %copy-done.1, bf16[512,128]{1,0:T(8,128)(2,1)S(1)} %copy-done.2, f32[128,128]{1,0:T(8,128)S(1)} %pair.2.refs_7_.refs_4_, f32[128,128]{1,0:T(8,128)S(1)} %pair.3.refs_5_, ...), custom_call_target="tpu_custom_call" | custom-call | tf_op jit(solution)/shard_map/update/pallas_call | solution.py:516
  (59 shorter events, 13.3 us)
Async XLA Ops:
  1.0 5.2 %collective-permute-start = (bf16[144,256]{1,0:T(8,128)(2,1)S(1)}, bf16[144,256]{1,0:T(8,128)(2,1)S(1)}, u32[]{:S(2)}, u32[]{:S(2)}) collective-permute-start(bf16[144,256]{1,0:T(8,128)(2,1)S(1)} %get-tuple-element.37.refs_1_.refs_0_), channel_id=1, source_target_pairs={{0,4},{4,0},{8,12},{12,8},{16,20},{20,16},{24,28},{28,24},{1,5},{5... | collective-permute-start | bytes 221192 | tf_op jit(solution)/shard_map/ppermute | solution.py:527
  1.6 6.4 %collective-permute-start.1 = (bf16[144,256]{1,0:T(8,128)(2,1)S(1)}, bf16[144,256]{1,0:T(8,128)(2,1)S(1)}, u32[]{:S(2)}, u32[]{:S(2)}) collective-permute-start(bf16[144,256]{1,0:T(8,128)(2,1)S(1)} %get-tuple-element.37.refs_1_.refs_0_), channel_id=1, source_target_pairs={{0,3},{1,2},{2,1},{3,0},{4,7},{5,6},{6,5},{7,4},{8,11},{9,10},{10,... | collective-permute-start | bytes 221192 | tf_op jit(solution)/shard_map/ppermute | solution.py:527
  5.1 4.4 %collective-permute-start.2 = (bf16[144,256]{1,0:T(8,128)(2,1)S(1)}, bf16[144,256]{1,0:T(8,128)(2,1)S(1)}, u32[]{:S(2)}, u32[]{:S(2)}) collective-permute-start(bf16[144,256]{1,0:T(8,128)(2,1)S(1)} %get-tuple-element.37.refs_1_.refs_0_), channel_id=1, source_target_pairs={{0,2},{1,3},{2,0},{3,1},{4,6},{5,7},{6,4},{7,5},{8,10},{9,11},{10,... | collective-permute-start | bytes 221192 | tf_op jit(solution)/shard_map/ppermute | solution.py:527
  5.6 4.4 %collective-permute-start.3 = (bf16[144,256]{1,0:T(8,128)(2,1)S(1)}, bf16[144,256]{1,0:T(8,128)(2,1)S(1)}, u32[]{:S(2)}, u32[]{:S(2)}) collective-permute-start(bf16[144,256]{1,0:T(8,128)(2,1)S(1)} %get-tuple-element.37.refs_1_.refs_0_), channel_id=1, source_target_pairs={{0,1},{1,0},{2,3},{3,2},{4,5},{5,4},{6,7},{7,6},{8,9},{9,8},{10,11... | collective-permute-start | bytes 221192 | tf_op jit(solution)/shard_map/ppermute | solution.py:527
  10.0 10.7 %collective-permute-start.4 = (bf16[3,144,256]{2,1,0:T(8,128)(2,1)S(1)}, bf16[3,144,256]{2,1,0:T(8,128)(2,1)S(1)}, u32[]{:S(2)}, u32[]{:S(2)}) collective-permute-start(bf16[3,144,256]{2,1,0:T(8,128)(2,1)S(1)} %collect.4.refs_1_.refs_2_), channel_id=1, source_target_pairs={{0,4},{4,0},{8,12},{12,8},{16,20},{20,16},{24,28},{28,24},{1,5},{5... | collective-permute-start | bytes 663560 | tf_op jit(solution)/shard_map/ppermute | solution.py:527
  10.0 7.1 %collective-permute-start.6 = (bf16[144,256]{1,0:T(8,128)(2,1)S(1)}, bf16[144,256]{1,0:T(8,128)(2,1)S(1)}, u32[]{:S(2)}, u32[]{:S(2)}) collective-permute-start(bf16[144,256]{1,0:T(8,128)(2,1)S(1)} %get-tuple-element.37.refs_1_.refs_0_), channel_id=1, source_target_pairs={{0,16},{4,20},{8,24},{12,28},{16,0},{20,4},{24,8},{28,12},{1,17},{... | collective-permute-start | bytes 221192 | tf_op jit(solution)/shard_map/ppermute | solution.py:527
  17.2 5.3 %collective-permute-start.7 = (bf16[1,144,256]{2,1,0:T(8,128)(2,1)S(1)}, bf16[1,144,256]{2,1,0:T(8,128)(2,1)S(1)}, u32[]{:S(2)}, u32[]{:S(2)}) collective-permute-start(bf16[1,144,256]{2,1,0:T(8,128)(2,1)S(1)} %collect.6.refs_0_), channel_id=1, source_target_pairs={{0,3},{1,2},{2,1},{3,0},{4,7},{5,6},{6,5},{7,4},{8,11},{9,10},{10,... | collective-permute-start | bytes 221192 | tf_op jit(solution)/shard_map/ppermute | solution.py:527
  18.7 4.6 %collective-permute-start.8 = (bf16[1,144,256]{2,1,0:T(8,128)(2,1)S(1)}, bf16[1,144,256]{2,1,0:T(8,128)(2,1)S(1)}, u32[]{:S(2)}, u32[]{:S(2)}) collective-permute-start(bf16[1,144,256]{2,1,0:T(8,128)(2,1)S(1)} %collect.6.refs_0_), channel_id=1, source_target_pairs={{0,2},{1,3},{2,0},{3,1},{4,6},{5,7},{6,4},{7,5},{8,10},{9,11},{10,... | collective-permute-start | bytes 221192 | tf_op jit(solution)/shard_map/ppermute | solution.py:527
  20.0 4.4 %collective-permute-start.9 = (bf16[1,144,256]{2,1,0:T(8,128)(2,1)S(1)}, bf16[1,144,256]{2,1,0:T(8,128)(2,1)S(1)}, u32[]{:S(2)}, u32[]{:S(2)}) collective-permute-start(bf16[1,144,256]{2,1,0:T(8,128)(2,1)S(1)} %collect.6.refs_0_), channel_id=1, source_target_pairs={{0,1},{1,0},{2,3},{3,2},{4,5},{5,4},{6,7},{7,6},{8,9},{9,8},{10,11... | collective-permute-start | bytes 221192 | tf_op jit(solution)/shard_map/ppermute | solution.py:527
  24.4 5.3 %collective-permute-start.10 = (bf16[4,144,256]{2,1,0:T(8,128)(2,1)S(1)}, bf16[4,144,256]{2,1,0:T(8,128)(2,1)S(1)}, u32[]{:S(2)}, u32[]{:S(2)}) collective-permute-start(bf16[4,144,256]{2,1,0:T(8,128)(2,1)S(1)} %collect.7.refs_4_.refs_1_), channel_id=1, source_target_pairs={{0,4},{4,0},{8,12},{12,8},{16,20},{20,16},{24,28},{28,24},{1,5},{5... | collective-permute-start | bytes 884744 | tf_op jit(solution)/shard_map/ppermute | solution.py:527
  24.5 14.6 %collective-permute-start.5 = (bf16[4,144,256]{2,1,0:T(8,128)(2,1)S(1)}, bf16[4,144,256]{2,1,0:T(8,128)(2,1)S(1)}, u32[]{:S(2)}, u32[]{:S(2)}) collective-permute-start(bf16[4,144,256]{2,1,0:T(8,128)(2,1)S(1)} %collect.5), channel_id=1, source_target_pairs={{0,28},{4,8},{8,4},{12,16},{16,12},{20,24},{24,20},{28,0},{1,29},{... | collective-permute-start | bytes 884744 | tf_op jit(solution)/shard_map/ppermute | solution.py:577
  37.0 5.5 %collective-permute-start.13 = (bf16[2,128,256]{2,1,0:T(8,128)(2,1)S(1)}, bf16[2,128,256]{2,1,0:T(8,128)(2,1)S(1)}, u32[]{:S(2)}, u32[]{:S(2)}) collective-permute-start(bf16[2,128,256]{2,1,0:T(8,128)(2,1)S(1)} %get-tuple-element.47.refs_6_), channel_id=1, source_target_pairs={{0,8},{4,12},{8,0},{12,4},{16,24},{20,28},{24,16},{28,20},{1,9},{5... | collective-permute-start | bytes 393224 | tf_op jit(solution)/shard_map/ppermute | solution.py:527
  37.1 6.8 %collective-permute-start.12 = (bf16[2,128,256]{2,1,0:T(8,128)(2,1)S(1)}, bf16[2,128,256]{2,1,0:T(8,128)(2,1)S(1)}, u32[]{:S(2)}, u32[]{:S(2)}) collective-permute-start(bf16[2,128,256]{2,1,0:T(8,128)(2,1)S(1)} %get-tuple-element.46.refs_4_), channel_id=1, source_target_pairs={{0,8},{4,12},{8,0},{12,4},{16,24},{20,28},{24,16},{28,20},{1,9},{5... | collective-permute-start | bytes 393224 | tf_op jit(solution)/shard_map/ppermute | solution.py:527
  39.1 6.2 %collective-permute-start.11 = (bf16[2,128,256]{2,1,0:T(8,128)(2,1)S(1)}, bf16[2,128,256]{2,1,0:T(8,128)(2,1)S(1)}, u32[]{:S(2)}, u32[]{:S(2)}) collective-permute-start(bf16[2,128,256]{2,1,0:T(8,128)(2,1)S(1)} %get-tuple-element.45.refs_4_), channel_id=1, source_target_pairs={{0,8},{4,12},{8,0},{12,4},{16,24},{20,28},{24,16},{28,20},{1,9},{5... | collective-permute-start | bytes 393224 | tf_op jit(solution)/shard_map/ppermute | solution.py:527
  45.9 1.8 %collective-permute-start.18 = (bf16[128,1024]{1,0:T(8,128)(2,1)S(1)}, bf16[128,1024]{1,0:T(8,128)(2,1)S(1)}, u32[]{:S(2)}, u32[]{:S(2)}) collective-permute-start(bf16[128,1024]{1,0:T(8,128)(2,1)S(1)} %get-tuple-element.64), channel_id=1, source_target_pairs={{0,4},{4,0},{8,12},{12,8},{16,20},{20,16},{24,28},{28,24},{1,5},{5... | collective-permute-start | bytes 786440 | tf_op jit(solution)/shard_map/ppermute | solution.py:527
  46.6 5.4 %collective-permute-start.14 = (bf16[128,1024]{1,0:T(8,128)(2,1)S(1)}, bf16[128,1024]{1,0:T(8,128)(2,1)S(1)}, u32[]{:S(2)}, u32[]{:S(2)}) collective-permute-start(bf16[128,1024]{1,0:T(8,128)(2,1)S(1)} %inverse.4), channel_id=1, source_target_pairs={{0,4},{4,0},{8,12},{12,8},{16,20},{20,16},{24,28},{28,24},{1,5},{5... | collective-permute-start | bytes 786440 | tf_op jit(solution)/shard_map/ppermute | solution.py:527
  47.8 6.7 %collective-permute-start.19 = (bf16[128,256]{1,0:T(8,128)(2,1)S(1)}, bf16[128,256]{1,0:T(8,128)(2,1)S(1)}, u32[]{:S(2)}, u32[]{:S(2)}) collective-permute-start(bf16[128,256]{1,0:T(8,128)(2,1)S(1)} %get-tuple-element.66), channel_id=1, source_target_pairs={{0,3},{1,2},{2,1},{3,0},{4,7},{5,6},{6,5},{7,4},{8,11},{9,10},{10,... | collective-permute-start | bytes 196616 | tf_op jit(solution)/shard_map/ppermute | solution.py:527
  49.5 6.1 %collective-permute-start.20 = (bf16[128,256]{1,0:T(8,128)(2,1)S(1)}, bf16[128,256]{1,0:T(8,128)(2,1)S(1)}, u32[]{:S(2)}, u32[]{:S(2)}) collective-permute-start(bf16[128,256]{1,0:T(8,128)(2,1)S(1)} %get-tuple-element.67), channel_id=1, source_target_pairs={{0,2},{1,3},{2,0},{3,1},{4,6},{5,7},{6,4},{7,5},{8,10},{9,11},{10,... | collective-permute-start | bytes 196616 | tf_op jit(solution)/shard_map/ppermute | solution.py:527
  50.2 5.4 %collective-permute-start.21 = (bf16[128,256]{1,0:T(8,128)(2,1)S(1)}, bf16[128,256]{1,0:T(8,128)(2,1)S(1)}, u32[]{:S(2)}, u32[]{:S(2)}) collective-permute-start(bf16[128,256]{1,0:T(8,128)(2,1)S(1)} %get-tuple-element.68), channel_id=1, source_target_pairs={{0,1},{1,0},{2,3},{3,2},{4,5},{5,4},{6,7},{7,6},{8,9},{9,8},{10,11... | collective-permute-start | bytes 196616 | tf_op jit(solution)/shard_map/ppermute | solution.py:527
  51.9 9.7 %copy-start = (bf16[256,128]{1,0:T(8,128)(2,1)S(1)}, bf16[256,128]{1,0:T(8,128)(2,1)}, u32[]{:S(2)}) copy-start(bf16[256,128]{1,0:T(8,128)(2,1)} %refs_0_.3) | copy-start | bytes 196612
  52.0 8.6 %collective-permute-start.15 = (bf16[128,256]{1,0:T(8,128)(2,1)S(1)}, bf16[128,256]{1,0:T(8,128)(2,1)S(1)}, u32[]{:S(2)}, u32[]{:S(2)}) collective-permute-start(bf16[128,256]{1,0:T(8,128)(2,1)S(1)} %get-tuple-element.61), channel_id=1, source_target_pairs={{0,3},{1,2},{2,1},{3,0},{4,7},{5,6},{6,5},{7,4},{8,11},{9,10},{10,... | collective-permute-start | bytes 196616 | tf_op jit(solution)/shard_map/ppermute | solution.py:527
  53.7 6.9 %collective-permute-start.16 = (bf16[128,256]{1,0:T(8,128)(2,1)S(1)}, bf16[128,256]{1,0:T(8,128)(2,1)S(1)}, u32[]{:S(2)}, u32[]{:S(2)}) collective-permute-start(bf16[128,256]{1,0:T(8,128)(2,1)S(1)} %get-tuple-element.62), channel_id=1, source_target_pairs={{0,2},{1,3},{2,0},{3,1},{4,6},{5,7},{6,4},{7,5},{8,10},{9,11},{10,... | collective-permute-start | bytes 196616 | tf_op jit(solution)/shard_map/ppermute | solution.py:527
  54.5 6.2 %collective-permute-start.17 = (bf16[128,256]{1,0:T(8,128)(2,1)S(1)}, bf16[128,256]{1,0:T(8,128)(2,1)S(1)}, u32[]{:S(2)}, u32[]{:S(2)}) collective-permute-start(bf16[128,256]{1,0:T(8,128)(2,1)S(1)} %get-tuple-element.63), channel_id=1, source_target_pairs={{0,1},{1,0},{2,3},{3,2},{4,5},{5,4},{6,7},{7,6},{8,9},{9,8},{10,11... | collective-permute-start | bytes 196616 | tf_op jit(solution)/shard_map/ppermute | solution.py:527
  55.6 5.9 %collective-permute-start.22 = (bf16[128,256]{1,0:T(8,128)(2,1)S(1)}, bf16[128,256]{1,0:T(8,128)(2,1)S(1)}, u32[]{:S(2)}, u32[]{:S(2)}) collective-permute-start(bf16[128,256]{1,0:T(8,128)(2,1)S(1)} %add_convert_fusion), channel_id=1, source_target_pairs={{0,16},{4,20},{8,24},{12,28},{16,0},{20,4},{24,8},{28,12},{1,17},{... | collective-permute-start | bytes 196616 | tf_op jit(solution)/shard_map/ppermute | solution.py:527
  (6 other events, 49.7 us)

commit v8 on v7

--- a/solution.py
+++ b/solution.py
@@ -135,22 +135,23 @@
     )(lattice, kfilter)
 
 
-def wave_kernel(picks, arrays, first, start, waits, low, *refs):
+def wave_kernel(picks, arrays, first, start, waits, low, packed, *refs):
     refs = list(refs)
     take = lambda n: [refs.pop(0) for _ in range(n)]
     (lattice_ref,) = take(1)
     messages = take(arrays)
+    laid = take(2) if packed == "in" else None
     before_ref = None if start else take(1)[0]
     take(waits)
     table_ref, total_ref = take(2)
     low_ref = take(1)[0] if low else None
-    feat_scr, pos_scr = take(2)
+    feat_scr, pos_scr = laid or take(2)
     phases, buffers = take(2), take(2)
     blocks, width = table_ref.shape[0] // 2, table_ref.shape[1]
     every = lattice_ref.shape[0]
     pairs, channels, both = feat_scr.shape
     shard = both // 2
-    for place, (array, index) in enumerate(picks):
+    for place, (array, index) in enumerate(picks if packed != "in" else ()):
         item = messages[array] if index is None else messages[array].at[index]
         lanes = slice(place % 2 * shard, (place % 2 + 1) * shard)
         feat_scr[place // 2, :, lanes] = item[0:channels, :]
@@ -215,13 +216,15 @@
         low_ref[...] = total_ref[...].astype(BF16)
 
 
-def wave(lattice, arrays, picks, before, subset=None, after=(), low=False):
+def wave(lattice, arrays, picks, before, subset=None, after=(), low=False, packed=None, laid=()):
     every, width, _ = lattice.shape
     first, blocks = subset or (0, every)
     pieces = len(picks)
     rows, shard = arrays[0].shape[-2:]
     channels = rows - TAIL
-    args = [lattice, *arrays] + ([] if before is None else [before])
+    if packed == "in":
+        arrays = []
+    args = [lattice, *arrays, *laid] + ([] if before is None else [before])
     factor = (2 * blocks, channels, width)
     shapes = [
         jax.ShapeDtypeStruct((2 * blocks, width, pieces * shard), BF16),
@@ -229,17 +232,20 @@
     ]
     if low:
         shapes.append(jax.ShapeDtypeStruct(factor, BF16))
+    feat = (pieces // 2, channels, 2 * shard)
+    spot = (pieces // 2, TAIL, 2 * shard)
+    if packed == "out":
+        shapes += [jax.ShapeDtypeStruct(feat, BF16), jax.ShapeDtypeStruct(spot, BF16)]
     pairs = blocks * width * pieces * shard
     return pl.pallas_call(
         functools.partial(
-            wave_kernel, tuple(picks), len(arrays), first, before is None, len(after), low
+            wave_kernel, tuple(picks), len(arrays), first, before is None, len(after), low, packed
         ),
         in_specs=[VMEM] * len(args) + [ANY] * len(after),
         out_specs=[VMEM] * len(shapes),
         out_shape=shapes,
         scratch_shapes=[
-            pltpu.VMEM((pieces // 2, channels, 2 * shard), BF16),
-            pltpu.VMEM((pieces // 2, TAIL, 2 * shard), BF16),
+            *([] if packed else [pltpu.VMEM(feat, BF16), pltpu.VMEM(spot, BF16)]),
             pltpu.VMEM((width, 2 * shard), F32),
             pltpu.VMEM((width, 2 * shard), F32),
             pltpu.VMEM((2, width, 2 * shard), BF16),
@@ -586,10 +592,21 @@
     arrays = [far_own, far_x]
     picks = [(core, i) for core in range(2) for i in range(len(every))]
     spots = [(core, z, k) for core in range(2) for k in (0, *others) for z in zs]
-    own_factors, other_factors, low = [], [], None
+    own_factors, other_factors, low, laid = [], [], None, ()
     for j in range(blocks):
         after = () if low is None else (low,)
-        table, part, low = wave(waves, arrays, picks, total, subset=(j, 1), after=after, low=True)
+        table, part, low, *more = wave(
+            waves,
+            arrays,
+            picks,
+            total,
+            subset=(j, 1),
+            after=after,
+            low=True,
+            packed="in" if j else "out",
+            laid=laid,
+        )
+        laid = laid or tuple(more)
         tables.append(table)
         own_factors.append(part)
         other_factors.append(swap(low, "atoms", 2))

time: 63 us -> 62.9 us (level)
  no operation moved by 1% of the time
where the time goes in v8:
time: 62.9 us; the launch traced here: 62.8 us
  starting transfers between devices  26.4 us (42%)
  Pallas kernels  24.8 us (39%)
  waiting for transfers between devices  11.2 us (18%)
    ppermute x22, starting transfers between devices, swap(): lax.ppermute(value, axis, [(i, i ^ bits) for i in range(lax.axis_size(axi...  22.7 us
    pallas_call x7, Pallas kernels, wave(): pl.pallas_call(functools.partial(wave_kernel, tuple(picks), len(arrays),...  13.2 us
    ppermute x22, waiting for transfers between devices, swap(): lax.ppermute(value, axis, [(i, i ^ bits) for i in range(lax.axis_size(axi...  11.2 us
    pallas_call x2, Pallas kernels, pair_message(): pl.pallas_call(functools.partial(pair_kernel, nbasis, pieces, scale, pick...  6.36 us
    ppermute x1, starting transfers between devices, per_device(): lax.ppermute(collect([message, near_own], group), 'atoms', halo_pairs)  3.64 us
    pallas_call x3, Pallas kernels, inverse(): pl.pallas_call(functools.partial(inverse_kernel, pieces, shard), in_specs...  1.73 us
    pallas_call x1, Pallas kernels, update(): pl.pallas_call(functools.partial(update_kernel, len(pairs)), in_specs=[VM...  1.26 us
  transfers between devices with their start and end apart: 23, of which 11 were waited for; matrix products, arithmetic and copies ran while one was open for 0% of the time, Pallas kernels for 35%

profile of v8, /device:TPU:0, one launch (start us, length us, event | category | flops | bytes accessed | tf_op | source)
XLA Modules:
  0.0 62.8 jit_solution(14250218447914015767)
XLA Ops:
  1.6 3.5 %collective-permute-start.1 = (bf16[144,256]{1,0:T(8,128)(2,1)S(1)}, bf16[144,256]{1,0:T(8,128)(2,1)S(1)}, u32[]{:S(2)}, u32[]{:S(2)}) collective-permute-start(bf16[144,256]{1,0:T(8,128)(2,1)S(1)} %get-tuple-element.39.refs_1_.refs_0_), channel_id=1, source_target_pairs={{0,3},{1,2},{2,1},{3,0},{4,7},{5,6},{6,5},{7,4},{8,11},{9,10},{10,... | collective-permute-start | bytes 221192 | tf_op jit(solution)/shard_map/ppermute | solution.py:533
  6.2 1.5 %wave.7 = (bf16[6,256,512]{2,1,0:T(8,128)(2,1)S(1)}, f32[6,128,256]{2,1,0:T(8,128)S(1)}) custom-call(bf16[3,256,16]{2,1,0:T(8,128)(2,1)S(1)} %get-tuple-element.42.refs_0_, bf16[144,256]{1,0:T(8,128)(2,1)S(1)} %get-tuple-element.39.refs_1_.refs_0_, bf16[144,256]{1,0:T(8,128)(2,1)S(1)} %collective-permute-done.refs_2_.refs_1_), custom_call_target="tpu_custom_call" | custom-call | flops 201326592 | bytes 1572864 | tf_op jit(solution)/shard_map/wave/pallas_call | solution.py:240
  8.0 1.6 %collective-permute-done.2.refs_1_ = bf16[144,256]{1,0:T(8,128)(2,1)S(1)} collective-permute-done((bf16[144,256]{1,0:T(8,128)(2,1)S(1)}, bf16[144,256]{1,0:T(8,128)(2,1)S(1)}, u32[]{:S(2)}, u32[]{:S(2)}) %collective-permute-start.2) | collective-permute-done | bytes 73760 | tf_op jit(solution)/shard_map/ppermute | solution.py:533
  10.0 2.7 %collective-permute-start.6 = (bf16[144,256]{1,0:T(8,128)(2,1)S(1)}, bf16[144,256]{1,0:T(8,128)(2,1)S(1)}, u32[]{:S(2)}, u32[]{:S(2)}) collective-permute-start(bf16[144,256]{1,0:T(8,128)(2,1)S(1)} %get-tuple-element.39.refs_1_.refs_0_), channel_id=1, source_target_pairs={{0,16},{4,20},{8,24},{12,28},{16,0},{20,4},{24,8},{28,12},{1,17},{... | collective-permute-start | bytes 221192 | tf_op jit(solution)/shard_map/ppermute | solution.py:533
  12.7 1.5 %wave.8 = (bf16[6,256,512]{2,1,0:T(8,128)(2,1)S(1)}, f32[6,128,256]{2,1,0:T(8,128)S(1)}) custom-call(bf16[3,256,16]{2,1,0:T(8,128)(2,1)S(1)} %get-tuple-element.42.refs_0_, bf16[3,144,256]{2,1,0:T(8,128)(2,1)S(1)} %collect.4.refs_1_.refs_2_, f32[6,128,256]{2,1,0:T(8,128)S(1)} %get-tuple-element.43.refs_3_.refs_2_), custom_call_target="tpu_custom_call" | custom-call | flops 201326592 | bytes 1572864 | tf_op jit(solution)/shard_map/wave/pallas_call | solution.py:240
  14.2 3.0 %collective-permute-done.6.refs_0_ = bf16[144,256]{1,0:T(8,128)(2,1)S(1)} collective-permute-done((bf16[144,256]{1,0:T(8,128)(2,1)S(1)}, bf16[144,256]{1,0:T(8,128)(2,1)S(1)}, u32[]{:S(2)}, u32[]{:S(2)}) %collective-permute-start.6) | collective-permute-done | bytes 73760 | tf_op jit(solution)/shard_map/ppermute | solution.py:533
  17.2 1.5 %collective-permute-start.7 = (bf16[1,144,256]{2,1,0:T(8,128)(2,1)S(1)}, bf16[1,144,256]{2,1,0:T(8,128)(2,1)S(1)}, u32[]{:S(2)}, u32[]{:S(2)}) collective-permute-start(bf16[1,144,256]{2,1,0:T(8,128)(2,1)S(1)} %collect.6.refs_0_), channel_id=1, source_target_pairs={{0,3},{1,2},{2,1},{3,0},{4,7},{5,6},{6,5},{7,4},{8,11},{9,10},{10,... | collective-permute-start | bytes 221192 | tf_op jit(solution)/shard_map/ppermute | solution.py:533
  18.7 1.3 %collective-permute-start.8 = (bf16[1,144,256]{2,1,0:T(8,128)(2,1)S(1)}, bf16[1,144,256]{2,1,0:T(8,128)(2,1)S(1)}, u32[]{:S(2)}, u32[]{:S(2)}) collective-permute-start(bf16[1,144,256]{2,1,0:T(8,128)(2,1)S(1)} %collect.6.refs_0_), channel_id=1, source_target_pairs={{0,2},{1,3},{2,0},{3,1},{4,6},{5,7},{6,4},{7,5},{8,10},{9,11},{10,... | collective-permute-start | bytes 221192 | tf_op jit(solution)/shard_map/ppermute | solution.py:533
  20.7 1.5 %wave.9 = (bf16[6,256,512]{2,1,0:T(8,128)(2,1)S(1)}, f32[6,128,256]{2,1,0:T(8,128)S(1)}) custom-call(bf16[3,256,16]{2,1,0:T(8,128)(2,1)S(1)} %get-tuple-element.42.refs_0_, bf16[3,144,256]{2,1,0:T(8,128)(2,1)S(1)} %collect.4.refs_1_.refs_2_, bf16[3,144,256]{2,1,0:T(8,128)(2,1)S(1)} %collective-permute-done.4.refs_2_.refs_3_, ...), custom_call_target="tpu_custom_call" | custom-call | flops 201326592 | bytes 1572864 | tf_op jit(solution)/shard_map/wave/pallas_call | solution.py:240
  23.2 1.1 %collective-permute-done.9.refs_3_ = bf16[1,144,256]{2,1,0:T(8,128)(2,1)S(1)} collective-permute-done((bf16[1,144,256]{2,1,0:T(8,128)(2,1)S(1)}, bf16[1,144,256]{2,1,0:T(8,128)(2,1)S(1)}, u32[]{:S(2)}, u32[]{:S(2)}) %collective-permute-start.9) | collective-permute-done | bytes 73760 | tf_op jit(solution)/shard_map/ppermute | solution.py:533
  24.5 3.6 %collective-permute-start.5 = (bf16[4,144,256]{2,1,0:T(8,128)(2,1)S(1)}, bf16[4,144,256]{2,1,0:T(8,128)(2,1)S(1)}, u32[]{:S(2)}, u32[]{:S(2)}) collective-permute-start(bf16[4,144,256]{2,1,0:T(8,128)(2,1)S(1)} %collect.5), channel_id=1, source_target_pairs={{0,28},{4,8},{8,4},{12,16},{16,12},{20,24},{24,20},{28,0},{1,29},{... | collective-permute-start | bytes 884744 | tf_op jit(solution)/shard_map/ppermute | solution.py:583
  28.2 1.5 %wave.10 = (bf16[6,256,512]{2,1,0:T(8,128)(2,1)S(1)}, f32[6,128,256]{2,1,0:T(8,128)S(1)}) custom-call(bf16[3,256,16]{2,1,0:T(8,128)(2,1)S(1)} %get-tuple-element.42.refs_0_, bf16[3,144,256]{2,1,0:T(8,128)(2,1)S(1)} %collect.4.refs_1_.refs_2_, bf16[3,144,256]{2,1,0:T(8,128)(2,1)S(1)} %collective-permute-done.4.refs_2_.refs_3_, ...), custom_call_target="tpu_custom_call" | custom-call | flops 201326592 | bytes 1572864 | tf_op jit(solution)/shard_map/wave/pallas_call | solution.py:240
  29.7 2.5 %wave.11 = (bf16[2,256,2048]{2,1,0:T(8,128)(2,1)S(1)}, f32[2,128,256]{2,1,0:T(8,128)S(1)}, bf16[2,128,256]{2,1,0:T(8,128)(2,1)S(1)}, bf16[4,128,512]{2,1,0:T(8,128)(2,1)S(1)}, bf16[4,16,512]{2,1,0:T(8,128)(2,1)S(1)}) custom-call(bf16[3,256,16]{2,1,0:T(8,128)(2,1)S(1)} %get-tuple-element.42.refs_0_, bf16[4,144,256]{2,1,0:T(8,128)(2,1)S(1)} %collect.7.refs_4_.refs_1_, ...), custom_call_target="tpu_custom_call" | custom-call | flops 268435456 | bytes 2097152 | tf_op jit(solution)/shard_map/wave/pallas_call | solution.py:240
  32.3 2.3 %wave.12 = (bf16[2,256,2048]{2,1,0:T(8,128)(2,1)S(1)}, f32[2,128,256]{2,1,0:T(8,128)S(1)}, bf16[2,128,256]{2,1,0:T(8,128)(2,1)S(1)}) custom-call(bf16[3,256,16]{2,1,0:T(8,128)(2,1)S(1)} %get-tuple-element.42.refs_0_, bf16[4,128,512]{2,1,0:T(8,128)(2,1)S(1)} %get-tuple-element.47.refs_1_, bf16[4,16,512]{2,1,0:T(8,128)(2,1)S(1)} %get-tuple-element.48.refs_2_, ...), custom_call_target="tpu_custom_call" | custom-call | flops 268435456 | bytes 2097152 | tf_op jit(solution)/shard_map/wave/pallas_call | solution.py:240
  34.6 2.3 %wave.13 = (bf16[2,256,2048]{2,1,0:T(8,128)(2,1)S(1)}, f32[2,128,256]{2,1,0:T(8,128)S(1)}, bf16[2,128,256]{2,1,0:T(8,128)(2,1)S(1)}) custom-call(bf16[3,256,16]{2,1,0:T(8,128)(2,1)S(1)} %get-tuple-element.42.refs_0_, bf16[4,128,512]{2,1,0:T(8,128)(2,1)S(1)} %get-tuple-element.47.refs_1_, bf16[4,16,512]{2,1,0:T(8,128)(2,1)S(1)} %get-tuple-element.48.refs_2_, ...), custom_call_target="tpu_custom_call" | custom-call | flops 268435456 | bytes 2097152 | tf_op jit(solution)/shard_map/wave/pallas_call | solution.py:240
  37.0 2.0 %collective-permute-start.12 = (bf16[2,128,256]{2,1,0:T(8,128)(2,1)S(1)}, bf16[2,128,256]{2,1,0:T(8,128)(2,1)S(1)}, u32[]{:S(2)}, u32[]{:S(2)}) collective-permute-start(bf16[2,128,256]{2,1,0:T(8,128)(2,1)S(1)} %get-tuple-element.50.refs_4_), channel_id=1, source_target_pairs={{0,8},{4,12},{8,0},{12,4},{16,24},{20,28},{24,16},{28,20},{1,9},{5... | collective-permute-start | bytes 393224 | tf_op jit(solution)/shard_map/ppermute | solution.py:533
  39.1 3.2 %pair.2.refs_7_.refs_4_ = f32[128,128]{1,0:T(8,128)S(1)} custom-call(s32[2,12]{1,0:T(2,128)S(1)} %copy-done.6, f32[3,256]{1,0:T(4,128)S(1)} %copy-done.3, bf16[144,256]{1,0:T(8,128)(2,1)S(1)} %get-tuple-element.39.refs_1_.refs_0_, bf16[144,256]{1,0:T(8,128)(2,1)S(1)} %collective-permute-done.refs_2_.refs_1_, ...), custom_call_target="tpu_custom_call" | custom-call | flops 418381824 | bytes 786432 | tf_op jit(solution)/shard_map/pair/pallas_call | solution.py:480
  42.4 1.4 %collective-permute-done.12.refs_4_ = bf16[2,128,256]{2,1,0:T(8,128)(2,1)S(1)} collective-permute-done((bf16[2,128,256]{2,1,0:T(8,128)(2,1)S(1)}, bf16[2,128,256]{2,1,0:T(8,128)(2,1)S(1)}, u32[]{:S(2)}, u32[]{:S(2)}) %collective-permute-start.12) | collective-permute-done | bytes 131104 | tf_op jit(solution)/shard_map/ppermute | solution.py:533
  43.8 1.4 %collective-permute-done.11.refs_3_ = bf16[2,128,256]{2,1,0:T(8,128)(2,1)S(1)} collective-permute-done((bf16[2,128,256]{2,1,0:T(8,128)(2,1)S(1)}, bf16[2,128,256]{2,1,0:T(8,128)(2,1)S(1)}, u32[]{:S(2)}, u32[]{:S(2)}) %collective-permute-start.11) | collective-permute-done | bytes 131104 | tf_op jit(solution)/shard_map/ppermute | solution.py:533
  47.7 1.7 %collective-permute-start.19 = (bf16[128,256]{1,0:T(8,128)(2,1)S(1)}, bf16[128,256]{1,0:T(8,128)(2,1)S(1)}, u32[]{:S(2)}, u32[]{:S(2)}) collective-permute-start(bf16[128,256]{1,0:T(8,128)(2,1)S(1)} %get-tuple-element.70), channel_id=1, source_target_pairs={{0,3},{1,2},{2,1},{3,0},{4,7},{5,6},{6,5},{7,4},{8,11},{9,10},{10,... | collective-permute-start | bytes 196616 | tf_op jit(solution)/shard_map/ppermute | solution.py:533
  52.0 1.7 %collective-permute-start.15 = (bf16[128,256]{1,0:T(8,128)(2,1)S(1)}, bf16[128,256]{1,0:T(8,128)(2,1)S(1)}, u32[]{:S(2)}, u32[]{:S(2)}) collective-permute-start(bf16[128,256]{1,0:T(8,128)(2,1)S(1)} %get-tuple-element.65), channel_id=1, source_target_pairs={{0,3},{1,2},{2,1},{3,0},{4,7},{5,6},{6,5},{7,4},{8,11},{9,10},{10,... | collective-permute-start | bytes 196616 | tf_op jit(solution)/shard_map/ppermute | solution.py:533
  55.6 1.8 %collective-permute-start.22 = (bf16[128,256]{1,0:T(8,128)(2,1)S(1)}, bf16[128,256]{1,0:T(8,128)(2,1)S(1)}, u32[]{:S(2)}, u32[]{:S(2)}) collective-permute-start(bf16[128,256]{1,0:T(8,128)(2,1)S(1)} %add_convert_fusion), channel_id=1, source_target_pairs={{0,16},{4,20},{8,24},{12,28},{16,0},{20,4},{24,8},{28,12},{1,17},{... | collective-permute-start | bytes 196616 | tf_op jit(solution)/shard_map/ppermute | solution.py:533
  57.4 3.2 %pair.3.refs_5_ = f32[128,128]{1,0:T(8,128)S(1)} custom-call(s32[2,12]{1,0:T(2,128)S(1)} %copy-done.6, f32[3,256]{1,0:T(4,128)S(1)} %copy-done.3, bf16[144,256]{1,0:T(8,128)(2,1)S(1)} %get-tuple-element.39.refs_1_.refs_0_, bf16[144,256]{1,0:T(8,128)(2,1)S(1)} %collective-permute-done.refs_2_.refs_1_, bf16[3,144,256]{2,1,0:T(8,128)(2,1)S(1)} %collect.4.refs_1_.refs_2_, ...), custom_call_target="tpu_custom_call" | custom-call | flops 418381824 | bytes 786432 | tf_op jit(solution)/shard_map/pair/pallas_call | solution.py:480
  61.5 1.3 %update.1 = bf16[256,128]{1,0:T(8,128)(2,1)} custom-call(bf16[256,128]{1,0:T(8,128)(2,1)S(1)} %copy-done, f32[1,128]{1,0:T(1,128)S(1)} %bitcast.2, bf16[128,512]{1,0:T(8,128)(2,1)S(1)} %copy-done.1, bf16[512,128]{1,0:T(8,128)(2,1)S(1)} %copy-done.2, f32[128,128]{1,0:T(8,128)S(1)} %pair.2.refs_7_.refs_4_, f32[128,128]{1,0:T(8,128)S(1)} %pair.3.refs_5_, ...), custom_call_target="tpu_custom_call" | custom-call | tf_op jit(solution)/shard_map/update/pallas_call | solution.py:522
  (59 shorter events, 13.3 us)
Async XLA Ops:
  1.0 5.2 %collective-permute-start = (bf16[144,256]{1,0:T(8,128)(2,1)S(1)}, bf16[144,256]{1,0:T(8,128)(2,1)S(1)}, u32[]{:S(2)}, u32[]{:S(2)}) collective-permute-start(bf16[144,256]{1,0:T(8,128)(2,1)S(1)} %get-tuple-element.39.refs_1_.refs_0_), channel_id=1, source_target_pairs={{0,4},{4,0},{8,12},{12,8},{16,20},{20,16},{24,28},{28,24},{1,5},{5... | collective-permute-start | bytes 221192 | tf_op jit(solution)/shard_map/ppermute | solution.py:533
  1.6 6.4 %collective-permute-start.1 = (bf16[144,256]{1,0:T(8,128)(2,1)S(1)}, bf16[144,256]{1,0:T(8,128)(2,1)S(1)}, u32[]{:S(2)}, u32[]{:S(2)}) collective-permute-start(bf16[144,256]{1,0:T(8,128)(2,1)S(1)} %get-tuple-element.39.refs_1_.refs_0_), channel_id=1, source_target_pairs={{0,3},{1,2},{2,1},{3,0},{4,7},{5,6},{6,5},{7,4},{8,11},{9,10},{10,... | collective-permute-start | bytes 221192 | tf_op jit(solution)/shard_map/ppermute | solution.py:533
  5.1 4.4 %collective-permute-start.2 = (bf16[144,256]{1,0:T(8,128)(2,1)S(1)}, bf16[144,256]{1,0:T(8,128)(2,1)S(1)}, u32[]{:S(2)}, u32[]{:S(2)}) collective-permute-start(bf16[144,256]{1,0:T(8,128)(2,1)S(1)} %get-tuple-element.39.refs_1_.refs_0_), channel_id=1, source_target_pairs={{0,2},{1,3},{2,0},{3,1},{4,6},{5,7},{6,4},{7,5},{8,10},{9,11},{10,... | collective-permute-start | bytes 221192 | tf_op jit(solution)/shard_map/ppermute | solution.py:533
  5.6 4.4 %collective-permute-start.3 = (bf16[144,256]{1,0:T(8,128)(2,1)S(1)}, bf16[144,256]{1,0:T(8,128)(2,1)S(1)}, u32[]{:S(2)}, u32[]{:S(2)}) collective-permute-start(bf16[144,256]{1,0:T(8,128)(2,1)S(1)} %get-tuple-element.39.refs_1_.refs_0_), channel_id=1, source_target_pairs={{0,1},{1,0},{2,3},{3,2},{4,5},{5,4},{6,7},{7,6},{8,9},{9,8},{10,11... | collective-permute-start | bytes 221192 | tf_op jit(solution)/shard_map/ppermute | solution.py:533
  10.0 10.7 %collective-permute-start.4 = (bf16[3,144,256]{2,1,0:T(8,128)(2,1)S(1)}, bf16[3,144,256]{2,1,0:T(8,128)(2,1)S(1)}, u32[]{:S(2)}, u32[]{:S(2)}) collective-permute-start(bf16[3,144,256]{2,1,0:T(8,128)(2,1)S(1)} %collect.4.refs_1_.refs_2_), channel_id=1, source_target_pairs={{0,4},{4,0},{8,12},{12,8},{16,20},{20,16},{24,28},{28,24},{1,5},{5... | collective-permute-start | bytes 663560 | tf_op jit(solution)/shard_map/ppermute | solution.py:533
  10.0 7.1 %collective-permute-start.6 = (bf16[144,256]{1,0:T(8,128)(2,1)S(1)}, bf16[144,256]{1,0:T(8,128)(2,1)S(1)}, u32[]{:S(2)}, u32[]{:S(2)}) collective-permute-start(bf16[144,256]{1,0:T(8,128)(2,1)S(1)} %get-tuple-element.39.refs_1_.refs_0_), channel_id=1, source_target_pairs={{0,16},{4,20},{8,24},{12,28},{16,0},{20,4},{24,8},{28,12},{1,17},{... | collective-permute-start | bytes 221192 | tf_op jit(solution)/shard_map/ppermute | solution.py:533
  17.2 5.3 %collective-permute-start.7 = (bf16[1,144,256]{2,1,0:T(8,128)(2,1)S(1)}, bf16[1,144,256]{2,1,0:T(8,128)(2,1)S(1)}, u32[]{:S(2)}, u32[]{:S(2)}) collective-permute-start(bf16[1,144,256]{2,1,0:T(8,128)(2,1)S(1)} %collect.6.refs_0_), channel_id=1, source_target_pairs={{0,3},{1,2},{2,1},{3,0},{4,7},{5,6},{6,5},{7,4},{8,11},{9,10},{10,... | collective-permute-start | bytes 221192 | tf_op jit(solution)/shard_map/ppermute | solution.py:533
  18.7 4.6 %collective-permute-start.8 = (bf16[1,144,256]{2,1,0:T(8,128)(2,1)S(1)}, bf16[1,144,256]{2,1,0:T(8,128)(2,1)S(1)}, u32[]{:S(2)}, u32[]{:S(2)}) collective-permute-start(bf16[1,144,256]{2,1,0:T(8,128)(2,1)S(1)} %collect.6.refs_0_), channel_id=1, source_target_pairs={{0,2},{1,3},{2,0},{3,1},{4,6},{5,7},{6,4},{7,5},{8,10},{9,11},{10,... | collective-permute-start | bytes 221192 | tf_op jit(solution)/shard_map/ppermute | solution.py:533
  20.0 4.4 %collective-permute-start.9 = (bf16[1,144,256]{2,1,0:T(8,128)(2,1)S(1)}, bf16[1,144,256]{2,1,0:T(8,128)(2,1)S(1)}, u32[]{:S(2)}, u32[]{:S(2)}) collective-permute-start(bf16[1,144,256]{2,1,0:T(8,128)(2,1)S(1)} %collect.6.refs_0_), channel_id=1, source_target_pairs={{0,1},{1,0},{2,3},{3,2},{4,5},{5,4},{6,7},{7,6},{8,9},{9,8},{10,11... | collective-permute-start | bytes 221192 | tf_op jit(solution)/shard_map/ppermute | solution.py:533
  24.4 5.3 %collective-permute-start.10 = (bf16[4,144,256]{2,1,0:T(8,128)(2,1)S(1)}, bf16[4,144,256]{2,1,0:T(8,128)(2,1)S(1)}, u32[]{:S(2)}, u32[]{:S(2)}) collective-permute-start(bf16[4,144,256]{2,1,0:T(8,128)(2,1)S(1)} %collect.7.refs_4_.refs_1_), channel_id=1, source_target_pairs={{0,4},{4,0},{8,12},{12,8},{16,20},{20,16},{24,28},{28,24},{1,5},{5... | collective-permute-start | bytes 884744 | tf_op jit(solution)/shard_map/ppermute | solution.py:533
  24.5 14.5 %collective-permute-start.5 = (bf16[4,144,256]{2,1,0:T(8,128)(2,1)S(1)}, bf16[4,144,256]{2,1,0:T(8,128)(2,1)S(1)}, u32[]{:S(2)}, u32[]{:S(2)}) collective-permute-start(bf16[4,144,256]{2,1,0:T(8,128)(2,1)S(1)} %collect.5), channel_id=1, source_target_pairs={{0,28},{4,8},{8,4},{12,16},{16,12},{20,24},{24,20},{28,0},{1,29},{... | collective-permute-start | bytes 884744 | tf_op jit(solution)/shard_map/ppermute | solution.py:583
  36.9 5.5 %collective-permute-start.13 = (bf16[2,128,256]{2,1,0:T(8,128)(2,1)S(1)}, bf16[2,128,256]{2,1,0:T(8,128)(2,1)S(1)}, u32[]{:S(2)}, u32[]{:S(2)}) collective-permute-start(bf16[2,128,256]{2,1,0:T(8,128)(2,1)S(1)} %get-tuple-element.51.refs_6_), channel_id=1, source_target_pairs={{0,8},{4,12},{8,0},{12,4},{16,24},{20,28},{24,16},{28,20},{1,9},{5... | collective-permute-start | bytes 393224 | tf_op jit(solution)/shard_map/ppermute | solution.py:533
  37.0 6.8 %collective-permute-start.12 = (bf16[2,128,256]{2,1,0:T(8,128)(2,1)S(1)}, bf16[2,128,256]{2,1,0:T(8,128)(2,1)S(1)}, u32[]{:S(2)}, u32[]{:S(2)}) collective-permute-start(bf16[2,128,256]{2,1,0:T(8,128)(2,1)S(1)} %get-tuple-element.50.refs_4_), channel_id=1, source_target_pairs={{0,8},{4,12},{8,0},{12,4},{16,24},{20,28},{24,16},{28,20},{1,9},{5... | collective-permute-start | bytes 393224 | tf_op jit(solution)/shard_map/ppermute | solution.py:533
  39.0 6.2 %collective-permute-start.11 = (bf16[2,128,256]{2,1,0:T(8,128)(2,1)S(1)}, bf16[2,128,256]{2,1,0:T(8,128)(2,1)S(1)}, u32[]{:S(2)}, u32[]{:S(2)}) collective-permute-start(bf16[2,128,256]{2,1,0:T(8,128)(2,1)S(1)} %get-tuple-element.49.refs_4_), channel_id=1, source_target_pairs={{0,8},{4,12},{8,0},{12,4},{16,24},{20,28},{24,16},{28,20},{1,9},{5... | collective-permute-start | bytes 393224 | tf_op jit(solution)/shard_map/ppermute | solution.py:533
  45.8 1.8 %collective-permute-start.18 = (bf16[128,1024]{1,0:T(8,128)(2,1)S(1)}, bf16[128,1024]{1,0:T(8,128)(2,1)S(1)}, u32[]{:S(2)}, u32[]{:S(2)}) collective-permute-start(bf16[128,1024]{1,0:T(8,128)(2,1)S(1)} %get-tuple-element.68), channel_id=1, source_target_pairs={{0,4},{4,0},{8,12},{12,8},{16,20},{20,16},{24,28},{28,24},{1,5},{5... | collective-permute-start | bytes 786440 | tf_op jit(solution)/shard_map/ppermute | solution.py:533
  46.5 5.4 %collective-permute-start.14 = (bf16[128,1024]{1,0:T(8,128)(2,1)S(1)}, bf16[128,1024]{1,0:T(8,128)(2,1)S(1)}, u32[]{:S(2)}, u32[]{:S(2)}) collective-permute-start(bf16[128,1024]{1,0:T(8,128)(2,1)S(1)} %inverse.4), channel_id=1, source_target_pairs={{0,4},{4,0},{8,12},{12,8},{16,20},{20,16},{24,28},{28,24},{1,5},{5... | collective-permute-start | bytes 786440 | tf_op jit(solution)/shard_map/ppermute | solution.py:533
  47.7 6.7 %collective-permute-start.19 = (bf16[128,256]{1,0:T(8,128)(2,1)S(1)}, bf16[128,256]{1,0:T(8,128)(2,1)S(1)}, u32[]{:S(2)}, u32[]{:S(2)}) collective-permute-start(bf16[128,256]{1,0:T(8,128)(2,1)S(1)} %get-tuple-element.70), channel_id=1, source_target_pairs={{0,3},{1,2},{2,1},{3,0},{4,7},{5,6},{6,5},{7,4},{8,11},{9,10},{10,... | collective-permute-start | bytes 196616 | tf_op jit(solution)/shard_map/ppermute | solution.py:533
  49.4 6.1 %collective-permute-start.20 = (bf16[128,256]{1,0:T(8,128)(2,1)S(1)}, bf16[128,256]{1,0:T(8,128)(2,1)S(1)}, u32[]{:S(2)}, u32[]{:S(2)}) collective-permute-start(bf16[128,256]{1,0:T(8,128)(2,1)S(1)} %get-tuple-element.71), channel_id=1, source_target_pairs={{0,2},{1,3},{2,0},{3,1},{4,6},{5,7},{6,4},{7,5},{8,10},{9,11},{10,... | collective-permute-start | bytes 196616 | tf_op jit(solution)/shard_map/ppermute | solution.py:533
  50.1 5.4 %collective-permute-start.21 = (bf16[128,256]{1,0:T(8,128)(2,1)S(1)}, bf16[128,256]{1,0:T(8,128)(2,1)S(1)}, u32[]{:S(2)}, u32[]{:S(2)}) collective-permute-start(bf16[128,256]{1,0:T(8,128)(2,1)S(1)} %get-tuple-element.72), channel_id=1, source_target_pairs={{0,1},{1,0},{2,3},{3,2},{4,5},{5,4},{6,7},{7,6},{8,9},{9,8},{10,11... | collective-permute-start | bytes 196616 | tf_op jit(solution)/shard_map/ppermute | solution.py:533
  51.8 9.7 %copy-start = (bf16[256,128]{1,0:T(8,128)(2,1)S(1)}, bf16[256,128]{1,0:T(8,128)(2,1)}, u32[]{:S(2)}) copy-start(bf16[256,128]{1,0:T(8,128)(2,1)} %refs_0_.3) | copy-start | bytes 196612
  52.0 8.6 %collective-permute-start.15 = (bf16[128,256]{1,0:T(8,128)(2,1)S(1)}, bf16[128,256]{1,0:T(8,128)(2,1)S(1)}, u32[]{:S(2)}, u32[]{:S(2)}) collective-permute-start(bf16[128,256]{1,0:T(8,128)(2,1)S(1)} %get-tuple-element.65), channel_id=1, source_target_pairs={{0,3},{1,2},{2,1},{3,0},{4,7},{5,6},{6,5},{7,4},{8,11},{9,10},{10,... | collective-permute-start | bytes 196616 | tf_op jit(solution)/shard_map/ppermute | solution.py:533
  53.6 7.0 %collective-permute-start.16 = (bf16[128,256]{1,0:T(8,128)(2,1)S(1)}, bf16[128,256]{1,0:T(8,128)(2,1)S(1)}, u32[]{:S(2)}, u32[]{:S(2)}) collective-permute-start(bf16[128,256]{1,0:T(8,128)(2,1)S(1)} %get-tuple-element.66), channel_id=1, source_target_pairs={{0,2},{1,3},{2,0},{3,1},{4,6},{5,7},{6,4},{7,5},{8,10},{9,11},{10,... | collective-permute-start | bytes 196616 | tf_op jit(solution)/shard_map/ppermute | solution.py:533
  54.4 6.2 %collective-permute-start.17 = (bf16[128,256]{1,0:T(8,128)(2,1)S(1)}, bf16[128,256]{1,0:T(8,128)(2,1)S(1)}, u32[]{:S(2)}, u32[]{:S(2)}) collective-permute-start(bf16[128,256]{1,0:T(8,128)(2,1)S(1)} %get-tuple-element.67), channel_id=1, source_target_pairs={{0,1},{1,0},{2,3},{3,2},{4,5},{5,4},{6,7},{7,6},{8,9},{9,8},{10,11... | collective-permute-start | bytes 196616 | tf_op jit(solution)/shard_map/ppermute | solution.py:533
  55.6 5.9 %collective-permute-start.22 = (bf16[128,256]{1,0:T(8,128)(2,1)S(1)}, bf16[128,256]{1,0:T(8,128)(2,1)S(1)}, u32[]{:S(2)}, u32[]{:S(2)}) collective-permute-start(bf16[128,256]{1,0:T(8,128)(2,1)S(1)} %add_convert_fusion), channel_id=1, source_target_pairs={{0,16},{4,20},{8,24},{12,28},{16,0},{20,4},{24,8},{28,12},{1,17},{... | collective-permute-start | bytes 196616 | tf_op jit(solution)/shard_map/ppermute | solution.py:533
  (6 other events, 49.5 us)

commit v9 on v8

--- a/solution.py
+++ b/solution.py
@@ -13,8 +13,8 @@
 F32 = jnp.float32
 BF16 = jnp.bfloat16
 
-SIN_COEF = (4.442879586561992, -7.307818050390618, 3.5977887417720016, -0.7912382192058507)
-SLACK = 1e-5
+SIN_COEF = (4.442866003912508, -7.307368462859549, 3.5940784351469652, -0.7825084116727845)
+SLACK = 1e-6
 TAIL = 16
 
 
@@ -633,13 +633,13 @@
     crossed_near = swap(away_near, "atoms", 1)
     here_far = inverse(filt, tables, runs(0, zs), shard, F32)
     sum_far, *sends = join(here_far, crossed_far, n_kvec)
-    for k in others:
+    for k in range(1, n_kvec):
         sum_far = sum_far + swap(sends[k - 1], "kvec", k).astype(F32)
     sum_far = sum_far.astype(BF16)
     here_near = inverse(filt, tables, runs(0, (0,)), shard, F32)
     own_near, *sends = join(here_near, crossed_near, n_kvec)
     parts = [own_near]
-    for k in others:
+    for k in range(1, n_kvec):
         parts.append(swap(sends[k - 1], "kvec", k))
     for z in zs:
         parts.append(swap(sum_far[:, (z - 1) * shard : z * shard], "atoms", 4 * z))

time: 62.9 us -> 63.2 us (level)
  transfers between devices with their start and end apart: 23 -> 23, of which waited for: 11 -> 12; matrix products, arithmetic and copies ran while one was open for 0% -> 0% of each run, Pallas kernels for 35% -> 35%
where the time goes in v9:
time: 63.2 us; the launch traced here: 63 us
  starting transfers between devices  26.1 us (41%)
  Pallas kernels  24.8 us (39%)
  waiting for transfers between devices  11.8 us (19%)
    ppermute x22, starting transfers between devices, swap(): lax.ppermute(value, axis, [(i, i ^ bits) for i in range(lax.axis_size(axi...  22.5 us
    pallas_call x7, Pallas kernels, wave(): pl.pallas_call(functools.partial(wave_kernel, tuple(picks), len(arrays),...  13.2 us
    ppermute x22, waiting for transfers between devices, swap(): lax.ppermute(value, axis, [(i, i ^ bits) for i in range(lax.axis_size(axi...  11.8 us
    pallas_call x2, Pallas kernels, pair_message(): pl.pallas_call(functools.partial(pair_kernel, nbasis, pieces, scale, pick...  6.35 us
    ppermute x1, starting transfers between devices, per_device(): lax.ppermute(collect([message, near_own], group), 'atoms', halo_pairs)  3.64 us
    pallas_call x3, Pallas kernels, inverse(): pl.pallas_call(functools.partial(inverse_kernel, pieces, shard), in_specs...  1.73 us
  transfers between devices with their start and end apart: 23, of which 12 were waited for; matrix products, arithmetic and copies ran while one was open for 0% of the time, Pallas kernels for 35%

profile of v9, /device:TPU:0, one launch (start us, length us, event | category | flops | bytes accessed | tf_op | source)
XLA Modules:
  0.0 63.0 jit_solution(9365563272648743242)
XLA Ops:
  1.6 3.5 %collective-permute-start.1 = (bf16[144,256]{1,0:T(8,128)(2,1)S(1)}, bf16[144,256]{1,0:T(8,128)(2,1)S(1)}, u32[]{:S(2)}, u32[]{:S(2)}) collective-permute-start(bf16[144,256]{1,0:T(8,128)(2,1)S(1)} %get-tuple-element.39.refs_1_.refs_0_), channel_id=1, source_target_pairs={{0,3},{1,2},{2,1},{3,0},{4,7},{5,6},{6,5},{7,4},{8,11},{9,10},{10,... | collective-permute-start | bytes 221192 | tf_op jit(solution)/shard_map/ppermute | solution.py:533
  6.2 1.5 %wave.7 = (bf16[6,256,512]{2,1,0:T(8,128)(2,1)S(1)}, f32[6,128,256]{2,1,0:T(8,128)S(1)}) custom-call(bf16[3,256,16]{2,1,0:T(8,128)(2,1)S(1)} %get-tuple-element.42.refs_0_, bf16[144,256]{1,0:T(8,128)(2,1)S(1)} %get-tuple-element.39.refs_1_.refs_0_, bf16[144,256]{1,0:T(8,128)(2,1)S(1)} %collective-permute-done.refs_2_.refs_1_), custom_call_target="tpu_custom_call" | custom-call | flops 201326592 | bytes 1572864 | tf_op jit(solution)/shard_map/wave/pallas_call | solution.py:240
  8.0 1.6 %collective-permute-done.2.refs_1_ = bf16[144,256]{1,0:T(8,128)(2,1)S(1)} collective-permute-done((bf16[144,256]{1,0:T(8,128)(2,1)S(1)}, bf16[144,256]{1,0:T(8,128)(2,1)S(1)}, u32[]{:S(2)}, u32[]{:S(2)}) %collective-permute-start.2) | collective-permute-done | bytes 73760 | tf_op jit(solution)/shard_map/ppermute | solution.py:533
  10.0 2.7 %collective-permute-start.6 = (bf16[144,256]{1,0:T(8,128)(2,1)S(1)}, bf16[144,256]{1,0:T(8,128)(2,1)S(1)}, u32[]{:S(2)}, u32[]{:S(2)}) collective-permute-start(bf16[144,256]{1,0:T(8,128)(2,1)S(1)} %get-tuple-element.39.refs_1_.refs_0_), channel_id=1, source_target_pairs={{0,16},{4,20},{8,24},{12,28},{16,0},{20,4},{24,8},{28,12},{1,17},{... | collective-permute-start | bytes 221192 | tf_op jit(solution)/shard_map/ppermute | solution.py:533
  12.7 1.5 %wave.8 = (bf16[6,256,512]{2,1,0:T(8,128)(2,1)S(1)}, f32[6,128,256]{2,1,0:T(8,128)S(1)}) custom-call(bf16[3,256,16]{2,1,0:T(8,128)(2,1)S(1)} %get-tuple-element.42.refs_0_, bf16[3,144,256]{2,1,0:T(8,128)(2,1)S(1)} %collect.4.refs_1_.refs_2_, f32[6,128,256]{2,1,0:T(8,128)S(1)} %get-tuple-element.43.refs_3_.refs_2_), custom_call_target="tpu_custom_call" | custom-call | flops 201326592 | bytes 1572864 | tf_op jit(solution)/shard_map/wave/pallas_call | solution.py:240
  14.2 3.0 %collective-permute-done.6.refs_0_ = bf16[144,256]{1,0:T(8,128)(2,1)S(1)} collective-permute-done((bf16[144,256]{1,0:T(8,128)(2,1)S(1)}, bf16[144,256]{1,0:T(8,128)(2,1)S(1)}, u32[]{:S(2)}, u32[]{:S(2)}) %collective-permute-start.6) | collective-permute-done | bytes 73760 | tf_op jit(solution)/shard_map/ppermute | solution.py:533
  17.2 1.5 %collective-permute-start.7 = (bf16[1,144,256]{2,1,0:T(8,128)(2,1)S(1)}, bf16[1,144,256]{2,1,0:T(8,128)(2,1)S(1)}, u32[]{:S(2)}, u32[]{:S(2)}) collective-permute-start(bf16[1,144,256]{2,1,0:T(8,128)(2,1)S(1)} %collect.6.refs_0_), channel_id=1, source_target_pairs={{0,3},{1,2},{2,1},{3,0},{4,7},{5,6},{6,5},{7,4},{8,11},{9,10},{10,... | collective-permute-start | bytes 221192 | tf_op jit(solution)/shard_map/ppermute | solution.py:533
  18.7 1.3 %collective-permute-start.8 = (bf16[1,144,256]{2,1,0:T(8,128)(2,1)S(1)}, bf16[1,144,256]{2,1,0:T(8,128)(2,1)S(1)}, u32[]{:S(2)}, u32[]{:S(2)}) collective-permute-start(bf16[1,144,256]{2,1,0:T(8,128)(2,1)S(1)} %collect.6.refs_0_), channel_id=1, source_target_pairs={{0,2},{1,3},{2,0},{3,1},{4,6},{5,7},{6,4},{7,5},{8,10},{9,11},{10,... | collective-permute-start | bytes 221192 | tf_op jit(solution)/shard_map/ppermute | solution.py:533
  20.7 1.5 %wave.9 = (bf16[6,256,512]{2,1,0:T(8,128)(2,1)S(1)}, f32[6,128,256]{2,1,0:T(8,128)S(1)}) custom-call(bf16[3,256,16]{2,1,0:T(8,128)(2,1)S(1)} %get-tuple-element.42.refs_0_, bf16[3,144,256]{2,1,0:T(8,128)(2,1)S(1)} %collect.4.refs_1_.refs_2_, bf16[3,144,256]{2,1,0:T(8,128)(2,1)S(1)} %collective-permute-done.4.refs_2_.refs_3_, ...), custom_call_target="tpu_custom_call" | custom-call | flops 201326592 | bytes 1572864 | tf_op jit(solution)/shard_map/wave/pallas_call | solution.py:240
  24.5 3.6 %collective-permute-start.5 = (bf16[4,144,256]{2,1,0:T(8,128)(2,1)S(1)}, bf16[4,144,256]{2,1,0:T(8,128)(2,1)S(1)}, u32[]{:S(2)}, u32[]{:S(2)}) collective-permute-start(bf16[4,144,256]{2,1,0:T(8,128)(2,1)S(1)} %collect.5), channel_id=1, source_target_pairs={{0,28},{4,8},{8,4},{12,16},{16,12},{20,24},{24,20},{28,0},{1,29},{... | collective-permute-start | bytes 884744 | tf_op jit(solution)/shard_map/ppermute | solution.py:583
  28.2 1.5 %wave.10 = (bf16[6,256,512]{2,1,0:T(8,128)(2,1)S(1)}, f32[6,128,256]{2,1,0:T(8,128)S(1)}) custom-call(bf16[3,256,16]{2,1,0:T(8,128)(2,1)S(1)} %get-tuple-element.42.refs_0_, bf16[3,144,256]{2,1,0:T(8,128)(2,1)S(1)} %collect.4.refs_1_.refs_2_, bf16[3,144,256]{2,1,0:T(8,128)(2,1)S(1)} %collective-permute-done.4.refs_2_.refs_3_, ...), custom_call_target="tpu_custom_call" | custom-call | flops 201326592 | bytes 1572864 | tf_op jit(solution)/shard_map/wave/pallas_call | solution.py:240
  29.7 2.5 %wave.11 = (bf16[2,256,2048]{2,1,0:T(8,128)(2,1)S(1)}, f32[2,128,256]{2,1,0:T(8,128)S(1)}, bf16[2,128,256]{2,1,0:T(8,128)(2,1)S(1)}, bf16[4,128,512]{2,1,0:T(8,128)(2,1)S(1)}, bf16[4,16,512]{2,1,0:T(8,128)(2,1)S(1)}) custom-call(bf16[3,256,16]{2,1,0:T(8,128)(2,1)S(1)} %get-tuple-element.42.refs_0_, bf16[4,144,256]{2,1,0:T(8,128)(2,1)S(1)} %collect.7.refs_4_.refs_1_, ...), custom_call_target="tpu_custom_call" | custom-call | flops 268435456 | bytes 2097152 | tf_op jit(solution)/shard_map/wave/pallas_call | solution.py:240
  32.3 2.3 %wave.12 = (bf16[2,256,2048]{2,1,0:T(8,128)(2,1)S(1)}, f32[2,128,256]{2,1,0:T(8,128)S(1)}, bf16[2,128,256]{2,1,0:T(8,128)(2,1)S(1)}) custom-call(bf16[3,256,16]{2,1,0:T(8,128)(2,1)S(1)} %get-tuple-element.42.refs_0_, bf16[4,128,512]{2,1,0:T(8,128)(2,1)S(1)} %get-tuple-element.47.refs_1_, bf16[4,16,512]{2,1,0:T(8,128)(2,1)S(1)} %get-tuple-element.48.refs_2_, ...), custom_call_target="tpu_custom_call" | custom-call | flops 268435456 | bytes 2097152 | tf_op jit(solution)/shard_map/wave/pallas_call | solution.py:240
  34.6 2.3 %wave.13 = (bf16[2,256,2048]{2,1,0:T(8,128)(2,1)S(1)}, f32[2,128,256]{2,1,0:T(8,128)S(1)}, bf16[2,128,256]{2,1,0:T(8,128)(2,1)S(1)}) custom-call(bf16[3,256,16]{2,1,0:T(8,128)(2,1)S(1)} %get-tuple-element.42.refs_0_, bf16[4,128,512]{2,1,0:T(8,128)(2,1)S(1)} %get-tuple-element.47.refs_1_, bf16[4,16,512]{2,1,0:T(8,128)(2,1)S(1)} %get-tuple-element.48.refs_2_, ...), custom_call_target="tpu_custom_call" | custom-call | flops 268435456 | bytes 2097152 | tf_op jit(solution)/shard_map/wave/pallas_call | solution.py:240
  37.0 2.0 %collective-permute-start.12 = (bf16[2,128,256]{2,1,0:T(8,128)(2,1)S(1)}, bf16[2,128,256]{2,1,0:T(8,128)(2,1)S(1)}, u32[]{:S(2)}, u32[]{:S(2)}) collective-permute-start(bf16[2,128,256]{2,1,0:T(8,128)(2,1)S(1)} %get-tuple-element.50.refs_4_), channel_id=1, source_target_pairs={{0,8},{4,12},{8,0},{12,4},{16,24},{20,28},{24,16},{28,20},{1,9},{5... | collective-permute-start | bytes 393224 | tf_op jit(solution)/shard_map/ppermute | solution.py:533
  39.1 3.2 %pair.2.refs_7_.refs_4_ = f32[128,128]{1,0:T(8,128)S(1)} custom-call(s32[2,12]{1,0:T(2,128)S(1)} %copy-done.6, f32[3,256]{1,0:T(4,128)S(1)} %copy-done.3, bf16[144,256]{1,0:T(8,128)(2,1)S(1)} %get-tuple-element.39.refs_1_.refs_0_, bf16[144,256]{1,0:T(8,128)(2,1)S(1)} %collective-permute-done.refs_2_.refs_1_, ...), custom_call_target="tpu_custom_call" | custom-call | flops 418381824 | bytes 786432 | tf_op jit(solution)/shard_map/pair/pallas_call | solution.py:480
  42.4 1.4 %collective-permute-done.12.refs_4_ = bf16[2,128,256]{2,1,0:T(8,128)(2,1)S(1)} collective-permute-done((bf16[2,128,256]{2,1,0:T(8,128)(2,1)S(1)}, bf16[2,128,256]{2,1,0:T(8,128)(2,1)S(1)}, u32[]{:S(2)}, u32[]{:S(2)}) %collective-permute-start.12) | collective-permute-done | bytes 131104 | tf_op jit(solution)/shard_map/ppermute | solution.py:533
  43.8 1.4 %collective-permute-done.11.refs_3_ = bf16[2,128,256]{2,1,0:T(8,128)(2,1)S(1)} collective-permute-done((bf16[2,128,256]{2,1,0:T(8,128)(2,1)S(1)}, bf16[2,128,256]{2,1,0:T(8,128)(2,1)S(1)}, u32[]{:S(2)}, u32[]{:S(2)}) %collective-permute-start.11) | collective-permute-done | bytes 131104 | tf_op jit(solution)/shard_map/ppermute | solution.py:533
  48.7 1.3 %collective-permute-start.20 = (bf16[128,256]{1,0:T(8,128)(2,1)S(1)}, bf16[128,256]{1,0:T(8,128)(2,1)S(1)}, u32[]{:S(2)}, u32[]{:S(2)}) collective-permute-start(bf16[128,256]{1,0:T(8,128)(2,1)S(1)} %get-tuple-element.71), channel_id=1, source_target_pairs={{0,2},{1,3},{2,0},{3,1},{4,6},{5,7},{6,4},{7,5},{8,10},{9,11},{10,... | collective-permute-start | bytes 196616 | tf_op jit(solution)/shard_map/ppermute | solution.py:533
  50.0 1.3 %collective-permute-start.21 = (bf16[128,256]{1,0:T(8,128)(2,1)S(1)}, bf16[128,256]{1,0:T(8,128)(2,1)S(1)}, u32[]{:S(2)}, u32[]{:S(2)}) collective-permute-start(bf16[128,256]{1,0:T(8,128)(2,1)S(1)} %get-tuple-element.72), channel_id=1, source_target_pairs={{0,3},{1,2},{2,1},{3,0},{4,7},{5,6},{6,5},{7,4},{8,11},{9,10},{10,... | collective-permute-start | bytes 196616 | tf_op jit(solution)/shard_map/ppermute | solution.py:533
  52.9 1.3 %collective-permute-start.16 = (bf16[128,256]{1,0:T(8,128)(2,1)S(1)}, bf16[128,256]{1,0:T(8,128)(2,1)S(1)}, u32[]{:S(2)}, u32[]{:S(2)}) collective-permute-start(bf16[128,256]{1,0:T(8,128)(2,1)S(1)} %get-tuple-element.66), channel_id=1, source_target_pairs={{0,2},{1,3},{2,0},{3,1},{4,6},{5,7},{6,4},{7,5},{8,10},{9,11},{10,... | collective-permute-start | bytes 196616 | tf_op jit(solution)/shard_map/ppermute | solution.py:533
  54.2 1.3 %collective-permute-start.17 = (bf16[128,256]{1,0:T(8,128)(2,1)S(1)}, bf16[128,256]{1,0:T(8,128)(2,1)S(1)}, u32[]{:S(2)}, u32[]{:S(2)}) collective-permute-start(bf16[128,256]{1,0:T(8,128)(2,1)S(1)} %get-tuple-element.67), channel_id=1, source_target_pairs={{0,3},{1,2},{2,1},{3,0},{4,7},{5,6},{6,5},{7,4},{8,11},{9,10},{10,... | collective-permute-start | bytes 196616 | tf_op jit(solution)/shard_map/ppermute | solution.py:533
  55.8 1.6 %collective-permute-start.22 = (bf16[128,256]{1,0:T(8,128)(2,1)S(1)}, bf16[128,256]{1,0:T(8,128)(2,1)S(1)}, u32[]{:S(2)}, u32[]{:S(2)}) collective-permute-start(bf16[128,256]{1,0:T(8,128)(2,1)S(1)} %add_convert_fusion), channel_id=1, source_target_pairs={{0,16},{4,20},{8,24},{12,28},{16,0},{20,4},{24,8},{28,12},{1,17},{... | collective-permute-start | bytes 196616 | tf_op jit(solution)/shard_map/ppermute | solution.py:533
  57.4 3.2 %pair.3.refs_5_ = f32[128,128]{1,0:T(8,128)S(1)} custom-call(s32[2,12]{1,0:T(2,128)S(1)} %copy-done.6, f32[3,256]{1,0:T(4,128)S(1)} %copy-done.3, bf16[144,256]{1,0:T(8,128)(2,1)S(1)} %get-tuple-element.39.refs_1_.refs_0_, bf16[144,256]{1,0:T(8,128)(2,1)S(1)} %collective-permute-done.refs_2_.refs_1_, bf16[3,144,256]{2,1,0:T(8,128)(2,1)S(1)} %collect.4.refs_1_.refs_2_, ...), custom_call_target="tpu_custom_call" | custom-call | flops 418381824 | bytes 786432 | tf_op jit(solution)/shard_map/pair/pallas_call | solution.py:480
  (59 shorter events, 14.4 us)
Async XLA Ops:
  1.0 5.2 %collective-permute-start = (bf16[144,256]{1,0:T(8,128)(2,1)S(1)}, bf16[144,256]{1,0:T(8,128)(2,1)S(1)}, u32[]{:S(2)}, u32[]{:S(2)}) collective-permute-start(bf16[144,256]{1,0:T(8,128)(2,1)S(1)} %get-tuple-element.39.refs_1_.refs_0_), channel_id=1, source_target_pairs={{0,4},{4,0},{8,12},{12,8},{16,20},{20,16},{24,28},{28,24},{1,5},{5... | collective-permute-start | bytes 221192 | tf_op jit(solution)/shard_map/ppermute | solution.py:533
  1.6 6.4 %collective-permute-start.1 = (bf16[144,256]{1,0:T(8,128)(2,1)S(1)}, bf16[144,256]{1,0:T(8,128)(2,1)S(1)}, u32[]{:S(2)}, u32[]{:S(2)}) collective-permute-start(bf16[144,256]{1,0:T(8,128)(2,1)S(1)} %get-tuple-element.39.refs_1_.refs_0_), channel_id=1, source_target_pairs={{0,3},{1,2},{2,1},{3,0},{4,7},{5,6},{6,5},{7,4},{8,11},{9,10},{10,... | collective-permute-start | bytes 221192 | tf_op jit(solution)/shard_map/ppermute | solution.py:533
  5.1 4.4 %collective-permute-start.2 = (bf16[144,256]{1,0:T(8,128)(2,1)S(1)}, bf16[144,256]{1,0:T(8,128)(2,1)S(1)}, u32[]{:S(2)}, u32[]{:S(2)}) collective-permute-start(bf16[144,256]{1,0:T(8,128)(2,1)S(1)} %get-tuple-element.39.refs_1_.refs_0_), channel_id=1, source_target_pairs={{0,2},{1,3},{2,0},{3,1},{4,6},{5,7},{6,4},{7,5},{8,10},{9,11},{10,... | collective-permute-start | bytes 221192 | tf_op jit(solution)/shard_map/ppermute | solution.py:533
  5.6 4.4 %collective-permute-start.3 = (bf16[144,256]{1,0:T(8,128)(2,1)S(1)}, bf16[144,256]{1,0:T(8,128)(2,1)S(1)}, u32[]{:S(2)}, u32[]{:S(2)}) collective-permute-start(bf16[144,256]{1,0:T(8,128)(2,1)S(1)} %get-tuple-element.39.refs_1_.refs_0_), channel_id=1, source_target_pairs={{0,1},{1,0},{2,3},{3,2},{4,5},{5,4},{6,7},{7,6},{8,9},{9,8},{10,11... | collective-permute-start | bytes 221192 | tf_op jit(solution)/shard_map/ppermute | solution.py:533
  10.0 10.7 %collective-permute-start.4 = (bf16[3,144,256]{2,1,0:T(8,128)(2,1)S(1)}, bf16[3,144,256]{2,1,0:T(8,128)(2,1)S(1)}, u32[]{:S(2)}, u32[]{:S(2)}) collective-permute-start(bf16[3,144,256]{2,1,0:T(8,128)(2,1)S(1)} %collect.4.refs_1_.refs_2_), channel_id=1, source_target_pairs={{0,4},{4,0},{8,12},{12,8},{16,20},{20,16},{24,28},{28,24},{1,5},{5... | collective-permute-start | bytes 663560 | tf_op jit(solution)/shard_map/ppermute | solution.py:533
  10.0 7.1 %collective-permute-start.6 = (bf16[144,256]{1,0:T(8,128)(2,1)S(1)}, bf16[144,256]{1,0:T(8,128)(2,1)S(1)}, u32[]{:S(2)}, u32[]{:S(2)}) collective-permute-start(bf16[144,256]{1,0:T(8,128)(2,1)S(1)} %get-tuple-element.39.refs_1_.refs_0_), channel_id=1, source_target_pairs={{0,16},{4,20},{8,24},{12,28},{16,0},{20,4},{24,8},{28,12},{1,17},{... | collective-permute-start | bytes 221192 | tf_op jit(solution)/shard_map/ppermute | solution.py:533
  17.2 5.3 %collective-permute-start.7 = (bf16[1,144,256]{2,1,0:T(8,128)(2,1)S(1)}, bf16[1,144,256]{2,1,0:T(8,128)(2,1)S(1)}, u32[]{:S(2)}, u32[]{:S(2)}) collective-permute-start(bf16[1,144,256]{2,1,0:T(8,128)(2,1)S(1)} %collect.6.refs_0_), channel_id=1, source_target_pairs={{0,3},{1,2},{2,1},{3,0},{4,7},{5,6},{6,5},{7,4},{8,11},{9,10},{10,... | collective-permute-start | bytes 221192 | tf_op jit(solution)/shard_map/ppermute | solution.py:533
  18.7 4.6 %collective-permute-start.8 = (bf16[1,144,256]{2,1,0:T(8,128)(2,1)S(1)}, bf16[1,144,256]{2,1,0:T(8,128)(2,1)S(1)}, u32[]{:S(2)}, u32[]{:S(2)}) collective-permute-start(bf16[1,144,256]{2,1,0:T(8,128)(2,1)S(1)} %collect.6.refs_0_), channel_id=1, source_target_pairs={{0,2},{1,3},{2,0},{3,1},{4,6},{5,7},{6,4},{7,5},{8,10},{9,11},{10,... | collective-permute-start | bytes 221192 | tf_op jit(solution)/shard_map/ppermute | solution.py:533
  20.0 4.4 %collective-permute-start.9 = (bf16[1,144,256]{2,1,0:T(8,128)(2,1)S(1)}, bf16[1,144,256]{2,1,0:T(8,128)(2,1)S(1)}, u32[]{:S(2)}, u32[]{:S(2)}) collective-permute-start(bf16[1,144,256]{2,1,0:T(8,128)(2,1)S(1)} %collect.6.refs_0_), channel_id=1, source_target_pairs={{0,1},{1,0},{2,3},{3,2},{4,5},{5,4},{6,7},{7,6},{8,9},{9,8},{10,11... | collective-permute-start | bytes 221192 | tf_op jit(solution)/shard_map/ppermute | solution.py:533
  24.4 5.3 %collective-permute-start.10 = (bf16[4,144,256]{2,1,0:T(8,128)(2,1)S(1)}, bf16[4,144,256]{2,1,0:T(8,128)(2,1)S(1)}, u32[]{:S(2)}, u32[]{:S(2)}) collective-permute-start(bf16[4,144,256]{2,1,0:T(8,128)(2,1)S(1)} %collect.7.refs_4_.refs_1_), channel_id=1, source_target_pairs={{0,4},{4,0},{8,12},{12,8},{16,20},{20,16},{24,28},{28,24},{1,5},{5... | collective-permute-start | bytes 884744 | tf_op jit(solution)/shard_map/ppermute | solution.py:533
  24.5 14.5 %collective-permute-start.5 = (bf16[4,144,256]{2,1,0:T(8,128)(2,1)S(1)}, bf16[4,144,256]{2,1,0:T(8,128)(2,1)S(1)}, u32[]{:S(2)}, u32[]{:S(2)}) collective-permute-start(bf16[4,144,256]{2,1,0:T(8,128)(2,1)S(1)} %collect.5), channel_id=1, source_target_pairs={{0,28},{4,8},{8,4},{12,16},{16,12},{20,24},{24,20},{28,0},{1,29},{... | collective-permute-start | bytes 884744 | tf_op jit(solution)/shard_map/ppermute | solution.py:583
  36.9 5.5 %collective-permute-start.13 = (bf16[2,128,256]{2,1,0:T(8,128)(2,1)S(1)}, bf16[2,128,256]{2,1,0:T(8,128)(2,1)S(1)}, u32[]{:S(2)}, u32[]{:S(2)}) collective-permute-start(bf16[2,128,256]{2,1,0:T(8,128)(2,1)S(1)} %get-tuple-element.51.refs_6_), channel_id=1, source_target_pairs={{0,8},{4,12},{8,0},{12,4},{16,24},{20,28},{24,16},{28,20},{1,9},{5... | collective-permute-start | bytes 393224 | tf_op jit(solution)/shard_map/ppermute | solution.py:533
  37.0 6.8 %collective-permute-start.12 = (bf16[2,128,256]{2,1,0:T(8,128)(2,1)S(1)}, bf16[2,128,256]{2,1,0:T(8,128)(2,1)S(1)}, u32[]{:S(2)}, u32[]{:S(2)}) collective-permute-start(bf16[2,128,256]{2,1,0:T(8,128)(2,1)S(1)} %get-tuple-element.50.refs_4_), channel_id=1, source_target_pairs={{0,8},{4,12},{8,0},{12,4},{16,24},{20,28},{24,16},{28,20},{1,9},{5... | collective-permute-start | bytes 393224 | tf_op jit(solution)/shard_map/ppermute | solution.py:533
  39.0 6.2 %collective-permute-start.11 = (bf16[2,128,256]{2,1,0:T(8,128)(2,1)S(1)}, bf16[2,128,256]{2,1,0:T(8,128)(2,1)S(1)}, u32[]{:S(2)}, u32[]{:S(2)}) collective-permute-start(bf16[2,128,256]{2,1,0:T(8,128)(2,1)S(1)} %get-tuple-element.49.refs_4_), channel_id=1, source_target_pairs={{0,8},{4,12},{8,0},{12,4},{16,24},{20,28},{24,16},{28,20},{1,9},{5... | collective-permute-start | bytes 393224 | tf_op jit(solution)/shard_map/ppermute | solution.py:533
  45.8 1.8 %collective-permute-start.18 = (bf16[128,1024]{1,0:T(8,128)(2,1)S(1)}, bf16[128,1024]{1,0:T(8,128)(2,1)S(1)}, u32[]{:S(2)}, u32[]{:S(2)}) collective-permute-start(bf16[128,1024]{1,0:T(8,128)(2,1)S(1)} %get-tuple-element.68), channel_id=1, source_target_pairs={{0,4},{4,0},{8,12},{12,8},{16,20},{20,16},{24,28},{28,24},{1,5},{5... | collective-permute-start | bytes 786440 | tf_op jit(solution)/shard_map/ppermute | solution.py:533
  46.5 5.4 %collective-permute-start.14 = (bf16[128,1024]{1,0:T(8,128)(2,1)S(1)}, bf16[128,1024]{1,0:T(8,128)(2,1)S(1)}, u32[]{:S(2)}, u32[]{:S(2)}) collective-permute-start(bf16[128,1024]{1,0:T(8,128)(2,1)S(1)} %inverse.4), channel_id=1, source_target_pairs={{0,4},{4,0},{8,12},{12,8},{16,20},{20,16},{24,28},{28,24},{1,5},{5... | collective-permute-start | bytes 786440 | tf_op jit(solution)/shard_map/ppermute | solution.py:533
  47.7 6.5 %collective-permute-start.19 = (bf16[128,256]{1,0:T(8,128)(2,1)S(1)}, bf16[128,256]{1,0:T(8,128)(2,1)S(1)}, u32[]{:S(2)}, u32[]{:S(2)}) collective-permute-start(bf16[128,256]{1,0:T(8,128)(2,1)S(1)} %get-tuple-element.70), channel_id=1, source_target_pairs={{0,1},{1,0},{2,3},{3,2},{4,5},{5,4},{6,7},{7,6},{8,9},{9,8},{10,11... | collective-permute-start | bytes 196616 | tf_op jit(solution)/shard_map/ppermute | solution.py:533
  48.7 6.9 %collective-permute-start.20 = (bf16[128,256]{1,0:T(8,128)(2,1)S(1)}, bf16[128,256]{1,0:T(8,128)(2,1)S(1)}, u32[]{:S(2)}, u32[]{:S(2)}) collective-permute-start(bf16[128,256]{1,0:T(8,128)(2,1)S(1)} %get-tuple-element.71), channel_id=1, source_target_pairs={{0,2},{1,3},{2,0},{3,1},{4,6},{5,7},{6,4},{7,5},{8,10},{9,11},{10,... | collective-permute-start | bytes 196616 | tf_op jit(solution)/shard_map/ppermute | solution.py:533
  50.0 5.8 %collective-permute-start.21 = (bf16[128,256]{1,0:T(8,128)(2,1)S(1)}, bf16[128,256]{1,0:T(8,128)(2,1)S(1)}, u32[]{:S(2)}, u32[]{:S(2)}) collective-permute-start(bf16[128,256]{1,0:T(8,128)(2,1)S(1)} %get-tuple-element.72), channel_id=1, source_target_pairs={{0,3},{1,2},{2,1},{3,0},{4,7},{5,6},{6,5},{7,4},{8,11},{9,10},{10,... | collective-permute-start | bytes 196616 | tf_op jit(solution)/shard_map/ppermute | solution.py:533
  51.8 9.9 %copy-start = (bf16[256,128]{1,0:T(8,128)(2,1)S(1)}, bf16[256,128]{1,0:T(8,128)(2,1)}, u32[]{:S(2)}) copy-start(bf16[256,128]{1,0:T(8,128)(2,1)} %refs_0_.3) | copy-start | bytes 196612
  52.0 8.6 %collective-permute-start.15 = (bf16[128,256]{1,0:T(8,128)(2,1)S(1)}, bf16[128,256]{1,0:T(8,128)(2,1)S(1)}, u32[]{:S(2)}, u32[]{:S(2)}) collective-permute-start(bf16[128,256]{1,0:T(8,128)(2,1)S(1)} %get-tuple-element.65), channel_id=1, source_target_pairs={{0,1},{1,0},{2,3},{3,2},{4,5},{5,4},{6,7},{7,6},{8,9},{9,8},{10,11... | collective-permute-start | bytes 196616 | tf_op jit(solution)/shard_map/ppermute | solution.py:533
  52.9 7.7 %collective-permute-start.16 = (bf16[128,256]{1,0:T(8,128)(2,1)S(1)}, bf16[128,256]{1,0:T(8,128)(2,1)S(1)}, u32[]{:S(2)}, u32[]{:S(2)}) collective-permute-start(bf16[128,256]{1,0:T(8,128)(2,1)S(1)} %get-tuple-element.66), channel_id=1, source_target_pairs={{0,2},{1,3},{2,0},{3,1},{4,6},{5,7},{6,4},{7,5},{8,10},{9,11},{10,... | collective-permute-start | bytes 196616 | tf_op jit(solution)/shard_map/ppermute | solution.py:533
  54.2 6.4 %collective-permute-start.17 = (bf16[128,256]{1,0:T(8,128)(2,1)S(1)}, bf16[128,256]{1,0:T(8,128)(2,1)S(1)}, u32[]{:S(2)}, u32[]{:S(2)}) collective-permute-start(bf16[128,256]{1,0:T(8,128)(2,1)S(1)} %get-tuple-element.67), channel_id=1, source_target_pairs={{0,3},{1,2},{2,1},{3,0},{4,7},{5,6},{6,5},{7,4},{8,11},{9,10},{10,... | collective-permute-start | bytes 196616 | tf_op jit(solution)/shard_map/ppermute | solution.py:533
  55.8 5.9 %collective-permute-start.22 = (bf16[128,256]{1,0:T(8,128)(2,1)S(1)}, bf16[128,256]{1,0:T(8,128)(2,1)S(1)}, u32[]{:S(2)}, u32[]{:S(2)}) collective-permute-start(bf16[128,256]{1,0:T(8,128)(2,1)S(1)} %add_convert_fusion), channel_id=1, source_target_pairs={{0,16},{4,20},{8,24},{12,28},{16,0},{20,4},{24,8},{28,12},{1,17},{... | collective-permute-start | bytes 196616 | tf_op jit(solution)/shard_map/ppermute | solution.py:533
  (6 other events, 50.2 us)
